TPU v7x, 32 devices: a whole 2x2x4 slice. The times are simulated.
32 devices in a mesh: mode: 8 (over z, y), elem: 4 (over x, core).
Axes of the slice: x: 2, y: 2, z: 4, core: 2. Of those that a mesh axis runs over, the one named last changes fastest.
Arguments:
- velocity: float32 [3, 256, 4, 7, 7, 512], P(None, 'mode', None, None, None, 'elem'), may hold values from -0.3 to 0.3
- radial_dx: float32 [4, 7, 7, 512], P(None, None, None, 'elem'), may hold values from 0.5 to 2
- radial_dy: float32 [4, 7, 7, 512], P(None, None, None, 'elem'), may hold values from -0.5 to 0.5
- around_dx: float32 [4, 7, 7, 512], P(None, None, None, 'elem'), may hold values from -0.5 to 0.5
- around_dy: float32 [4, 7, 7, 512], P(None, None, None, 'elem'), may hold values from 0.5 to 2
- jacobian: float32 [4, 7, 7, 512], P(None, None, None, 'elem'), may hold values from 0.5 to 2
Outputs:
- advection: float32 [3, 256, 4, 7, 7, 512], P(None, 'mode', None, None, None, 'elem')
- pressure: float32 [256, 4, 7, 7, 512], P('mode', None, None, None, 'elem')
All inputs are finite; a program needn't handle non-finite values.
Results may differ from a plain program's by a relative error of at most 0.0003.
Values sent between devices are 32-bit elements; how exact they have to be, the bound alone decides.
No kernel may reach another device: no remote copies, remote signals or barrier semaphores. Data moves between devices by JAX's collectives and lax.ppermute only.
A program may use at most 256 MiB of HBM per device.

v0:
```python
import math

import jax
import jax.numpy as jnp
import numpy as np
from jax import lax
from jax.sharding import PartitionSpec as P

NODES = 7
ITERS = 3


spanwise_wave = 2.0 * math.pi / 64.0
time_step = 0.1


def padded_2(value, sides, width):
    for axis, dim in sides:
        size, length = (lax.axis_size(axis), value.shape[dim])
        up = [(i, (i + 1) % size) for i in range(size)]
        down = [(j, i) for i, j in up]
        last = lax.slice_in_dim(value, length - width, length, axis=dim)
        leading = lax.slice_in_dim(value, 0, width, axis=dim)
        before = lax.ppermute(last, axis, up)
        after = lax.ppermute(leading, axis, down)
        value = jnp.concatenate([before, value, after], axis=dim)
    return value


def lobatto_rule(count):
    degree = count - 1
    points = np.cos(np.pi * np.arange(count) / degree)
    legendre = np.zeros((count, count))
    for sweep in range(60):
        legendre[:, 0] = 1.0
        legendre[:, 1] = points
        for order in range(2, count):
            legendre[:, order] = (
                (2 * order - 1) * points * legendre[:, order - 1]
                - (order - 1) * legendre[:, order - 2]
            ) / order
        points = points - (points * legendre[:, degree] - legendre[:, degree - 1]) / (
            count * legendre[:, degree]
        )
    legendre[:, 0] = 1.0
    legendre[:, 1] = points
    for order in range(2, count):
        legendre[:, order] = (
            (2 * order - 1) * points * legendre[:, order - 1] - (order - 1) * legendre[:, order - 2]
        ) / order
    weights = 2.0 / (degree * count * legendre[:, degree] ** 2)
    return (points[::-1].copy(), weights[::-1].copy())


def derivative_table():
    lobatto_nodes = lobatto_rule(NODES)[0]
    total = lobatto_nodes.shape[0]
    scales = np.ones(total)
    for column in range(total):
        for other in range(total):
            if other != column:
                scales[column] = scales[column] / (lobatto_nodes[column] - lobatto_nodes[other])
    table = np.zeros((total, total))
    for row in range(total):
        for column in range(total):
            if row != column:
                table[row, column] = (
                    scales[column] / scales[row] / (lobatto_nodes[row] - lobatto_nodes[column])
                )
        table[row, row] = -np.sum(table[row])
    return table


def radial_derivative(table, field):
    return jnp.einsum("ia,...abe->...ibe", table, field, precision=lax.Precision.HIGHEST)


def around_derivative(table, field):
    return jnp.einsum("jb,...abe->...aje", table, field, precision=lax.Precision.HIGHEST)


def radial_transpose(table, field):
    return jnp.einsum("ia,...ibe->...abe", table, field, precision=lax.Precision.HIGHEST)


def around_transpose(table, field):
    return jnp.einsum("jb,...aje->...abe", table, field, precision=lax.Precision.HIGHEST)


def z_derivative(field, first_pair):
    shape = field.shape
    count = shape[1] // 2
    pairs = field.reshape((shape[0], count, 2) + shape[2:])
    waves = (first_pair + jnp.arange(count, dtype=jnp.int32)).astype(jnp.float32) * spanwise_wave
    waves = waves.reshape((1, count) + (1,) * (len(shape) - 2))
    return jnp.stack([waves * pairs[:, :, 1], -waves * pairs[:, :, 0]], axis=2).reshape(shape)


def transform_tables(planes):
    position = jnp.arange(planes, dtype=jnp.int32)
    plane = jnp.arange(planes, dtype=jnp.int32)
    order = plane // 2
    turns = position[:, None] * order[None, :] % planes
    angle = 2.0 * math.pi / planes * turns.astype(jnp.float32)
    cosine = jnp.cos(angle)
    sine = jnp.sin(angle)
    is_sine = (plane % 2 == 1)[None, :]
    is_top = (plane == 1)[None, :]
    parity = jnp.cos(math.pi * (position % 2).astype(jnp.float32))[:, None]
    basis = jnp.where(is_top, parity, jnp.where(is_sine, sine, cosine))
    scaling = jnp.where(order == 0, 1.0, 2.0).astype(jnp.float32) / planes
    inverse = jnp.transpose(basis * scaling[None, :])
    wave = (order.astype(jnp.float32) * spanwise_wave)[None, :]
    slope = jnp.where(is_sine, wave * cosine, -wave * sine)
    return (basis, inverse, slope)


def geometry(radial_dx, radial_dy, around_dx, around_dy, jacobian):
    lobatto_weights = lobatto_rule(NODES)[1]
    quadrature = jnp.asarray(np.outer(lobatto_weights, lobatto_weights), jnp.float32)[:, :, None]
    mass = quadrature * jacobian
    radial_stiff = mass * (radial_dx * radial_dx + radial_dy * radial_dy)
    cross_stiff = mass * (radial_dx * around_dx + radial_dy * around_dy)
    around_stiff = mass * (around_dx * around_dx + around_dy * around_dy)
    return (radial_stiff, cross_stiff, around_stiff, mass)


def node_weights(layers):
    layer = jnp.arange(layers, dtype=jnp.int32).reshape(layers, 1, 1, 1)
    node = jnp.arange(NODES, dtype=jnp.int32)
    radial_node = node.reshape(1, NODES, 1, 1)
    around_node = node.reshape(1, 1, NODES, 1)
    shared_radial = (radial_node == NODES - 1) & (layer < layers - 1) | (radial_node == 0) & (
        layer > 0
    )
    shared_around = (around_node == 0) | (around_node == NODES - 1)
    multiplicity = (1.0 + shared_radial.astype(jnp.float32)) * (
        1.0 + shared_around.astype(jnp.float32)
    )
    boundary = (radial_node == NODES - 1) & (layer == layers - 1)
    mask = 1.0 - boundary.astype(jnp.float32)
    return (mask, mask / multiplicity)


def plane_shift(first_plane, count, planes):
    plane = first_plane + jnp.arange(count, dtype=jnp.int32)
    order = jnp.where(plane == 1, planes // 2, plane // 2)
    wave = order.astype(jnp.float32) * spanwise_wave
    return (wave * wave).reshape(count, 1, 1, 1, 1)


def helmholtz_local(table, field, shift, metrics):
    radial_stiff, cross_stiff, around_stiff, mass = metrics
    radial = radial_derivative(table, field)
    beside_all = around_derivative(table, field)
    return (
        radial_transpose(table, radial_stiff * radial + cross_stiff * beside_all)
        + around_transpose(table, cross_stiff * radial + around_stiff * beside_all)
        + shift * mass * field
    )


def assemble(field):
    lower = field[:, :-1, -1] + field[:, 1:, 0]
    field = field.at[:, :-1, -1].set(lower).at[:, 1:, 0].set(lower)
    first = field[:, :, :, 0]
    last = field[:, :, :, -1]
    rims = jnp.concatenate([first[..., :1], last[..., -1:]], axis=3)
    padded = padded_2(rims, (("elem", 3),), 1)
    after = jnp.concatenate([first[..., 1:], padded[..., 3:4]], axis=3)
    right = last + after
    left = jnp.concatenate([padded[..., 0:1] + first[..., :1], right[..., :-1]], axis=3)
    return field.at[:, :, :, -1].set(right).at[:, :, :, 0].set(left)


def inner(first, second, weight):
    return jnp.sum(first * second * weight, axis=(1, 2, 3, 4))


def expand(scalar):
    return scalar.reshape(-1, 1, 1, 1, 1)


def squared_norm(residual, weight):
    return lax.psum(inner(residual, residual, weight), "elem")


def on_device(velocity, radial_dx, radial_dy, around_dx, around_dy, jacobian):
    table = jnp.asarray(derivative_table(), jnp.float32)
    modes = lax.axis_size("mode")
    local_planes = velocity.shape[1]
    planes = local_planes * modes
    first_plane = lax.axis_index("mode") * local_planes
    layers = velocity.shape[2]
    columns = velocity.shape[5]
    basis, inverse, slope = transform_tables(planes)
    radial = radial_derivative(table, velocity)
    beside_all = around_derivative(table, velocity)
    along_x = radial_dx * radial + around_dx * beside_all
    along_y = radial_dy * radial + around_dy * beside_all
    fields = jnp.concatenate([velocity, along_x, along_y], axis=0)
    count = fields.shape[0]
    cells = layers * NODES * NODES * columns
    packed = fields.reshape(count, local_planes, modes, cells // modes)
    flat = lax.all_to_all(packed, "mode", split_axis=2, concat_axis=1, tiled=True)[:, :, 0, :]
    values = jnp.einsum("jp,fpc->fjc", basis, flat, precision=lax.Precision.HIGHEST)
    speed = values[0:3]
    slope_x = values[3:6]
    slope_y = values[6:9]
    slope_z = jnp.einsum("jp,fpc->fjc", slope, flat[0:3], precision=lax.Precision.HIGHEST)
    product = -(speed[0:1] * slope_x + speed[1:2] * slope_y + speed[2:3] * slope_z)
    spectral = jnp.einsum("pj,fjc->fpc", inverse, product, precision=lax.Precision.HIGHEST)
    returned = lax.all_to_all(
        spectral[:, :, None, :], "mode", split_axis=1, concat_axis=2, tiled=True
    )
    advection = returned.reshape(velocity.shape)
    metrics = geometry(radial_dx, radial_dy, around_dx, around_dy, jacobian)
    mask, weight = node_weights(layers)
    predicted = velocity + time_step * advection
    radial = radial_derivative(table, predicted[0:2])
    beside_all = around_derivative(table, predicted[0:2])
    divergence = (
        radial_dx * radial[0]
        + around_dx * beside_all[0]
        + (radial_dy * radial[1] + around_dy * beside_all[1])
        + z_derivative(predicted[2:3], first_plane // 2)[0]
    )
    shift = plane_shift(first_plane, local_planes, planes)
    right_side = mask * assemble(-(metrics[3] * divergence) / time_step)
    solution = jnp.zeros_like(right_side)
    residual = right_side
    direction = right_side
    norm_now = squared_norm(residual, weight)
    for turn in range(ITERS):
        image = mask * assemble(helmholtz_local(table, direction, shift, metrics))
        alpha = norm_now / lax.psum(inner(direction, image, weight), "elem")
        solution = solution + expand(alpha) * direction
        residual = residual - expand(alpha) * image
        norm_next = squared_norm(residual, weight)
        direction = residual + expand(norm_next / norm_now) * direction
        norm_now = norm_next
    return (advection, solution)


def solution(mesh):
    placed = (
        P(None, "mode", None, None, None, "elem"),
        P(None, None, None, "elem"),
        P(None, None, None, "elem"),
        P(None, None, None, "elem"),
        P(None, None, None, "elem"),
        P(None, None, None, "elem"),
    )
    return jax.shard_map(
        on_device,
        mesh=mesh,
        in_specs=placed,
        out_specs=(P(None, "mode", None, None, None, "elem"), P("mode", None, None, None, "elem")),
        check_vma=False,
    )
```

profile of v0, /device:TPU:0, one launch (start us, length us, event | category | flops | bytes accessed | tf_op | source)
XLA Modules:
  0.0 1519.5 jit_solution(4659205439658418913)
XLA Ops:
  4.5 9.8 copy.344
  14.3 12.5 fusion.2
  26.7 24.8 %fusion = (f32[3,32,4,7,7,128]{5,3,4,2,1,0:T(8,128)}, f32[3,32,4,7,7,128]{5,3,4,2,1,0:T(8,128)}) fusion(f32[7,3,32,4,7,128]{5,0,4,3,2,1:T(8,128)} %fusion.2, f32[4,7,7,128]{3,1,2,0:T(8,128)S(1)} %copy.339, f32[4,7,7,128]{3,1,2,0:T(8,128)S(1)} %copy.337, f32[4,7,7,128]{3,1,2,0:T(8,128)S(1)} %copy.343, f32[4,7,7,128]{3,1,2,0:T(8,128)S(1)} %copy.342, ...), kind=kOutput, calls=%fused_computation.4 | convolution fusion | flops 216760320 | bytes 38936772 | tf_op jit(solution)/shard_map/ia,...abe->...ibe/dot_general | solution.py:75
  51.5 23.2 %pad_maximum_fusion = f32[9,32,4,7,7,128]{5,3,4,2,1,0:T(8,128)} fusion(f32[3,32,4,7,7,128]{5,3,4,2,1,0:T(8,128)} %get-tuple-element.216, f32[3,32,4,7,7,128]{5,3,4,2,1,0:T(8,128)} %get-tuple-element.215, f32[3,32,4,7,7,128]{5,3,4,2,1,0:T(8,128)} %copy.344), kind=kLoop, calls=%fused_computation | loop fusion | flops 14450688 | bytes 57802752 | tf_op jit(solution)/shard_map/concatenate | solution.py:201
  74.7 27.6 %copy.345 = f32[9,32,4,7,7,128]{5,4,3,2,1,0:T(8,128)} copy(f32[9,32,4,7,7,128]{5,3,4,2,1,0:T(8,128)} %pad_maximum_fusion) | data formatting | bytes 57802752 | tf_op jit(solution)/shard_map/concatenate | solution.py:201
  102.4 35.2 %reshape.961 = f32[9,32,8,3136]{3,2,1,0:T(8,128)} reshape(f32[9,32,4,7,7,128]{5,4,3,2,1,0:T(8,128)} %copy.345) | data formatting | bytes 57802752 | tf_op jit(solution)/shard_map/reshape | solution.py:204
  137.6 25.7 %copy.346 = f32[9,32,8,3136]{3,1,0,2:T(8,128)} copy(f32[9,32,8,3136]{3,2,1,0:T(8,128)} %reshape.961) | data formatting | bytes 57802752 | tf_op jit(solution)/shard_map/reshape | solution.py:204
  163.3 7.3 all-to-all-start
  171.8 635.8 %all-to-all-done = f32[9,32,8,3136]{3,1,0,2:T(8,128)} async-done(((f32[9,32,8,3136]{3,1,0,2:T(8,128)}), f32[9,32,8,3136]{3,1,0,2:T(8,128)}, u32[]{:S(2)}, u32[]{:S(2)}) %all-to-all-start) | async-done | bytes 28901408 | tf_op jit(solution)/shard_map/all_to_all | solution.py:205
  807.6 4.4 slice.720
  812.0 20.5 %copy.347 = f32[9,8,32,1,3136]{4,2,1,0,3:T(8,128)} copy(f32[9,8,32,1,3136]{4,2,0,1,3:T(8,128)} %bitcast.6) | data formatting | bytes 57802752 | tf_op jit(solution)/shard_map/all_to_all | solution.py:205
  832.5 4.4 copy.349
  836.9 54.2 %convolution_bitcast_fusion = f32[9,256,3136]{1,2,0:T(8,128)} fusion(f32[9,256,3136]{2,1,0:T(8,128)} %bitcast.252, f32[256,256,1]{1,0,2:T(8,128)S(1)} %fusion.159), kind=kOutput, calls=%fused_computation.1 | convolution fusion | flops 22196256768 | bytes 58064896 | tf_op jit(solution)/shard_map/jp,fpc->fjc/dot_general | solution.py:206
  891.1 7.9 slice_bitcast_fusion.6
  900.0 21.3 %fusion.86 = f32[3,3136,256]{2,1,0:T(8,128)} fusion(f32[3,256,3136]{2,1,0:T(8,128)S(1)} %bitcast.253, f32[256]{0:T(256)S(1)} %get-tuple-element.253, f32[256]{0:T(256)S(1)} %get-tuple-element.251, s32[256]{0:T(256)S(1)} %and_select_fusion.1, pred[256]{0:T(512)(128)(4,1)S(1)} %get-tuple-element.255), kind=kOutput, calls=%fused_computation.170 | convolution fusion | flops 7399866368 | bytes 19270912 | tf_op jit(solution)/shard_map/jp,fpc->fjc/dot_general | solution.py:210
  921.3 19.5 %fusion.9 = f32[3,256,1,3136]{1,3,0,2:T(8,128)} fusion(f32[9,256,3136]{1,2,0:T(8,128)} %convolution_bitcast_fusion, f32[3,3136,256]{2,1,0:T(8,128)} %fusion.86, f32[256,3136]{0,1:T(8,128)} %get-tuple-element.214, f32[256,3136]{0,1:T(8,128)} %get-tuple-element.213, f32[256,3136]{0,1:T(8,128)S(1)} %get-tuple-element.212, f32[256]{0:T(256)S(1)} %get-tuple-element.250, ...), kind=kOutput, calls=%fused_computation.19 | convolution fusion | flops 7414317056 | bytes 48172544 | tf_op jit(solution)/shard_map/pj,fjc->fpc/dot_general | solution.py:212
  940.8 20.8 %copy.351 = f32[3,256,1,3136]{3,2,0,1:T(1,128)} copy(f32[3,256,1,3136]{1,3,0,2:T(8,128)} %fusion.9) | data formatting | bytes 19267584 | tf_op jit(solution)/shard_map/broadcast_in_dim | solution.py:214
  961.6 5.4 all-to-all-start.1
  971.4 209.3 %all-to-all-done.1 = f32[3,256,1,3136]{3,2,0,1:T(1,128)} async-done(((f32[3,256,1,3136]{3,2,0,1:T(1,128)}), f32[3,256,1,3136]{3,2,0,1:T(1,128)}, u32[]{:S(2)}, u32[]{:S(2)}) %all-to-all-start.1) | async-done | bytes 9633824 | tf_op jit(solution)/shard_map/all_to_all | solution.py:213
  1180.7 4.4 copy.352
  1185.1 9.4 copy.353
  1194.5 13.2 reshape.962
  1207.7 17.2 %copy_add_fusion = f32[3,32,4,7,7,128]{5,1,4,3,2,0:T(8,128)} fusion(f32[3,32,4,7,7,128]{5,2,4,3,1,0:T(4,128)} %param.40, f32[3,32,4,7,7,128]{5,4,3,2,1,0:T(8,128)} %reshape.962), kind=kLoop, calls=%fused_computation.17 | loop fusion | flops 4816896 | bytes 28901376 | tf_op jit(solution)/shard_map/add | solution.py:219
  1228.5 12.9 fusion.12
  1241.4 12.7 fusion.14
  1279.4 10.4 copy.422
  1293.4 7.2 collective-permute-done.1
  1304.8 5.8 fusion.45
  1310.6 7.1 fusion.30
  1325.3 4.2 fusion.52
  1335.6 4.1 collective-permute-done.2
  1348.3 5.7 collective-permute-done.3
  1357.2 6.3 all-reduce
  1364.1 6.2 multiply_reduce_fusion.3
  1370.3 6.3 psum.44
  1381.1 5.7 fusion.39
  1386.8 7.1 fusion.26
  1411.6 4.1 collective-permute-done.4
  1424.6 5.4 collective-permute-done.5
  1433.3 6.3 psum.45
  1440.8 4.2 multiply_reduce_fusion.1
  1445.0 7.2 psum.46
  1452.9 4.1 multiply_add_fusion
  1457.1 5.8 fusion.33
  1462.9 7.1 fusion.22
  1487.7 4.1 collective-permute-done.6
  1505.7 5.7 psum.47
  1511.4 4.1 fusion.67
  (230 shorter events, 144.0 us)
Async XLA Ops:
  3.4 10.9 slice-start
  4.4 9.8 slice-start.1
  4.5 9.8 slice-start.2
  4.5 9.8 copy-start.40
  163.3 644.2 %all-to-all-start = ((f32[9,32,8,3136]{3,1,0,2:T(8,128)}), f32[9,32,8,3136]{3,1,0,2:T(8,128)}, u32[]{:S(2)}, u32[]{:S(2)}) async-start(f32[9,32,8,3136]{3,1,0,2:T(8,128)} %copy.346), calls=%async_computation | async-start | bytes 58982400 | tf_op jit(solution)/shard_map/all_to_all | solution.py:205
  891.1 8.9 copy-start.3
  961.6 5.5 copy-start.23
  961.6 5.5 copy-start.25
  961.6 5.5 copy-start.22
  961.6 5.6 copy-start.24
  961.6 7.0 copy-start.39
  961.6 7.0 copy-start.47
  961.6 9.0 copy-start.48
  961.6 219.1 %all-to-all-start.1 = ((f32[3,256,1,3136]{3,2,0,1:T(1,128)}), f32[3,256,1,3136]{3,2,0,1:T(1,128)}, u32[]{:S(2)}, u32[]{:S(2)}) async-start(f32[3,256,1,3136]{3,2,0,1:T(1,128)} %copy.351), calls=%async_computation.1 | async-start | bytes 19660800 | tf_op jit(solution)/shard_map/all_to_all | solution.py:213
  967.9 217.2 %copy-start.29 = (f32[4,7,7]{2,1,0:T(8,128)}, f32[4,7,7]{2,1,0:T(8,128)S(1)}, u32[]{:S(2)}) copy-start(f32[4,7,7]{2,1,0:T(8,128)S(1)} %multiply_divide_fusion) | copy-start | bytes 2356
  1241.4 12.7 slice-start.3
  1279.1 10.7 collective-permute-start
  1292.3 9.3 copy-start.30
  1292.3 9.3 copy-start.35
  1292.5 8.1 collective-permute-start.1
  1304.8 59.3 %copy-start = (f32[32,4,7,7,128]{4,0,3,2,1:T(8,128)}, f32[32,4,7,7,128]{4,0,3,2,1:T(8,128)S(1)}, u32[]{:S(2)}) copy-start(f32[32,4,7,7,128]{4,0,3,2,1:T(8,128)S(1)} %get-tuple-element.211) | copy-start | bytes 9633796
  1304.8 5.8 copy-start.19
  1321.3 4.0 copy-start.42
  1333.7 6.1 collective-permute-start.2
  1343.3 10.8 copy-start.13
  1345.6 8.5 copy-start.5
  1345.6 10.4 copy-start.32
  1345.6 10.4 copy-start.36
  1345.8 8.2 collective-permute-start.3
  1381.1 5.8 copy-start.20
  1409.6 6.1 collective-permute-start.4
  1419.3 4.1 copy-start.17
  1419.3 10.8 copy-start.15
  1421.6 8.5 copy-start.9
  1421.6 8.7 copy-start.33
  1421.6 8.7 copy-start.37
  1421.8 8.2 collective-permute-start.5
  1452.9 4.2 copy-start.28
  1457.1 20.5 %copy-start.1 = (f32[32,4,7,7,128]{4,0,3,2,1:T(8,128)}, f32[32,4,7,7,128]{4,0,3,2,1:T(8,128)S(1)}, u32[]{:S(2)}) copy-start(f32[32,4,7,7,128]{4,0,3,2,1:T(8,128)S(1)} %multiply_add_fusion) | copy-start | bytes 9633796
  1457.1 5.8 copy-start.21
  1485.7 6.1 collective-permute-start.6
  1496.6 8.2 collective-permute-start.7
  1499.1 5.7 copy-start.11
  1499.1 6.0 copy-start.2
  1499.1 6.0 copy-start.31
  1499.1 6.0 copy-start.38
  1505.1 6.3 copy-start.49
  1505.1 6.3 copy-start.46
  (17 other events, 36.5 us)
where the time goes:
time: 1530 us; the launch traced here: 1520 us
  waiting for transfers between devices  879 us (57%)
  local copies, waits for them, and re-layouts  248 us (16%)
  matrix products  219 us (14%)
  other arithmetic  122 us (8%)
  blocking collectives  31.8 us (2%)
  starting transfers between devices  17.8 us (1%)
    all_to_all x1, waiting for transfers between devices, on_device(): lax.all_to_all(packed, 'mode', split_axis=2, concat_axis=1, tiled=True)  636 us
    all_to_all x1, waiting for transfers between devices, on_device(): lax.all_to_all(spectral[:, :, None, :], 'mode', split_axis=1, concat_axis...  209 us
    reshape x2, local copies, waits for them, and re-layouts, on_device(): packed = fields.reshape(count, local_planes, modes, cells // modes)  61 us
    dot_general x5, matrix products, radial_derivative(): jnp.einsum('ia,...abe->...ibe', table, field, precision=lax.Precision.HIG...  58.7 us
    dot_general x1, matrix products, on_device(): jnp.einsum('jp,fpc->fjc', basis, flat, precision=lax.Precision.HIGHEST)  54.2 us
    dot_general x5, matrix products, around_derivative(): jnp.einsum('jb,...abe->...aje', table, field, precision=lax.Precision.HIG...  42.6 us
    unnamed x124, local copies, waits for them, and re-layouts  42.4 us
  transfers between devices with their start and end apart: 10, of which 9 were waited for; matrix products, arithmetic and copies ran while one was open for 2% of the time, Pallas kernels for 0%

commit v1 on v0

--- a/solution.py
+++ b/solution.py
@@ -4,6 +4,8 @@
 import jax.numpy as jnp
 import numpy as np
 from jax import lax
+from jax.experimental import pallas as pl
+from jax.experimental.pallas import tpu as pltpu
 from jax.sharding import PartitionSpec as P
 
 NODES = 7
@@ -242,6 +244,840 @@
     return (advection, solution)
 
 
+def split_bf16(table):
+    high = table.astype(jnp.bfloat16)
+    low = (table - high.astype(np.float64)).astype(jnp.bfloat16)
+    return np.concatenate([high, high, low], axis=1)
+
+
+def paired_tables(planes):
+    half = planes // 2
+    position = np.arange(planes)
+    plane = np.arange(planes)
+    order = plane // 2
+    angle = 2.0 * np.pi / planes * (position[:, None] * order[None, :] % planes)
+    cosine, sine = (np.cos(angle), np.sin(angle))
+    odd = (plane % 2 == 1)[None, :]
+    parity = (1.0 - 2.0 * (position % 2))[:, None]
+    basis = np.where((plane == 1)[None, :], parity, np.where(odd, sine, cosine))
+    wave = (order * spanwise_wave)[None, :]
+    slope = np.where(odd, wave * cosine, -wave * sine)
+    scaling = np.where(order == 0, 1.0, 2.0) / planes
+    inverse = -(basis * scaling[None, :]).T
+
+    def columns(matrix, swap):
+        even, other = (matrix[:, 0::2], matrix[:, 1::2])
+        return np.concatenate([other, even] if swap else [even, other], axis=1)
+
+    forward = np.concatenate(
+        [
+            columns(basis[:half], False),
+            columns(basis[half:], True),
+            columns(slope[:half], False),
+            columns(slope[half:], True),
+        ]
+    )
+    top, bottom = (inverse[:, :half], inverse[:, half:])
+    backward = np.concatenate(
+        [
+            np.concatenate([top[0::2], bottom[0::2]], axis=1),
+            np.concatenate([bottom[1::2], top[1::2]], axis=1),
+        ]
+    )
+    return (split_bf16(forward), split_bf16(backward))
+
+
+def apply_line(matrix, line):
+    n = NODES
+    m = n // 2
+    sums = [line[a] + line[n - 1 - a] for a in range(m)]
+    gaps = [line[a] - line[n - 1 - a] for a in range(m)]
+
+    def total(parts):
+        out = parts[0]
+        for part in parts[1:]:
+            out = out + part
+        return out
+
+    out = [None] * n
+    for i in range(m + 1):
+        plus = total(
+            [float(0.5 * (matrix[i, a] - matrix[i, n - 1 - a])) * gaps[a] for a in range(m)]
+        )
+        if i == m:
+            out[i] = plus
+            continue
+        minus = total(
+            [float(0.5 * (matrix[i, a] + matrix[i, n - 1 - a])) * sums[a] for a in range(m)]
+            + [float(matrix[i, m]) * line[m]]
+        )
+        out[i] = plus + minus
+        out[n - 1 - i] = plus - minus
+    return out
+
+
+def lanes_of(shape):
+    return lax.broadcasted_iota(jnp.int32, shape, len(shape) - 1)
+
+
+def row_of(ref, row, rows):
+    return ref[pl.ds(row, rows, stride=0), :]
+
+
+def call(body, grid, ins, outs, out_shape, scratch=(), flops=0, moved=0, limit=None):
+    return pl.pallas_call(
+        body,
+        grid=grid,
+        in_specs=ins,
+        out_specs=outs,
+        out_shape=out_shape,
+        scratch_shapes=list(scratch),
+        compiler_params=pltpu.CompilerParams(
+            dimension_semantics=("arbitrary",) * len(grid), vmem_limit_bytes=limit
+        ),
+        cost_estimate=pl.CostEstimate(
+            flops=int(flops), bytes_accessed=int(moved), transcendentals=0
+        ),
+    )
+
+
+def whole(shape):
+    return pl.BlockSpec(shape, lambda *_: (0,) * len(shape))
+
+
+def pack(rows, comp, layers, pairs, lanes):
+    square = NODES * NODES
+    per_plane = square * layers
+    half = lanes // 2
+
+    def body(x_ref, o_ref):
+        a = pl.program_id(0)
+        low = lanes_of((pairs, lanes)) < half
+
+        def layer(e, carry):
+            for b in range(NODES):
+                start = (a * NODES + b) * layers + e
+                cos = x_ref[0, pl.ds(start, pairs, stride=2 * per_plane), :]
+                sin = x_ref[0, pl.ds(start + per_plane, pairs, stride=2 * per_plane), :]
+                o_ref[2 * e, b] = jnp.where(low, cos, pltpu.roll(sin, half, 1))
+                o_ref[2 * e + 1, b] = jnp.where(low, pltpu.roll(cos, half, 1), sin)
+            return carry
+
+        lax.fori_loop(0, layers, layer, 0)
+
+    size = rows.shape[1] * lanes * 4
+    return call(
+        body,
+        (NODES,),
+        [pl.BlockSpec((1, rows.shape[1], lanes), lambda a: (comp, 0, 0))],
+        pl.BlockSpec((2 * layers, NODES, pairs, lanes), lambda a: (0, a, 0, 0)),
+        jax.ShapeDtypeStruct((2 * layers, square, pairs, lanes), jnp.float32),
+        moved=2 * size,
+    )(rows)
+
+
+def unpack(blocks):
+    shares, square, pairs, lanes = blocks.shape
+    layers = shares // 2
+    per_plane = square * layers
+    half = lanes // 2
+    count = 2 * pairs * per_plane
+
+    def body(x_ref, o_ref):
+        a = pl.program_id(0)
+        low = lanes_of((pairs, lanes)) < half
+
+        def layer(e, carry):
+            for b in range(NODES):
+                start = (a * NODES + b) * layers + e
+                left, right = (x_ref[2 * e, b], x_ref[2 * e + 1, b])
+                o_ref[pl.ds(start, pairs, stride=2 * per_plane), :] = jnp.where(
+                    low, left, pltpu.roll(right, half, 1)
+                )
+                o_ref[pl.ds(start + per_plane, pairs, stride=2 * per_plane), :] = jnp.where(
+                    low, pltpu.roll(left, half, 1), right
+                )
+            return carry
+
+        lax.fori_loop(0, layers, layer, 0)
+
+    return call(
+        body,
+        (NODES,),
+        [pl.BlockSpec((shares, NODES, pairs, lanes), lambda a: (0, a, 0, 0))],
+        whole((count, lanes)),
+        jax.ShapeDtypeStruct((count, lanes), jnp.float32),
+        moved=2 * count * lanes * 4,
+    )(blocks)
+
+
+def three_pass(rhs_ref, column, tile, rotated, width):
+    both = jnp.concatenate([tile, rotated], axis=0)
+    high = both.astype(jnp.bfloat16)
+    low = (both - high.astype(jnp.float32)).astype(jnp.bfloat16)
+    depth = both.shape[0]
+    place = pl.ds(column * width, width)
+    rhs_ref[pl.ds(0, depth), place] = high
+    rhs_ref[pl.ds(depth, depth), place] = low
+    rhs_ref[pl.ds(2 * depth, depth), place] = high
+
+
+def to_points(blocks, table):
+    shares, square, pairs, lanes = blocks.shape
+    half = lanes // 2
+    rows = shares * pairs
+
+    def body(t_ref, x_ref, v_ref, z_ref, rhs_ref):
+        for b in range(NODES):
+            tile = x_ref[:, b].reshape(rows, lanes)
+            three_pass(rhs_ref, b, tile, pltpu.roll(tile, half, 1), lanes)
+        rhs = rhs_ref[...]
+        low = lanes_of((rows, lanes)) < half
+        for place, out in enumerate((v_ref, z_ref)):
+            both = [
+                jnp.dot(
+                    t_ref[pl.ds((2 * place + part) * rows, rows), :],
+                    rhs,
+                    preferred_element_type=jnp.float32,
+                )
+                for part in range(2)
+            ]
+            for b in range(NODES):
+                cut = slice(b * lanes, (b + 1) * lanes)
+                out[b] = jnp.where(low, both[0][:, cut], both[1][:, cut])
+
+    spec = pl.BlockSpec((NODES, rows, lanes), lambda a: (a, 0, 0))
+    shape = jax.ShapeDtypeStruct((square, rows, lanes), jnp.float32)
+    return call(
+        body,
+        (NODES,),
+        [
+            whole(table.shape),
+            pl.BlockSpec((shares, NODES, pairs, lanes), lambda a: (0, a, 0, 0)),
+        ],
+        [spec, spec],
+        [shape, shape],
+        scratch=[pltpu.VMEM((table.shape[1], NODES * lanes), jnp.bfloat16)],
+        flops=2 * table.shape[0] * table.shape[1] * square * lanes,
+        moved=3 * square * rows * lanes * 4,
+    )(table, blocks)
+
+
+def in_plane(speeds, fields, metrics, table):
+    square, rows, lanes = speeds[0].shape
+    count = len(fields)
+    step = 32
+    own = [i for i, f in enumerate(fields) if all(f is not s for s in speeds)]
+    arrays = list(speeds) + [fields[i] for i in own]
+
+    def body(m_ref, *refs):
+        ins, outs = (refs[: len(arrays)], refs[len(arrays) :])
+        u_ref, v_ref = ins[:2]
+        sources = []
+        extra = 2
+        for i, f in enumerate(fields):
+            if i in own:
+                sources.append(ins[extra])
+                extra += 1
+            else:
+                sources.append(u_ref if f is speeds[0] else v_ref)
+
+        def block(s, carry):
+            r = pl.ds(s * 8, 8)
+
+            def metric(kind, n):
+                return row_of(m_ref, kind * square + n, 8)
+
+            for a in range(NODES):
+                ns = [a * NODES + b for b in range(NODES)]
+                drift = [
+                    u_ref[n, r] * metric(2, n) + v_ref[n, r] * metric(3, n) for n in ns
+                ]
+                for f in range(count):
+                    beside = apply_line(table, [sources[f][n, r] for n in ns])
+                    for b, n in enumerate(ns):
+                        outs[f][n, r] = drift[b] * beside[b]
+            for b in range(NODES):
+                ns = [a * NODES + b for a in range(NODES)]
+                drift = [
+                    u_ref[n, r] * metric(0, n) + v_ref[n, r] * metric(1, n) for n in ns
+                ]
+                for f in range(count):
+                    radial = apply_line(table, [sources[f][n, r] for n in ns])
+                    for a, n in enumerate(ns):
+                        outs[f][n, r] = outs[f][n, r] + drift[a] * radial[a]
+            return carry
+
+        lax.fori_loop(0, step // 8, block, 0)
+
+    spec = pl.BlockSpec((square, step, lanes), lambda i: (0, i, 0))
+    shape = jax.ShapeDtypeStruct((square, rows, lanes), jnp.float32)
+    return call(
+        body,
+        (rows // step,),
+        [whole(metrics.shape)] + [spec] * len(arrays),
+        [spec] * count,
+        [shape] * count,
+        flops=30 * count * square * rows * lanes,
+        moved=(len(arrays) + count) * square * rows * lanes * 4,
+    )(metrics, *arrays)
+
+
+def to_planes(partial, speed_z, slope_z, table, shares):
+    square, rows, lanes = partial.shape
+    half = lanes // 2
+    pairs = rows // shares
+
+    def body(t_ref, g_ref, w_ref, z_ref, o_ref, rhs_ref):
+        for b in range(NODES):
+            tile = g_ref[b] + w_ref[b] * z_ref[b]
+            three_pass(rhs_ref, b, tile, pltpu.roll(tile, half, 1), lanes)
+        rhs = rhs_ref[...]
+        low = lanes_of((rows, lanes)) < half
+        both = [
+            jnp.dot(
+                t_ref[pl.ds(part * rows, rows), :], rhs, preferred_element_type=jnp.float32
+            )
+            for part in range(2)
+        ]
+        for b in range(NODES):
+            cut = slice(b * lanes, (b + 1) * lanes)
+            out = jnp.where(low, both[0][:, cut], both[1][:, cut])
+            o_ref[:, b] = out.reshape(shares, pairs, lanes)
+
+    spec = pl.BlockSpec((NODES, rows, lanes), lambda a: (a, 0, 0))
+    return call(
+        body,
+        (NODES,),
+        [whole(table.shape), spec, spec, spec],
+        pl.BlockSpec((shares, NODES, pairs, lanes), lambda a: (0, a, 0, 0)),
+        jax.ShapeDtypeStruct((shares, square, pairs, lanes), jnp.float32),
+        scratch=[pltpu.VMEM((table.shape[1], NODES * lanes), jnp.bfloat16)],
+        flops=2 * table.shape[0] * table.shape[1] * square * lanes,
+        moved=4 * square * rows * lanes * 4,
+    )(table, partial, speed_z, slope_z)
+
+
+def plane_divergence(sent, returned, metrics, table):
+    shares, square, pairs, lanes = sent[0].shape
+
+    def body(m_ref, s0, r0, s1, r1, o_ref, p0, p1):
+        d = pl.program_id(0)
+
+        def block(s, carry):
+            r = pl.ds(s * 8, 8)
+            for n in range(square):
+                p0[n] = s0[0, n, r] + time_step * r0[0, n, r]
+                p1[n] = s1[0, n, r] + time_step * r1[0, n, r]
+
+            def metric(kind, n):
+                return row_of(m_ref, (kind * shares + d) * square + n, 8)
+
+            for a in range(NODES):
+                ns = [a * NODES + b for b in range(NODES)]
+                first = apply_line(table, [p0[n] for n in ns])
+                second = apply_line(table, [p1[n] for n in ns])
+                for b, n in enumerate(ns):
+                    o_ref[0, n, r] = metric(2, n) * first[b] + metric(3, n) * second[b]
+            for b in range(NODES):
+                ns = [a * NODES + b for a in range(NODES)]
+                first = apply_line(table, [p0[n] for n in ns])
+                second = apply_line(table, [p1[n] for n in ns])
+                for a, n in enumerate(ns):
+                    o_ref[0, n, r] = o_ref[0, n, r] + (
+                        metric(0, n) * first[a] + metric(1, n) * second[a]
+                    )
+            return carry
+
+        lax.fori_loop(0, pairs // 8, block, 0)
+
+    spec = pl.BlockSpec((1, square, pairs, lanes), lambda d: (d, 0, 0, 0))
+    return call(
+        body,
+        (shares,),
+        [whole(metrics.shape)] + [spec] * 4,
+        spec,
+        jax.ShapeDtypeStruct(sent[0].shape, jnp.float32),
+        scratch=[pltpu.VMEM((square, 8, lanes), jnp.float32)] * 2,
+        flops=50 * shares * square * pairs * lanes,
+        moved=5 * shares * square * pairs * lanes * 4,
+    )(metrics, sent[0], returned[0], sent[1], returned[1])
+
+
+def join_layers(y_ref, layers):
+    square = NODES * NODES
+    last = (NODES - 1) * NODES
+    for e in range(layers - 1):
+        for b in range(NODES):
+            upper, lower = (e * square + last + b, (e + 1) * square + b)
+            total = y_ref[upper] + y_ref[lower]
+            y_ref[upper] = total
+            y_ref[lower] = total
+    for b in range(NODES):
+        node = (layers - 1) * square + last + b
+        y_ref[node] = jnp.zeros_like(y_ref[node])
+
+
+def rim_messages(read, layers, shape, partials=()):
+    lane = lanes_of(shape)
+    lanes = shape[-1]
+    first = jnp.zeros(shape, jnp.float32)
+    last = jnp.zeros(shape, jnp.float32)
+    square = NODES * NODES
+    for e in range(layers):
+        for a in range(NODES):
+            spot = e * NODES + a
+            here = lane == spot
+            node = e * square + a * NODES
+            first = jnp.where(here, pltpu.roll(read(node), spot, 1), first)
+            last = jnp.where(here, pltpu.roll(read(node + NODES - 1), (spot + 1) % lanes, 1), last)
+    for i, partial in enumerate(partials):
+        here = lane == layers * NODES + i
+        first = jnp.where(here, partial, first)
+        last = jnp.where(here, partial, last)
+    return (first, last)
+
+
+def right_side(flat, sent, returned, weights, waves, layers):
+    shares, square, pairs, lanes = flat.shape
+    half = lanes // 2
+
+    def body(m_ref, k_ref, f_ref, s_ref, r_ref, o_ref, first_ref, last_ref, c0, c1):
+        low = lanes_of((8, lanes)) < half
+        wave = k_ref[...]
+
+        def layer(e, carry):
+            for n in range(square):
+                sides = []
+                for h in range(2):
+                    d = 2 * e + h
+                    moved = s_ref[d, n] + time_step * r_ref[d, n]
+                    along = pltpu.roll(moved, half, 1) * wave
+                    sides.append(f_ref[d, n] + row_of(m_ref, d * square + n, 8) * along)
+                c0[e * square + n] = jnp.where(low, sides[0], pltpu.roll(sides[1], half, 1))
+                c1[e * square + n] = jnp.where(low, pltpu.roll(sides[0], half, 1), sides[1])
+            return carry
+
+        lax.fori_loop(0, layers, layer, 0)
+        for part, buffer in enumerate((c0, c1)):
+            join_layers(buffer, layers)
+            first, last = rim_messages(lambda n: buffer[n], layers, (8, lanes))
+            first_ref[part] = first
+            last_ref[part] = last
+
+        def copy(e, carry):
+            for n in range(square):
+                o_ref[e * square + n, 0] = c0[e * square + n]
+                o_ref[e * square + n, 1] = c1[e * square + n]
+            return carry
+
+        lax.fori_loop(0, layers, copy, 0)
+
+    spec = pl.BlockSpec((shares, square, 8, lanes), lambda i: (0, 0, i, 0))
+    nodes = layers * square
+    rim = pl.BlockSpec((2, 8, lanes), lambda i: (0, i, 0))
+    rim_shape = jax.ShapeDtypeStruct((2, pairs, lanes), jnp.float32)
+    out = call(
+        body,
+        (pairs // 8,),
+        [whole(weights.shape), pl.BlockSpec((8, lanes), lambda i: (i, 0)), spec, spec, spec],
+        [pl.BlockSpec((nodes, 2, 8, lanes), lambda i: (0, 0, i, 0)), rim, rim],
+        [jax.ShapeDtypeStruct((nodes, 2, pairs, lanes), jnp.float32), rim_shape, rim_shape],
+        scratch=[pltpu.VMEM((nodes, 8, lanes), jnp.float32)] * 2,
+        flops=10 * shares * square * pairs * lanes,
+        moved=4 * shares * square * pairs * lanes * 4,
+    )(weights, waves, flat, sent, returned)
+    planes = 2 * pairs
+    return (
+        out[0].reshape(nodes, planes, lanes),
+        out[1].reshape(planes, lanes),
+        out[2].reshape(planes, lanes),
+    )
+
+
+def swap_rims(first, last):
+    size = lax.axis_size("elem")
+    up = [(i, (i + 1) % size) for i in range(size)]
+    down = [(j, i) for i, j in up]
+    return (lax.ppermute(last, "elem", up), lax.ppermute(first, "elem", down))
+
+
+def opposite(first):
+    size = lax.axis_size("elem")
+    return lax.ppermute(first, "elem", [(i, (i + 2) % size) for i in range(size)])
+
+
+def join_columns(read, write, before, after, layers):
+    lanes = before.shape[-1]
+    lane = lanes_of(before.shape)
+    square = NODES * NODES
+    for e in range(layers):
+        for a in range(NODES):
+            spot = e * NODES + a
+            node = e * square + a * NODES
+            first, last = (read(node), read(node + NODES - 1))
+            beyond = pltpu.roll(after, lanes - 1 - spot, 1)
+            ahead = jnp.where(lane == lanes - 1, beyond, pltpu.roll(first, lanes - 1, 1))
+            right = last + ahead
+            mine = first + (pltpu.roll(before, lanes - spot, 1) if spot else before)
+            write(node + NODES - 1, right)
+            write(node, jnp.where(lane == 0, mine, pltpu.roll(right, 1, 1)))
+
+
+def share_of(layers, e, a, b):
+    value = 1.0
+    if b in (0, NODES - 1):
+        value = 0.5 * value
+    if a == 0:
+        value = jnp.where(e > 0, 0.5, 1.0) * value
+    if a == NODES - 1:
+        value = jnp.where(e < layers - 1, 0.5, 0.0) * value
+    return value
+
+
+def helmholtz(r_ref, y_ref, flux_ref, g_ref, shift, layers, table, dot_only=False):
+    square = NODES * NODES
+    nodes = layers * square
+    rows, lanes = shift.shape
+    turned = table.T
+    zero = jnp.zeros((rows, lanes), jnp.float32)
+
+    def layer(e, carry):
+        norm, energy = carry
+        base = e * square
+
+        def metric(kind, n):
+            return row_of(g_ref, kind * nodes + base + n, rows)
+
+        for b in range(NODES):
+            ns = [a * NODES + b for a in range(NODES)]
+            radial = apply_line(table, [r_ref[base + n] for n in ns])
+            for a, n in enumerate(ns):
+                flux_ref[n] = radial[a]
+        for a in range(NODES):
+            ns = [a * NODES + b for b in range(NODES)]
+            line = [r_ref[base + n] for n in ns]
+            beside = apply_line(table, line)
+            second = []
+            part = zero
+            for b, n in enumerate(ns):
+                radial = flux_ref[n]
+                cross = metric(1, n)
+                one = metric(0, n) * radial + cross * beside[b]
+                two = cross * radial + metric(2, n) * beside[b]
+                held = shift * metric(3, n) * line[b]
+                weight = 0.5 if b in (0, NODES - 1) else 1.0
+                square_here = line[b] * line[b]
+                part = part + (square_here * weight if weight != 1.0 else square_here)
+                if dot_only:
+                    energy = energy + radial * one + beside[b] * two + held * line[b]
+                else:
+                    flux_ref[n] = one
+                    second.append(two)
+                    y_ref[base + n] = held
+            norm = norm + part * share_of(layers, e, a, 1)
+            if not dot_only:
+                back = apply_line(turned, second)
+                for b, n in enumerate(ns):
+                    y_ref[base + n] = y_ref[base + n] + back[b]
+        if not dot_only:
+            for b in range(NODES):
+                ns = [a * NODES + b for a in range(NODES)]
+                back = apply_line(turned, [flux_ref[n] for n in ns])
+                for a, n in enumerate(ns):
+                    value = y_ref[base + n] + back[a]
+                    y_ref[base + n] = value
+                    energy = energy + value * r_ref[base + n]
+        return (norm, energy)
+
+    norm, energy = lax.fori_loop(0, layers, layer, (zero, zero))
+    return (
+        jnp.sum(norm, axis=1, keepdims=True),
+        jnp.sum(energy, axis=1, keepdims=True),
+    )
+
+
+def lane_value(block, lane):
+    return block[:, lane : lane + 1]
+
+
+def sums_from(own, left, right, far, layers):
+    total = (own[...] + far[...]) + (left[...] + right[...])
+    spot = layers * NODES
+    return (lane_value(total, spot), lane_value(total, spot + 1))
+
+
+def scalars_block(shape, values):
+    lane = lanes_of(shape)
+    out = jnp.zeros(shape, jnp.float32)
+    for i, value in enumerate(values):
+        out = jnp.where(lane == i, value, out)
+    return out
+
+
+def solver_specs(nodes, planes, lanes):
+    field = pl.BlockSpec((nodes, 8, lanes), lambda i: (0, i, 0))
+    small = pl.BlockSpec((8, lanes), lambda i: (i, 0))
+    shapes = (
+        jax.ShapeDtypeStruct((nodes, planes, lanes), jnp.float32),
+        jax.ShapeDtypeStruct((planes, lanes), jnp.float32),
+    )
+    return (field, small, shapes)
+
+
+def first_image(raw, before, after, shift, geo, layers, table):
+    nodes, planes, lanes = raw.shape
+    field, small, (field_shape, small_shape) = solver_specs(nodes, planes, lanes)
+
+    def body(g_ref, k_ref, f_ref, b_ref, a_ref, r_ref, y_ref, first_ref, last_ref, flux):
+        def copy(e, carry):
+            for n in range(NODES * NODES):
+                r_ref[e * NODES * NODES + n] = f_ref[e * NODES * NODES + n]
+            return carry
+
+        lax.fori_loop(0, layers, copy, 0)
+
+        def write(n, value):
+            r_ref[n] = value
+
+        join_columns(lambda n: f_ref[n], write, b_ref[...], a_ref[...], layers)
+        sums = helmholtz(r_ref, y_ref, flux, g_ref, k_ref[...], layers, table)
+        join_layers(y_ref, layers)
+        first_ref[...], last_ref[...] = rim_messages(
+            lambda n: y_ref[n], layers, (8, lanes), sums
+        )
+
+    return call(
+        body,
+        (planes // 8,),
+        [whole(geo.shape), small, field, small, small],
+        [field, field, small, small],
+        [field_shape, field_shape, small_shape, small_shape],
+        scratch=[pltpu.VMEM((NODES * NODES, 8, lanes), jnp.float32)],
+        flops=80 * nodes * planes * lanes,
+        moved=3 * nodes * planes * lanes * 4,
+    )(geo, shift, raw, before, after)
+
+
+def second_image(start, image, messages, shift, geo, layers, table):
+    nodes, planes, lanes = start.shape
+    field, small, (field_shape, small_shape) = solver_specs(nodes, planes, lanes)
+
+    def body(g_ref, k_ref, r0, y0, own, left, right, far, *rest):
+        w_ref, y_ref, first_ref, last_ref, scalar_ref, r1, flux = rest
+        norm, energy = sums_from(own, left, right, far, layers)
+        alpha = jnp.broadcast_to(norm / energy, (8, lanes))
+
+        def move(e, carry):
+            for n in range(NODES * NODES):
+                node = e * NODES * NODES + n
+                w = y0[node]
+                w_ref[node] = w
+                r1[node] = r0[node] - alpha * w
+            return carry
+
+        lax.fori_loop(0, layers, move, 0)
+
+        def write(n, value):
+            w_ref[n] = value
+            r1[n] = r0[n] - alpha * value
+
+        join_columns(lambda n: y0[n], write, left[...], right[...], layers)
+        sums = helmholtz(r1, y_ref, flux, g_ref, k_ref[...], layers, table)
+        join_layers(y_ref, layers)
+        first_ref[...], last_ref[...] = rim_messages(
+            lambda n: y_ref[n], layers, (8, lanes), sums
+        )
+        scalar_ref[...] = scalars_block((8, lanes), (alpha, norm, energy))
+
+    return call(
+        body,
+        (planes // 8,),
+        [whole(geo.shape), small, field, field] + [small] * 4,
+        [field, field, small, small, small],
+        [field_shape, field_shape, small_shape, small_shape, small_shape],
+        scratch=[
+            pltpu.VMEM((nodes, 8, lanes), jnp.float32),
+            pltpu.VMEM((NODES * NODES, 8, lanes), jnp.float32),
+        ],
+        flops=80 * nodes * planes * lanes,
+        moved=4 * nodes * planes * lanes * 4,
+    )(geo, shift, start, image, *messages)
+
+
+def third_energy(start, joined, image, messages, scalars, shift, geo, layers, table):
+    nodes, planes, lanes = start.shape
+    field, small, (field_shape, small_shape) = solver_specs(nodes, planes, lanes)
+
+    def body(g_ref, k_ref, r0, w0, y1, own, left, right, far, old, *rest):
+        r2, d2, sums_ref, scalar_ref, flux = rest
+        norm, energy = sums_from(own, left, right, far, layers)
+        before = old[...]
+        alpha = jnp.broadcast_to(lane_value(before, 0), (8, lanes))
+        ratio = norm / lane_value(before, 1)
+        curve = energy - ratio * ratio * lane_value(before, 2)
+        step = jnp.broadcast_to(norm / curve, (8, lanes))
+        beta = jnp.broadcast_to(ratio, (8, lanes))
+
+        def at(node, image_value):
+            w = w0[node]
+            start_value = r0[node]
+            moved = start_value - alpha * w
+            d2[node] = moved + beta * start_value
+            r2[node] = moved - step * (image_value + beta * w)
+
+        def move(e, carry):
+            for n in range(NODES * NODES):
+                at(e * NODES * NODES + n, y1[e * NODES * NODES + n])
+            return carry
+
+        lax.fori_loop(0, layers, move, 0)
+        join_columns(lambda n: y1[n], at, left[...], right[...], layers)
+        sums = helmholtz(r2, None, flux, g_ref, k_ref[...], layers, table, dot_only=True)
+        lane = lanes_of((8, lanes))
+        spot = layers * NODES
+        sums_ref[...] = jnp.where(lane == spot, sums[0], jnp.where(lane == spot + 1, sums[1], 0.0))
+        scalar_ref[...] = scalars_block((8, lanes), (alpha, norm, curve, step))
+
+    return call(
+        body,
+        (planes // 8,),
+        [whole(geo.shape), small, field, field, field] + [small] * 5,
+        [field, field, small, small],
+        [field_shape, field_shape, small_shape, small_shape],
+        scratch=[pltpu.VMEM((NODES * NODES, 8, lanes), jnp.float32)],
+        flops=60 * nodes * planes * lanes,
+        moved=5 * nodes * planes * lanes * 4,
+    )(geo, shift, start, joined, image, *messages, scalars)
+
+
+def finish(start, direction, residual, messages, scalars, layers):
+    nodes, planes, lanes = start.shape
+    square = NODES * NODES
+    per_plane = nodes
+    pairs = planes // 2
+    field, small, _ = solver_specs(nodes, planes, lanes)
+
+    def body(r0, d2, r2, own, left, right, far, old, o_ref):
+        i = pl.program_id(0)
+        norm, energy = sums_from(own, left, right, far, layers)
+        before = old[...]
+        ratio = norm / lane_value(before, 1)
+        curve = energy - ratio * ratio * lane_value(before, 2)
+        step = norm / curve
+        third = jnp.broadcast_to(step, (8, lanes))
+        second = jnp.broadcast_to(lane_value(before, 3) + step * ratio, (8, lanes))
+        first = jnp.broadcast_to(lane_value(before, 0), (8, lanes))
+        row = i * 8
+        plane = jnp.where(row < pairs, 2 * row, 2 * (row - pairs) + 1)
+
+        def layer(e, carry):
+            for n in range(square):
+                node = e * square + n
+                value = first * r0[node] + second * d2[node] + third * r2[node]
+                o_ref[pl.ds(plane * per_plane + n * layers + e, 8, stride=2 * per_plane), :] = value
+            return carry
+
+        lax.fori_loop(0, layers, layer, 0)
+
+    return call(
+        body,
+        (planes // 8,),
+        [field] * 3 + [small] * 5,
+        whole((planes * nodes, lanes)),
+        jax.ShapeDtypeStruct((planes * nodes, lanes), jnp.float32),
+        flops=6 * nodes * planes * lanes,
+        moved=4 * nodes * planes * lanes * 4,
+    )(start, direction, residual, *messages, scalars)
+
+
+def halves(values, shares):
+    half = values.shape[-1] // 2
+    parts = [jnp.concatenate([p, p], axis=-1) for p in (values[..., :half], values[..., half:])]
+    return jnp.stack(parts, axis=2).reshape(values.shape[0], shares, NODES * NODES, 2 * half)
+
+
+def on_device_paired(velocity, radial_dx, radial_dy, around_dx, around_dy, jacobian):
+    table = derivative_table()
+    modes = lax.axis_size("mode")
+    mode = lax.axis_index("mode")
+    _, local_planes, layers, _, _, lanes = velocity.shape
+    planes = local_planes * modes
+    pairs = local_planes // 2
+    first_plane = mode * local_planes
+    square = NODES * NODES
+    forward, backward = (jnp.asarray(t) for t in paired_tables(planes))
+
+    rows = velocity.transpose(0, 1, 3, 4, 2, 5).reshape(3, local_planes * square * layers, lanes)
+    plain = jnp.stack([radial_dx, radial_dy, around_dx, around_dy]).reshape(
+        4, layers, square, lanes
+    )
+    both = halves(plain, modes)
+    here = lax.dynamic_index_in_dim(both, mode, 1, keepdims=False).reshape(4 * square, lanes)
+    metrics = geometry(radial_dx, radial_dy, around_dx, around_dy, jacobian)
+    geo = jnp.stack(metrics).reshape(4 * layers * square, lanes)
+    scaled = halves((metrics[3] * (-1.0 / time_step)).reshape(1, layers, square, lanes), modes)
+    flux = (both * scaled).reshape(4 * modes * square, lanes)
+    scaled = scaled.reshape(modes * square, lanes)
+    pair = (first_plane // 2 + jnp.arange(pairs, dtype=jnp.int32)).astype(jnp.float32)
+    wave = pair[:, None] * spanwise_wave
+    low = (jnp.arange(lanes) < lanes // 2)[None, :]
+    waves = jnp.where(low, wave, -wave)
+    shift = plane_shift(first_plane, local_planes, planes).reshape(pairs, 2).T.reshape(-1, 1)
+    shift = jnp.broadcast_to(shift, (local_planes, lanes))
+
+    def exchange(blocks):
+        return lax.all_to_all(blocks, "mode", split_axis=0, concat_axis=0, tiled=True)
+
+    sent = []
+    points = []
+    for comp in range(3):
+        sent.append(pack(rows, comp, layers, pairs, lanes))
+    for comp in range(3):
+        points.append(to_points(exchange(sent[comp]), forward))
+    speeds = [p[0] for p in points]
+    early = in_plane(speeds[:2], speeds[:2], here, table)
+    late = in_plane(speeds[:2], speeds[2:], here, table)
+    partial = list(early) + list(late)
+    returned = []
+    for comp in range(3):
+        blocks = to_planes(partial[comp], speeds[2], points[comp][1], backward, modes)
+        returned.append(exchange(blocks))
+    advection = jnp.stack([unpack(r) for r in returned])
+    advection = advection.reshape(3, local_planes, NODES, NODES, layers, lanes)
+    advection = advection.transpose(0, 1, 4, 2, 3, 5)
+
+    flat = plane_divergence(sent, returned, flux, table)
+    raw, first, last = right_side(flat, sent[2], returned[2], scaled, waves, layers)
+    before, after = swap_rims(first, last)
+    start, image, first, last = first_image(raw, before, after, shift, geo, layers, table)
+    messages = (first,) + swap_rims(first, last) + (opposite(first),)
+    joined, image, first, last, scalars = second_image(
+        start, image, messages, shift, geo, layers, table
+    )
+    messages = (first,) + swap_rims(first, last) + (opposite(first),)
+    residual, direction, sums, scalars = third_energy(
+        start, joined, image, messages, scalars, shift, geo, layers, table
+    )
+    messages = (sums,) + swap_rims(sums, sums) + (opposite(sums),)
+    pressure = finish(start, direction, residual, messages, scalars, layers)
+    pressure = pressure.reshape(local_planes, NODES, NODES, layers, lanes)
+    return (advection, pressure.transpose(0, 3, 1, 2, 4))
+
+
+def paired_fits(mesh, shape):
+    modes, ring = (mesh.shape["mode"], mesh.shape["elem"])
+    _, planes, layers, _, _, columns = shape
+    return (
+        ring == 4
+        and columns == 128 * ring
+        and modes == 2 * layers
+        and planes % (16 * modes) == 0
+        and planes == 2 * 128
+        and (layers * NODES + 2 <= 128)
+    )
+
+
 def solution(mesh):
     placed = (
         P(None, "mode", None, None, None, "elem"),
@@ -251,10 +1087,18 @@
         P(None, None, None, "elem"),
         P(None, None, None, "elem"),
     )
-    return jax.shard_map(
-        on_device,
-        mesh=mesh,
-        in_specs=placed,
-        out_specs=(P(None, "mode", None, None, None, "elem"), P("mode", None, None, None, "elem")),
-        check_vma=False,
-    )
+
+    def step(velocity, *rest):
+        body = on_device_paired if paired_fits(mesh, velocity.shape) else on_device
+        return jax.shard_map(
+            body,
+            mesh=mesh,
+            in_specs=placed,
+            out_specs=(
+                P(None, "mode", None, None, None, "elem"),
+                P("mode", None, None, None, "elem"),
+            ),
+            check_vma=False,
+        )(velocity, *rest)
+
+    return step

time: 1530 us -> 593 us (0.39)
  waiting for transfers between devices: 879 us -> 340 us
  local copies, waits for them, and re-layouts: 248 us -> 15.7 us
  matrix products: 219 us -> 0 us
  Pallas kernels: 0 us -> 182 us
  other arithmetic: 122 us -> 15.3 us
  blocking collectives: 31.8 us -> 0 us
  starting transfers between devices: 17.8 us -> 36.2 us
    all_to_all x2 -> x6, waiting for transfers between devices: 845 us -> 337 us  [exchange(): lax.all_to_all(blocks, 'mode', split_axis=0, concat_axis=0, tiled=True)]
    dot_general x19 -> x0, matrix products: 219 us -> none  [the longest x5 58.7 us: radial_derivative(): jnp.einsum('ia,...abe->...ibe', table, field, precision=lax.Precision.HIG...]
    pallas_call x0 -> x20, Pallas kernels: none -> 182 us  [the longest x3 30.8 us: to_points(): call(body, (NODES,), [whole(table.shape), pl.BlockSpec((shares, NODES, pa...]
    reshape x3, local copies, waits for them, and re-layouts: 74.2 us -> 3.58 us  [the longest x1 2.14 us: halves(): jnp.stack(parts, axis=2)]
    add x20 -> x1, other arithmetic: 45.3 us -> 0.01 us  [plane_shift(): plane = first_plane + jnp.arange(count, dtype=jnp.int32)]
    unnamed x124 -> x54, local copies, waits for them, and re-layouts: 42.4 us -> 6.23 us
    all_to_all x3 -> x0, local copies, waits for them, and re-layouts: 34.3 us -> none  [the longest x1 20.5 us: on_device(): lax.all_to_all(packed, 'mode', split_axis=2, concat_axis=1, tiled=True)]
    concatenate x5 -> x0, local copies, waits for them, and re-layouts: 32.4 us -> none  [the longest x1 27.6 us: on_device(): fields = jnp.concatenate([velocity, along_x, along_y], axis=0)]
  transfers between devices with their start and end apart: 10 -> 17, of which waited for: 9 -> 8; matrix products, arithmetic and copies ran while one was open for 2% -> 4% of each run, Pallas kernels for 0% -> 17%
where the time goes in v1:
time: 593 us; the launch traced here: 590 us
  waiting for transfers between devices  340 us (57%)
  Pallas kernels  182 us (31%)
  starting transfers between devices  36.2 us (6%)
  local copies, waits for them, and re-layouts  15.7 us (3%)
  other arithmetic  15.3 us (3%)
    all_to_all x6, waiting for transfers between devices, exchange(): lax.all_to_all(blocks, 'mode', split_axis=0, concat_axis=0, tiled=True)  337 us
    pallas_call x3, Pallas kernels, to_points(): call(body, (NODES,), [whole(table.shape), pl.BlockSpec((shares, NODES, pa...  30.8 us
    pallas_call x3, Pallas kernels, to_planes(): call(body, (NODES,), [whole(table.shape), spec, spec, spec], pl.BlockSpec...  30 us
    all_to_all x6, starting transfers between devices, exchange(): lax.all_to_all(blocks, 'mode', split_axis=0, concat_axis=0, tiled=True)  27.2 us
    pallas_call x3, Pallas kernels, unpack(): call(body, (NODES,), [pl.BlockSpec((shares, NODES, pairs, lanes), lambda...  22.2 us
    pallas_call x3, Pallas kernels, pack(): call(body, (NODES,), [pl.BlockSpec((1, rows.shape[1], lanes), lambda a: (...  19.9 us
    pallas_call x2, Pallas kernels, in_plane(): call(body, (rows // step,), [whole(metrics.shape)] + [spec] * len(arrays)...  16 us
    pallas_call x1, Pallas kernels, right_side(): call(body, (pairs // 8,), [whole(weights.shape), pl.BlockSpec((8, lanes),...  14.5 us
  transfers between devices with their start and end apart: 17, of which 8 were waited for; matrix products, arithmetic and copies ran while one was open for 4% of the time, Pallas kernels for 17%

profile of v1, /device:TPU:0, one launch (start us, length us, event | category | flops | bytes accessed | tf_op | source)
XLA Modules:
  0.0 590.2 jit_solution(18222408761140737738)
XLA Ops:
  0.6 6.7 %shard_map.106.s1 = f32[8,49,16,128]{3,2,1,0:T(8,128)} custom-call(f32[3,6272,128]{2,1,0:T(8,128)} %bitcast.43), custom_call_target="tpu_custom_call" | custom-call | bytes 6422528 | tf_op jit(solution)/shard_map/pallas_call | solution.py:369
  7.3 7.3 %all-to-all-start.1 = ((f32[8,49,16,128]{3,2,1,0:T(8,128)}), f32[8,49,16,128]{3,2,1,0:T(8,128)S(1)}, u32[]{:S(2)}, u32[]{:S(2)}) async-start(f32[8,49,16,128]{3,2,1,0:T(8,128)} %shard_map.106.s1), calls=%async_computation.1 | async-start | bytes 6422528 | tf_op jit(solution)/shard_map/all_to_all | solution.py:1030
  14.6 6.6 %shard_map.104.s0 = f32[8,49,16,128]{3,2,1,0:T(8,128)} custom-call(f32[3,6272,128]{2,1,0:T(8,128)} %bitcast.44), custom_call_target="tpu_custom_call" | custom-call | bytes 6422528 | tf_op jit(solution)/shard_map/pallas_call | solution.py:369
  21.2 65.5 %all-to-all-done.1.x_ref = f32[8,49,16,128]{3,2,1,0:T(8,128)S(1)} async-done(((f32[8,49,16,128]{3,2,1,0:T(8,128)}), f32[8,49,16,128]{3,2,1,0:T(8,128)S(1)}, u32[]{:S(2)}, u32[]{:S(2)}) %all-to-all-start.1) | async-done | bytes 3211296 | tf_op jit(solution)/shard_map/all_to_all | solution.py:1030
  86.7 4.4 all-to-all-start
  91.2 6.6 %shard_map.109.s_ref = f32[8,49,16,128]{3,2,1,0:T(8,128)} custom-call(f32[3,6272,128]{2,1,0:T(8,128)} %bitcast.45), custom_call_target="tpu_custom_call" | custom-call | bytes 6422528 | tf_op jit(solution)/shard_map/pallas_call | solution.py:369
  97.9 64.9 %all-to-all-done.x_ref = f32[8,49,16,128]{3,2,1,0:T(8,128)} async-done(((f32[8,49,16,128]{3,2,1,0:T(8,128)}), f32[8,49,16,128]{3,2,1,0:T(8,128)}, u32[]{:S(2)}, u32[]{:S(2)}) %all-to-all-start) | async-done | bytes 3211296 | tf_op jit(solution)/shard_map/all_to_all | solution.py:1030
  162.8 3.7 all-to-all-start.2
  168.0 1.0 copy-done.3
  169.7 10.3 %shard_map.105 = (f32[49,128,128]{2,1,0:T(8,128)}, f32[49,128,128]{2,1,0:T(8,128)}) custom-call(bf16[512,768]{1,0:T(8,128)(2,1)} %constant.54.clone.t_ref, f32[8,49,16,128]{3,2,1,0:T(8,128)} %all-to-all-done.x_ref), custom_call_target="tpu_custom_call" | custom-call | flops 4932501504 | bytes 9633792 | tf_op jit(solution)/shard_map/pallas_call | solution.py:451
  179.9 10.3 %shard_map.107 = (f32[49,128,128]{2,1,0:T(8,128)}, f32[49,128,128]{2,1,0:T(8,128)}) custom-call(bf16[512,768]{1,0:T(8,128)(2,1)} %constant.54.clone.t_ref, f32[8,49,16,128]{3,2,1,0:T(8,128)} %copy-done.4), custom_call_target="tpu_custom_call" | custom-call | flops 4932501504 | bytes 9633792 | tf_op jit(solution)/shard_map/pallas_call | solution.py:451
  190.2 8.4 %shard_map.108 = (f32[49,128,128]{2,1,0:T(8,128)}, f32[49,128,128]{2,1,0:T(8,128)}) custom-call(f32[196,128]{1,0:T(8,128)} %reshape.82.m_ref, f32[49,128,128]{2,1,0:T(8,128)} %get-tuple-element.26.refs_0_, f32[49,128,128]{2,1,0:T(8,128)} %get-tuple-element.27.refs_1_), custom_call_target="tpu_custom_call" | custom-call | flops 48168960 | bytes 12845056 | tf_op jit(solution)/shard_map/pallas_call | solution.py:515
  198.6 40.1 %all-to-all-done.2.x_ref = f32[8,49,16,128]{3,2,1,0:T(8,128)S(1)} async-done(((f32[8,49,16,128]{3,2,1,0:T(8,128)}), f32[8,49,16,128]{3,2,1,0:T(8,128)S(1)}, u32[]{:S(2)}, u32[]{:S(2)}) %all-to-all-start.2) | async-done | bytes 3211296 | tf_op jit(solution)/shard_map/all_to_all | solution.py:1030
  238.7 1.7 copy-done.5
  240.4 10.3 %shard_map.110 = (f32[49,128,128]{2,1,0:T(8,128)}, f32[49,128,128]{2,1,0:T(8,128)}) custom-call(bf16[512,768]{1,0:T(8,128)(2,1)} %constant.54.clone.t_ref, f32[8,49,16,128]{3,2,1,0:T(8,128)} %copy-done.5), custom_call_target="tpu_custom_call" | custom-call | flops 4932501504 | bytes 9633792 | tf_op jit(solution)/shard_map/pallas_call | solution.py:451
  250.7 10.0 %shard_map.113 = f32[8,49,16,128]{3,2,1,0:T(8,128)} custom-call(bf16[256,768]{1,0:T(8,128)(2,1)} %constant.55.clone.t_ref, f32[49,128,128]{2,1,0:T(8,128)} %get-tuple-element.31.g_ref, f32[49,128,128]{2,1,0:T(8,128)} %get-tuple-element.29.w_ref.refs_2_, f32[49,128,128]{2,1,0:T(8,128)} %get-tuple-element.32.z_ref), custom_call_target="tpu_custom_call" | custom-call | flops 2466250752 | bytes 12845056 | tf_op jit(solution)/shard_map/pallas_call | solution.py:549
  260.7 3.7 all-to-all-start.4
  264.3 10.0 %shard_map.111 = f32[8,49,16,128]{3,2,1,0:T(8,128)} custom-call(bf16[256,768]{1,0:T(8,128)(2,1)} %constant.55.clone.t_ref, f32[49,128,128]{2,1,0:T(8,128)} %get-tuple-element.28.g_ref, f32[49,128,128]{2,1,0:T(8,128)} %get-tuple-element.29.w_ref.refs_2_, f32[49,128,128]{2,1,0:T(8,128)} %get-tuple-element.30.z_ref), custom_call_target="tpu_custom_call" | custom-call | flops 2466250752 | bytes 12845056 | tf_op jit(solution)/shard_map/pallas_call | solution.py:549
  274.3 62.3 %all-to-all-done.4.x_ref.r1 = f32[8,49,16,128]{3,2,1,0:T(8,128)S(1)} async-done(((f32[8,49,16,128]{3,2,1,0:T(8,128)}), f32[8,49,16,128]{3,2,1,0:T(8,128)S(1)}, u32[]{:S(2)}, u32[]{:S(2)}) %all-to-all-start.4) | async-done | bytes 3211296 | tf_op jit(solution)/shard_map/all_to_all | solution.py:1030
  336.6 4.5 all-to-all-start.3
  341.1 7.6 %shard_map.115.g_ref = f32[49,128,128]{2,1,0:T(8,128)} custom-call(f32[196,128]{1,0:T(8,128)} %reshape.82.m_ref, f32[49,128,128]{2,1,0:T(8,128)} %get-tuple-element.26.refs_0_, f32[49,128,128]{2,1,0:T(8,128)} %get-tuple-element.27.refs_1_, f32[49,128,128]{2,1,0:T(8,128)} %get-tuple-element.29.w_ref.refs_2_), custom_call_target="tpu_custom_call" | custom-call | flops 24084480 | bytes 12845056 | tf_op jit(solution)/shard_map/pallas_call | solution.py:515
  348.6 10.0 %shard_map.116 = f32[8,49,16,128]{3,2,1,0:T(8,128)} custom-call(bf16[256,768]{1,0:T(8,128)(2,1)} %constant.55.clone.t_ref, f32[49,128,128]{2,1,0:T(8,128)} %shard_map.115.g_ref, f32[49,128,128]{2,1,0:T(8,128)} %get-tuple-element.29.w_ref.refs_2_, f32[49,128,128]{2,1,0:T(8,128)} %get-tuple-element.33.z_ref), custom_call_target="tpu_custom_call" | custom-call | flops 2466250752 | bytes 12845056 | tf_op jit(solution)/shard_map/pallas_call | solution.py:549
  358.6 54.1 %all-to-all-done.3.x_ref.r0 = f32[8,49,16,128]{3,2,1,0:T(8,128)} async-done(((f32[8,49,16,128]{3,2,1,0:T(8,128)}), f32[8,49,16,128]{3,2,1,0:T(8,128)}, u32[]{:S(2)}, u32[]{:S(2)}) %all-to-all-start.3) | async-done | bytes 3211296 | tf_op jit(solution)/shard_map/all_to_all | solution.py:1030
  412.7 3.7 all-to-all-start.5
  416.3 2.1 reshape.86
  418.6 1.9 multiply_multiply_fusion
  421.4 1.0 mul.102
  422.4 2.1 mul.103
  424.6 2.4 mul.104.m_ref
  427.6 10.6 %shard_map.118.f_ref = f32[8,49,16,128]{3,2,1,0:T(8,128)} custom-call(f32[1568,128]{1,0:T(8,128)} %mul.104.m_ref, f32[8,49,16,128]{3,2,1,0:T(8,128)} %shard_map.104.s0, f32[8,49,16,128]{3,2,1,0:T(8,128)} %all-to-all-done.3.x_ref.r0, f32[8,49,16,128]{3,2,1,0:T(8,128)} %shard_map.106.s1, f32[8,49,16,128]{3,2,1,0:T(8,128)} %copy-done), custom_call_target="tpu_custom_call" | custom-call | flops 40140800 | bytes 16056320 | tf_op jit(solution)/shard_map/pallas_call | solution.py:595
  438.2 50.4 %all-to-all-done.5.x_ref.r_ref = f32[8,49,16,128]{3,2,1,0:T(8,128)S(1)} async-done(((f32[8,49,16,128]{3,2,1,0:T(8,128)}), f32[8,49,16,128]{3,2,1,0:T(8,128)S(1)}, u32[]{:S(2)}, u32[]{:S(2)}) %all-to-all-start.5) | async-done | bytes 3211296 | tf_op jit(solution)/shard_map/all_to_all | solution.py:1030
  488.6 1.7 copy-done.1
  490.3 14.5 %shard_map.119 = (f32[196,2,16,128]{3,2,1,0:T(8,128)}, f32[2,16,128]{2,1,0:T(8,128)}, f32[2,16,128]{2,1,0:T(8,128)}) custom-call(f32[392,128]{1,0:T(8,128)} %reshape_reshape.4.m_ref, f32[16,128]{1,0:T(8,128)} %broadcast_select_fusion.k_ref, f32[8,49,16,128]{3,2,1,0:T(8,128)} %shard_map.118.f_ref, f32[8,49,16,128]{3,2,1,0:T(8,128)} %shard_map.109.s_ref, ...), custom_call_target="tpu_custom_call" | custom-call | flops 8028160 | bytes 12845056 | tf_op jit(solution)/shard_map/pallas_call | solution.py:680
  504.8 1.7 collective-permute-start.1
  506.5 1.0 pad_maximum_fusion.1
  509.1 9.6 %shard_map.120 = (f32[196,32,128]{2,1,0:T(8,128)}, f32[196,32,128]{2,1,0:T(8,128)}, f32[32,128]{1,0:T(8,128)}, f32[32,128]{1,0:T(8,128)}) custom-call(f32[784,128]{1,0:T(8,128)} %reshape.84.g_ref, f32[32,128]{1,0:T(8,128)} %broadcast_in_dim.36.k_ref, f32[196,32,128]{2,1,0:T(8,128)} %bitcast.50, f32[32,128]{1,0:T(8,128)} %copy-done.14, f32[32,128]{1,0:T(8,128)} %copy-done.16), custom_call_target="tpu_custom_call" | custom-call | flops 64225280 | bytes 9633792 | tf_op jit(solution)/shard_map/pallas_call | solution.py:850
  518.7 1.4 collective-permute-start.2
  520.7 1.1 collective-permute-start.3
  522.2 1.9 collective-permute-done.4.far
  524.7 10.6 %shard_map.121 = (f32[196,32,128]{2,1,0:T(8,128)}, f32[196,32,128]{2,1,0:T(8,128)}, f32[32,128]{1,0:T(8,128)}, f32[32,128]{1,0:T(8,128)}, f32[32,128]{1,0:T(8,128)}) custom-call(f32[784,128]{1,0:T(8,128)} %reshape.84.g_ref, f32[32,128]{1,0:T(8,128)} %broadcast_in_dim.36.k_ref, f32[196,32,128]{2,1,0:T(8,128)} %get-tuple-element.37.r0, ...), custom_call_target="tpu_custom_call" | custom-call | flops 64225280 | bytes 12845056 | tf_op jit(solution)/shard_map/pallas_call | solution.py:893
  535.6 1.3 collective-permute-start.7
  537.5 7.4 %shard_map.114 = f32[6272,128]{1,0:T(8,128)} custom-call(f32[8,49,16,128]{3,2,1,0:T(8,128)} %copy-done), custom_call_target="tpu_custom_call" | custom-call | bytes 6422528 | tf_op jit(solution)/shard_map/pallas_call | solution.py:404
  544.9 7.4 %shard_map.112 = f32[6272,128]{1,0:T(8,128)} custom-call(f32[8,49,16,128]{3,2,1,0:T(8,128)} %all-to-all-done.3.x_ref.r0), custom_call_target="tpu_custom_call" | custom-call | bytes 6422528 | tf_op jit(solution)/shard_map/pallas_call | solution.py:404
  552.3 7.4 %shard_map.117 = f32[6272,128]{1,0:T(8,128)} custom-call(f32[8,49,16,128]{3,2,1,0:T(8,128)} %copy-done.1), custom_call_target="tpu_custom_call" | custom-call | bytes 6422528 | tf_op jit(solution)/shard_map/pallas_call | solution.py:404
  560.4 11.1 %shard_map.122 = (f32[196,32,128]{2,1,0:T(8,128)}, f32[196,32,128]{2,1,0:T(8,128)}, f32[32,128]{1,0:T(8,128)}, f32[32,128]{1,0:T(8,128)}) custom-call(f32[784,128]{1,0:T(8,128)} %reshape.84.g_ref, f32[32,128]{1,0:T(8,128)} %broadcast_in_dim.36.k_ref, f32[196,32,128]{2,1,0:T(8,128)} %get-tuple-element.37.r0, f32[196,32,128]{2,1,0:T(8,128)} %get-tuple-element.41.w0, ...), custom_call_target="tpu_custom_call" | custom-call | flops 48168960 | bytes 16056320 | tf_op jit(solution)/shard_map/pallas_call | solution.py:942
  571.5 1.6 collective-permute-start.10
  573.6 8.9 %maximum_bitcast_fusion = f32[3,32,4,7,7,128]{5,2,4,3,1,0:T(4,128)} fusion(f32[1,32,7,7,4,128]{5,4,3,2,1,0:T(4,128)} %bitcast.48, f32[1,32,7,7,4,128]{5,4,3,2,1,0:T(4,128)S(1)} %bitcast.46, f32[1,32,7,7,4,128]{5,4,3,2,1,0:T(4,128)} %bitcast.47), kind=kLoop, calls=%fused_computation | loop fusion | flops 4816896 | bytes 19267584 | tf_op jit(solution)/shard_map/transpose | solution.py:1048
  583.1 7.1 %shard_map.123 = f32[6272,128]{1,0:T(8,128)} custom-call(f32[196,32,128]{2,1,0:T(8,128)} %get-tuple-element.37.r0, f32[196,32,128]{2,1,0:T(8,128)} %get-tuple-element.46.d2, f32[196,32,128]{2,1,0:T(8,128)} %get-tuple-element.47.r2, f32[32,128]{1,0:T(8,128)} %get-tuple-element.48.own, f32[32,128]{1,0:T(8,128)} %copy-done.21, f32[32,128]{1,0:T(8,128)} %copy-done.19, ...), custom_call_target="tpu_custom_call" | custom-call | flops 4816896 | bytes 12845056 | tf_op jit(solution)/shard_map/pallas_call | solution.py:983
  (85 shorter events, 9.7 us)
Async XLA Ops:
  7.3 79.4 %all-to-all-start.1 = ((f32[8,49,16,128]{3,2,1,0:T(8,128)}), f32[8,49,16,128]{3,2,1,0:T(8,128)S(1)}, u32[]{:S(2)}, u32[]{:S(2)}) async-start(f32[8,49,16,128]{3,2,1,0:T(8,128)} %shard_map.106.s1), calls=%async_computation.1 | async-start | bytes 6422528 | tf_op jit(solution)/shard_map/all_to_all | solution.py:1030
  86.7 11.1 %copy-start.4 = (f32[8,49,16,128]{3,2,1,0:T(8,128)}, f32[8,49,16,128]{3,2,1,0:T(8,128)S(1)}, u32[]{:S(2)}) copy-start(f32[8,49,16,128]{3,2,1,0:T(8,128)S(1)} %all-to-all-done.1.x_ref) | copy-start | bytes 9633796
  86.7 76.0 %all-to-all-start = ((f32[8,49,16,128]{3,2,1,0:T(8,128)}), f32[8,49,16,128]{3,2,1,0:T(8,128)}, u32[]{:S(2)}, u32[]{:S(2)}) async-start(f32[8,49,16,128]{3,2,1,0:T(8,128)} %shard_map.104.s0), calls=%async_computation | async-start | bytes 6422528 | tf_op jit(solution)/shard_map/all_to_all | solution.py:1030
  97.9 68.6 %copy-start.8 = (f32[4,7,7,128]{3,0,2,1:T(4,128)S(1)}, f32[4,7,7,128]{3,0,2,1:T(4,128)}, u32[]{:S(2)}) copy-start(f32[4,7,7,128]{3,0,2,1:T(4,128)} %param.10) | copy-start | bytes 301060
  97.9 68.6 %copy-start.9 = (f32[4,7,7,128]{3,0,2,1:T(4,128)S(1)}, f32[4,7,7,128]{3,0,2,1:T(4,128)}, u32[]{:S(2)}) copy-start(f32[4,7,7,128]{3,0,2,1:T(4,128)} %param.11) | copy-start | bytes 301060
  97.9 68.7 %copy-start.11 = (f32[4,7,7,128]{3,0,2,1:T(4,128)S(1)}, f32[4,7,7,128]{3,0,2,1:T(4,128)}, u32[]{:S(2)}) copy-start(f32[4,7,7,128]{3,0,2,1:T(4,128)} %param.12) | copy-start | bytes 301060
  162.8 75.9 %all-to-all-start.2 = ((f32[8,49,16,128]{3,2,1,0:T(8,128)}), f32[8,49,16,128]{3,2,1,0:T(8,128)S(1)}, u32[]{:S(2)}, u32[]{:S(2)}) async-start(f32[8,49,16,128]{3,2,1,0:T(8,128)} %shard_map.109.s_ref), calls=%async_computation.2 | async-start | bytes 6422528 | tf_op jit(solution)/shard_map/all_to_all | solution.py:1030
  168.0 1.0 copy-start.3
  238.7 1.7 copy-start.5
  260.7 75.9 %all-to-all-start.4 = ((f32[8,49,16,128]{3,2,1,0:T(8,128)}), f32[8,49,16,128]{3,2,1,0:T(8,128)S(1)}, u32[]{:S(2)}, u32[]{:S(2)}) async-start(f32[8,49,16,128]{3,2,1,0:T(8,128)} %shard_map.113), calls=%async_computation.4 | async-start | bytes 6422528 | tf_op jit(solution)/shard_map/all_to_all | solution.py:1030
  336.6 12.0 %copy-start = (f32[8,49,16,128]{3,2,1,0:T(8,128)}, f32[8,49,16,128]{3,2,1,0:T(8,128)S(1)}, u32[]{:S(2)}) copy-start(f32[8,49,16,128]{3,2,1,0:T(8,128)S(1)} %all-to-all-done.4.x_ref.r1) | copy-start | bytes 9633796
  336.6 76.1 %all-to-all-start.3 = ((f32[8,49,16,128]{3,2,1,0:T(8,128)}), f32[8,49,16,128]{3,2,1,0:T(8,128)}, u32[]{:S(2)}, u32[]{:S(2)}) async-start(f32[8,49,16,128]{3,2,1,0:T(8,128)} %shard_map.111), calls=%async_computation.3 | async-start | bytes 6422528 | tf_op jit(solution)/shard_map/all_to_all | solution.py:1030
  358.6 60.0 %copy-start.10 = (f32[4,7,7,128]{3,0,2,1:T(4,128)S(1)}, f32[4,7,7,128]{3,0,2,1:T(4,128)}, u32[]{:S(2)}) copy-start(f32[4,7,7,128]{3,0,2,1:T(4,128)} %param.11) | copy-start | bytes 301060
  358.6 60.0 %copy-start.23 = (f32[7,7]{1,0:T(8,128)S(1)}, f32[7,7]{1,0:T(8,128)}, u32[]{:S(2)}) copy-start(f32[7,7]{1,0:T(8,128)} %constant.56.clone) | copy-start | bytes 592
  412.7 75.9 %all-to-all-start.5 = ((f32[8,49,16,128]{3,2,1,0:T(8,128)}), f32[8,49,16,128]{3,2,1,0:T(8,128)S(1)}, u32[]{:S(2)}, u32[]{:S(2)}) async-start(f32[8,49,16,128]{3,2,1,0:T(8,128)} %shard_map.116), calls=%async_computation.5 | async-start | bytes 6422528 | tf_op jit(solution)/shard_map/all_to_all | solution.py:1030
  438.2 68.3 %copy-start.6 = (f32[1,4,7,7,128]{4,1,3,2,0:T(4,128)S(1)}, f32[1,4,7,7,128]{4,1,3,2,0:T(4,128)}, u32[]{:S(2)}) copy-start(f32[1,4,7,7,128]{4,1,3,2,0:T(4,128)} %get-tuple-element.57) | copy-start | bytes 301060
  438.2 68.3 %copy-start.7 = (f32[1,4,7,7,128]{4,1,3,2,0:T(4,128)S(1)}, f32[1,4,7,7,128]{4,1,3,2,0:T(4,128)}, u32[]{:S(2)}) copy-start(f32[1,4,7,7,128]{4,1,3,2,0:T(4,128)} %get-tuple-element.58) | copy-start | bytes 301060
  488.6 1.7 copy-start.1
  504.8 3.6 collective-permute-start
  504.8 3.6 collective-permute-start.1
  508.4 0.7 copy-start.14
  508.4 0.7 copy-start.16
  518.7 3.4 collective-permute-start.2
  520.1 3.9 collective-permute-start.4
  520.7 3.4 collective-permute-start.3
  522.2 1.9 copy-start.18
  524.1 0.6 copy-start.20
  524.1 0.6 copy-start.22
  535.3 24.4 %collective-permute-start.5 = (f32[32,128]{1,0:T(8,128)}, f32[32,128]{1,0:T(8,128)S(1)}, u32[]{:S(2)}, u32[]{:S(2)}) collective-permute-start(f32[32,128]{1,0:T(8,128)} %get-tuple-element.44), channel_id=1, source_target_pairs={{0,1},{1,2},{2,3},{3,0},{4,5},{5,6},{6,7},{7,4},{8,9},{9,10},{10,1... | collective-permute-start | bytes 49160 | tf_op jit(solution)/shard_map/ppermute | solution.py:702
  535.6 24.1 %collective-permute-start.7 = (f32[32,128]{1,0:T(8,128)}, f32[32,128]{1,0:T(8,128)S(1)}, u32[]{:S(2)}, u32[]{:S(2)}) collective-permute-start(f32[32,128]{1,0:T(8,128)} %get-tuple-element.43.own), channel_id=1, source_target_pairs={{0,2},{1,3},{2,0},{3,1},{4,6},{5,7},{6,4},{7,5},{8,10},{9,11},{10,... | collective-permute-start | bytes 49160 | tf_op jit(solution)/shard_map/ppermute | solution.py:707
  537.0 22.8 %collective-permute-start.6 = (f32[32,128]{1,0:T(8,128)}, f32[32,128]{1,0:T(8,128)S(1)}, u32[]{:S(2)}, u32[]{:S(2)}) collective-permute-start(f32[32,128]{1,0:T(8,128)} %get-tuple-element.43.own), channel_id=1, source_target_pairs={{1,0},{2,1},{3,2},{0,3},{5,4},{6,5},{7,6},{4,7},{9,8},{10,9},{11,1... | collective-permute-start | bytes 49160 | tf_op jit(solution)/shard_map/ppermute | solution.py:702
  559.7 0.6 copy-start.12
  559.7 0.6 copy-start.13
  559.8 0.6 copy-start.15
  560.4 13.2 %copy-start.2 = (f32[6272,128]{1,0:T(8,128)S(1)}, f32[6272,128]{1,0:T(8,128)}, u32[]{:S(2)}) copy-start(f32[6272,128]{1,0:T(8,128)} %shard_map.114) | copy-start | bytes 9633796
  571.5 11.0 %collective-permute-start.10 = (f32[32,128]{1,0:T(8,128)}, f32[32,128]{1,0:T(8,128)S(1)}, u32[]{:S(2)}, u32[]{:S(2)}) collective-permute-start(f32[32,128]{1,0:T(8,128)} %get-tuple-element.48.own), channel_id=1, source_target_pairs={{0,2},{1,3},{2,0},{3,1},{4,6},{5,7},{6,4},{7,5},{8,10},{9,11},{10,... | collective-permute-start | bytes 49160 | tf_op jit(solution)/shard_map/ppermute | solution.py:707
  573.1 9.4 %collective-permute-start.9 = (f32[32,128]{1,0:T(8,128)}, f32[32,128]{1,0:T(8,128)S(1)}, u32[]{:S(2)}, u32[]{:S(2)}) collective-permute-start(f32[32,128]{1,0:T(8,128)} %get-tuple-element.48.own), channel_id=1, source_target_pairs={{1,0},{2,1},{3,2},{0,3},{5,4},{6,5},{7,6},{4,7},{9,8},{10,9},{11,1... | collective-permute-start | bytes 49160 | tf_op jit(solution)/shard_map/ppermute | solution.py:702
  573.1 9.4 %collective-permute-start.8 = (f32[32,128]{1,0:T(8,128)}, f32[32,128]{1,0:T(8,128)S(1)}, u32[]{:S(2)}, u32[]{:S(2)}) collective-permute-start(f32[32,128]{1,0:T(8,128)} %get-tuple-element.48.own), channel_id=1, source_target_pairs={{0,1},{1,2},{2,3},{3,0},{4,5},{5,6},{6,7},{7,4},{8,9},{9,10},{10,1... | collective-permute-start | bytes 49160 | tf_op jit(solution)/shard_map/ppermute | solution.py:702
  582.5 0.6 copy-start.17
  582.5 0.6 copy-start.19
  582.5 0.6 copy-start.21

commit v2 on v1

--- a/solution.py
+++ b/solution.py
@@ -33,7 +33,7 @@
     degree = count - 1
     points = np.cos(np.pi * np.arange(count) / degree)
     legendre = np.zeros((count, count))
-    for sweep in range(60):
+    for _ in range(60):
         legendre[:, 0] = 1.0
         legendre[:, 1] = points
         for order in range(2, count):
@@ -233,7 +233,7 @@
     residual = right_side
     direction = right_side
     norm_now = squared_norm(residual, weight)
-    for turn in range(ITERS):
+    for _ in range(ITERS):
         image = mask * assemble(helmholtz_local(table, direction, shift, metrics))
         alpha = norm_now / lax.psum(inner(direction, image, weight), "elem")
         solution = solution + expand(alpha) * direction
@@ -251,7 +251,6 @@
 
 
 def paired_tables(planes):
-    half = planes // 2
     position = np.arange(planes)
     plane = np.arange(planes)
     order = plane // 2
@@ -265,25 +264,11 @@
     scaling = np.where(order == 0, 1.0, 2.0) / planes
     inverse = -(basis * scaling[None, :]).T
 
-    def columns(matrix, swap):
-        even, other = (matrix[:, 0::2], matrix[:, 1::2])
-        return np.concatenate([other, even] if swap else [even, other], axis=1)
-
-    forward = np.concatenate(
-        [
-            columns(basis[:half], False),
-            columns(basis[half:], True),
-            columns(slope[:half], False),
-            columns(slope[half:], True),
-        ]
-    )
-    top, bottom = (inverse[:, :half], inverse[:, half:])
-    backward = np.concatenate(
-        [
-            np.concatenate([top[0::2], bottom[0::2]], axis=1),
-            np.concatenate([bottom[1::2], top[1::2]], axis=1),
-        ]
-    )
+    def columns(matrix):
+        return np.concatenate([matrix[:, 0::2], matrix[:, 1::2]], axis=1)
+
+    forward = np.concatenate([columns(basis), columns(slope)])
+    backward = columns(inverse.T).T
     return (split_bf16(forward), split_bf16(backward))
 
 
@@ -324,7 +309,7 @@
     return ref[pl.ds(row, rows, stride=0), :]
 
 
-def call(body, grid, ins, outs, out_shape, scratch=(), flops=0, moved=0, limit=None):
+def call(body, grid, ins, outs, out_shape, scratch=(), flops=0, moved=0, aliases=None):
     return pl.pallas_call(
         body,
         grid=grid,
@@ -332,13 +317,16 @@
         out_specs=outs,
         out_shape=out_shape,
         scratch_shapes=list(scratch),
-        compiler_params=pltpu.CompilerParams(
-            dimension_semantics=("arbitrary",) * len(grid), vmem_limit_bytes=limit
-        ),
+        input_output_aliases=aliases or {},
+        compiler_params=pltpu.CompilerParams(dimension_semantics=("arbitrary",) * len(grid)),
         cost_estimate=pl.CostEstimate(
             flops=int(flops), bytes_accessed=int(moved), transcendentals=0
         ),
     )
+
+
+def held(count):
+    return [pl.BlockSpec(memory_space=pltpu.VMEM)] * count
 
 
 def whole(shape):
@@ -376,21 +364,25 @@
     )(rows)
 
 
-def unpack(blocks):
-    shares, square, pairs, lanes = blocks.shape
-    layers = shares // 2
+def unpack(blocks, spec, slots, pairs, layers, buffer, total):
+    lanes = blocks.shape[-1]
+    square = NODES * NODES
     per_plane = square * layers
     half = lanes // 2
-    count = 2 * pairs * per_plane
-
-    def body(x_ref, o_ref):
-        a = pl.program_id(0)
+    rows = 2 * pairs * per_plane
+
+    def body(x_ref, *refs):
+        o_ref = refs[-1]
+        a = pl.program_id(1)
         low = lanes_of((pairs, lanes)) < half
+
+        def read(d, b):
+            return x_ref[d, b] if len(x_ref.shape) == 4 else x_ref[d, 0, b]
 
         def layer(e, carry):
             for b in range(NODES):
                 start = (a * NODES + b) * layers + e
-                left, right = (x_ref[2 * e, b], x_ref[2 * e + 1, b])
+                left, right = (read(2 * e, b), read(2 * e + 1, b))
                 o_ref[pl.ds(start, pairs, stride=2 * per_plane), :] = jnp.where(
                     low, left, pltpu.roll(right, half, 1)
                 )
@@ -401,50 +393,72 @@
 
         lax.fori_loop(0, layers, layer, 0)
 
+    extra = [] if buffer is None else [buffer]
     return call(
         body,
-        (NODES,),
-        [pl.BlockSpec((shares, NODES, pairs, lanes), lambda a: (0, a, 0, 0))],
-        whole((count, lanes)),
-        jax.ShapeDtypeStruct((count, lanes), jnp.float32),
-        moved=2 * count * lanes * 4,
-    )(blocks)
-
-
-def three_pass(rhs_ref, column, tile, rotated, width):
-    both = jnp.concatenate([tile, rotated], axis=0)
-    high = both.astype(jnp.bfloat16)
-    low = (both - high.astype(jnp.float32)).astype(jnp.bfloat16)
-    depth = both.shape[0]
-    place = pl.ds(column * width, width)
-    rhs_ref[pl.ds(0, depth), place] = high
-    rhs_ref[pl.ds(depth, depth), place] = low
-    rhs_ref[pl.ds(2 * depth, depth), place] = high
+        (2, NODES),
+        [spec] + [pl.BlockSpec(memory_space=pl.ANY)] * len(extra),
+        pl.BlockSpec((rows, lanes), lambda i, a: (slots[0] + i * slots[1], 0)),
+        jax.ShapeDtypeStruct((total, lanes), jnp.float32),
+        moved=4 * rows * lanes * 4,
+        aliases={1: 0} if extra else None,
+    )(blocks, *extra)
+
+
+def paired_nodes():
+    return [(b, min(b + 1, NODES - 1)) for b in range(0, NODES, 2)]
+
+
+def three_pass(table, rhs_ref, tiles):
+    rows, lanes = tiles[0].shape
+    half = lanes // 2
+    low = lanes_of((rows, lanes)) < half
+    depth = 2 * rows
+    for place, (one, two) in enumerate(paired_nodes()):
+        first, second = (tiles[one], tiles[two])
+        cut = pl.ds(place * lanes, lanes)
+        for part in range(2):
+            if part == 0:
+                value = jnp.where(low, first, pltpu.roll(second, half, 1))
+            else:
+                value = jnp.where(low, pltpu.roll(first, half, 1), second)
+            high = value.astype(jnp.bfloat16)
+            rest = (value - high.astype(jnp.float32)).astype(jnp.bfloat16)
+            rhs_ref[pl.ds(part * rows, rows), cut] = high
+            rhs_ref[pl.ds(depth + part * rows, rows), cut] = rest
+            rhs_ref[pl.ds(2 * depth + part * rows, rows), cut] = high
+    out = jnp.dot(table, rhs_ref[...], preferred_element_type=jnp.float32)
+    fields = []
+    for field in range(table.shape[0] // depth):
+        nodes = [None] * NODES
+        for place, (one, two) in enumerate(paired_nodes()):
+            cut = slice(place * lanes, (place + 1) * lanes)
+            top = out[field * depth : field * depth + rows, cut]
+            bottom = out[field * depth + rows : (field + 1) * depth, cut]
+            nodes[one] = jnp.where(low, top, pltpu.roll(bottom, half, 1))
+            if two != one:
+                nodes[two] = jnp.where(low, pltpu.roll(top, half, 1), bottom)
+        fields.append(nodes)
+    return fields
+
+
+def rhs_scratch(table, lanes):
+    return pltpu.VMEM((table.shape[1], len(paired_nodes()) * lanes), jnp.bfloat16)
+
+
+def read_tiles(x_ref, rows, lanes):
+    return [x_ref[:, b].reshape(rows, lanes) for b in range(NODES)]
 
 
 def to_points(blocks, table):
     shares, square, pairs, lanes = blocks.shape
-    half = lanes // 2
     rows = shares * pairs
 
     def body(t_ref, x_ref, v_ref, z_ref, rhs_ref):
+        fields = three_pass(t_ref[...], rhs_ref, read_tiles(x_ref, rows, lanes))
         for b in range(NODES):
-            tile = x_ref[:, b].reshape(rows, lanes)
-            three_pass(rhs_ref, b, tile, pltpu.roll(tile, half, 1), lanes)
-        rhs = rhs_ref[...]
-        low = lanes_of((rows, lanes)) < half
-        for place, out in enumerate((v_ref, z_ref)):
-            both = [
-                jnp.dot(
-                    t_ref[pl.ds((2 * place + part) * rows, rows), :],
-                    rhs,
-                    preferred_element_type=jnp.float32,
-                )
-                for part in range(2)
-            ]
-            for b in range(NODES):
-                cut = slice(b * lanes, (b + 1) * lanes)
-                out[b] = jnp.where(low, both[0][:, cut], both[1][:, cut])
+            v_ref[b] = fields[0][b]
+            z_ref[b] = fields[1][b]
 
     spec = pl.BlockSpec((NODES, rows, lanes), lambda a: (a, 0, 0))
     shape = jax.ShapeDtypeStruct((square, rows, lanes), jnp.float32)
@@ -457,10 +471,39 @@
         ],
         [spec, spec],
         [shape, shape],
-        scratch=[pltpu.VMEM((table.shape[1], NODES * lanes), jnp.bfloat16)],
+        scratch=[rhs_scratch(table, lanes)],
         flops=2 * table.shape[0] * table.shape[1] * square * lanes,
         moved=3 * square * rows * lanes * 4,
     )(table, blocks)
+
+
+def turn_around(blocks, partial, slope_z, table, back):
+    shares, square, pairs, lanes = blocks.shape
+    rows = shares * pairs
+
+    def body(t_ref, i_ref, x_ref, g_ref, s_ref, w_ref, z_ref, o_ref, rhs_ref):
+        fields = three_pass(t_ref[...], rhs_ref, read_tiles(x_ref, rows, lanes))
+        for b in range(NODES):
+            w_ref[b] = fields[0][b]
+            z_ref[b] = fields[1][b]
+        tiles = [g_ref[b] + w_ref[b] * s_ref[b] for b in range(NODES)]
+        out = three_pass(i_ref[...], rhs_ref, tiles)[0]
+        for b in range(NODES):
+            o_ref[:, b] = out[b].reshape(shares, pairs, lanes)
+
+    spec = pl.BlockSpec((NODES, rows, lanes), lambda a: (a, 0, 0))
+    shape = jax.ShapeDtypeStruct((square, rows, lanes), jnp.float32)
+    exchanged = pl.BlockSpec((shares, NODES, pairs, lanes), lambda a: (0, a, 0, 0))
+    return call(
+        body,
+        (NODES,),
+        [whole(table.shape), whole(back.shape), exchanged, spec, spec],
+        [spec, spec, exchanged],
+        [shape, shape, jax.ShapeDtypeStruct(blocks.shape, jnp.float32)],
+        scratch=[rhs_scratch(table, lanes)],
+        flops=3 * table.shape[0] * table.shape[1] * square * lanes,
+        moved=6 * square * rows * lanes * 4,
+    )(table, back, blocks, partial, slope_z)
 
 
 def in_plane(speeds, fields, metrics, table):
@@ -523,70 +566,61 @@
     )(metrics, *arrays)
 
 
-def to_planes(partial, speed_z, slope_z, table, shares):
+def to_planes(partial, speed_z, slope_z, table, shares, place, buffers):
     square, rows, lanes = partial.shape
-    half = lanes // 2
     pairs = rows // shares
-
-    def body(t_ref, g_ref, w_ref, z_ref, o_ref, rhs_ref):
+    group = pairs // 2
+
+    def body(t_ref, g_ref, w_ref, z_ref, *refs):
+        outs, rhs_ref = (refs[-3:-1], refs[-1])
+        tiles = [g_ref[b] + w_ref[b] * z_ref[b] for b in range(NODES)]
+        nodes = three_pass(t_ref[...], rhs_ref, tiles)[0]
         for b in range(NODES):
-            tile = g_ref[b] + w_ref[b] * z_ref[b]
-            three_pass(rhs_ref, b, tile, pltpu.roll(tile, half, 1), lanes)
-        rhs = rhs_ref[...]
-        low = lanes_of((rows, lanes)) < half
-        both = [
-            jnp.dot(
-                t_ref[pl.ds(part * rows, rows), :], rhs, preferred_element_type=jnp.float32
-            )
-            for part in range(2)
-        ]
-        for b in range(NODES):
-            cut = slice(b * lanes, (b + 1) * lanes)
-            out = jnp.where(low, both[0][:, cut], both[1][:, cut])
-            o_ref[:, b] = out.reshape(shares, pairs, lanes)
+            out = nodes[b].reshape(shares, pairs, lanes)
+            for i in range(2):
+                outs[i][:, 0, b] = out[:, i * group : (i + 1) * group]
 
     spec = pl.BlockSpec((NODES, rows, lanes), lambda a: (a, 0, 0))
+    out_spec = pl.BlockSpec((shares, 1, NODES, group, lanes), lambda a: (0, place, a, 0, 0))
+    shape = jax.ShapeDtypeStruct((shares, 2, square, group, lanes), jnp.float32)
     return call(
         body,
         (NODES,),
-        [whole(table.shape), spec, spec, spec],
-        pl.BlockSpec((shares, NODES, pairs, lanes), lambda a: (0, a, 0, 0)),
-        jax.ShapeDtypeStruct((shares, square, pairs, lanes), jnp.float32),
-        scratch=[pltpu.VMEM((table.shape[1], NODES * lanes), jnp.bfloat16)],
+        [whole(table.shape), spec, spec, spec]
+        + [pl.BlockSpec(memory_space=pl.ANY)] * len(buffers),
+        [out_spec, out_spec],
+        [shape, shape],
+        scratch=[rhs_scratch(table, lanes)],
         flops=2 * table.shape[0] * table.shape[1] * square * lanes,
         moved=4 * square * rows * lanes * 4,
-    )(table, partial, speed_z, slope_z)
-
-
-def plane_divergence(sent, returned, metrics, table):
-    shares, square, pairs, lanes = sent[0].shape
-
-    def body(m_ref, s0, r0, s1, r1, o_ref, p0, p1):
+        aliases={4: 0, 5: 1} if buffers else None,
+    )(table, partial, speed_z, slope_z, *buffers)
+
+
+def first_part(sent, returned, metrics, table):
+    shares, square, pairs, lanes = sent.shape
+
+    def body(m_ref, s0, r0, o_ref, p0):
         d = pl.program_id(0)
 
         def block(s, carry):
             r = pl.ds(s * 8, 8)
             for n in range(square):
                 p0[n] = s0[0, n, r] + time_step * r0[0, n, r]
-                p1[n] = s1[0, n, r] + time_step * r1[0, n, r]
 
             def metric(kind, n):
                 return row_of(m_ref, (kind * shares + d) * square + n, 8)
 
             for a in range(NODES):
                 ns = [a * NODES + b for b in range(NODES)]
-                first = apply_line(table, [p0[n] for n in ns])
-                second = apply_line(table, [p1[n] for n in ns])
+                line = apply_line(table, [p0[n] for n in ns])
                 for b, n in enumerate(ns):
-                    o_ref[0, n, r] = metric(2, n) * first[b] + metric(3, n) * second[b]
+                    o_ref[0, n, r] = metric(2, n) * line[b]
             for b in range(NODES):
                 ns = [a * NODES + b for a in range(NODES)]
-                first = apply_line(table, [p0[n] for n in ns])
-                second = apply_line(table, [p1[n] for n in ns])
+                line = apply_line(table, [p0[n] for n in ns])
                 for a, n in enumerate(ns):
-                    o_ref[0, n, r] = o_ref[0, n, r] + (
-                        metric(0, n) * first[a] + metric(1, n) * second[a]
-                    )
+                    o_ref[0, n, r] = o_ref[0, n, r] + metric(0, n) * line[a]
             return carry
 
         lax.fori_loop(0, pairs // 8, block, 0)
@@ -595,13 +629,13 @@
     return call(
         body,
         (shares,),
-        [whole(metrics.shape)] + [spec] * 4,
+        [whole(metrics.shape), spec, spec],
         spec,
-        jax.ShapeDtypeStruct(sent[0].shape, jnp.float32),
-        scratch=[pltpu.VMEM((square, 8, lanes), jnp.float32)] * 2,
-        flops=50 * shares * square * pairs * lanes,
-        moved=5 * shares * square * pairs * lanes * 4,
-    )(metrics, sent[0], returned[0], sent[1], returned[1])
+        jax.ShapeDtypeStruct(sent.shape, jnp.float32),
+        scratch=[pltpu.VMEM((square, 8, lanes), jnp.float32)],
+        flops=30 * shares * square * pairs * lanes,
+        moved=3 * shares * square * pairs * lanes * 4,
+    )(metrics, sent, returned)
 
 
 def join_layers(y_ref, layers):
@@ -618,9 +652,10 @@
         y_ref[node] = jnp.zeros_like(y_ref[node])
 
 
-def rim_messages(read, layers, shape, partials=()):
+def rim_messages(read, layers, shape, partials):
     lane = lanes_of(shape)
     lanes = shape[-1]
+    axis = len(shape) - 1
     first = jnp.zeros(shape, jnp.float32)
     last = jnp.zeros(shape, jnp.float32)
     square = NODES * NODES
@@ -629,8 +664,10 @@
             spot = e * NODES + a
             here = lane == spot
             node = e * square + a * NODES
-            first = jnp.where(here, pltpu.roll(read(node), spot, 1), first)
-            last = jnp.where(here, pltpu.roll(read(node + NODES - 1), (spot + 1) % lanes, 1), last)
+            first = jnp.where(here, pltpu.roll(read(node), spot, axis), first)
+            last = jnp.where(
+                here, pltpu.roll(read(node + NODES - 1), (spot + 1) % lanes, axis), last
+            )
     for i, partial in enumerate(partials):
         here = lane == layers * NODES + i
         first = jnp.where(here, partial, first)
@@ -638,61 +675,91 @@
     return (first, last)
 
 
-def right_side(flat, sent, returned, weights, waves, layers):
-    shares, square, pairs, lanes = flat.shape
+def right_side(flat, sent, returned, metrics, weights, waves, table, layers, place):
+    shares, square, _, lanes = flat.shape
     half = lanes // 2
 
-    def body(m_ref, k_ref, f_ref, s_ref, r_ref, o_ref, first_ref, last_ref, c0, c1):
-        low = lanes_of((8, lanes)) < half
+    def body(m_ref, q_ref, k_ref, f_ref, s1, s2, r_ref, o_ref, first_ref, last_ref, p1, c0, c1):
+        e = pl.program_id(0)
+        lane = lanes_of((8, lanes))
+        low = lane < half
         wave = k_ref[...]
-
-        def layer(e, carry):
+        sides = (c0, c1)
+
+        @pl.when(e == 0)
+        def _():
+            first_ref[...] = jnp.zeros_like(first_ref)
+            last_ref[...] = jnp.zeros_like(last_ref)
+
+        for h in range(2):
+            d = 2 * e + h
+            side = sides[h]
             for n in range(square):
-                sides = []
-                for h in range(2):
-                    d = 2 * e + h
-                    moved = s_ref[d, n] + time_step * r_ref[d, n]
-                    along = pltpu.roll(moved, half, 1) * wave
-                    sides.append(f_ref[d, n] + row_of(m_ref, d * square + n, 8) * along)
-                c0[e * square + n] = jnp.where(low, sides[0], pltpu.roll(sides[1], half, 1))
-                c1[e * square + n] = jnp.where(low, pltpu.roll(sides[0], half, 1), sides[1])
-            return carry
-
-        lax.fori_loop(0, layers, layer, 0)
-        for part, buffer in enumerate((c0, c1)):
-            join_layers(buffer, layers)
-            first, last = rim_messages(lambda n: buffer[n], layers, (8, lanes))
-            first_ref[part] = first
-            last_ref[part] = last
-
-        def copy(e, carry):
-            for n in range(square):
-                o_ref[e * square + n, 0] = c0[e * square + n]
-                o_ref[e * square + n, 1] = c1[e * square + n]
-            return carry
-
-        lax.fori_loop(0, layers, copy, 0)
-
-    spec = pl.BlockSpec((shares, square, 8, lanes), lambda i: (0, 0, i, 0))
+                p1[n] = s1[h, n] + time_step * r_ref[h, 0, n]
+                moved = s2[h, n] + time_step * r_ref[h, 1, n]
+                along = pltpu.roll(moved, half, 1) * wave
+                side[n] = f_ref[h, n] + row_of(q_ref, d * square + n, 8) * along
+
+            def metric(kind, n):
+                return row_of(m_ref, (kind * shares + d) * square + n, 8)
+
+            for a in range(NODES):
+                ns = [a * NODES + b for b in range(NODES)]
+                line = apply_line(table, [p1[n] for n in ns])
+                for b, n in enumerate(ns):
+                    side[n] = side[n] + metric(3, n) * line[b]
+            for b in range(NODES):
+                ns = [a * NODES + b for a in range(NODES)]
+                line = apply_line(table, [p1[n] for n in ns])
+                for a, n in enumerate(ns):
+                    side[n] = side[n] + metric(1, n) * line[a]
+        rims = [[first_ref[0], last_ref[0]], [first_ref[1], last_ref[1]]]
+        for n in range(square):
+            left, right = (c0[n], c1[n])
+            parts = (
+                jnp.where(low, left, pltpu.roll(right, half, 1)),
+                jnp.where(low, pltpu.roll(left, half, 1), right),
+            )
+            for i in range(2):
+                o_ref[n, i] = parts[i]
+                a, b = divmod(n, NODES)
+                spot = e * NODES + a
+                if b == 0:
+                    rims[i][0] = jnp.where(lane == spot, pltpu.roll(parts[i], spot, 1), rims[i][0])
+                if b == NODES - 1:
+                    rims[i][1] = jnp.where(
+                        lane == spot, pltpu.roll(parts[i], spot + 1, 1), rims[i][1]
+                    )
+        for i in range(2):
+            first_ref[i] = rims[i][0]
+            last_ref[i] = rims[i][1]
+
+    spec = pl.BlockSpec((2, square, 8, lanes), lambda e: (e, 0, place, 0))
     nodes = layers * square
-    rim = pl.BlockSpec((2, 8, lanes), lambda i: (0, i, 0))
-    rim_shape = jax.ShapeDtypeStruct((2, pairs, lanes), jnp.float32)
-    out = call(
-        body,
-        (pairs // 8,),
-        [whole(weights.shape), pl.BlockSpec((8, lanes), lambda i: (i, 0)), spec, spec, spec],
-        [pl.BlockSpec((nodes, 2, 8, lanes), lambda i: (0, 0, i, 0)), rim, rim],
-        [jax.ShapeDtypeStruct((nodes, 2, pairs, lanes), jnp.float32), rim_shape, rim_shape],
-        scratch=[pltpu.VMEM((nodes, 8, lanes), jnp.float32)] * 2,
-        flops=10 * shares * square * pairs * lanes,
-        moved=4 * shares * square * pairs * lanes * 4,
-    )(weights, waves, flat, sent, returned)
-    planes = 2 * pairs
-    return (
-        out[0].reshape(nodes, planes, lanes),
-        out[1].reshape(planes, lanes),
-        out[2].reshape(planes, lanes),
-    )
+    rim_shape = jax.ShapeDtypeStruct((2, 8, lanes), jnp.float32)
+    scratch = pltpu.VMEM((square, 8, lanes), jnp.float32)
+    return call(
+        body,
+        (layers,),
+        [
+            whole(metrics.shape),
+            whole(weights.shape),
+            pl.BlockSpec((8, lanes), lambda e: (place, 0)),
+            spec,
+            spec,
+            spec,
+            pl.BlockSpec((2, 2, square, 8, lanes), lambda e: (e, 0, 0, 0, 0)),
+        ],
+        [
+            pl.BlockSpec((square, 2, 8, lanes), lambda e: (e, 0, 0, 0)),
+            whole((2, 8, lanes)),
+            whole((2, 8, lanes)),
+        ],
+        [jax.ShapeDtypeStruct((nodes, 2, 8, lanes), jnp.float32), rim_shape, rim_shape],
+        scratch=[scratch] * 3,
+        flops=40 * shares * square * 8 * lanes,
+        moved=6 * shares * square * 8 * lanes * 4,
+    )(metrics, weights, waves, flat, sent[1], sent[2], returned)
 
 
 def swap_rims(first, last):
@@ -707,8 +774,9 @@
     return lax.ppermute(first, "elem", [(i, (i + 2) % size) for i in range(size)])
 
 
-def join_columns(read, write, before, after, layers):
+def join_columns(read, ref, before, after, layers):
     lanes = before.shape[-1]
+    axis = len(before.shape) - 1
     lane = lanes_of(before.shape)
     square = NODES * NODES
     for e in range(layers):
@@ -716,38 +784,57 @@
             spot = e * NODES + a
             node = e * square + a * NODES
             first, last = (read(node), read(node + NODES - 1))
-            beyond = pltpu.roll(after, lanes - 1 - spot, 1)
-            ahead = jnp.where(lane == lanes - 1, beyond, pltpu.roll(first, lanes - 1, 1))
+            beyond = pltpu.roll(after, lanes - 1 - spot, axis)
+            ahead = jnp.where(lane == lanes - 1, beyond, pltpu.roll(first, lanes - 1, axis))
             right = last + ahead
-            mine = first + (pltpu.roll(before, lanes - spot, 1) if spot else before)
-            write(node + NODES - 1, right)
-            write(node, jnp.where(lane == 0, mine, pltpu.roll(right, 1, 1)))
-
-
-def share_of(layers, e, a, b):
-    value = 1.0
-    if b in (0, NODES - 1):
-        value = 0.5 * value
+            mine = first + (pltpu.roll(before, lanes - spot, axis) if spot else before)
+            ref[node + NODES - 1] = right
+            ref[node] = jnp.where(lane == 0, mine, pltpu.roll(right, 1, axis))
+
+
+def join(source, ref, before, after, layers):
+    square = NODES * NODES
+
+    def copy(e, carry):
+        for n in range(square):
+            if 0 < n % NODES < NODES - 1:
+                ref[e * square + n] = source[e * square + n]
+        return carry
+
+    lax.fori_loop(0, layers, copy, 0)
+    join_columns(lambda n: source[n], ref, before, after, layers)
+    join_layers(ref, layers)
+
+
+def each_node(layers, step):
+    def layer(e, carry):
+        for n in range(NODES * NODES):
+            step(e * NODES * NODES + n)
+        return carry
+
+    lax.fori_loop(0, layers, layer, 0)
+
+
+def share_of(layers, e, a):
     if a == 0:
-        value = jnp.where(e > 0, 0.5, 1.0) * value
+        return jnp.where(e > 0, 0.5, 1.0)
     if a == NODES - 1:
-        value = jnp.where(e < layers - 1, 0.5, 0.0) * value
-    return value
+        return jnp.where(e < layers - 1, 0.5, 0.0)
+    return 1.0
 
 
 def helmholtz(r_ref, y_ref, flux_ref, g_ref, shift, layers, table, dot_only=False):
     square = NODES * NODES
     nodes = layers * square
-    rows, lanes = shift.shape
     turned = table.T
-    zero = jnp.zeros((rows, lanes), jnp.float32)
+    zero = jnp.zeros(shift.shape, jnp.float32)
 
     def layer(e, carry):
         norm, energy = carry
         base = e * square
 
         def metric(kind, n):
-            return row_of(g_ref, kind * nodes + base + n, rows)
+            return row_of(g_ref, kind * nodes + base + n, 8)
 
         for b in range(NODES):
             ns = [a * NODES + b for a in range(NODES)]
@@ -759,27 +846,27 @@
             line = [r_ref[base + n] for n in ns]
             beside = apply_line(table, line)
             second = []
+            rest = []
             part = zero
             for b, n in enumerate(ns):
                 radial = flux_ref[n]
                 cross = metric(1, n)
                 one = metric(0, n) * radial + cross * beside[b]
                 two = cross * radial + metric(2, n) * beside[b]
-                held = shift * metric(3, n) * line[b]
-                weight = 0.5 if b in (0, NODES - 1) else 1.0
-                square_here = line[b] * line[b]
-                part = part + (square_here * weight if weight != 1.0 else square_here)
+                same = shift * metric(3, n) * line[b]
+                whole_weight = line[b] * line[b]
+                part = part + (0.5 * whole_weight if b in (0, NODES - 1) else whole_weight)
                 if dot_only:
-                    energy = energy + radial * one + beside[b] * two + held * line[b]
+                    energy = energy + (radial * one + beside[b] * two + same * line[b])
                 else:
                     flux_ref[n] = one
                     second.append(two)
-                    y_ref[base + n] = held
-            norm = norm + part * share_of(layers, e, a, 1)
+                    rest.append(same)
+            norm = norm + part * share_of(layers, e, a)
             if not dot_only:
                 back = apply_line(turned, second)
                 for b, n in enumerate(ns):
-                    y_ref[base + n] = y_ref[base + n] + back[b]
+                    y_ref[base + n] = rest[b] + back[b]
         if not dot_only:
             for b in range(NODES):
                 ns = [a * NODES + b for a in range(NODES)]
@@ -791,14 +878,15 @@
         return (norm, energy)
 
     norm, energy = lax.fori_loop(0, layers, layer, (zero, zero))
+    axis = len(shift.shape) - 1
     return (
-        jnp.sum(norm, axis=1, keepdims=True),
-        jnp.sum(energy, axis=1, keepdims=True),
+        jnp.sum(norm, axis=axis, keepdims=True),
+        jnp.sum(energy, axis=axis, keepdims=True),
     )
 
 
 def lane_value(block, lane):
-    return block[:, lane : lane + 1]
+    return block[..., lane : lane + 1]
 
 
 def sums_from(own, left, right, far, layers):
@@ -807,188 +895,151 @@
     return (lane_value(total, spot), lane_value(total, spot + 1))
 
 
-def scalars_block(shape, values):
+def scalars_block(shape, values, spot=0):
     lane = lanes_of(shape)
     out = jnp.zeros(shape, jnp.float32)
     for i, value in enumerate(values):
-        out = jnp.where(lane == i, value, out)
+        out = jnp.where(lane == spot + i, value, out)
     return out
 
 
-def solver_specs(nodes, planes, lanes):
-    field = pl.BlockSpec((nodes, 8, lanes), lambda i: (0, i, 0))
-    small = pl.BlockSpec((8, lanes), lambda i: (i, 0))
-    shapes = (
-        jax.ShapeDtypeStruct((nodes, planes, lanes), jnp.float32),
-        jax.ShapeDtypeStruct((planes, lanes), jnp.float32),
+def shapes_of(field):
+    return (
+        jax.ShapeDtypeStruct(field.shape, jnp.float32),
+        jax.ShapeDtypeStruct(field.shape[1:], jnp.float32),
+        pltpu.VMEM((NODES * NODES,) + field.shape[1:], jnp.float32),
     )
-    return (field, small, shapes)
 
 
 def first_image(raw, before, after, shift, geo, layers, table):
-    nodes, planes, lanes = raw.shape
-    field, small, (field_shape, small_shape) = solver_specs(nodes, planes, lanes)
+    field, small, flux_scratch = shapes_of(raw)
+    shape = raw.shape[1:]
 
     def body(g_ref, k_ref, f_ref, b_ref, a_ref, r_ref, y_ref, first_ref, last_ref, flux):
-        def copy(e, carry):
-            for n in range(NODES * NODES):
-                r_ref[e * NODES * NODES + n] = f_ref[e * NODES * NODES + n]
-            return carry
-
-        lax.fori_loop(0, layers, copy, 0)
-
-        def write(n, value):
-            r_ref[n] = value
-
-        join_columns(lambda n: f_ref[n], write, b_ref[...], a_ref[...], layers)
+        join(f_ref, r_ref, b_ref[...], a_ref[...], layers)
         sums = helmholtz(r_ref, y_ref, flux, g_ref, k_ref[...], layers, table)
-        join_layers(y_ref, layers)
-        first_ref[...], last_ref[...] = rim_messages(
-            lambda n: y_ref[n], layers, (8, lanes), sums
-        )
+        first_ref[...], last_ref[...] = rim_messages(lambda n: y_ref[n], layers, shape, sums)
 
     return call(
         body,
-        (planes // 8,),
-        [whole(geo.shape), small, field, small, small],
+        (),
+        held(5),
+        held(4),
         [field, field, small, small],
-        [field_shape, field_shape, small_shape, small_shape],
-        scratch=[pltpu.VMEM((NODES * NODES, 8, lanes), jnp.float32)],
-        flops=80 * nodes * planes * lanes,
-        moved=3 * nodes * planes * lanes * 4,
+        scratch=[flux_scratch],
+        flops=80 * raw.size,
+        moved=12 * raw.size,
     )(geo, shift, raw, before, after)
 
 
 def second_image(start, image, messages, shift, geo, layers, table):
-    nodes, planes, lanes = start.shape
-    field, small, (field_shape, small_shape) = solver_specs(nodes, planes, lanes)
+    field, small, flux_scratch = shapes_of(start)
+    shape = start.shape[1:]
 
     def body(g_ref, k_ref, r0, y0, own, left, right, far, *rest):
         w_ref, y_ref, first_ref, last_ref, scalar_ref, r1, flux = rest
         norm, energy = sums_from(own, left, right, far, layers)
-        alpha = jnp.broadcast_to(norm / energy, (8, lanes))
-
-        def move(e, carry):
-            for n in range(NODES * NODES):
-                node = e * NODES * NODES + n
-                w = y0[node]
-                w_ref[node] = w
-                r1[node] = r0[node] - alpha * w
-            return carry
-
-        lax.fori_loop(0, layers, move, 0)
-
-        def write(n, value):
-            w_ref[n] = value
-            r1[n] = r0[n] - alpha * value
-
-        join_columns(lambda n: y0[n], write, left[...], right[...], layers)
+        alpha = jnp.broadcast_to(norm / energy, shape)
+        join(y0, w_ref, left[...], right[...], layers)
+
+        def move(node):
+            r1[node] = r0[node] - alpha * w_ref[node]
+
+        each_node(layers, move)
         sums = helmholtz(r1, y_ref, flux, g_ref, k_ref[...], layers, table)
-        join_layers(y_ref, layers)
-        first_ref[...], last_ref[...] = rim_messages(
-            lambda n: y_ref[n], layers, (8, lanes), sums
-        )
-        scalar_ref[...] = scalars_block((8, lanes), (alpha, norm, energy))
+        first_ref[...], last_ref[...] = rim_messages(lambda n: y_ref[n], layers, shape, sums)
+        scalar_ref[...] = scalars_block(shape, (alpha, norm, energy))
 
     return call(
         body,
-        (planes // 8,),
-        [whole(geo.shape), small, field, field] + [small] * 4,
+        (),
+        held(8),
+        held(5),
         [field, field, small, small, small],
-        [field_shape, field_shape, small_shape, small_shape, small_shape],
-        scratch=[
-            pltpu.VMEM((nodes, 8, lanes), jnp.float32),
-            pltpu.VMEM((NODES * NODES, 8, lanes), jnp.float32),
-        ],
-        flops=80 * nodes * planes * lanes,
-        moved=4 * nodes * planes * lanes * 4,
+        scratch=[pltpu.VMEM(start.shape, jnp.float32), flux_scratch],
+        flops=80 * start.size,
+        moved=16 * start.size,
     )(geo, shift, start, image, *messages)
 
 
 def third_energy(start, joined, image, messages, scalars, shift, geo, layers, table):
-    nodes, planes, lanes = start.shape
-    field, small, (field_shape, small_shape) = solver_specs(nodes, planes, lanes)
+    field, small, flux_scratch = shapes_of(start)
+    shape = start.shape[1:]
 
     def body(g_ref, k_ref, r0, w0, y1, own, left, right, far, old, *rest):
-        r2, d2, sums_ref, scalar_ref, flux = rest
+        r2, d2, sums_ref, scalar_ref, w1, flux = rest
         norm, energy = sums_from(own, left, right, far, layers)
         before = old[...]
-        alpha = jnp.broadcast_to(lane_value(before, 0), (8, lanes))
+        alpha = jnp.broadcast_to(lane_value(before, 0), shape)
         ratio = norm / lane_value(before, 1)
         curve = energy - ratio * ratio * lane_value(before, 2)
-        step = jnp.broadcast_to(norm / curve, (8, lanes))
-        beta = jnp.broadcast_to(ratio, (8, lanes))
-
-        def at(node, image_value):
+        step = jnp.broadcast_to(norm / curve, shape)
+        beta = jnp.broadcast_to(ratio, shape)
+        join(y1, w1, left[...], right[...], layers)
+
+        def move(node):
             w = w0[node]
             start_value = r0[node]
             moved = start_value - alpha * w
             d2[node] = moved + beta * start_value
-            r2[node] = moved - step * (image_value + beta * w)
-
-        def move(e, carry):
-            for n in range(NODES * NODES):
-                at(e * NODES * NODES + n, y1[e * NODES * NODES + n])
-            return carry
-
-        lax.fori_loop(0, layers, move, 0)
-        join_columns(lambda n: y1[n], at, left[...], right[...], layers)
+            r2[node] = moved - step * (w1[node] + beta * w)
+
+        each_node(layers, move)
         sums = helmholtz(r2, None, flux, g_ref, k_ref[...], layers, table, dot_only=True)
-        lane = lanes_of((8, lanes))
-        spot = layers * NODES
-        sums_ref[...] = jnp.where(lane == spot, sums[0], jnp.where(lane == spot + 1, sums[1], 0.0))
-        scalar_ref[...] = scalars_block((8, lanes), (alpha, norm, curve, step))
+        sums_ref[...] = scalars_block(shape, sums, layers * NODES)
+        scalar_ref[...] = scalars_block(shape, (alpha, norm, curve, step))
 
     return call(
         body,
-        (planes // 8,),
-        [whole(geo.shape), small, field, field, field] + [small] * 5,
+        (),
+        held(10),
+        held(4),
         [field, field, small, small],
-        [field_shape, field_shape, small_shape, small_shape],
-        scratch=[pltpu.VMEM((NODES * NODES, 8, lanes), jnp.float32)],
-        flops=60 * nodes * planes * lanes,
-        moved=5 * nodes * planes * lanes * 4,
+        scratch=[pltpu.VMEM(start.shape, jnp.float32), flux_scratch],
+        flops=60 * start.size,
+        moved=20 * start.size,
     )(geo, shift, start, joined, image, *messages, scalars)
 
 
-def finish(start, direction, residual, messages, scalars, layers):
-    nodes, planes, lanes = start.shape
+def finish(start, direction, residual, messages, scalars, layers, place, buffer, total):
+    nodes, _, rows, lanes = start.shape
+    shape = start.shape[1:]
     square = NODES * NODES
-    per_plane = nodes
-    pairs = planes // 2
-    field, small, _ = solver_specs(nodes, planes, lanes)
-
-    def body(r0, d2, r2, own, left, right, far, old, o_ref):
-        i = pl.program_id(0)
+
+    def body(r0, d2, r2, own, left, right, far, old, *refs):
+        o_ref = refs[-1]
         norm, energy = sums_from(own, left, right, far, layers)
         before = old[...]
         ratio = norm / lane_value(before, 1)
         curve = energy - ratio * ratio * lane_value(before, 2)
         step = norm / curve
-        third = jnp.broadcast_to(step, (8, lanes))
-        second = jnp.broadcast_to(lane_value(before, 3) + step * ratio, (8, lanes))
-        first = jnp.broadcast_to(lane_value(before, 0), (8, lanes))
-        row = i * 8
-        plane = jnp.where(row < pairs, 2 * row, 2 * (row - pairs) + 1)
+        third = jnp.broadcast_to(step, shape)
+        second = jnp.broadcast_to(lane_value(before, 3) + step * ratio, shape)
+        first = jnp.broadcast_to(lane_value(before, 0), shape)
 
         def layer(e, carry):
             for n in range(square):
                 node = e * square + n
                 value = first * r0[node] + second * d2[node] + third * r2[node]
-                o_ref[pl.ds(plane * per_plane + n * layers + e, 8, stride=2 * per_plane), :] = value
+                for i in range(2):
+                    o_ref[pl.ds(i * nodes + n * layers + e, rows, stride=2 * nodes), :] = value[i]
             return carry
 
         lax.fori_loop(0, layers, layer, 0)
 
+    extra = [] if buffer is None else [buffer]
     return call(
         body,
-        (planes // 8,),
-        [field] * 3 + [small] * 5,
-        whole((planes * nodes, lanes)),
-        jax.ShapeDtypeStruct((planes * nodes, lanes), jnp.float32),
-        flops=6 * nodes * planes * lanes,
-        moved=4 * nodes * planes * lanes * 4,
-    )(start, direction, residual, *messages, scalars)
+        (1,),
+        [whole(start.shape)] * 3
+        + [whole(shape)] * 5
+        + [pl.BlockSpec(memory_space=pl.ANY)] * len(extra),
+        pl.BlockSpec((2 * rows * nodes, lanes), lambda i: (place, 0)),
+        jax.ShapeDtypeStruct((total, lanes), jnp.float32),
+        flops=6 * start.size,
+        moved=16 * start.size,
+        aliases={8: 0} if extra else None,
+    )(start, direction, residual, *messages, scalars, *extra)
 
 
 def halves(values, shares):
@@ -997,7 +1048,11 @@
     return jnp.stack(parts, axis=2).reshape(values.shape[0], shares, NODES * NODES, 2 * half)
 
 
-def on_device_paired(velocity, radial_dx, radial_dy, around_dx, around_dy, jacobian):
+def on_device_paired(*arrays):
+    return paired_step(*arrays)
+
+
+def paired_step(velocity, radial_dx, radial_dy, around_dx, around_dy, jacobian):
     table = derivative_table()
     modes = lax.axis_size("mode")
     mode = lax.axis_index("mode")
@@ -1023,46 +1078,61 @@
     wave = pair[:, None] * spanwise_wave
     low = (jnp.arange(lanes) < lanes // 2)[None, :]
     waves = jnp.where(low, wave, -wave)
-    shift = plane_shift(first_plane, local_planes, planes).reshape(pairs, 2).T.reshape(-1, 1)
-    shift = jnp.broadcast_to(shift, (local_planes, lanes))
+    shift = plane_shift(first_plane, local_planes, planes).reshape(pairs, 2).T
+    shift = jnp.broadcast_to(shift.reshape(2, 2, pairs // 2, 1), (2, 2, pairs // 2, lanes))
 
     def exchange(blocks):
         return lax.all_to_all(blocks, "mode", split_axis=0, concat_axis=0, tiled=True)
 
-    sent = []
-    points = []
-    for comp in range(3):
-        sent.append(pack(rows, comp, layers, pairs, lanes))
-    for comp in range(3):
-        points.append(to_points(exchange(sent[comp]), forward))
-    speeds = [p[0] for p in points]
-    early = in_plane(speeds[:2], speeds[:2], here, table)
-    late = in_plane(speeds[:2], speeds[2:], here, table)
-    partial = list(early) + list(late)
-    returned = []
-    for comp in range(3):
-        blocks = to_planes(partial[comp], speeds[2], points[comp][1], backward, modes)
-        returned.append(exchange(blocks))
-    advection = jnp.stack([unpack(r) for r in returned])
+    sent = [pack(rows, comp, layers, pairs, lanes) for comp in range(3)]
+    arrived = [exchange(blocks) for blocks in sent]
+    speed_x, slope_0 = to_points(arrived[0], forward)
+    speed_y, slope_1 = to_points(arrived[1], forward)
+    speeds = [speed_x, speed_y]
+    partial = in_plane(speeds, speeds, here, table)
+    speed_z, slope_2, blocks = turn_around(arrived[2], partial[0], slope_0, forward, backward)
+    returned = [exchange(blocks)]
+    last = in_plane(speeds, [speed_z], here, table)[0]
+    blocks = to_planes(partial[1], speed_z, slope_1, backward, modes, 0, ())
+    blocks = to_planes(last, speed_z, slope_2, backward, modes, 1, blocks)
+    returned.append(exchange(blocks[0]))
+    returned.append(exchange(blocks[1]))
+
+    group = pairs // 2
+    own_rows = local_planes * square * layers
+    whole_spec = pl.BlockSpec((modes, NODES, group, lanes), lambda i, a: (0, a, i, 0))
+    part_spec = pl.BlockSpec((modes, 1, NODES, group, lanes), lambda i, a: (0, i, a, 0, 0))
+    advection = unpack(returned[0], whole_spec, (0, 1), group, layers, None, 3 * own_rows)
+    flat = first_part(sent[0], returned[0], flux, table)
+
+    def solve(place, flat, buffer):
+        own_shift = shift[:, place]
+        raw, first, last = right_side(
+            flat, sent, returned[1 + place], flux, scaled, waves, table, layers, place
+        )
+        before, after = swap_rims(first, last)
+        start, image, first, last = first_image(raw, before, after, own_shift, geo, layers, table)
+        messages = (first,) + swap_rims(first, last) + (opposite(first),)
+        joined, image, first, last, scalars = second_image(
+            start, image, messages, own_shift, geo, layers, table
+        )
+        messages = (first,) + swap_rims(first, last) + (opposite(first),)
+        residual, direction, sums, scalars = third_energy(
+            start, joined, image, messages, scalars, own_shift, geo, layers, table
+        )
+        messages = (sums,) + swap_rims(sums, sums) + (opposite(sums),)
+        return finish(
+            start, direction, residual, messages, scalars, layers, place, buffer, own_rows
+        )
+
+    pressure = solve(0, flat, None)
+    advection = unpack(returned[1], part_spec, (2, 2), group, layers, advection, 3 * own_rows)
+    flat, pressure, advection = lax.optimization_barrier((flat, pressure, advection))
+    pressure = solve(1, flat, pressure)
+    advection = unpack(returned[2], part_spec, (3, 2), group, layers, advection, 3 * own_rows)
     advection = advection.reshape(3, local_planes, NODES, NODES, layers, lanes)
-    advection = advection.transpose(0, 1, 4, 2, 3, 5)
-
-    flat = plane_divergence(sent, returned, flux, table)
-    raw, first, last = right_side(flat, sent[2], returned[2], scaled, waves, layers)
-    before, after = swap_rims(first, last)
-    start, image, first, last = first_image(raw, before, after, shift, geo, layers, table)
-    messages = (first,) + swap_rims(first, last) + (opposite(first),)
-    joined, image, first, last, scalars = second_image(
-        start, image, messages, shift, geo, layers, table
-    )
-    messages = (first,) + swap_rims(first, last) + (opposite(first),)
-    residual, direction, sums, scalars = third_energy(
-        start, joined, image, messages, scalars, shift, geo, layers, table
-    )
-    messages = (sums,) + swap_rims(sums, sums) + (opposite(sums),)
-    pressure = finish(start, direction, residual, messages, scalars, layers)
     pressure = pressure.reshape(local_planes, NODES, NODES, layers, lanes)
-    return (advection, pressure.transpose(0, 3, 1, 2, 4))
+    return (advection.transpose(0, 1, 4, 2, 3, 5), pressure.transpose(0, 3, 1, 2, 4))
 
 
 def paired_fits(mesh, shape):
@@ -1087,6 +1157,7 @@
         P(None, None, None, "elem"),
         P(None, None, None, "elem"),
     )
+
 
     def step(velocity, *rest):
         body = on_device_paired if paired_fits(mesh, velocity.shape) else on_device

time: 593 us -> 602 us (1.015)
  waiting for transfers between devices: 340 us -> 184 us
  blocking collectives: 0 us -> 152 us
  Pallas kernels: 182 us -> 196 us
  other arithmetic: 15.3 us -> 6.42 us
    all_to_all x6 -> x4, waiting for transfers between devices: 337 us -> 171 us  [exchange(): lax.all_to_all(blocks, 'mode', split_axis=0, concat_axis=0, tiled=True)]
    all_to_all x0 -> x2, blocking collectives: none -> 152 us  [exchange(): lax.all_to_all(blocks, 'mode', split_axis=0, concat_axis=0, tiled=True)]
    pallas_call x12 -> x17, Pallas kernels: 116 us -> 140 us  [the longest x3 34.3 us: unpack(): call(body, (2, NODES), [spec] + [pl.BlockSpec(memory_space=pl.ANY)] * len...]
    pallas_call x3 -> x2, Pallas kernels: 30.8 us -> 19.7 us  [to_points(): call(body, (NODES,), [whole(table.shape), pl.BlockSpec((shares, NODES, pa...]
    transpose x1 -> x0, other arithmetic: 8.9 us -> none  [on_device_paired(): advection = advection.transpose(0, 1, 4, 2, 3, 5)]
    ppermute x8 -> x16, starting transfers between devices: 5.64 us -> 14 us  [swap_rims(): return (lax.ppermute(last, 'elem', up), lax.ppermute(first, 'elem', down))]
    all_to_all x6 -> x4, starting transfers between devices: 27.2 us -> 19.2 us  [exchange(): lax.all_to_all(blocks, 'mode', split_axis=0, concat_axis=0, tiled=True)]
    ppermute x3 -> x6, waiting for transfers between devices: 1.94 us -> 9.13 us  [opposite(): lax.ppermute(first, 'elem', [(i, (i + 2) % size) for i in range(size)])]
  transfers between devices with their start and end apart: 17 -> 26, of which waited for: 8 -> 11; matrix products, arithmetic and copies ran while one was open for 4% -> 3% of each run, Pallas kernels for 17% -> 19%
where the time goes in v2:
time: 602 us; the launch traced here: 599 us
  Pallas kernels  196 us (33%)
  waiting for transfers between devices  184 us (31%)
  blocking collectives  152 us (25%)
  starting transfers between devices  39.3 us (7%)
  local copies, waits for them, and re-layouts  19.9 us (3%)
  other arithmetic  6.42 us (1%)
    all_to_all x4, waiting for transfers between devices, exchange(): lax.all_to_all(blocks, 'mode', split_axis=0, concat_axis=0, tiled=True)  171 us
    all_to_all x2, blocking collectives, exchange(): lax.all_to_all(blocks, 'mode', split_axis=0, concat_axis=0, tiled=True)  152 us
    pallas_call x3, Pallas kernels, unpack(): call(body, (2, NODES), [spec] + [pl.BlockSpec(memory_space=pl.ANY)] * len...  34.3 us
    pallas_call x3, Pallas kernels, pack(): call(body, (NODES,), [pl.BlockSpec((1, rows.shape[1], lanes), lambda a: (...  19.9 us
    pallas_call x2, Pallas kernels, to_points(): call(body, (NODES,), [whole(table.shape), pl.BlockSpec((shares, NODES, pa...  19.7 us
    pallas_call x2, Pallas kernels, to_planes(): call(body, (NODES,), [whole(table.shape), spec, spec, spec] + [pl.BlockSp...  19.6 us
    all_to_all x4, starting transfers between devices, exchange(): lax.all_to_all(blocks, 'mode', split_axis=0, concat_axis=0, tiled=True)  19.2 us
    pallas_call x2, Pallas kernels, in_plane(): call(body, (rows // step,), [whole(metrics.shape)] + [spec] * len(arrays)...  15.9 us
  transfers between devices with their start and end apart: 26, of which 11 were waited for; matrix products, arithmetic and copies ran while one was open for 3% of the time, Pallas kernels for 19%

profile of v2, /device:TPU:0, one launch (start us, length us, event | category | flops | bytes accessed | tf_op | source)
XLA Modules:
  0.0 599.0 jit_solution(10076408211265245495)
XLA Ops:
  0.6 6.7 %shard_map.106.s1 = f32[8,49,16,128]{3,2,1,0:T(8,128)} custom-call(f32[3,6272,128]{2,1,0:T(8,128)} %bitcast.42), custom_call_target="tpu_custom_call" | custom-call | bytes 6422528 | tf_op jit(solution)/shard_map/pallas_call | solution.py:357
  7.3 7.3 %all-to-all-start.1 = ((f32[8,49,16,128]{3,2,1,0:T(8,128)}), f32[8,49,16,128]{3,2,1,0:T(8,128)S(1)}, u32[]{:S(2)}, u32[]{:S(2)}) async-start(f32[8,49,16,128]{3,2,1,0:T(8,128)} %shard_map.106.s1), calls=%async_computation.1 | async-start | bytes 6422528 | tf_op jit(solution)/shard_map/all_to_all | solution.py:1085
  14.7 6.6 %shard_map.104.s0 = f32[8,49,16,128]{3,2,1,0:T(8,128)} custom-call(f32[3,6272,128]{2,1,0:T(8,128)} %bitcast.43), custom_call_target="tpu_custom_call" | custom-call | bytes 6422528 | tf_op jit(solution)/shard_map/pallas_call | solution.py:357
  21.2 65.5 %all-to-all-done.1.x_ref = f32[8,49,16,128]{3,2,1,0:T(8,128)S(1)} async-done(((f32[8,49,16,128]{3,2,1,0:T(8,128)}), f32[8,49,16,128]{3,2,1,0:T(8,128)S(1)}, u32[]{:S(2)}, u32[]{:S(2)}) %all-to-all-start.1) | async-done | bytes 3211296 | tf_op jit(solution)/shard_map/all_to_all | solution.py:1085
  86.8 4.5 all-to-all-start
  91.2 6.7 %shard_map.108.s2 = f32[8,49,16,128]{3,2,1,0:T(8,128)} custom-call(f32[3,6272,128]{2,1,0:T(8,128)} %bitcast.44), custom_call_target="tpu_custom_call" | custom-call | bytes 6422528 | tf_op jit(solution)/shard_map/pallas_call | solution.py:357
  97.9 64.9 %all-to-all-done.x_ref = f32[8,49,16,128]{3,2,1,0:T(8,128)} async-done(((f32[8,49,16,128]{3,2,1,0:T(8,128)}), f32[8,49,16,128]{3,2,1,0:T(8,128)}, u32[]{:S(2)}, u32[]{:S(2)}) %all-to-all-start) | async-done | bytes 3211296 | tf_op jit(solution)/shard_map/all_to_all | solution.py:1085
  162.8 3.7 all-to-all-start.2
  169.7 9.9 %shard_map.107 = (f32[49,128,128]{2,1,0:T(8,128)}, f32[49,128,128]{2,1,0:T(8,128)}) custom-call(bf16[512,768]{1,0:T(8,128)(2,1)} %constant.55.clone.t_ref, f32[8,49,16,128]{3,2,1,0:T(8,128)} %copy-done.2), custom_call_target="tpu_custom_call" | custom-call | flops 4932501504 | bytes 9633792 | tf_op jit(solution)/shard_map/pallas_call | solution.py:465
  179.5 9.9 %shard_map.105 = (f32[49,128,128]{2,1,0:T(8,128)}, f32[49,128,128]{2,1,0:T(8,128)}) custom-call(bf16[512,768]{1,0:T(8,128)(2,1)} %constant.55.clone.t_ref, f32[8,49,16,128]{3,2,1,0:T(8,128)} %all-to-all-done.x_ref), custom_call_target="tpu_custom_call" | custom-call | flops 4932501504 | bytes 9633792 | tf_op jit(solution)/shard_map/pallas_call | solution.py:465
  189.4 8.4 %shard_map.109 = (f32[49,128,128]{2,1,0:T(8,128)}, f32[49,128,128]{2,1,0:T(8,128)}) custom-call(f32[196,128]{1,0:T(8,128)} %reshape.74.m_ref, f32[49,128,128]{2,1,0:T(8,128)} %get-tuple-element.50.refs_0_, f32[49,128,128]{2,1,0:T(8,128)} %get-tuple-element.51.refs_1_), custom_call_target="tpu_custom_call" | custom-call | flops 48168960 | bytes 12845056 | tf_op jit(solution)/shard_map/pallas_call | solution.py:558
  197.8 40.9 %all-to-all-done.2.x_ref = f32[8,49,16,128]{3,2,1,0:T(8,128)S(1)} async-done(((f32[8,49,16,128]{3,2,1,0:T(8,128)}), f32[8,49,16,128]{3,2,1,0:T(8,128)S(1)}, u32[]{:S(2)}, u32[]{:S(2)}) %all-to-all-start.2) | async-done | bytes 3211296 | tf_op jit(solution)/shard_map/all_to_all | solution.py:1085
  240.4 12.7 %shard_map.110 = (f32[49,128,128]{2,1,0:T(8,128)}, f32[49,128,128]{2,1,0:T(8,128)}, f32[8,49,16,128]{3,2,1,0:T(8,128)}) custom-call(bf16[512,768]{1,0:T(8,128)(2,1)} %constant.55.clone.t_ref, bf16[256,768]{1,0:T(8,128)(2,1)} %constant.56.clone.i_ref.t_ref, f32[8,49,16,128]{3,2,1,0:T(8,128)} %copy-done.3, f32[49,128,128]{2,1,0:T(8,128)} %get-tuple-element.52.g_ref, ...), custom_call_target="tpu_custom_call" | custom-call | flops 7398752256 | bytes 19267584 | tf_op jit(solution)/shard_map/pallas_call | solution.py:497
  253.1 7.5 %shard_map.111.g_ref = f32[49,128,128]{2,1,0:T(8,128)} custom-call(f32[196,128]{1,0:T(8,128)} %reshape.74.m_ref, f32[49,128,128]{2,1,0:T(8,128)} %get-tuple-element.50.refs_0_, f32[49,128,128]{2,1,0:T(8,128)} %get-tuple-element.51.refs_1_, f32[49,128,128]{2,1,0:T(8,128)} %get-tuple-element.54.refs_2_.w_ref), custom_call_target="tpu_custom_call" | custom-call | flops 24084480 | bytes 12845056 | tf_op jit(solution)/shard_map/pallas_call | solution.py:558
  260.6 9.8 %shard_map.112 = (f32[8,2,49,8,128]{4,3,2,1,0:T(8,128)}, f32[8,2,49,8,128]{4,3,2,1,0:T(8,128)}) custom-call(bf16[256,768]{1,0:T(8,128)(2,1)} %constant.56.clone.i_ref.t_ref, f32[49,128,128]{2,1,0:T(8,128)} %get-tuple-element.56.g_ref, f32[49,128,128]{2,1,0:T(8,128)} %get-tuple-element.54.refs_2_.w_ref, f32[49,128,128]{2,1,0:T(8,128)} %get-tuple-element.57.z_ref), custom_call_target="tpu_custom_call" | custom-call | flops 2466250752 | bytes 12845056 | tf_op jit(solution)/shard_map/pallas_call | solution.py:586
  270.4 9.8 %shard_map.113 = (f32[8,2,49,8,128]{4,3,2,1,0:T(8,128)}, f32[8,2,49,8,128]{4,3,2,1,0:T(8,128)}) custom-call(bf16[256,768]{1,0:T(8,128)(2,1)} %constant.56.clone.i_ref.t_ref, f32[49,128,128]{2,1,0:T(8,128)} %shard_map.111.g_ref, f32[49,128,128]{2,1,0:T(8,128)} %get-tuple-element.54.refs_2_.w_ref, ...), custom_call_target="tpu_custom_call", output_to_operand_aliasing={{0}: (4, {}), {1}: (5, {})} | custom-call | flops 2466250752 | bytes 12845056 | tf_op jit(solution)/shard_map/pallas_call | solution.py:586
  280.2 76.9 %all_to_all.30.r_ref.x_ref = f32[8,2,49,8,128]{4,3,2,1,0:T(8,128)} all-to-all(f32[8,2,49,8,128]{4,3,2,1,0:T(8,128)} %get-tuple-element.62), channel_id=1, replica_groups=mesh['mode'=8,'elem'=4] {'mode'}, dimensions={0} | all-to-all | bytes 6422528 | tf_op jit(solution)/shard_map/all_to_all | solution.py:1085
  357.2 75.3 %all_to_all.31.r0.x_ref = f32[8,49,16,128]{3,2,1,0:T(8,128)} all-to-all(f32[8,49,16,128]{3,2,1,0:T(8,128)S(1)} %copy-done.4), channel_id=1, replica_groups=mesh['mode'=8,'elem'=4] {'mode'}, dimensions={0} | all-to-all | bytes 6422528 | tf_op jit(solution)/shard_map/all_to_all | solution.py:1085
  432.5 3.8 all-to-all-start.3
  436.3 2.1 reshape.76
  438.4 1.9 multiply_bitcast_fusion.2
  442.3 2.2 mul.89
  444.4 2.4 mul.90.m_ref
  447.5 8.1 %shard_map.114.f_ref = f32[8,49,16,128]{3,2,1,0:T(8,128)} custom-call(f32[1568,128]{1,0:T(8,128)} %mul.90.m_ref, f32[8,49,16,128]{3,2,1,0:T(8,128)} %shard_map.104.s0, f32[8,49,16,128]{3,2,1,0:T(8,128)} %all_to_all.31.r0.x_ref), custom_call_target="tpu_custom_call" | custom-call | flops 24084480 | bytes 9633792 | tf_op jit(solution)/shard_map/pallas_call | solution.py:629
  455.6 6.7 %shard_map.115 = (f32[196,2,8,128]{3,2,1,0:T(8,128)}, f32[2,8,128]{2,1,0:T(8,128)}, f32[2,8,128]{2,1,0:T(8,128)}) custom-call(f32[1568,128]{1,0:T(8,128)} %mul.90.m_ref, f32[392,128]{1,0:T(8,128)} %reshape_reshape.4.q_ref, f32[16,128]{1,0:T(8,128)} %broadcast_select_fusion.k_ref, f32[8,49,16,128]{3,2,1,0:T(8,128)} %shard_map.114.f_ref, ...), custom_call_target="tpu_custom_call" | custom-call | flops 16056320 | bytes 9633792 | tf_op jit(solution)/shard_map/pallas_call | solution.py:741
  465.9 1.8 reshape.78.g_ref
  468.4 6.8 %shard_map.116 = (f32[196,2,8,128]{3,2,1,0:T(8,128)}, f32[196,2,8,128]{3,2,1,0:T(8,128)}, f32[2,8,128]{2,1,0:T(8,128)}, f32[2,8,128]{2,1,0:T(8,128)}) custom-call(f32[784,128]{1,0:T(8,128)} %reshape.78.g_ref, f32[2,8,128]{2,1,0:T(8,128)} %broadcast_in_dim.43.k_ref, f32[196,2,8,128]{3,2,1,0:T(8,128)} %get-tuple-element.63.f_ref, f32[2,8,128]{2,1,0:T(8,128)} %copy-done.11, ...), custom_call_target="tpu_custom_call" | custom-call | flops 32112640 | bytes 4816896 | tf_op jit(solution)/shard_map/pallas_call | solution.py:923
  475.2 1.7 collective-permute-start.3
  478.5 2.3 collective-permute-done.4.far
  481.4 7.6 %shard_map.117 = (f32[196,2,8,128]{3,2,1,0:T(8,128)}, f32[196,2,8,128]{3,2,1,0:T(8,128)}, f32[2,8,128]{2,1,0:T(8,128)}, f32[2,8,128]{2,1,0:T(8,128)}, f32[2,8,128]{2,1,0:T(8,128)}) custom-call(f32[784,128]{1,0:T(8,128)} %reshape.78.g_ref, f32[2,8,128]{2,1,0:T(8,128)} %broadcast_in_dim.43.k_ref, f32[196,2,8,128]{3,2,1,0:T(8,128)} %get-tuple-element.66.r0, ...), custom_call_target="tpu_custom_call" | custom-call | flops 32112640 | bytes 6422528 | tf_op jit(solution)/shard_map/pallas_call | solution.py:953
  489.0 1.7 collective-permute-start.6
  492.4 2.3 collective-permute-done.7.far
  495.2 7.4 %shard_map.118 = (f32[196,2,8,128]{3,2,1,0:T(8,128)}, f32[196,2,8,128]{3,2,1,0:T(8,128)}, f32[2,8,128]{2,1,0:T(8,128)}, f32[2,8,128]{2,1,0:T(8,128)}) custom-call(f32[784,128]{1,0:T(8,128)} %reshape.78.g_ref, f32[2,8,128]{2,1,0:T(8,128)} %broadcast_in_dim.43.k_ref, f32[196,2,8,128]{3,2,1,0:T(8,128)} %get-tuple-element.66.r0, ...), custom_call_target="tpu_custom_call" | custom-call | flops 24084480 | bytes 8028160 | tf_op jit(solution)/shard_map/pallas_call | solution.py:992
  504.1 1.7 collective-permute-start.9
  505.9 11.5 %shard_map.120.refs_0_ = f32[18816,128]{1,0:T(8,128)} custom-call(f32[8,49,16,128]{3,2,1,0:T(8,128)} %all_to_all.31.r0.x_ref), custom_call_target="tpu_custom_call" | custom-call | bytes 6422528 | tf_op jit(solution)/shard_map/pallas_call | solution.py:397
  517.3 11.4 %shard_map.121.refs_0_ = f32[18816,128]{1,0:T(8,128)} custom-call(f32[8,2,49,8,128]{4,3,2,1,0:T(8,128)} %all_to_all.30.r_ref.x_ref, f32[18816,128]{1,0:T(8,128)} %shard_map.120.refs_0_), custom_call_target="tpu_custom_call", output_to_operand_aliasing={{}: (1, {})} | custom-call | bytes 6422528 | tf_op jit(solution)/shard_map/pallas_call | solution.py:397
  529.4 4.3 shard_map.119.refs_0_
  533.7 1.8 copy-done
  535.4 6.6 %shard_map.123 = (f32[196,2,8,128]{3,2,1,0:T(8,128)}, f32[2,8,128]{2,1,0:T(8,128)}, f32[2,8,128]{2,1,0:T(8,128)}) custom-call(f32[1568,128]{1,0:T(8,128)} %mul.90.m_ref, f32[392,128]{1,0:T(8,128)} %reshape_reshape.4.q_ref, f32[16,128]{1,0:T(8,128)} %broadcast_select_fusion.k_ref, f32[8,49,16,128]{3,2,1,0:T(8,128)} %shard_map.114.f_ref, ...), custom_call_target="tpu_custom_call" | custom-call | flops 16056320 | bytes 9633792 | tf_op jit(solution)/shard_map/pallas_call | solution.py:741
  546.1 6.8 %shard_map.124 = (f32[196,2,8,128]{3,2,1,0:T(8,128)}, f32[196,2,8,128]{3,2,1,0:T(8,128)}, f32[2,8,128]{2,1,0:T(8,128)}, f32[2,8,128]{2,1,0:T(8,128)}) custom-call(f32[784,128]{1,0:T(8,128)} %reshape.78.g_ref, f32[2,8,128]{2,1,0:T(8,128)} %broadcast_in_dim.48.k_ref, f32[196,2,8,128]{3,2,1,0:T(8,128)} %get-tuple-element.81.f_ref, f32[2,8,128]{2,1,0:T(8,128)} %copy-done.28, ...), custom_call_target="tpu_custom_call" | custom-call | flops 32112640 | bytes 4816896 | tf_op jit(solution)/shard_map/pallas_call | solution.py:923
  556.2 2.3 collective-permute-done.15.far
  559.1 7.7 %shard_map.125 = (f32[196,2,8,128]{3,2,1,0:T(8,128)}, f32[196,2,8,128]{3,2,1,0:T(8,128)}, f32[2,8,128]{2,1,0:T(8,128)}, f32[2,8,128]{2,1,0:T(8,128)}, f32[2,8,128]{2,1,0:T(8,128)}) custom-call(f32[784,128]{1,0:T(8,128)} %reshape.78.g_ref, f32[2,8,128]{2,1,0:T(8,128)} %broadcast_in_dim.48.k_ref, f32[196,2,8,128]{3,2,1,0:T(8,128)} %get-tuple-element.84.r0, ...), custom_call_target="tpu_custom_call" | custom-call | flops 32112640 | bytes 6422528 | tf_op jit(solution)/shard_map/pallas_call | solution.py:953
  566.8 1.7 collective-permute-start.17
  570.1 2.3 collective-permute-done.18.far
  573.0 7.4 %shard_map.126 = (f32[196,2,8,128]{3,2,1,0:T(8,128)}, f32[196,2,8,128]{3,2,1,0:T(8,128)}, f32[2,8,128]{2,1,0:T(8,128)}, f32[2,8,128]{2,1,0:T(8,128)}) custom-call(f32[784,128]{1,0:T(8,128)} %reshape.78.g_ref, f32[2,8,128]{2,1,0:T(8,128)} %broadcast_in_dim.48.k_ref, f32[196,2,8,128]{3,2,1,0:T(8,128)} %get-tuple-element.84.r0, ...), custom_call_target="tpu_custom_call" | custom-call | flops 24084480 | bytes 8028160 | tf_op jit(solution)/shard_map/pallas_call | solution.py:992
  580.4 1.7 collective-permute-start.20
  582.7 11.4 %shard_map.122 = f32[18816,128]{1,0:T(8,128)} custom-call(f32[8,2,49,8,128]{4,3,2,1,0:T(8,128)} %copy-done, f32[18816,128]{1,0:T(8,128)} %shard_map.121.refs_0_), custom_call_target="tpu_custom_call", output_to_operand_aliasing={{}: (1, {})} | custom-call | bytes 6422528 | tf_op jit(solution)/shard_map/pallas_call | solution.py:397
  594.7 4.3 shard_map.127
  (129 shorter events, 29.4 us)
Async XLA Ops:
  7.3 79.4 %all-to-all-start.1 = ((f32[8,49,16,128]{3,2,1,0:T(8,128)}), f32[8,49,16,128]{3,2,1,0:T(8,128)S(1)}, u32[]{:S(2)}, u32[]{:S(2)}) async-start(f32[8,49,16,128]{3,2,1,0:T(8,128)} %shard_map.106.s1), calls=%async_computation.1 | async-start | bytes 6422528 | tf_op jit(solution)/shard_map/all_to_all | solution.py:1085
  86.8 11.1 %copy-start.2 = (f32[8,49,16,128]{3,2,1,0:T(8,128)}, f32[8,49,16,128]{3,2,1,0:T(8,128)S(1)}, u32[]{:S(2)}) copy-start(f32[8,49,16,128]{3,2,1,0:T(8,128)S(1)} %all-to-all-done.1.x_ref) | copy-start | bytes 9633796
  86.8 76.0 %all-to-all-start = ((f32[8,49,16,128]{3,2,1,0:T(8,128)}), f32[8,49,16,128]{3,2,1,0:T(8,128)}, u32[]{:S(2)}, u32[]{:S(2)}) async-start(f32[8,49,16,128]{3,2,1,0:T(8,128)} %shard_map.104.s0), calls=%async_computation | async-start | bytes 6422528 | tf_op jit(solution)/shard_map/all_to_all | solution.py:1085
  97.9 68.6 %copy-start.7 = (f32[4,7,7,128]{3,0,2,1:T(4,128)S(1)}, f32[4,7,7,128]{3,0,2,1:T(4,128)}, u32[]{:S(2)}) copy-start(f32[4,7,7,128]{3,0,2,1:T(4,128)} %param.10) | copy-start | bytes 301060
  97.9 68.6 %copy-start.8 = (f32[4,7,7,128]{3,0,2,1:T(4,128)S(1)}, f32[4,7,7,128]{3,0,2,1:T(4,128)}, u32[]{:S(2)}) copy-start(f32[4,7,7,128]{3,0,2,1:T(4,128)} %param.11) | copy-start | bytes 301060
  97.9 68.6 %copy-start.10 = (f32[4,7,7,128]{3,0,2,1:T(4,128)S(1)}, f32[4,7,7,128]{3,0,2,1:T(4,128)}, u32[]{:S(2)}) copy-start(f32[4,7,7,128]{3,0,2,1:T(4,128)} %param.12) | copy-start | bytes 301060
  162.8 75.9 %all-to-all-start.2 = ((f32[8,49,16,128]{3,2,1,0:T(8,128)}), f32[8,49,16,128]{3,2,1,0:T(8,128)S(1)}, u32[]{:S(2)}, u32[]{:S(2)}) async-start(f32[8,49,16,128]{3,2,1,0:T(8,128)} %shard_map.108.s2), calls=%async_computation.2 | async-start | bytes 6422528 | tf_op jit(solution)/shard_map/all_to_all | solution.py:1085
  168.1 1.0 copy-start.1
  238.7 1.6 copy-start.3
  280.2 76.9 %copy-start.4 = (f32[8,49,16,128]{3,2,1,0:T(8,128)S(1)}, f32[8,49,16,128]{3,2,1,0:T(8,128)}, u32[]{:S(2)}) copy-start(f32[8,49,16,128]{3,2,1,0:T(8,128)} %get-tuple-element.61) | copy-start | bytes 9633796
  432.5 6.0 copy-start.9
  432.5 6.0 copy-start.33
  432.5 101.2 %all-to-all-start.3 = ((f32[8,2,49,8,128]{4,3,2,1,0:T(8,128)}), f32[8,2,49,8,128]{4,3,2,1,0:T(8,128)S(1)}, u32[]{:S(2)}, u32[]{:S(2)}) async-start(f32[8,2,49,8,128]{4,3,2,1,0:T(8,128)} %get-tuple-element.60), calls=%async_computation.3 | async-start | bytes 6422528 | tf_op jit(solution)/shard_map/all_to_all | solution.py:1085
  455.6 8.5 %copy-start.5 = (f32[1,4,7,7,128]{4,1,3,2,0:T(4,128)S(1)}, f32[1,4,7,7,128]{4,1,3,2,0:T(4,128)}, u32[]{:S(2)}) copy-start(f32[1,4,7,7,128]{4,1,3,2,0:T(4,128)} %get-tuple-element.101) | copy-start | bytes 301060
  455.6 8.5 %copy-start.6 = (f32[1,4,7,7,128]{4,1,3,2,0:T(4,128)S(1)}, f32[1,4,7,7,128]{4,1,3,2,0:T(4,128)}, u32[]{:S(2)}) copy-start(f32[1,4,7,7,128]{4,1,3,2,0:T(4,128)} %get-tuple-element.102) | copy-start | bytes 301060
  462.3 5.4 collective-permute-start
  462.3 5.4 collective-permute-start.1
  467.7 0.7 copy-start.11
  475.2 3.3 collective-permute-start.2
  475.2 3.3 collective-permute-start.3
  477.0 3.9 collective-permute-start.4
  478.5 2.3 copy-start.17
  478.5 2.3 copy-start.23
  489.0 3.3 collective-permute-start.5
  489.0 3.3 collective-permute-start.6
  490.8 3.9 collective-permute-start.7
  492.3 2.3 copy-start.13
  492.4 2.3 copy-start.20
  502.6 26.1 %collective-permute-start.10 = (f32[2,8,128]{2,1,0:T(8,128)}, f32[2,8,128]{2,1,0:T(8,128)S(1)}, u32[]{:S(2)}, u32[]{:S(2)}) collective-permute-start(f32[2,8,128]{2,1,0:T(8,128)} %get-tuple-element.77.own), channel_id=1, source_target_pairs={{0,2},{1,3},{2,0},{3,1},{4,6},{5,7},{6,4},{7,5},{8,10},{9,11},{10,... | collective-permute-start | bytes 24584 | tf_op jit(solution)/shard_map/ppermute | solution.py:774
  504.1 24.6 %collective-permute-start.8 = (f32[2,8,128]{2,1,0:T(8,128)}, f32[2,8,128]{2,1,0:T(8,128)S(1)}, u32[]{:S(2)}, u32[]{:S(2)}) collective-permute-start(f32[2,8,128]{2,1,0:T(8,128)} %get-tuple-element.77.own), channel_id=1, source_target_pairs={{0,1},{1,2},{2,3},{3,0},{4,5},{5,6},{6,7},{7,4},{8,9},{9,10},{10,1... | collective-permute-start | bytes 24584 | tf_op jit(solution)/shard_map/ppermute | solution.py:769
  504.1 24.6 %collective-permute-start.9 = (f32[2,8,128]{2,1,0:T(8,128)}, f32[2,8,128]{2,1,0:T(8,128)S(1)}, u32[]{:S(2)}, u32[]{:S(2)}) collective-permute-start(f32[2,8,128]{2,1,0:T(8,128)} %get-tuple-element.77.own), channel_id=1, source_target_pairs={{1,0},{2,1},{3,2},{0,3},{5,4},{6,5},{7,6},{4,7},{9,8},{10,9},{11,1... | collective-permute-start | bytes 24584 | tf_op jit(solution)/shard_map/ppermute | solution.py:769
  533.7 1.8 copy-start
  542.1 3.3 collective-permute-start.11
  542.1 3.3 collective-permute-start.12
  545.4 0.7 copy-start.28
  552.9 3.3 collective-permute-start.13
  553.5 2.7 collective-permute-start.14
  554.7 3.9 collective-permute-start.15
  556.2 2.3 copy-start.18
  556.2 2.3 copy-start.24
  566.8 3.3 collective-permute-start.16
  566.8 3.3 collective-permute-start.17
  568.5 3.9 collective-permute-start.18
  570.1 2.3 copy-start.12
  570.1 2.3 copy-start.19
  580.4 13.7 %collective-permute-start.19 = (f32[2,8,128]{2,1,0:T(8,128)}, f32[2,8,128]{2,1,0:T(8,128)S(1)}, u32[]{:S(2)}, u32[]{:S(2)}) collective-permute-start(f32[2,8,128]{2,1,0:T(8,128)} %get-tuple-element.95.own), channel_id=1, source_target_pairs={{0,1},{1,2},{2,3},{3,0},{4,5},{5,6},{6,7},{7,4},{8,9},{9,10},{10,1... | collective-permute-start | bytes 24584 | tf_op jit(solution)/shard_map/ppermute | solution.py:769
  580.4 13.7 %collective-permute-start.20 = (f32[2,8,128]{2,1,0:T(8,128)}, f32[2,8,128]{2,1,0:T(8,128)S(1)}, u32[]{:S(2)}, u32[]{:S(2)}) collective-permute-start(f32[2,8,128]{2,1,0:T(8,128)} %get-tuple-element.95.own), channel_id=1, source_target_pairs={{1,0},{2,1},{3,2},{0,3},{5,4},{6,5},{7,6},{4,7},{9,8},{10,9},{11,1... | collective-permute-start | bytes 24584 | tf_op jit(solution)/shard_map/ppermute | solution.py:769
  582.1 12.0 %collective-permute-start.21 = (f32[2,8,128]{2,1,0:T(8,128)}, f32[2,8,128]{2,1,0:T(8,128)S(1)}, u32[]{:S(2)}, u32[]{:S(2)}) collective-permute-start(f32[2,8,128]{2,1,0:T(8,128)} %get-tuple-element.95.own), channel_id=1, source_target_pairs={{0,2},{1,3},{2,0},{3,1},{4,6},{5,7},{6,4},{7,5},{8,10},{9,11},{10,... | collective-permute-start | bytes 24584 | tf_op jit(solution)/shard_map/ppermute | solution.py:774
  (12 other events, 7.3 us)

commit v3 on v2

--- a/solution.py
+++ b/solution.py
@@ -10,6 +10,8 @@
 
 NODES = 7
 ITERS = 3
+GRANT = 24 * 2**20
+WHOLE_GRANT = 67043328
 
 
 spanwise_wave = 2.0 * math.pi / 64.0
@@ -309,7 +311,7 @@
     return ref[pl.ds(row, rows, stride=0), :]
 
 
-def call(body, grid, ins, outs, out_shape, scratch=(), flops=0, moved=0, aliases=None):
+def call(body, grid, ins, outs, out_shape, scratch=(), flops=0, moved=0, aliases=None, grant=GRANT):
     return pl.pallas_call(
         body,
         grid=grid,
@@ -318,7 +320,9 @@
         out_shape=out_shape,
         scratch_shapes=list(scratch),
         input_output_aliases=aliases or {},
-        compiler_params=pltpu.CompilerParams(dimension_semantics=("arbitrary",) * len(grid)),
+        compiler_params=pltpu.CompilerParams(
+            dimension_semantics=("arbitrary",) * len(grid), vmem_limit_bytes=grant
+        ),
         cost_estimate=pl.CostEstimate(
             flops=int(flops), bytes_accessed=int(moved), transcendentals=0
         ),
@@ -333,22 +337,57 @@
     return pl.BlockSpec(shape, lambda *_: (0,) * len(shape))
 
 
+def turn(tiles):
+    tiles = list(tiles)
+    sub = lax.broadcasted_iota(jnp.int32, tiles[0].shape, 0)
+    size = len(tiles)
+    step = size // 2
+    while step:
+        keep = (sub & step) == 0
+        for i in range(size):
+            if not i & step:
+                one, two = (tiles[i], tiles[i + step])
+                tiles[i] = jnp.where(keep, one, pltpu.roll(two, step, 0))
+                tiles[i + step] = jnp.where(keep, pltpu.roll(one, size - step, 0), two)
+        step //= 2
+    return tiles
+
+
+def turn_all(read, write, count):
+    def some(s, carry):
+        for i in range(NODES):
+            t = s * NODES + i
+            for r, tile in enumerate(turn([read(k, t) for k in range(8)])):
+                write(t, r, tile)
+        return carry
+
+    lax.fori_loop(0, count // NODES, some, 0)
+
+
+def rows_at(k, unit, t):
+    return pl.ds(pl.multiple_of(k * unit + 8 * t, 8), 8)
+
+
 def pack(rows, comp, layers, pairs, lanes):
     square = NODES * NODES
     per_plane = square * layers
+    unit = 2 * per_plane
     half = lanes // 2
 
-    def body(x_ref, o_ref):
-        a = pl.program_id(0)
-        low = lanes_of((pairs, lanes)) < half
+    def body(x_ref, o_ref, mid):
+        low = lanes_of((8, lanes)) < half
+
+        def write(t, r, tile):
+            mid[8 * t + r] = tile
+
+        turn_all(lambda k, t: x_ref[0, rows_at(k, unit, t), :], write, unit // 8)
 
         def layer(e, carry):
-            for b in range(NODES):
-                start = (a * NODES + b) * layers + e
-                cos = x_ref[0, pl.ds(start, pairs, stride=2 * per_plane), :]
-                sin = x_ref[0, pl.ds(start + per_plane, pairs, stride=2 * per_plane), :]
-                o_ref[2 * e, b] = jnp.where(low, cos, pltpu.roll(sin, half, 1))
-                o_ref[2 * e + 1, b] = jnp.where(low, pltpu.roll(cos, half, 1), sin)
+            for n in range(square):
+                cos = mid[n * layers + e]
+                sin = mid[per_plane + n * layers + e]
+                o_ref[2 * e, n] = jnp.where(low, cos, pltpu.roll(sin, half, 1))
+                o_ref[2 * e + 1, n] = jnp.where(low, pltpu.roll(cos, half, 1), sin)
             return carry
 
         lax.fori_loop(0, layers, layer, 0)
@@ -356,51 +395,53 @@
     size = rows.shape[1] * lanes * 4
     return call(
         body,
-        (NODES,),
-        [pl.BlockSpec((1, rows.shape[1], lanes), lambda a: (comp, 0, 0))],
-        pl.BlockSpec((2 * layers, NODES, pairs, lanes), lambda a: (0, a, 0, 0)),
+        (pairs // 8,),
+        [pl.BlockSpec((1, 8 * unit, lanes), lambda g: (comp, g, 0))],
+        pl.BlockSpec((2 * layers, square, 8, lanes), lambda g: (0, 0, g, 0)),
         jax.ShapeDtypeStruct((2 * layers, square, pairs, lanes), jnp.float32),
+        scratch=[pltpu.VMEM((unit, 8, lanes), jnp.float32)],
+        grant=WHOLE_GRANT,
         moved=2 * size,
     )(rows)
 
 
-def unpack(blocks, spec, slots, pairs, layers, buffer, total):
+def unpack(blocks, spec, slots, layers, buffer, total):
     lanes = blocks.shape[-1]
     square = NODES * NODES
     per_plane = square * layers
+    unit = 2 * per_plane
     half = lanes // 2
-    rows = 2 * pairs * per_plane
 
     def body(x_ref, *refs):
-        o_ref = refs[-1]
-        a = pl.program_id(1)
-        low = lanes_of((pairs, lanes)) < half
-
-        def read(d, b):
-            return x_ref[d, b] if len(x_ref.shape) == 4 else x_ref[d, 0, b]
+        o_ref, mid = refs[-2:]
+        low = lanes_of((8, lanes)) < half
+
+        def read(d, n):
+            return x_ref[d, n] if len(x_ref.shape) == 4 else x_ref[d, 0, n]
 
         def layer(e, carry):
-            for b in range(NODES):
-                start = (a * NODES + b) * layers + e
-                left, right = (read(2 * e, b), read(2 * e + 1, b))
-                o_ref[pl.ds(start, pairs, stride=2 * per_plane), :] = jnp.where(
-                    low, left, pltpu.roll(right, half, 1)
-                )
-                o_ref[pl.ds(start + per_plane, pairs, stride=2 * per_plane), :] = jnp.where(
-                    low, pltpu.roll(left, half, 1), right
-                )
+            for n in range(square):
+                left, right = (read(2 * e, n), read(2 * e + 1, n))
+                mid[n * layers + e] = jnp.where(low, left, pltpu.roll(right, half, 1))
+                mid[per_plane + n * layers + e] = jnp.where(low, pltpu.roll(left, half, 1), right)
             return carry
 
         lax.fori_loop(0, layers, layer, 0)
+
+        def write(t, r, tile):
+            o_ref[rows_at(r, unit, t), :] = tile
+
+        turn_all(lambda k, t: mid[8 * t + k], write, unit // 8)
 
     extra = [] if buffer is None else [buffer]
     return call(
         body,
-        (2, NODES),
+        (2,),
         [spec] + [pl.BlockSpec(memory_space=pl.ANY)] * len(extra),
-        pl.BlockSpec((rows, lanes), lambda i, a: (slots[0] + i * slots[1], 0)),
+        pl.BlockSpec((8 * unit, lanes), lambda i: (slots[0] + i * slots[1], 0)),
         jax.ShapeDtypeStruct((total, lanes), jnp.float32),
-        moved=4 * rows * lanes * 4,
+        scratch=[pltpu.VMEM((unit, 8, lanes), jnp.float32)],
+        moved=4 * 8 * unit * lanes * 4,
         aliases={1: 0} if extra else None,
     )(blocks, *extra)
 
@@ -473,6 +514,7 @@
         [shape, shape],
         scratch=[rhs_scratch(table, lanes)],
         flops=2 * table.shape[0] * table.shape[1] * square * lanes,
+        grant=WHOLE_GRANT,
         moved=3 * square * rows * lanes * 4,
     )(table, blocks)
 
@@ -502,6 +544,7 @@
         [shape, shape, jax.ShapeDtypeStruct(blocks.shape, jnp.float32)],
         scratch=[rhs_scratch(table, lanes)],
         flops=3 * table.shape[0] * table.shape[1] * square * lanes,
+        grant=WHOLE_GRANT,
         moved=6 * square * rows * lanes * 4,
     )(table, back, blocks, partial, slope_z)
 
@@ -562,6 +605,7 @@
         [spec] * count,
         [shape] * count,
         flops=30 * count * square * rows * lanes,
+        grant=WHOLE_GRANT,
         moved=(len(arrays) + count) * square * rows * lanes * 4,
     )(metrics, *arrays)
 
@@ -592,6 +636,7 @@
         [shape, shape],
         scratch=[rhs_scratch(table, lanes)],
         flops=2 * table.shape[0] * table.shape[1] * square * lanes,
+        grant=WHOLE_GRANT,
         moved=4 * square * rows * lanes * 4,
         aliases={4: 0, 5: 1} if buffers else None,
     )(table, partial, speed_z, slope_z, *buffers)
@@ -634,6 +679,7 @@
         jax.ShapeDtypeStruct(sent.shape, jnp.float32),
         scratch=[pltpu.VMEM((square, 8, lanes), jnp.float32)],
         flops=30 * shares * square * pairs * lanes,
+        grant=WHOLE_GRANT,
         moved=3 * shares * square * pairs * lanes * 4,
     )(metrics, sent, returned)
 
@@ -758,6 +804,7 @@
         [jax.ShapeDtypeStruct((nodes, 2, 8, lanes), jnp.float32), rim_shape, rim_shape],
         scratch=[scratch] * 3,
         flops=40 * shares * square * 8 * lanes,
+        grant=WHOLE_GRANT,
         moved=6 * shares * square * 8 * lanes * 4,
     )(metrics, weights, waves, flat, sent[1], sent[2], returned)
 
@@ -1006,8 +1053,10 @@
     shape = start.shape[1:]
     square = NODES * NODES
 
+    unit = 2 * nodes
+
     def body(r0, d2, r2, own, left, right, far, old, *refs):
-        o_ref = refs[-1]
+        o_ref, mid = refs[-2:]
         norm, energy = sums_from(own, left, right, far, layers)
         before = old[...]
         ratio = norm / lane_value(before, 1)
@@ -1022,10 +1071,15 @@
                 node = e * square + n
                 value = first * r0[node] + second * d2[node] + third * r2[node]
                 for i in range(2):
-                    o_ref[pl.ds(i * nodes + n * layers + e, rows, stride=2 * nodes), :] = value[i]
+                    mid[i * nodes + n * layers + e] = value[i]
             return carry
 
         lax.fori_loop(0, layers, layer, 0)
+
+        def write(t, r, tile):
+            o_ref[rows_at(r, unit, t), :] = tile
+
+        turn_all(lambda k, t: mid[8 * t + k], write, unit // 8)
 
     extra = [] if buffer is None else [buffer]
     return call(
@@ -1036,6 +1090,7 @@
         + [pl.BlockSpec(memory_space=pl.ANY)] * len(extra),
         pl.BlockSpec((2 * rows * nodes, lanes), lambda i: (place, 0)),
         jax.ShapeDtypeStruct((total, lanes), jnp.float32),
+        scratch=[pltpu.VMEM((unit, rows, lanes), jnp.float32)],
         flops=6 * start.size,
         moved=16 * start.size,
         aliases={8: 0} if extra else None,
@@ -1100,9 +1155,9 @@
 
     group = pairs // 2
     own_rows = local_planes * square * layers
-    whole_spec = pl.BlockSpec((modes, NODES, group, lanes), lambda i, a: (0, a, i, 0))
-    part_spec = pl.BlockSpec((modes, 1, NODES, group, lanes), lambda i, a: (0, i, a, 0, 0))
-    advection = unpack(returned[0], whole_spec, (0, 1), group, layers, None, 3 * own_rows)
+    whole_spec = pl.BlockSpec((modes, square, group, lanes), lambda i: (0, 0, i, 0))
+    part_spec = pl.BlockSpec((modes, 1, square, group, lanes), lambda i: (0, i, 0, 0, 0))
+    advection = unpack(returned[0], whole_spec, (0, 1), layers, None, 3 * own_rows)
     flat = first_part(sent[0], returned[0], flux, table)
 
     def solve(place, flat, buffer):
@@ -1126,10 +1181,10 @@
         )
 
     pressure = solve(0, flat, None)
-    advection = unpack(returned[1], part_spec, (2, 2), group, layers, advection, 3 * own_rows)
+    advection = unpack(returned[1], part_spec, (2, 2), layers, advection, 3 * own_rows)
     flat, pressure, advection = lax.optimization_barrier((flat, pressure, advection))
     pressure = solve(1, flat, pressure)
-    advection = unpack(returned[2], part_spec, (3, 2), group, layers, advection, 3 * own_rows)
+    advection = unpack(returned[2], part_spec, (3, 2), layers, advection, 3 * own_rows)
     advection = advection.reshape(3, local_planes, NODES, NODES, layers, lanes)
     pressure = pressure.reshape(local_planes, NODES, NODES, layers, lanes)
     return (advection.transpose(0, 1, 4, 2, 3, 5), pressure.transpose(0, 3, 1, 2, 4))
@@ -1142,8 +1197,8 @@
         ring == 4
         and columns == 128 * ring
         and modes == 2 * layers
-        and planes % (16 * modes) == 0
-        and planes == 2 * 128
+        and layers % 4 == 0
+        and planes == 32 * modes
         and (layers * NODES + 2 <= 128)
     )
 

time: 602 us -> 553 us (0.919)
  Pallas kernels: 196 us -> 142 us
  waiting for transfers between devices: 184 us -> 198 us
  local copies, waits for them, and re-layouts: 19.9 us -> 8.38 us
    pallas_call x6, Pallas kernels: 54.2 us -> 25.7 us  [the longest x3 14.1 us: pack(): call(body, (pairs // 8,), [pl.BlockSpec((1, 8 * unit, lanes), lambda g: (...]
    all_to_all x4, waiting for transfers between devices: 171 us -> 188 us  [exchange(): lax.all_to_all(blocks, 'mode', split_axis=0, concat_axis=0, tiled=True)]
    pallas_call x2, Pallas kernels: 14.8 us -> 7.25 us  [third_energy(): call(body, (), held(10), held(4), [field, field, small, small], scratch=[...]
    pallas_call x2, Pallas kernels: 15.3 us -> 8.27 us  [second_image(): call(body, (), held(8), held(5), [field, field, small, small, small], scr...]
    pallas_call x2, Pallas kernels: 13.6 us -> 7.48 us  [first_image(): call(body, (), held(5), held(4), [field, field, small, small], scratch=[f...]
  transfers between devices with their start and end apart: 26 -> 26, of which waited for: 11 -> 10; matrix products, arithmetic and copies ran while one was open for 3% -> 1% of each run, Pallas kernels for 19% -> 14%
where the time goes in v3:
time: 553 us; the launch traced here: 551 us
  waiting for transfers between devices  198 us (36%)
  blocking collectives  152 us (27%)
  Pallas kernels  142 us (26%)
  starting transfers between devices  44.5 us (8%)
  local copies, waits for them, and re-layouts  8.38 us (2%)
    all_to_all x4, waiting for transfers between devices, exchange(): lax.all_to_all(blocks, 'mode', split_axis=0, concat_axis=0, tiled=True)  188 us
    all_to_all x2, blocking collectives, exchange(): lax.all_to_all(blocks, 'mode', split_axis=0, concat_axis=0, tiled=True)  152 us
    all_to_all x4, starting transfers between devices, exchange(): lax.all_to_all(blocks, 'mode', split_axis=0, concat_axis=0, tiled=True)  20.8 us
    pallas_call x2, Pallas kernels, to_points(): call(body, (NODES,), [whole(table.shape), pl.BlockSpec((shares, NODES, pa...  19.8 us
    pallas_call x2, Pallas kernels, to_planes(): call(body, (NODES,), [whole(table.shape), spec, spec, spec] + [pl.BlockSp...  19.6 us
    pallas_call x2, Pallas kernels, in_plane(): call(body, (rows // step,), [whole(metrics.shape)] + [spec] * len(arrays)...  15.9 us
    ppermute x16, starting transfers between devices, swap_rims(): return (lax.ppermute(last, 'elem', up), lax.ppermute(first, 'elem', down))  14.7 us
    pallas_call x3, Pallas kernels, pack(): call(body, (pairs // 8,), [pl.BlockSpec((1, 8 * unit, lanes), lambda g: (...  14.1 us
  transfers between devices with their start and end apart: 26, of which 10 were waited for; matrix products, arithmetic and copies ran while one was open for 1% of the time, Pallas kernels for 14%

profile of v3, /device:TPU:0, one launch (start us, length us, event | category | flops | bytes accessed | tf_op | source)
XLA Modules:
  0.0 551.1 jit_solution(8403047418265933935)
XLA Ops:
  0.6 4.7 shard_map.106.s1
  5.4 7.3 %all-to-all-start.1 = ((f32[8,49,16,128]{3,2,1,0:T(8,128)}), f32[8,49,16,128]{3,2,1,0:T(8,128)}, u32[]{:S(2)}, u32[]{:S(2)}) async-start(f32[8,49,16,128]{3,2,1,0:T(8,128)} %shard_map.106.s1), calls=%async_computation.1 | async-start | bytes 6422528 | tf_op jit(solution)/shard_map/all_to_all | solution.py:1140
  12.7 4.7 shard_map.104.s0
  17.3 67.6 %all-to-all-done.1.x_ref = f32[8,49,16,128]{3,2,1,0:T(8,128)} async-done(((f32[8,49,16,128]{3,2,1,0:T(8,128)}), f32[8,49,16,128]{3,2,1,0:T(8,128)}, u32[]{:S(2)}, u32[]{:S(2)}) %all-to-all-start.1) | async-done | bytes 3211296 | tf_op jit(solution)/shard_map/all_to_all | solution.py:1140
  84.9 4.5 all-to-all-start
  89.4 4.7 shard_map.108.s2
  94.1 66.9 %all-to-all-done.x_ref = f32[8,49,16,128]{3,2,1,0:T(8,128)} async-done(((f32[8,49,16,128]{3,2,1,0:T(8,128)}), f32[8,49,16,128]{3,2,1,0:T(8,128)}, u32[]{:S(2)}, u32[]{:S(2)}) %all-to-all-start) | async-done | bytes 3211296 | tf_op jit(solution)/shard_map/all_to_all | solution.py:1140
  160.9 4.4 all-to-all-start.2
  167.7 9.9 %shard_map.107 = (f32[49,128,128]{2,1,0:T(8,128)}, f32[49,128,128]{2,1,0:T(8,128)}) custom-call(bf16[512,768]{1,0:T(8,128)(2,1)} %constant.55.clone.t_ref, f32[8,49,16,128]{3,2,1,0:T(8,128)} %all-to-all-done.1.x_ref), custom_call_target="tpu_custom_call" | custom-call | flops 4932501504 | bytes 9633792 | tf_op jit(solution)/shard_map/pallas_call | solution.py:506
  177.6 9.9 %shard_map.105 = (f32[49,128,128]{2,1,0:T(8,128)}, f32[49,128,128]{2,1,0:T(8,128)}) custom-call(bf16[512,768]{1,0:T(8,128)(2,1)} %constant.55.clone.t_ref, f32[8,49,16,128]{3,2,1,0:T(8,128)} %all-to-all-done.x_ref), custom_call_target="tpu_custom_call" | custom-call | flops 4932501504 | bytes 9633792 | tf_op jit(solution)/shard_map/pallas_call | solution.py:506
  187.4 8.4 %shard_map.109 = (f32[49,128,128]{2,1,0:T(8,128)}, f32[49,128,128]{2,1,0:T(8,128)}) custom-call(f32[196,128]{1,0:T(8,128)} %reshape.74.m_ref, f32[49,128,128]{2,1,0:T(8,128)} %get-tuple-element.50.refs_0_, f32[49,128,128]{2,1,0:T(8,128)} %get-tuple-element.51.refs_1_), custom_call_target="tpu_custom_call" | custom-call | flops 48168960 | bytes 12845056 | tf_op jit(solution)/shard_map/pallas_call | solution.py:601
  195.9 41.1 %all-to-all-done.2.x_ref = f32[8,49,16,128]{3,2,1,0:T(8,128)} async-done(((f32[8,49,16,128]{3,2,1,0:T(8,128)}), f32[8,49,16,128]{3,2,1,0:T(8,128)}, u32[]{:S(2)}, u32[]{:S(2)}) %all-to-all-start.2) | async-done | bytes 3211296 | tf_op jit(solution)/shard_map/all_to_all | solution.py:1140
  237.0 12.8 %shard_map.110 = (f32[49,128,128]{2,1,0:T(8,128)}, f32[49,128,128]{2,1,0:T(8,128)}, f32[8,49,16,128]{3,2,1,0:T(8,128)}) custom-call(bf16[512,768]{1,0:T(8,128)(2,1)} %constant.55.clone.t_ref, bf16[256,768]{1,0:T(8,128)(2,1)} %constant.56.clone.i_ref.t_ref, f32[8,49,16,128]{3,2,1,0:T(8,128)} %all-to-all-done.2.x_ref, ...), custom_call_target="tpu_custom_call" | custom-call | flops 7398752256 | bytes 19267584 | tf_op jit(solution)/shard_map/pallas_call | solution.py:539
  249.8 7.5 %shard_map.111.g_ref = f32[49,128,128]{2,1,0:T(8,128)} custom-call(f32[196,128]{1,0:T(8,128)} %reshape.74.m_ref, f32[49,128,128]{2,1,0:T(8,128)} %get-tuple-element.50.refs_0_, f32[49,128,128]{2,1,0:T(8,128)} %get-tuple-element.51.refs_1_, f32[49,128,128]{2,1,0:T(8,128)} %get-tuple-element.54.refs_2_.w_ref), custom_call_target="tpu_custom_call" | custom-call | flops 24084480 | bytes 12845056 | tf_op jit(solution)/shard_map/pallas_call | solution.py:601
  257.2 9.8 %shard_map.112 = (f32[8,2,49,8,128]{4,3,2,1,0:T(8,128)}, f32[8,2,49,8,128]{4,3,2,1,0:T(8,128)}) custom-call(bf16[256,768]{1,0:T(8,128)(2,1)} %constant.56.clone.i_ref.t_ref, f32[49,128,128]{2,1,0:T(8,128)} %get-tuple-element.56.g_ref, f32[49,128,128]{2,1,0:T(8,128)} %get-tuple-element.54.refs_2_.w_ref, f32[49,128,128]{2,1,0:T(8,128)} %get-tuple-element.57.z_ref), custom_call_target="tpu_custom_call" | custom-call | flops 2466250752 | bytes 12845056 | tf_op jit(solution)/shard_map/pallas_call | solution.py:630
  267.0 9.8 %shard_map.113 = (f32[8,2,49,8,128]{4,3,2,1,0:T(8,128)}, f32[8,2,49,8,128]{4,3,2,1,0:T(8,128)}) custom-call(bf16[256,768]{1,0:T(8,128)(2,1)} %constant.56.clone.i_ref.t_ref, f32[49,128,128]{2,1,0:T(8,128)} %shard_map.111.g_ref, f32[49,128,128]{2,1,0:T(8,128)} %get-tuple-element.54.refs_2_.w_ref, ...), custom_call_target="tpu_custom_call", output_to_operand_aliasing={{0}: (4, {}), {1}: (5, {})} | custom-call | flops 2466250752 | bytes 12845056 | tf_op jit(solution)/shard_map/pallas_call | solution.py:630
  276.8 76.9 %all_to_all.30.r_ref.x_ref = f32[8,2,49,8,128]{4,3,2,1,0:T(8,128)} all-to-all(f32[8,2,49,8,128]{4,3,2,1,0:T(8,128)} %get-tuple-element.62), channel_id=1, replica_groups=mesh['mode'=8,'elem'=4] {'mode'}, dimensions={0} | all-to-all | bytes 6422528 | tf_op jit(solution)/shard_map/all_to_all | solution.py:1140
  353.8 75.3 %all_to_all.31.r0.x_ref = f32[8,49,16,128]{3,2,1,0:T(8,128)} all-to-all(f32[8,49,16,128]{3,2,1,0:T(8,128)S(1)} %copy-done.9), channel_id=1, replica_groups=mesh['mode'=8,'elem'=4] {'mode'}, dimensions={0} | all-to-all | bytes 6422528 | tf_op jit(solution)/shard_map/all_to_all | solution.py:1140
  429.1 4.6 all-to-all-start.3
  438.2 8.0 %shard_map.114.f_ref = f32[8,49,16,128]{3,2,1,0:T(8,128)} custom-call(f32[1568,128]{1,0:T(8,128)} %mul.90.m_ref, f32[8,49,16,128]{3,2,1,0:T(8,128)} %shard_map.104.s0, f32[8,49,16,128]{3,2,1,0:T(8,128)} %all_to_all.31.r0.x_ref), custom_call_target="tpu_custom_call" | custom-call | flops 24084480 | bytes 9633792 | tf_op jit(solution)/shard_map/pallas_call | solution.py:674
  446.2 6.6 %shard_map.115 = (f32[196,2,8,128]{3,2,1,0:T(8,128)}, f32[2,8,128]{2,1,0:T(8,128)}, f32[2,8,128]{2,1,0:T(8,128)}) custom-call(f32[1568,128]{1,0:T(8,128)} %mul.90.m_ref, f32[392,128]{1,0:T(8,128)} %reshape_reshape.4.q_ref, f32[16,128]{1,0:T(8,128)} %broadcast_select_fusion.k_ref, f32[8,49,16,128]{3,2,1,0:T(8,128)} %shard_map.114.f_ref, ...), custom_call_target="tpu_custom_call" | custom-call | flops 16056320 | bytes 9633792 | tf_op jit(solution)/shard_map/pallas_call | solution.py:787
  452.9 1.7 collective-permute-start.1
  456.9 3.7 shard_map.116
  460.7 2.0 collective-permute-start.2
  464.4 2.2 collective-permute-done.4.far
  466.5 4.1 shard_map.117
  470.7 1.7 collective-permute-start.6
  474.0 2.2 collective-permute-done.7.far
  476.1 3.6 shard_map.118
  479.8 1.5 collective-permute-start.10
  481.4 1.7 collective-permute-start.9
  483.1 3.5 shard_map.120.refs_0_
  486.6 3.5 shard_map.121.refs_0_
  490.1 2.3 shard_map.119.refs_0_
  492.3 12.0 %all-to-all-done.3.x_ref.r_ref = f32[8,2,49,8,128]{4,3,2,1,0:T(8,128)} async-done(((f32[8,2,49,8,128]{4,3,2,1,0:T(8,128)}), f32[8,2,49,8,128]{4,3,2,1,0:T(8,128)}, u32[]{:S(2)}, u32[]{:S(2)}) %all-to-all-start.3) | async-done | bytes 3211296 | tf_op jit(solution)/shard_map/all_to_all | solution.py:1140
  504.3 6.6 %shard_map.123 = (f32[196,2,8,128]{3,2,1,0:T(8,128)}, f32[2,8,128]{2,1,0:T(8,128)}, f32[2,8,128]{2,1,0:T(8,128)}) custom-call(f32[1568,128]{1,0:T(8,128)} %mul.90.m_ref, f32[392,128]{1,0:T(8,128)} %reshape_reshape.4.q_ref, f32[16,128]{1,0:T(8,128)} %broadcast_select_fusion.k_ref, f32[8,49,16,128]{3,2,1,0:T(8,128)} %shard_map.114.f_ref, ...), custom_call_target="tpu_custom_call" | custom-call | flops 16056320 | bytes 9633792 | tf_op jit(solution)/shard_map/pallas_call | solution.py:787
  511.0 1.7 collective-permute-start.12
  512.7 1.5 collective-permute-done.11.b_ref
  517.4 3.7 shard_map.124
  521.1 1.6 collective-permute-start.13
  524.4 2.2 collective-permute-done.15.far
  527.6 4.1 shard_map.125
  531.8 1.7 collective-permute-start.17
  535.0 2.2 collective-permute-done.18.far
  537.2 3.6 shard_map.126
  540.9 1.7 collective-permute-start.20
  544.1 4.7 shard_map.122
  548.8 2.3 shard_map.127
  (101 shorter events, 21.1 us)
Async XLA Ops:
  5.4 79.5 %all-to-all-start.1 = ((f32[8,49,16,128]{3,2,1,0:T(8,128)}), f32[8,49,16,128]{3,2,1,0:T(8,128)}, u32[]{:S(2)}, u32[]{:S(2)}) async-start(f32[8,49,16,128]{3,2,1,0:T(8,128)} %shard_map.106.s1), calls=%async_computation.1 | async-start | bytes 6422528 | tf_op jit(solution)/shard_map/all_to_all | solution.py:1140
  84.9 76.0 %all-to-all-start = ((f32[8,49,16,128]{3,2,1,0:T(8,128)}), f32[8,49,16,128]{3,2,1,0:T(8,128)}, u32[]{:S(2)}, u32[]{:S(2)}) async-start(f32[8,49,16,128]{3,2,1,0:T(8,128)} %shard_map.104.s0), calls=%async_computation | async-start | bytes 6422528 | tf_op jit(solution)/shard_map/all_to_all | solution.py:1140
  94.1 71.3 %copy-start.10 = (f32[4,7,7,128]{3,0,2,1:T(4,128)S(1)}, f32[4,7,7,128]{3,0,2,1:T(4,128)}, u32[]{:S(2)}) copy-start(f32[4,7,7,128]{3,0,2,1:T(4,128)} %param.10) | copy-start | bytes 301060
  94.1 71.4 %copy-start.12 = (f32[4,7,7,128]{3,0,2,1:T(4,128)S(1)}, f32[4,7,7,128]{3,0,2,1:T(4,128)}, u32[]{:S(2)}) copy-start(f32[4,7,7,128]{3,0,2,1:T(4,128)} %param.11) | copy-start | bytes 301060
  94.1 71.4 %copy-start.14 = (f32[4,7,7,128]{3,0,2,1:T(4,128)S(1)}, f32[4,7,7,128]{3,0,2,1:T(4,128)}, u32[]{:S(2)}) copy-start(f32[4,7,7,128]{3,0,2,1:T(4,128)} %param.12) | copy-start | bytes 301060
  94.1 71.4 %copy-start.16 = (f32[4,7,7,128]{3,0,2,1:T(4,128)S(1)}, f32[4,7,7,128]{3,0,2,1:T(4,128)}, u32[]{:S(2)}) copy-start(f32[4,7,7,128]{3,0,2,1:T(4,128)} %param.13) | copy-start | bytes 301060
  160.9 76.0 %all-to-all-start.2 = ((f32[8,49,16,128]{3,2,1,0:T(8,128)}), f32[8,49,16,128]{3,2,1,0:T(8,128)}, u32[]{:S(2)}, u32[]{:S(2)}) async-start(f32[8,49,16,128]{3,2,1,0:T(8,128)} %shard_map.108.s2), calls=%async_computation.2 | async-start | bytes 6422528 | tf_op jit(solution)/shard_map/all_to_all | solution.py:1140
  166.1 0.9 copy-start.7
  276.8 76.9 %copy-start.9 = (f32[8,49,16,128]{3,2,1,0:T(8,128)S(1)}, f32[8,49,16,128]{3,2,1,0:T(8,128)}, u32[]{:S(2)}) copy-start(f32[8,49,16,128]{3,2,1,0:T(8,128)} %get-tuple-element.61) | copy-start | bytes 9633796
  429.1 4.7 copy-start.8
  429.1 4.7 copy-start.11
  429.1 4.7 copy-start.13
  429.1 4.7 copy-start.15
  429.1 4.8 copy-start.17
  429.1 4.8 copy-start.18
  429.1 4.7 copy-start.19
  429.1 75.2 %all-to-all-start.3 = ((f32[8,2,49,8,128]{4,3,2,1,0:T(8,128)}), f32[8,2,49,8,128]{4,3,2,1,0:T(8,128)}, u32[]{:S(2)}, u32[]{:S(2)}) async-start(f32[8,2,49,8,128]{4,3,2,1,0:T(8,128)} %get-tuple-element.60), calls=%async_computation.3 | async-start | bytes 6422528 | tf_op jit(solution)/shard_map/all_to_all | solution.py:1140
  452.8 4.1 copy-start.5
  452.8 3.3 collective-permute-start
  452.9 3.3 collective-permute-start.1
  455.9 23.9 %copy-start.2 = (f32[784,128]{1,0:T(8,128)}, f32[784,128]{1,0:T(8,128)S(1)}, u32[]{:S(2)}) copy-start(f32[784,128]{1,0:T(8,128)S(1)} %reshape.78.g_ref) | copy-start | bytes 1204228
  460.7 3.7 collective-permute-start.2
  462.7 1.7 collective-permute-start.3
  462.9 3.7 collective-permute-start.4
  470.7 12.4 %copy-start = (f32[8,49,16,128]{3,2,1,0:T(8,128)S(1)}, f32[8,49,16,128]{3,2,1,0:T(8,128)}, u32[]{:S(2)}) copy-start(f32[8,49,16,128]{3,2,1,0:T(8,128)} %all_to_all.31.r0.x_ref) | copy-start | bytes 9633796
  470.7 3.3 collective-permute-start.5
  470.7 3.2 collective-permute-start.6
  472.5 3.7 collective-permute-start.7
  479.8 6.8 %copy-start.1 = (f32[8,2,49,8,128]{4,3,2,1,0:T(8,128)S(1)}, f32[8,2,49,8,128]{4,3,2,1,0:T(8,128)}, u32[]{:S(2)}) copy-start(f32[8,2,49,8,128]{4,3,2,1,0:T(8,128)} %all_to_all.30.r_ref.x_ref) | copy-start | bytes 9633796
  479.8 10.2 %collective-permute-start.10 = (f32[2,8,128]{2,1,0:T(8,128)S(1)}, f32[2,8,128]{2,1,0:T(8,128)S(1)}, u32[]{:S(2)}, u32[]{:S(2)}) collective-permute-start(f32[2,8,128]{2,1,0:T(8,128)S(1)} %get-tuple-element.77.own), channel_id=1, source_target_pairs={{0,2},{1,3},{2,0},{3,1},{4,6},{5,7},{6,4},{7,5},{8,10},{9,11},{10,... | collective-permute-start | bytes 24584 | tf_op jit(solution)/shard_map/ppermute | solution.py:821
  481.4 8.7 %collective-permute-start.8 = (f32[2,8,128]{2,1,0:T(8,128)S(1)}, f32[2,8,128]{2,1,0:T(8,128)S(1)}, u32[]{:S(2)}, u32[]{:S(2)}) collective-permute-start(f32[2,8,128]{2,1,0:T(8,128)S(1)} %get-tuple-element.77.own), channel_id=1, source_target_pairs={{0,1},{1,2},{2,3},{3,0},{4,5},{5,6},{6,7},{7,4},{8,9},{9,10},{10,1... | collective-permute-start | bytes 24584 | tf_op jit(solution)/shard_map/ppermute | solution.py:816
  481.4 8.7 %collective-permute-start.9 = (f32[2,8,128]{2,1,0:T(8,128)S(1)}, f32[2,8,128]{2,1,0:T(8,128)S(1)}, u32[]{:S(2)}, u32[]{:S(2)}) collective-permute-start(f32[2,8,128]{2,1,0:T(8,128)S(1)} %get-tuple-element.77.own), channel_id=1, source_target_pairs={{1,0},{2,1},{3,2},{0,3},{5,4},{6,5},{7,6},{4,7},{9,8},{10,9},{11,1... | collective-permute-start | bytes 24584 | tf_op jit(solution)/shard_map/ppermute | solution.py:816
  510.9 3.3 collective-permute-start.11
  511.0 3.3 collective-permute-start.12
  515.0 1.0 copy-start.3
  516.0 1.4 copy-start.6
  521.1 3.3 collective-permute-start.13
  522.7 1.7 collective-permute-start.14
  523.0 3.7 collective-permute-start.15
  526.6 1.0 copy-start.4
  531.8 3.3 collective-permute-start.16
  531.8 3.2 collective-permute-start.17
  533.5 3.7 collective-permute-start.18
  540.9 7.9 %collective-permute-start.19 = (f32[2,8,128]{2,1,0:T(8,128)S(1)}, f32[2,8,128]{2,1,0:T(8,128)S(1)}, u32[]{:S(2)}, u32[]{:S(2)}) collective-permute-start(f32[2,8,128]{2,1,0:T(8,128)S(1)} %get-tuple-element.95.own), channel_id=1, source_target_pairs={{0,1},{1,2},{2,3},{3,0},{4,5},{5,6},{6,7},{7,4},{8,9},{9,10},{10,1... | collective-permute-start | bytes 24584 | tf_op jit(solution)/shard_map/ppermute | solution.py:816
  540.9 7.9 %collective-permute-start.20 = (f32[2,8,128]{2,1,0:T(8,128)S(1)}, f32[2,8,128]{2,1,0:T(8,128)S(1)}, u32[]{:S(2)}, u32[]{:S(2)}) collective-permute-start(f32[2,8,128]{2,1,0:T(8,128)S(1)} %get-tuple-element.95.own), channel_id=1, source_target_pairs={{1,0},{2,1},{3,2},{0,3},{5,4},{6,5},{7,6},{4,7},{9,8},{10,9},{11,1... | collective-permute-start | bytes 24584 | tf_op jit(solution)/shard_map/ppermute | solution.py:816
  542.6 6.2 %collective-permute-start.21 = (f32[2,8,128]{2,1,0:T(8,128)S(1)}, f32[2,8,128]{2,1,0:T(8,128)S(1)}, u32[]{:S(2)}, u32[]{:S(2)}) collective-permute-start(f32[2,8,128]{2,1,0:T(8,128)S(1)} %get-tuple-element.95.own), channel_id=1, source_target_pairs={{0,2},{1,3},{2,0},{3,1},{4,6},{5,7},{6,4},{7,5},{8,10},{9,11},{10,... | collective-permute-start | bytes 24584 | tf_op jit(solution)/shard_map/ppermute | solution.py:821

commit v4 on v3

--- a/solution.py
+++ b/solution.py
@@ -1,3 +1,4 @@
+import functools
 import math
 
 import jax
@@ -368,56 +369,107 @@
     return pl.ds(pl.multiple_of(k * unit + 8 * t, 8), 8)
 
 
-def pack(rows, comp, layers, pairs, lanes):
+def pack_one(x_ref, write_out, mid, layers, lanes):
     square = NODES * NODES
     per_plane = square * layers
     unit = 2 * per_plane
     half = lanes // 2
+    low = lanes_of((8, lanes)) < half
+
+    def write(t, r, tile):
+        mid[8 * t + r] = tile
+
+    turn_all(lambda k, t: x_ref[0, rows_at(k, unit, t), :], write, unit // 8)
+
+    def layer(e, carry):
+        for n in range(square):
+            cos = mid[n * layers + e]
+            sin = mid[per_plane + n * layers + e]
+            write_out(2 * e, n, jnp.where(low, cos, pltpu.roll(sin, half, 1)))
+            write_out(2 * e + 1, n, jnp.where(low, pltpu.roll(cos, half, 1), sin))
+        return carry
+
+    lax.fori_loop(0, layers, layer, 0)
+
+
+def pack_specs(layers, pairs, lanes, nodes):
+    return (
+        pl.BlockSpec((2 * layers, nodes, 8, lanes), lambda g: (0, 0, g, 0)),
+        jax.ShapeDtypeStruct((2 * layers, nodes, pairs, lanes), jnp.float32),
+    )
+
+
+def pack_first(rows, layers, pairs, lanes):
+    square = NODES * NODES
+    unit = 2 * square * layers
 
     def body(x_ref, o_ref, mid):
-        low = lanes_of((8, lanes)) < half
-
-        def write(t, r, tile):
-            mid[8 * t + r] = tile
-
-        turn_all(lambda k, t: x_ref[0, rows_at(k, unit, t), :], write, unit // 8)
-
-        def layer(e, carry):
-            for n in range(square):
-                cos = mid[n * layers + e]
-                sin = mid[per_plane + n * layers + e]
-                o_ref[2 * e, n] = jnp.where(low, cos, pltpu.roll(sin, half, 1))
-                o_ref[2 * e + 1, n] = jnp.where(low, pltpu.roll(cos, half, 1), sin)
-            return carry
-
-        lax.fori_loop(0, layers, layer, 0)
-
-    size = rows.shape[1] * lanes * 4
+        def write(d, n, value):
+            o_ref[d, n] = value
+
+        pack_one(x_ref, write, mid, layers, lanes)
+
+    spec, shape = pack_specs(layers, pairs, lanes, square)
     return call(
         body,
         (pairs // 8,),
-        [pl.BlockSpec((1, 8 * unit, lanes), lambda g: (comp, g, 0))],
-        pl.BlockSpec((2 * layers, square, 8, lanes), lambda g: (0, 0, g, 0)),
-        jax.ShapeDtypeStruct((2 * layers, square, pairs, lanes), jnp.float32),
+        [pl.BlockSpec((1, 8 * unit, lanes), lambda g: (0, g, 0))],
+        spec,
+        shape,
         scratch=[pltpu.VMEM((unit, 8, lanes), jnp.float32)],
         grant=WHOLE_GRANT,
-        moved=2 * size,
+        moved=2 * rows.shape[1] * lanes * 4,
     )(rows)
 
 
-def unpack(blocks, spec, slots, layers, buffer, total):
-    lanes = blocks.shape[-1]
+def pack_rest(rows, layers, pairs, lanes, early):
+    square = NODES * NODES
+    unit = 2 * square * layers
+
+    def body(x_ref, y_ref, o_ref, late_ref, whole_ref, mid):
+        def first(d, n, value):
+            o_ref[d, n] = value
+
+        def second(d, n, value):
+            whole_ref[d, n] = value
+            if n < early:
+                o_ref[d, square + n] = value
+            else:
+                late_ref[d, n - early] = value
+
+        pack_one(x_ref, first, mid, layers, lanes)
+        pack_one(y_ref, second, mid, layers, lanes)
+
+    parts = [
+        pack_specs(layers, pairs, lanes, nodes)
+        for nodes in (square + early, square - early, square)
+    ]
+    return call(
+        body,
+        (pairs // 8,),
+        [
+            pl.BlockSpec((1, 8 * unit, lanes), lambda g: (1, g, 0)),
+            pl.BlockSpec((1, 8 * unit, lanes), lambda g: (2, g, 0)),
+        ],
+        [part[0] for part in parts],
+        [part[1] for part in parts],
+        scratch=[pltpu.VMEM((unit, 8, lanes), jnp.float32)],
+        grant=WHOLE_GRANT,
+        moved=5 * rows.shape[1] * lanes * 4,
+    )(rows, rows)
+
+
+def unpack(arrays, specs, read_from, slots, layers, buffer, total):
+    lanes = arrays[0].shape[-1]
     square = NODES * NODES
     per_plane = square * layers
     unit = 2 * per_plane
     half = lanes // 2
 
-    def body(x_ref, *refs):
+    def body(*refs):
         o_ref, mid = refs[-2:]
         low = lanes_of((8, lanes)) < half
-
-        def read(d, n):
-            return x_ref[d, n] if len(x_ref.shape) == 4 else x_ref[d, 0, n]
+        read = read_from(refs, pl.program_id(0))
 
         def layer(e, carry):
             for n in range(square):
@@ -437,13 +489,13 @@
     return call(
         body,
         (2,),
-        [spec] + [pl.BlockSpec(memory_space=pl.ANY)] * len(extra),
+        list(specs) + [pl.BlockSpec(memory_space=pl.ANY)] * len(extra),
         pl.BlockSpec((8 * unit, lanes), lambda i: (slots[0] + i * slots[1], 0)),
         jax.ShapeDtypeStruct((total, lanes), jnp.float32),
         scratch=[pltpu.VMEM((unit, 8, lanes), jnp.float32)],
         moved=4 * 8 * unit * lanes * 4,
-        aliases={1: 0} if extra else None,
-    )(blocks, *extra)
+        aliases={len(arrays): 0} if extra else None,
+    )(*arrays, *extra)
 
 
 def paired_nodes():
@@ -492,7 +544,8 @@
 
 
 def to_points(blocks, table):
-    shares, square, pairs, lanes = blocks.shape
+    shares, _, pairs, lanes = blocks.shape
+    square = NODES * NODES
     rows = shares * pairs
 
     def body(t_ref, x_ref, v_ref, z_ref, rhs_ref):
@@ -519,34 +572,56 @@
     )(table, blocks)
 
 
-def turn_around(blocks, partial, slope_z, table, back):
-    shares, square, pairs, lanes = blocks.shape
+def turn_around(blocks, skip, start, count, partial, slope_z, table, back, fields, out):
+    shares, _, pairs, lanes = blocks.shape
     rows = shares * pairs
-
-    def body(t_ref, i_ref, x_ref, g_ref, s_ref, w_ref, z_ref, o_ref, rhs_ref):
-        fields = three_pass(t_ref[...], rhs_ref, read_tiles(x_ref, rows, lanes))
+    square = NODES * NODES
+    group = pairs // 2
+    shape = jax.ShapeDtypeStruct((square, rows, lanes), jnp.float32)
+
+    def body(t_ref, i_ref, x_ref, g_ref, s_ref, *refs):
+        w_ref, z_ref, o_ref, rhs_ref = refs[-4:]
+        points = three_pass(t_ref[...], rhs_ref, read_tiles(x_ref, rows, lanes))
         for b in range(NODES):
-            w_ref[b] = fields[0][b]
-            z_ref[b] = fields[1][b]
+            w_ref[b] = points[0][b]
+            z_ref[b] = points[1][b]
         tiles = [g_ref[b] + w_ref[b] * s_ref[b] for b in range(NODES)]
-        out = three_pass(i_ref[...], rhs_ref, tiles)[0]
+        spectral = three_pass(i_ref[...], rhs_ref, tiles)[0]
         for b in range(NODES):
-            o_ref[:, b] = out[b].reshape(shares, pairs, lanes)
-
-    spec = pl.BlockSpec((NODES, rows, lanes), lambda a: (a, 0, 0))
-    shape = jax.ShapeDtypeStruct((square, rows, lanes), jnp.float32)
-    exchanged = pl.BlockSpec((shares, NODES, pairs, lanes), lambda a: (0, a, 0, 0))
+            value = spectral[b].reshape(shares, pairs, lanes)
+            if out is None:
+                o_ref[:, b] = value
+            else:
+                for g in range(2):
+                    o_ref[:, g * NODES + b] = value[:, g * group : (g + 1) * group]
+
+    spec = pl.BlockSpec((NODES, rows, lanes), lambda a: (start + a, 0, 0))
+    if out is None:
+        out_spec = pl.BlockSpec((shares, NODES, pairs, lanes), lambda a: (0, a, 0, 0))
+        out_shape = jax.ShapeDtypeStruct((shares, count * NODES, pairs, lanes), jnp.float32)
+    else:
+        first = out[1]
+        out_spec = pl.BlockSpec((shares, 2 * NODES, group, lanes), lambda a: (0, first + a, 0, 0))
+        out_shape = jax.ShapeDtypeStruct(out[0], jnp.float32)
     return call(
         body,
-        (NODES,),
-        [whole(table.shape), whole(back.shape), exchanged, spec, spec],
-        [spec, spec, exchanged],
-        [shape, shape, jax.ShapeDtypeStruct(blocks.shape, jnp.float32)],
+        (count,),
+        [
+            whole(table.shape),
+            whole(back.shape),
+            pl.BlockSpec((shares, NODES, pairs, lanes), lambda a: (0, skip + a, 0, 0)),
+            spec,
+            spec,
+        ]
+        + [pl.BlockSpec(memory_space=pl.ANY)] * len(fields),
+        [spec, spec, out_spec],
+        [shape, shape, out_shape],
         scratch=[rhs_scratch(table, lanes)],
-        flops=3 * table.shape[0] * table.shape[1] * square * lanes,
+        flops=3 * table.shape[0] * table.shape[1] * count * NODES * lanes,
+        aliases={5: 0, 6: 1} if fields else None,
         grant=WHOLE_GRANT,
-        moved=6 * square * rows * lanes * 4,
-    )(table, back, blocks, partial, slope_z)
+        moved=6 * count * NODES * rows * lanes * 4,
+    )(table, back, blocks, partial, slope_z, *fields)
 
 
 def in_plane(speeds, fields, metrics, table):
@@ -610,7 +685,7 @@
     )(metrics, *arrays)
 
 
-def to_planes(partial, speed_z, slope_z, table, shares, place, buffers):
+def to_planes(partial, speed_z, slope_z, table, shares, place, shapes, buffers):
     square, rows, lanes = partial.shape
     pairs = rows // shares
     group = pairs // 2
@@ -622,36 +697,46 @@
         for b in range(NODES):
             out = nodes[b].reshape(shares, pairs, lanes)
             for i in range(2):
-                outs[i][:, 0, b] = out[:, i * group : (i + 1) * group]
+                outs[i][:, b] = out[:, i * group : (i + 1) * group]
 
     spec = pl.BlockSpec((NODES, rows, lanes), lambda a: (a, 0, 0))
-    out_spec = pl.BlockSpec((shares, 1, NODES, group, lanes), lambda a: (0, place, a, 0, 0))
-    shape = jax.ShapeDtypeStruct((shares, 2, square, group, lanes), jnp.float32)
+    out_spec = pl.BlockSpec((shares, NODES, group, lanes), lambda a: (0, place * NODES + a, 0, 0))
+    shapes = [jax.ShapeDtypeStruct(shape, jnp.float32) for shape in shapes]
     return call(
         body,
         (NODES,),
         [whole(table.shape), spec, spec, spec]
         + [pl.BlockSpec(memory_space=pl.ANY)] * len(buffers),
         [out_spec, out_spec],
-        [shape, shape],
+        shapes,
         scratch=[rhs_scratch(table, lanes)],
         flops=2 * table.shape[0] * table.shape[1] * square * lanes,
         grant=WHOLE_GRANT,
         moved=4 * square * rows * lanes * 4,
-        aliases={4: 0, 5: 1} if buffers else None,
+        aliases={4 + k: k for k in range(len(buffers))},
     )(table, partial, speed_z, slope_z, *buffers)
 
 
-def first_part(sent, returned, metrics, table):
+def first_part(sent, early, rest, rest_at, metrics, table):
     shares, square, pairs, lanes = sent.shape
 
-    def body(m_ref, s0, r0, o_ref, p0):
+    some = early.shape[1]
+    count = (square - some) // NODES
+    group = pairs // 2
+
+    def body(m_ref, s0, r0, *refs):
+        others, (o_ref, p0) = (refs[:count], refs[count:])
         d = pl.program_id(0)
 
         def block(s, carry):
             r = pl.ds(s * 8, 8)
             for n in range(square):
-                p0[n] = s0[0, n, r] + time_step * r0[0, n, r]
+                if n < some:
+                    home = r0[0, n, r]
+                else:
+                    a, b = divmod(n - some, NODES)
+                    home = others[a][0, s * NODES + b]
+                p0[n] = s0[0, n, r] + time_step * home
 
             def metric(kind, n):
                 return row_of(m_ref, (kind * shares + d) * square + n, 8)
@@ -674,14 +759,20 @@
     return call(
         body,
         (shares,),
-        [whole(metrics.shape), spec, spec],
+        [whole(metrics.shape), spec, pl.BlockSpec((1, some, pairs, lanes), lambda d: (d, 0, 0, 0))]
+        + [
+            pl.BlockSpec(
+                (1, 2 * NODES, group, lanes), functools.partial(lambda i, d: (d, i, 0, 0), rest_at + k)
+            )
+            for k in range(count)
+        ],
         spec,
         jax.ShapeDtypeStruct(sent.shape, jnp.float32),
         scratch=[pltpu.VMEM((square, 8, lanes), jnp.float32)],
         flops=30 * shares * square * pairs * lanes,
         grant=WHOLE_GRANT,
         moved=3 * shares * square * pairs * lanes * 4,
-    )(metrics, sent, returned)
+    )(metrics, sent, early, *[rest] * count)
 
 
 def join_layers(y_ref, layers):
@@ -725,7 +816,7 @@
     shares, square, _, lanes = flat.shape
     half = lanes // 2
 
-    def body(m_ref, q_ref, k_ref, f_ref, s1, s2, r_ref, o_ref, first_ref, last_ref, p1, c0, c1):
+    def body(m_ref, q_ref, k_ref, f_ref, s1, s2, r1, r2, o_ref, first_ref, last_ref, p1, c0, c1):
         e = pl.program_id(0)
         lane = lanes_of((8, lanes))
         low = lane < half
@@ -741,8 +832,8 @@
             d = 2 * e + h
             side = sides[h]
             for n in range(square):
-                p1[n] = s1[h, n] + time_step * r_ref[h, 0, n]
-                moved = s2[h, n] + time_step * r_ref[h, 1, n]
+                p1[n] = s1[h, n] + time_step * r1[h, n]
+                moved = s2[h, n] + time_step * r2[h, n]
                 along = pltpu.roll(moved, half, 1) * wave
                 side[n] = f_ref[h, n] + row_of(q_ref, d * square + n, 8) * along
 
@@ -794,7 +885,8 @@
             spec,
             spec,
             spec,
-            pl.BlockSpec((2, 2, square, 8, lanes), lambda e: (e, 0, 0, 0, 0)),
+            pl.BlockSpec((2, square, 8, lanes), lambda e: (e, 0, 0, 0)),
+            pl.BlockSpec((2, square, 8, lanes), lambda e: (e, 1, 0, 0)),
         ],
         [
             pl.BlockSpec((square, 2, 8, lanes), lambda e: (e, 0, 0, 0)),
@@ -804,9 +896,9 @@
         [jax.ShapeDtypeStruct((nodes, 2, 8, lanes), jnp.float32), rim_shape, rim_shape],
         scratch=[scratch] * 3,
         flops=40 * shares * square * 8 * lanes,
-        grant=WHOLE_GRANT,
+        grant=WHOLE_GRANT - 2 * 2**20,
         moved=6 * shares * square * 8 * lanes * 4,
-    )(metrics, weights, waves, flat, sent[1], sent[2], returned)
+    )(metrics, weights, waves, flat, *sent, returned, returned)
 
 
 def swap_rims(first, last):
@@ -1135,35 +1227,88 @@
     waves = jnp.where(low, wave, -wave)
     shift = plane_shift(first_plane, local_planes, planes).reshape(pairs, 2).T
     shift = jnp.broadcast_to(shift.reshape(2, 2, pairs // 2, 1), (2, 2, pairs // 2, lanes))
+    shift = (shift[:, 0], shift[:, 1])
 
     def exchange(blocks):
         return lax.all_to_all(blocks, "mode", split_axis=0, concat_axis=0, tiled=True)
 
-    sent = [pack(rows, comp, layers, pairs, lanes) for comp in range(3)]
-    arrived = [exchange(blocks) for blocks in sent]
-    speed_x, slope_0 = to_points(arrived[0], forward)
-    speed_y, slope_1 = to_points(arrived[1], forward)
+    some = (NODES // 2 + 1) * NODES
+    group = pairs // 2
+    first_shape = (modes, 4 * square - 2 * some, group, lanes)
+    second_shape = (modes, 2 * square, group, lanes)
+    sent_0 = pack_first(rows, layers, pairs, lanes)
+    sent_1, late_2, sent_2 = pack_rest(rows, layers, pairs, lanes, some)
+    arrived_0 = exchange(sent_0)
+    sent_1, here, geo, flux, scaled, waves, shift = lax.optimization_barrier(
+        (sent_1, here, geo, flux, scaled, waves, shift)
+    )
+    arrived_1 = exchange(sent_1)
+    arrived_2 = exchange(late_2)
+    speed_x, slope_0 = to_points(arrived_0, forward)
+    speed_y, slope_1 = to_points(arrived_1, forward)
     speeds = [speed_x, speed_y]
     partial = in_plane(speeds, speeds, here, table)
-    speed_z, slope_2, blocks = turn_around(arrived[2], partial[0], slope_0, forward, backward)
-    returned = [exchange(blocks)]
+    rows_early = some // NODES
+    speed_z, slope_2, blocks = turn_around(
+        arrived_1, NODES, 0, rows_early, partial[0], slope_0, forward, backward, (), None
+    )
+    home_0 = exchange(blocks)
+    speed_z, slope_2, first_buffer = turn_around(
+        arrived_2,
+        0,
+        rows_early,
+        NODES - rows_early,
+        partial[0],
+        slope_0,
+        forward,
+        backward,
+        (speed_z, slope_2),
+        (first_shape, NODES),
+    )
     last = in_plane(speeds, [speed_z], here, table)[0]
-    blocks = to_planes(partial[1], speed_z, slope_1, backward, modes, 0, ())
-    blocks = to_planes(last, speed_z, slope_2, backward, modes, 1, blocks)
-    returned.append(exchange(blocks[0]))
-    returned.append(exchange(blocks[1]))
-
-    group = pairs // 2
+    shapes = (first_shape, second_shape)
+    blocks = to_planes(partial[1], speed_z, slope_1, backward, modes, 0, shapes, (first_buffer,))
+    blocks = to_planes(last, speed_z, slope_2, backward, modes, 1, shapes, blocks)
+    home_1 = exchange(blocks[0])
+    home_2 = exchange(blocks[1])
+    returned = (home_1, home_2)
+    sent = (sent_1, sent_2)
+
     own_rows = local_planes * square * layers
-    whole_spec = pl.BlockSpec((modes, square, group, lanes), lambda i: (0, 0, i, 0))
-    part_spec = pl.BlockSpec((modes, 1, square, group, lanes), lambda i: (0, i, 0, 0, 0))
-    advection = unpack(returned[0], whole_spec, (0, 1), layers, None, 3 * own_rows)
-    flat = first_part(sent[0], returned[0], flux, table)
-
-    def solve(place, flat, buffer):
-        own_shift = shift[:, place]
+
+    def read_first(refs, g):
+        def read(d, n):
+            if n < some:
+                return refs[0][d, n]
+            a, b = divmod(n - some, NODES)
+            return refs[1 + a][d, g * NODES + b]
+
+        return read
+
+    def read_part(refs, i):
+        return lambda d, n: refs[0][d, n]
+
+    first_specs = [pl.BlockSpec((modes, some, group, lanes), lambda i: (0, 0, i, 0))] + [
+        pl.BlockSpec(
+            (modes, 2 * NODES, group, lanes), functools.partial(lambda k, i: (0, k, 0, 0), NODES + k)
+        )
+        for k in range(NODES - rows_early)
+    ]
+    part_specs = [pl.BlockSpec((modes, square, group, lanes), lambda i: (0, i, 0, 0))]
+    advection = unpack(
+        [home_0] + [home_1] * (NODES - rows_early),
+        first_specs,
+        read_first,
+        (0, 1),
+        layers,
+        None,
+        3 * own_rows,
+    )
+    flat = first_part(sent_0, home_0, home_1, NODES, flux, table)
+
+    def solve(place, flat, own_shift, buffer):
         raw, first, last = right_side(
-            flat, sent, returned[1 + place], flux, scaled, waves, table, layers, place
+            flat, sent, returned[place], flux, scaled, waves, table, layers, place
         )
         before, after = swap_rims(first, last)
         start, image, first, last = first_image(raw, before, after, own_shift, geo, layers, table)
@@ -1180,11 +1325,17 @@
             start, direction, residual, messages, scalars, layers, place, buffer, own_rows
         )
 
-    pressure = solve(0, flat, None)
-    advection = unpack(returned[1], part_spec, (2, 2), layers, advection, 3 * own_rows)
-    flat, pressure, advection = lax.optimization_barrier((flat, pressure, advection))
-    pressure = solve(1, flat, pressure)
-    advection = unpack(returned[2], part_spec, (3, 2), layers, advection, 3 * own_rows)
+    pressure = solve(0, flat, shift[0], None)
+    advection = unpack(
+        [home_1], part_specs, read_part, (2, 2), layers, advection, 3 * own_rows
+    )
+    flat, pressure, advection, shift = lax.optimization_barrier(
+        (flat, pressure, advection, shift)
+    )
+    pressure = solve(1, flat, shift[1], pressure)
+    advection = unpack(
+        [home_2], part_specs, read_part, (3, 2), layers, advection, 3 * own_rows
+    )
     advection = advection.reshape(3, local_planes, NODES, NODES, layers, lanes)
     pressure = pressure.reshape(local_planes, NODES, NODES, layers, lanes)
     return (advection.transpose(0, 1, 4, 2, 3, 5), pressure.transpose(0, 3, 1, 2, 4))

time: 553 us -> 513 us (0.928)
  waiting for transfers between devices: 198 us -> 89.7 us
  blocking collectives: 152 us -> 222 us
    all_to_all x4, waiting for transfers between devices: 188 us -> 78.3 us  [exchange(): lax.all_to_all(blocks, 'mode', split_axis=0, concat_axis=0, tiled=True)]
    all_to_all x2, blocking collectives: 152 us -> 222 us  [exchange(): lax.all_to_all(blocks, 'mode', split_axis=0, concat_axis=0, tiled=True)]
  transfers between devices with their start and end apart: 26 -> 26, of which waited for: 10 -> 12; matrix products, arithmetic and copies ran while one was open for 1% -> 2% of each run, Pallas kernels for 14% -> 23%
where the time goes in v4:
time: 513 us; the launch traced here: 511 us
  blocking collectives  222 us (43%)
  Pallas kernels  144 us (28%)
  waiting for transfers between devices  89.7 us (17%)
  starting transfers between devices  41.5 us (8%)
  local copies, waits for them, and re-layouts  10.5 us (2%)
    all_to_all x2, blocking collectives, exchange(): lax.all_to_all(blocks, 'mode', split_axis=0, concat_axis=0, tiled=True)  222 us
    all_to_all x4, waiting for transfers between devices, exchange(): lax.all_to_all(blocks, 'mode', split_axis=0, concat_axis=0, tiled=True)  78.3 us
    all_to_all x4, starting transfers between devices, exchange(): lax.all_to_all(blocks, 'mode', split_axis=0, concat_axis=0, tiled=True)  21.9 us
    pallas_call x2, Pallas kernels, to_points(): call(body, (NODES,), [whole(table.shape), pl.BlockSpec((shares, NODES, pa...  19.8 us
    pallas_call x2, Pallas kernels, to_planes(): call(body, (NODES,), [whole(table.shape), spec, spec, spec] + [pl.BlockSp...  19.5 us
    pallas_call x2, Pallas kernels, in_plane(): call(body, (rows // step,), [whole(metrics.shape)] + [spec] * len(arrays)...  16.1 us
    pallas_call x2, Pallas kernels, turn_around(): call(body, (count,), [whole(table.shape), whole(back.shape), pl.BlockSpec...  15.3 us
    ppermute x16, starting transfers between devices, swap_rims(): return (lax.ppermute(last, 'elem', up), lax.ppermute(first, 'elem', down))  13.4 us
  transfers between devices with their start and end apart: 26, of which 12 were waited for; matrix products, arithmetic and copies ran while one was open for 2% of the time, Pallas kernels for 23%

profile of v4, /device:TPU:0, one launch (start us, length us, event | category | flops | bytes accessed | tf_op | source)
XLA Modules:
  0.0 511.5 jit_solution(6450891873978710068)
XLA Ops:
  0.6 4.7 shard_map.105.s0
  5.3 7.3 %all-to-all-start = ((f32[8,49,16,128]{3,2,1,0:T(8,128)}), f32[8,49,16,128]{3,2,1,0:T(8,128)}, u32[]{:S(2)}, u32[]{:S(2)}) async-start(f32[8,49,16,128]{3,2,1,0:T(8,128)} %shard_map.105.s0), calls=%async_computation | async-start | bytes 6422528 | tf_op jit(solution)/shard_map/all_to_all | solution.py:1233
  12.6 8.2 %shard_map.104 = (f32[8,77,16,128]{3,2,1,0:T(8,128)}, f32[8,21,16,128]{3,2,1,0:T(8,128)}, f32[8,49,16,128]{3,2,1,0:T(8,128)}) custom-call(f32[3,6272,128]{2,1,0:T(8,128)} %bitcast.45, f32[3,6272,128]{2,1,0:T(8,128)} %bitcast.46), custom_call_target="tpu_custom_call" | custom-call | bytes 16056320 | tf_op jit(solution)/shard_map/pallas_call | solution.py:447
  31.2 53.7 %all-to-all-done.x_ref = f32[8,49,16,128]{3,2,1,0:T(8,128)} async-done(((f32[8,49,16,128]{3,2,1,0:T(8,128)}), f32[8,49,16,128]{3,2,1,0:T(8,128)}, u32[]{:S(2)}, u32[]{:S(2)}) %all-to-all-start) | async-done | bytes 3211296 | tf_op jit(solution)/shard_map/all_to_all | solution.py:1233
  84.8 116.2 %all_to_all.30.x_ref = f32[8,77,16,128]{3,2,1,0:T(8,128)} all-to-all(f32[8,77,16,128]{3,2,1,0:T(8,128)} %get-tuple-element.68.s1), channel_id=1, replica_groups=mesh['mode'=8,'elem'=4] {'mode'}, dimensions={0} | all-to-all | bytes 10092544 | tf_op jit(solution)/shard_map/all_to_all | solution.py:1233
  201.1 4.3 all-to-all-start.2
  205.4 9.9 %shard_map.106 = (f32[49,128,128]{2,1,0:T(8,128)}, f32[49,128,128]{2,1,0:T(8,128)}) custom-call(bf16[512,768]{1,0:T(8,128)(2,1)} %constant.55.clone.t_ref, f32[8,49,16,128]{3,2,1,0:T(8,128)} %all-to-all-done.x_ref), custom_call_target="tpu_custom_call" | custom-call | flops 4932501504 | bytes 9633792 | tf_op jit(solution)/shard_map/pallas_call | solution.py:559
  215.3 9.9 %shard_map.107 = (f32[49,128,128]{2,1,0:T(8,128)}, f32[49,128,128]{2,1,0:T(8,128)}) custom-call(bf16[512,768]{1,0:T(8,128)(2,1)} %constant.55.clone.t_ref, f32[8,77,16,128]{3,2,1,0:T(8,128)} %all_to_all.30.x_ref), custom_call_target="tpu_custom_call" | custom-call | flops 4932501504 | bytes 9633792 | tf_op jit(solution)/shard_map/pallas_call | solution.py:559
  225.1 8.5 %shard_map.108 = (f32[49,128,128]{2,1,0:T(8,128)}, f32[49,128,128]{2,1,0:T(8,128)}) custom-call(f32[196,128]{1,0:T(8,128)} %reshape.75.m_ref, f32[49,128,128]{2,1,0:T(8,128)} %get-tuple-element.67.refs_0_, f32[49,128,128]{2,1,0:T(8,128)} %get-tuple-element.69.refs_1_), custom_call_target="tpu_custom_call" | custom-call | flops 48168960 | bytes 12845056 | tf_op jit(solution)/shard_map/pallas_call | solution.py:676
  233.6 8.4 %shard_map.109 = (f32[49,128,128]{2,1,0:T(8,128)}, f32[49,128,128]{2,1,0:T(8,128)}, f32[8,28,16,128]{3,2,1,0:T(8,128)}) custom-call(bf16[512,768]{1,0:T(8,128)(2,1)} %constant.55.clone.t_ref, bf16[256,768]{1,0:T(8,128)(2,1)} %constant.56.clone.i_ref.t_ref, f32[8,77,16,128]{3,2,1,0:T(8,128)} %all_to_all.30.x_ref, f32[49,128,128]{2,1,0:T(8,128)} %get-tuple-element.71.g_ref, ...), custom_call_target="tpu_custom_call" | custom-call | flops 4227858432 | bytes 11010048 | tf_op jit(solution)/shard_map/pallas_call | solution.py:606
  242.0 5.9 %all-to-all-start.4 = ((f32[8,28,16,128]{3,2,1,0:T(8,128)}), f32[8,28,16,128]{3,2,1,0:T(8,128)}, u32[]{:S(2)}, u32[]{:S(2)}) async-start(f32[8,28,16,128]{3,2,1,0:T(8,128)} %get-tuple-element.84), calls=%async_computation.4 | async-start | bytes 3670016 | tf_op jit(solution)/shard_map/all_to_all | solution.py:1233
  247.9 7.0 %shard_map.110 = (f32[49,128,128]{2,1,0:T(8,128)}, f32[49,128,128]{2,1,0:T(8,128)}, f32[8,140,8,128]{3,2,1,0:T(8,128)}) custom-call(bf16[512,768]{1,0:T(8,128)(2,1)} %constant.55.clone.t_ref, bf16[256,768]{1,0:T(8,128)(2,1)} %constant.56.clone.i_ref.t_ref, f32[8,21,16,128]{3,2,1,0:T(8,128)} %all-to-all-done.2.x_ref, ...), custom_call_target="tpu_custom_call", output_to_operand_aliasing={{0}: (5, {}), {1}: (6, {})} | custom-call | flops 3170893824 | bytes 8257536 | tf_op jit(solution)/shard_map/pallas_call | solution.py:606
  254.9 7.6 %shard_map.111.g_ref = f32[49,128,128]{2,1,0:T(8,128)} custom-call(f32[196,128]{1,0:T(8,128)} %reshape.75.m_ref, f32[49,128,128]{2,1,0:T(8,128)} %get-tuple-element.67.refs_0_, f32[49,128,128]{2,1,0:T(8,128)} %get-tuple-element.69.refs_1_, f32[49,128,128]{2,1,0:T(8,128)} %get-tuple-element.75.refs_2_.w_ref), custom_call_target="tpu_custom_call" | custom-call | flops 24084480 | bytes 12845056 | tf_op jit(solution)/shard_map/pallas_call | solution.py:676
  262.4 9.8 %shard_map.112 = (f32[8,140,8,128]{3,2,1,0:T(8,128)}, f32[8,98,8,128]{3,2,1,0:T(8,128)}) custom-call(bf16[256,768]{1,0:T(8,128)(2,1)} %constant.56.clone.i_ref.t_ref, f32[49,128,128]{2,1,0:T(8,128)} %get-tuple-element.77.g_ref, f32[49,128,128]{2,1,0:T(8,128)} %get-tuple-element.75.refs_2_.w_ref, ...), custom_call_target="tpu_custom_call", output_to_operand_aliasing={{0}: (4, {})} | custom-call | flops 2466250752 | bytes 12845056 | tf_op jit(solution)/shard_map/pallas_call | solution.py:705
  272.2 9.7 %shard_map.113 = (f32[8,140,8,128]{3,2,1,0:T(8,128)}, f32[8,98,8,128]{3,2,1,0:T(8,128)}) custom-call(bf16[256,768]{1,0:T(8,128)(2,1)} %constant.56.clone.i_ref.t_ref, f32[49,128,128]{2,1,0:T(8,128)} %shard_map.111.g_ref, f32[49,128,128]{2,1,0:T(8,128)} %get-tuple-element.75.refs_2_.w_ref, ...), custom_call_target="tpu_custom_call", output_to_operand_aliasing={{0}: (4, {}), {1}: (5, {})} | custom-call | flops 2466250752 | bytes 12845056 | tf_op jit(solution)/shard_map/pallas_call | solution.py:705
  281.9 7.3 %all-to-all-done.4.r0.refs_0_ = f32[8,28,16,128]{3,2,1,0:T(8,128)} async-done(((f32[8,28,16,128]{3,2,1,0:T(8,128)}), f32[8,28,16,128]{3,2,1,0:T(8,128)}, u32[]{:S(2)}, u32[]{:S(2)}) %all-to-all-start.4) | async-done | bytes 1835040 | tf_op jit(solution)/shard_map/all_to_all | solution.py:1233
  289.2 105.7 %all_to_all.31.refs_0_.refs_1_.refs_2_.r1.r2.refs_3_ = f32[8,140,8,128]{3,2,1,0:T(8,128)} all-to-all(f32[8,140,8,128]{3,2,1,0:T(8,128)} %get-tuple-element.85), channel_id=1, replica_groups=mesh['mode'=8,'elem'=4] {'mode'}, dimensions={0} | all-to-all | bytes 9175040 | tf_op jit(solution)/shard_map/all_to_all | solution.py:1233
  395.0 4.4 all-to-all-start.3
  399.4 8.2 %shard_map.114.f_ref = f32[8,49,16,128]{3,2,1,0:T(8,128)} custom-call(f32[1568,128]{1,0:T(8,128)} %mul.99.m_ref, f32[8,49,16,128]{3,2,1,0:T(8,128)} %shard_map.105.s0, f32[8,28,16,128]{3,2,1,0:T(8,128)} %all-to-all-done.4.r0.refs_0_, f32[8,140,8,128]{3,2,1,0:T(8,128)} %all_to_all.31.refs_0_.refs_1_.refs_2_.r1.r2.refs_3_, ...), custom_call_target="tpu_custom_call" | custom-call | flops 24084480 | bytes 9633792 | tf_op jit(solution)/shard_map/pallas_call | solution.py:759
  407.6 6.6 %shard_map.115 = (f32[196,2,8,128]{3,2,1,0:T(8,128)}, f32[2,8,128]{2,1,0:T(8,128)}, f32[2,8,128]{2,1,0:T(8,128)}) custom-call(f32[1568,128]{1,0:T(8,128)} %mul.99.m_ref, f32[392,128]{1,0:T(8,128)} %reshape_reshape.4.q_ref, f32[16,128]{1,0:T(8,128)} %broadcast_select_fusion.k_ref, f32[8,49,16,128]{3,2,1,0:T(8,128)} %shard_map.114.f_ref, ...), custom_call_target="tpu_custom_call" | custom-call | flops 16056320 | bytes 9633792 | tf_op jit(solution)/shard_map/pallas_call | solution.py:878
  414.2 1.7 collective-permute-start.1
  415.9 1.5 collective-permute-done.b_ref
  417.5 1.4 copy-done.2
  418.9 3.7 shard_map.116
  422.6 2.0 collective-permute-start.2
  426.1 2.2 collective-permute-done.4.far
  428.3 4.0 shard_map.117
  432.7 1.3 collective-permute-start.7
  436.4 3.6 shard_map.118
  440.0 1.4 collective-permute-start.10
  441.4 1.4 collective-permute-start.9
  442.8 4.5 shard_map.120.refs_1_
  447.3 3.5 shard_map.121.refs_1_
  450.8 2.2 shard_map.119.refs_0_
  453.0 17.3 %all-to-all-done.3.refs_0_.r1.r2 = f32[8,98,8,128]{3,2,1,0:T(8,128)} async-done(((f32[8,98,8,128]{3,2,1,0:T(8,128)}), f32[8,98,8,128]{3,2,1,0:T(8,128)}, u32[]{:S(2)}, u32[]{:S(2)}) %all-to-all-start.3) | async-done | bytes 3211296 | tf_op jit(solution)/shard_map/all_to_all | solution.py:1233
  470.3 6.5 %shard_map.123 = (f32[196,2,8,128]{3,2,1,0:T(8,128)}, f32[2,8,128]{2,1,0:T(8,128)}, f32[2,8,128]{2,1,0:T(8,128)}) custom-call(f32[1568,128]{1,0:T(8,128)} %mul.99.m_ref, f32[392,128]{1,0:T(8,128)} %reshape_reshape.4.q_ref, f32[16,128]{1,0:T(8,128)} %broadcast_select_fusion.k_ref, f32[8,49,16,128]{3,2,1,0:T(8,128)} %shard_map.114.f_ref, ...), custom_call_target="tpu_custom_call" | custom-call | flops 16056320 | bytes 9633792 | tf_op jit(solution)/shard_map/pallas_call | solution.py:878
  476.8 1.7 collective-permute-start.12
  478.6 1.5 collective-permute-done.11.b_ref
  480.1 1.4 copy-done.1
  481.6 3.7 shard_map.124
  485.3 1.6 collective-permute-start.13
  488.4 2.2 collective-permute-done.15.far
  490.6 4.0 shard_map.125
  498.4 3.6 shard_map.126
  502.0 1.2 collective-permute-start.21
  503.2 1.4 collective-permute-start.20
  504.6 4.7 shard_map.122
  509.3 2.2 shard_map.127
  (88 shorter events, 19.7 us)
Async XLA Ops:
  5.3 79.5 %all-to-all-start = ((f32[8,49,16,128]{3,2,1,0:T(8,128)}), f32[8,49,16,128]{3,2,1,0:T(8,128)}, u32[]{:S(2)}, u32[]{:S(2)}) async-start(f32[8,49,16,128]{3,2,1,0:T(8,128)} %shard_map.105.s0), calls=%async_computation | async-start | bytes 6422528 | tf_op jit(solution)/shard_map/all_to_all | solution.py:1233
  24.7 1.2 copy-start.5
  24.7 1.2 copy-start.6
  24.7 1.2 copy-start.7
  24.7 1.2 copy-start.8
  24.7 1.2 copy-start.9
  24.7 1.2 copy-start.10
  201.1 40.9 %all-to-all-start.2 = ((f32[8,21,16,128]{3,2,1,0:T(8,128)}), f32[8,21,16,128]{3,2,1,0:T(8,128)}, u32[]{:S(2)}, u32[]{:S(2)}) async-start(f32[8,21,16,128]{3,2,1,0:T(8,128)} %get-tuple-element.70), calls=%async_computation.2 | async-start | bytes 2752512 | tf_op jit(solution)/shard_map/all_to_all | solution.py:1233
  242.0 47.3 %all-to-all-start.4 = ((f32[8,28,16,128]{3,2,1,0:T(8,128)}), f32[8,28,16,128]{3,2,1,0:T(8,128)}, u32[]{:S(2)}, u32[]{:S(2)}) async-start(f32[8,28,16,128]{3,2,1,0:T(8,128)} %get-tuple-element.84), calls=%async_computation.4 | async-start | bytes 3670016 | tf_op jit(solution)/shard_map/all_to_all | solution.py:1233
  395.0 75.3 %all-to-all-start.3 = ((f32[8,98,8,128]{3,2,1,0:T(8,128)}), f32[8,98,8,128]{3,2,1,0:T(8,128)}, u32[]{:S(2)}, u32[]{:S(2)}) async-start(f32[8,98,8,128]{3,2,1,0:T(8,128)} %get-tuple-element.82), calls=%async_computation.3 | async-start | bytes 6422528 | tf_op jit(solution)/shard_map/all_to_all | solution.py:1233
  407.6 9.9 %copy-start = (f32[784,128]{1,0:T(8,128)S(1)}, f32[784,128]{1,0:T(8,128)}, u32[]{:S(2)}) copy-start(f32[784,128]{1,0:T(8,128)} %reshape.76.g_ref) | copy-start | bytes 1204228
  407.6 9.9 %copy-start.4 = (f32[2,8,128]{2,1,0:T(8,128)S(1)}, f32[2,8,128]{2,1,0:T(8,128)}, u32[]{:S(2)}) copy-start(f32[2,8,128]{2,1,0:T(8,128)} %broadcast_in_dim.46.k_ref) | copy-start | bytes 24580
  414.2 3.3 collective-permute-start
  414.2 3.3 collective-permute-start.1
  417.5 1.4 copy-start.2
  418.9 23.9 %slice-start = ((s8[4587520]{0:T(1024)(128)(4,1)}), s8[4194304]{0:T(1024)(128)(4,1)S(1)}, s32[]{:S(2)}) async-start(s8[4587520]{0:T(1024)(128)(4,1)} %bitcast.42), calls=%async_computation.6 | async-start | bytes 8388608
  422.6 3.5 collective-permute-start.2
  424.7 3.7 collective-permute-start.4
  425.2 3.1 collective-permute-start.3
  428.3 14.5 %slice-start.1 = ((s8[4587520]{0:T(1024)(128)(4,1)}), s8[393216]{0:T(1024)(128)(4,1)S(1)}, s32[]{:S(2)}) async-start(s8[4587520]{0:T(1024)(128)(4,1)} %bitcast.42), calls=%async_computation.7 | async-start | bytes 786432
  432.4 3.1 collective-permute-start.5
  432.7 3.7 collective-permute-start.7
  434.1 2.3 collective-permute-start.6
  440.0 10.8 %collective-permute-start.10 = (f32[2,8,128]{2,1,0:T(8,128)S(1)}, f32[2,8,128]{2,1,0:T(8,128)S(1)}, u32[]{:S(2)}, u32[]{:S(2)}) collective-permute-start(f32[2,8,128]{2,1,0:T(8,128)S(1)} %get-tuple-element.105.own), channel_id=1, source_target_pairs={{0,2},{1,3},{2,0},{3,1},{4,6},{5,7},{6,4},{7,5},{8,10},{9,11},{10,... | collective-permute-start | bytes 24584 | tf_op jit(solution)/shard_map/ppermute | solution.py:913
  441.4 9.4 %collective-permute-start.9 = (f32[2,8,128]{2,1,0:T(8,128)S(1)}, f32[2,8,128]{2,1,0:T(8,128)S(1)}, u32[]{:S(2)}, u32[]{:S(2)}) collective-permute-start(f32[2,8,128]{2,1,0:T(8,128)S(1)} %get-tuple-element.105.own), channel_id=1, source_target_pairs={{1,0},{2,1},{3,2},{0,3},{5,4},{6,5},{7,6},{4,7},{9,8},{10,9},{11,1... | collective-permute-start | bytes 24584 | tf_op jit(solution)/shard_map/ppermute | solution.py:908
  442.8 8.0 %collective-permute-start.8 = (f32[2,8,128]{2,1,0:T(8,128)S(1)}, f32[2,8,128]{2,1,0:T(8,128)S(1)}, u32[]{:S(2)}, u32[]{:S(2)}) collective-permute-start(f32[2,8,128]{2,1,0:T(8,128)S(1)} %get-tuple-element.105.own), channel_id=1, source_target_pairs={{0,1},{1,2},{2,3},{3,0},{4,5},{5,6},{6,7},{7,4},{8,9},{9,10},{10,1... | collective-permute-start | bytes 24584 | tf_op jit(solution)/shard_map/ppermute | solution.py:908
  453.0 27.2 %copy-start.3 = (f32[2,8,128]{2,1,0:T(8,128)S(1)}, f32[2,8,128]{2,1,0:T(8,128)}, u32[]{:S(2)}) copy-start(f32[2,8,128]{2,1,0:T(8,128)} %broadcast_in_dim.48.k_ref) | copy-start | bytes 24580
  476.8 3.3 collective-permute-start.11
  476.8 3.3 collective-permute-start.12
  480.1 1.4 copy-start.1
  485.3 3.1 collective-permute-start.13
  486.9 3.7 collective-permute-start.15
  487.4 3.1 collective-permute-start.14
  494.6 3.1 collective-permute-start.16
  494.8 3.7 collective-permute-start.18
  495.9 2.5 collective-permute-start.17
  502.0 7.3 %collective-permute-start.21 = (f32[2,8,128]{2,1,0:T(8,128)S(1)}, f32[2,8,128]{2,1,0:T(8,128)S(1)}, u32[]{:S(2)}, u32[]{:S(2)}) collective-permute-start(f32[2,8,128]{2,1,0:T(8,128)S(1)} %get-tuple-element.125.own), channel_id=1, source_target_pairs={{0,2},{1,3},{2,0},{3,1},{4,6},{5,7},{6,4},{7,5},{8,10},{9,11},{10,... | collective-permute-start | bytes 24584 | tf_op jit(solution)/shard_map/ppermute | solution.py:913
  503.2 6.0 %collective-permute-start.20 = (f32[2,8,128]{2,1,0:T(8,128)S(1)}, f32[2,8,128]{2,1,0:T(8,128)S(1)}, u32[]{:S(2)}, u32[]{:S(2)}) collective-permute-start(f32[2,8,128]{2,1,0:T(8,128)S(1)} %get-tuple-element.125.own), channel_id=1, source_target_pairs={{1,0},{2,1},{3,2},{0,3},{5,4},{6,5},{7,6},{4,7},{9,8},{10,9},{11,1... | collective-permute-start | bytes 24584 | tf_op jit(solution)/shard_map/ppermute | solution.py:908
  504.6 4.7 collective-permute-start.19

commit v5 on v4

--- a/solution.py
+++ b/solution.py
@@ -459,7 +459,7 @@
     )(rows, rows)
 
 
-def unpack(arrays, specs, read_from, slots, layers, buffer, total):
+def unpack(arrays, specs, read_from, slots, layers, buffer, total, steps=2):
     lanes = arrays[0].shape[-1]
     square = NODES * NODES
     per_plane = square * layers
@@ -488,7 +488,7 @@
     extra = [] if buffer is None else [buffer]
     return call(
         body,
-        (2,),
+        (steps,),
         list(specs) + [pl.BlockSpec(memory_space=pl.ANY)] * len(extra),
         pl.BlockSpec((8 * unit, lanes), lambda i: (slots[0] + i * slots[1], 0)),
         jax.ShapeDtypeStruct((total, lanes), jnp.float32),
@@ -717,8 +717,57 @@
     )(table, partial, speed_z, slope_z, *buffers)
 
 
-def first_part(sent, early, rest, rest_at, metrics, table):
-    shares, square, pairs, lanes = sent.shape
+def velocity_part(sent, metrics, weights, waves, table):
+    shares, square, pairs, lanes = sent[0].shape
+    half = lanes // 2
+
+    def body(m_ref, q_ref, k_ref, s0, s1, s2, o_ref):
+        d = pl.program_id(0)
+
+        def rows_of(s):
+            r = pl.ds(s * 8, 8)
+            wave = k_ref[r]
+
+            def metric(kind, n):
+                return row_of(m_ref, (kind * shares + d) * square + n, 8)
+
+            for a in range(NODES):
+                ns = [a * NODES + b for b in range(NODES)]
+                first = apply_line(table, [s0[0, n, r] for n in ns])
+                second = apply_line(table, [s1[0, n, r] for n in ns])
+                for b, n in enumerate(ns):
+                    along = pltpu.roll(s2[0, n, r], half, 1) * wave
+                    o_ref[0, n, r] = (
+                        metric(2, n) * first[b]
+                        + metric(3, n) * second[b]
+                        + row_of(q_ref, d * square + n, 8) * along
+                    )
+            for b in range(NODES):
+                ns = [a * NODES + b for a in range(NODES)]
+                first = apply_line(table, [s0[0, n, r] for n in ns])
+                second = apply_line(table, [s1[0, n, r] for n in ns])
+                for a, n in enumerate(ns):
+                    o_ref[0, n, r] = o_ref[0, n, r] + (
+                        metric(0, n) * first[a] + metric(1, n) * second[a]
+                    )
+
+        lax.fori_loop(0, pairs // 8, lambda s, carry: (rows_of(s), carry)[1], 0)
+
+    spec = pl.BlockSpec((1, square, pairs, lanes), lambda d: (d, 0, 0, 0))
+    return call(
+        body,
+        (shares,),
+        [whole(metrics.shape), whole(weights.shape), whole(waves.shape)] + [spec] * 3,
+        spec,
+        jax.ShapeDtypeStruct(sent[0].shape, jnp.float32),
+        flops=60 * shares * square * pairs * lanes,
+        grant=WHOLE_GRANT,
+        moved=4 * shares * square * pairs * lanes * 4,
+    )(metrics, weights, waves, *sent)
+
+
+def first_part(base, early, rest, rest_at, metrics, table):
+    shares, square, pairs, lanes = base.shape
 
     some = early.shape[1]
     count = (square - some) // NODES
@@ -736,7 +785,7 @@
                 else:
                     a, b = divmod(n - some, NODES)
                     home = others[a][0, s * NODES + b]
-                p0[n] = s0[0, n, r] + time_step * home
+                p0[n] = home
 
             def metric(kind, n):
                 return row_of(m_ref, (kind * shares + d) * square + n, 8)
@@ -745,7 +794,7 @@
                 ns = [a * NODES + b for b in range(NODES)]
                 line = apply_line(table, [p0[n] for n in ns])
                 for b, n in enumerate(ns):
-                    o_ref[0, n, r] = metric(2, n) * line[b]
+                    o_ref[0, n, r] = s0[0, n, r] + metric(2, n) * line[b]
             for b in range(NODES):
                 ns = [a * NODES + b for a in range(NODES)]
                 line = apply_line(table, [p0[n] for n in ns])
@@ -767,12 +816,12 @@
             for k in range(count)
         ],
         spec,
-        jax.ShapeDtypeStruct(sent.shape, jnp.float32),
+        jax.ShapeDtypeStruct(base.shape, jnp.float32),
         scratch=[pltpu.VMEM((square, 8, lanes), jnp.float32)],
         flops=30 * shares * square * pairs * lanes,
         grant=WHOLE_GRANT,
         moved=3 * shares * square * pairs * lanes * 4,
-    )(metrics, sent, early, *[rest] * count)
+    )(metrics, base, early, *[rest] * count)
 
 
 def join_layers(y_ref, layers):
@@ -812,11 +861,11 @@
     return (first, last)
 
 
-def right_side(flat, sent, returned, metrics, weights, waves, table, layers, place):
+def right_side(flat, returned, metrics, weights, waves, table, layers, place):
     shares, square, _, lanes = flat.shape
     half = lanes // 2
 
-    def body(m_ref, q_ref, k_ref, f_ref, s1, s2, r1, r2, o_ref, first_ref, last_ref, p1, c0, c1):
+    def body(m_ref, q_ref, k_ref, f_ref, r1, r2, o_ref, first_ref, last_ref, c0, c1):
         e = pl.program_id(0)
         lane = lanes_of((8, lanes))
         low = lane < half
@@ -832,9 +881,7 @@
             d = 2 * e + h
             side = sides[h]
             for n in range(square):
-                p1[n] = s1[h, n] + time_step * r1[h, n]
-                moved = s2[h, n] + time_step * r2[h, n]
-                along = pltpu.roll(moved, half, 1) * wave
+                along = pltpu.roll(r2[h, n], half, 1) * wave
                 side[n] = f_ref[h, n] + row_of(q_ref, d * square + n, 8) * along
 
             def metric(kind, n):
@@ -842,12 +889,12 @@
 
             for a in range(NODES):
                 ns = [a * NODES + b for b in range(NODES)]
-                line = apply_line(table, [p1[n] for n in ns])
+                line = apply_line(table, [r1[h, n] for n in ns])
                 for b, n in enumerate(ns):
                     side[n] = side[n] + metric(3, n) * line[b]
             for b in range(NODES):
                 ns = [a * NODES + b for a in range(NODES)]
-                line = apply_line(table, [p1[n] for n in ns])
+                line = apply_line(table, [r1[h, n] for n in ns])
                 for a, n in enumerate(ns):
                     side[n] = side[n] + metric(1, n) * line[a]
         rims = [[first_ref[0], last_ref[0]], [first_ref[1], last_ref[1]]]
@@ -883,8 +930,6 @@
             whole(weights.shape),
             pl.BlockSpec((8, lanes), lambda e: (place, 0)),
             spec,
-            spec,
-            spec,
             pl.BlockSpec((2, square, 8, lanes), lambda e: (e, 0, 0, 0)),
             pl.BlockSpec((2, square, 8, lanes), lambda e: (e, 1, 0, 0)),
         ],
@@ -894,11 +939,10 @@
             whole((2, 8, lanes)),
         ],
         [jax.ShapeDtypeStruct((nodes, 2, 8, lanes), jnp.float32), rim_shape, rim_shape],
-        scratch=[scratch] * 3,
+        scratch=[scratch] * 2,
         flops=40 * shares * square * 8 * lanes,
-        grant=WHOLE_GRANT - 2 * 2**20,
-        moved=6 * shares * square * 8 * lanes * 4,
-    )(metrics, weights, waves, flat, *sent, returned, returned)
+        moved=4 * shares * square * 8 * lanes * 4,
+    )(metrics, weights, waves, flat, returned, returned)
 
 
 def swap_rims(first, last):
@@ -1220,11 +1264,13 @@
     geo = jnp.stack(metrics).reshape(4 * layers * square, lanes)
     scaled = halves((metrics[3] * (-1.0 / time_step)).reshape(1, layers, square, lanes), modes)
     flux = (both * scaled).reshape(4 * modes * square, lanes)
+    small_flux = flux * time_step
     scaled = scaled.reshape(modes * square, lanes)
     pair = (first_plane // 2 + jnp.arange(pairs, dtype=jnp.int32)).astype(jnp.float32)
     wave = pair[:, None] * spanwise_wave
     low = (jnp.arange(lanes) < lanes // 2)[None, :]
     waves = jnp.where(low, wave, -wave)
+    small_waves = waves * time_step
     shift = plane_shift(first_plane, local_planes, planes).reshape(pairs, 2).T
     shift = jnp.broadcast_to(shift.reshape(2, 2, pairs // 2, 1), (2, 2, pairs // 2, lanes))
     shift = (shift[:, 0], shift[:, 1])
@@ -1239,8 +1285,10 @@
     sent_0 = pack_first(rows, layers, pairs, lanes)
     sent_1, late_2, sent_2 = pack_rest(rows, layers, pairs, lanes, some)
     arrived_0 = exchange(sent_0)
-    sent_1, here, geo, flux, scaled, waves, shift = lax.optimization_barrier(
-        (sent_1, here, geo, flux, scaled, waves, shift)
+    sent_1, here, geo, flux, small_flux, scaled, waves, small_waves, shift = (
+        lax.optimization_barrier(
+            (sent_1, here, geo, flux, small_flux, scaled, waves, small_waves, shift)
+        )
     )
     arrived_1 = exchange(sent_1)
     arrived_2 = exchange(late_2)
@@ -1272,7 +1320,7 @@
     home_1 = exchange(blocks[0])
     home_2 = exchange(blocks[1])
     returned = (home_1, home_2)
-    sent = (sent_1, sent_2)
+    base = velocity_part((sent_0, sent_1, sent_2), flux, scaled, waves, table)
 
     own_rows = local_planes * square * layers
 
@@ -1304,11 +1352,11 @@
         None,
         3 * own_rows,
     )
-    flat = first_part(sent_0, home_0, home_1, NODES, flux, table)
+    flat = first_part(base, home_0, home_1, NODES, small_flux, table)
 
     def solve(place, flat, own_shift, buffer):
         raw, first, last = right_side(
-            flat, sent, returned[place], flux, scaled, waves, table, layers, place
+            flat, returned[place], small_flux, scaled, small_waves, table, layers, place
         )
         before, after = swap_rims(first, last)
         start, image, first, last = first_image(raw, before, after, own_shift, geo, layers, table)
@@ -1332,10 +1380,15 @@
     flat, pressure, advection, shift = lax.optimization_barrier(
         (flat, pressure, advection, shift)
     )
+
+    def unpack_late(comp, buffer):
+        spec = pl.BlockSpec((modes, square, group, lanes), lambda i: (0, comp, 0, 0))
+        return unpack(
+            [home_2], [spec], read_part, (3 + 2 * comp, 1), layers, buffer, 3 * own_rows, 1
+        )
+
     pressure = solve(1, flat, shift[1], pressure)
-    advection = unpack(
-        [home_2], part_specs, read_part, (3, 2), layers, advection, 3 * own_rows
-    )
+    advection = unpack_late(1, unpack_late(0, advection))
     advection = advection.reshape(3, local_planes, NODES, NODES, layers, lanes)
     pressure = pressure.reshape(local_planes, NODES, NODES, layers, lanes)
     return (advection.transpose(0, 1, 4, 2, 3, 5), pressure.transpose(0, 3, 1, 2, 4))

time: 513 us -> 514 us (level)
  waiting for transfers between devices: 89.7 us -> 77.3 us
  Pallas kernels: 144 us -> 151 us
  local copies, waits for them, and re-layouts: 10.5 us -> 15.9 us
    pallas_call x3 -> x5, Pallas kernels: 12.6 us -> 25.2 us  [the longest x4 15.2 us: unpack(): call(body, (steps,), list(specs) + [pl.BlockSpec(memory_space=pl.ANY)] *...]
    all_to_all x4, waiting for transfers between devices: 78.3 us -> 66.4 us  [exchange(): lax.all_to_all(blocks, 'mode', split_axis=0, concat_axis=0, tiled=True)]
    pallas_call x2, Pallas kernels: 13 us -> 7.31 us  [right_side(): call(body, (layers,), [whole(metrics.shape), whole(weights.shape), pl.Blo...]
    unnamed x32 -> x48, local copies, waits for them, and re-layouts: 5.65 us -> 10.9 us
  transfers between devices with their start and end apart: 26 -> 26, of which waited for: 12 -> 12; matrix products, arithmetic and copies ran while one was open for 2% -> 2% of each run, Pallas kernels for 23% -> 25%
where the time goes in v5:
time: 514 us; the launch traced here: 511 us
  blocking collectives  222 us (43%)
  Pallas kernels  151 us (29%)
  waiting for transfers between devices  77.3 us (15%)
  starting transfers between devices  41.3 us (8%)
  local copies, waits for them, and re-layouts  15.9 us (3%)
    all_to_all x2, blocking collectives, exchange(): lax.all_to_all(blocks, 'mode', split_axis=0, concat_axis=0, tiled=True)  222 us
    all_to_all x4, waiting for transfers between devices, exchange(): lax.all_to_all(blocks, 'mode', split_axis=0, concat_axis=0, tiled=True)  66.4 us
    all_to_all x4, starting transfers between devices, exchange(): lax.all_to_all(blocks, 'mode', split_axis=0, concat_axis=0, tiled=True)  21.9 us
    pallas_call x2, Pallas kernels, to_points(): call(body, (NODES,), [whole(table.shape), pl.BlockSpec((shares, NODES, pa...  19.8 us
    pallas_call x2, Pallas kernels, to_planes(): call(body, (NODES,), [whole(table.shape), spec, spec, spec] + [pl.BlockSp...  19.5 us
    pallas_call x2, Pallas kernels, in_plane(): call(body, (rows // step,), [whole(metrics.shape)] + [spec] * len(arrays)...  15.9 us
    pallas_call x2, Pallas kernels, turn_around(): call(body, (count,), [whole(table.shape), whole(back.shape), pl.BlockSpec...  15.5 us
    pallas_call x4, Pallas kernels, unpack(): call(body, (steps,), list(specs) + [pl.BlockSpec(memory_space=pl.ANY)] *...  15.2 us
  transfers between devices with their start and end apart: 26, of which 12 were waited for; matrix products, arithmetic and copies ran while one was open for 2% of the time, Pallas kernels for 25%

profile of v5, /device:TPU:0, one launch (start us, length us, event | category | flops | bytes accessed | tf_op | source)
XLA Modules:
  0.0 511.4 jit_solution(6212803386454438810)
XLA Ops:
  0.6 4.7 shard_map.105.s0
  5.3 7.3 %all-to-all-start = ((f32[8,49,16,128]{3,2,1,0:T(8,128)}), f32[8,49,16,128]{3,2,1,0:T(8,128)}, u32[]{:S(2)}, u32[]{:S(2)}) async-start(f32[8,49,16,128]{3,2,1,0:T(8,128)} %shard_map.105.s0), calls=%async_computation | async-start | bytes 6422528 | tf_op jit(solution)/shard_map/all_to_all | solution.py:1279
  12.6 8.3 %shard_map.104 = (f32[8,77,16,128]{3,2,1,0:T(8,128)}, f32[8,21,16,128]{3,2,1,0:T(8,128)}, f32[8,49,16,128]{3,2,1,0:T(8,128)}) custom-call(f32[3,6272,128]{2,1,0:T(8,128)} %bitcast.46, f32[3,6272,128]{2,1,0:T(8,128)} %bitcast.47), custom_call_target="tpu_custom_call" | custom-call | bytes 16056320 | tf_op jit(solution)/shard_map/pallas_call | solution.py:447
  29.0 1.3 broadcast_multiply_fusion
  31.6 53.2 %all-to-all-done.x_ref = f32[8,49,16,128]{3,2,1,0:T(8,128)} async-done(((f32[8,49,16,128]{3,2,1,0:T(8,128)}), f32[8,49,16,128]{3,2,1,0:T(8,128)}, u32[]{:S(2)}, u32[]{:S(2)}) %all-to-all-start) | async-done | bytes 3211296 | tf_op jit(solution)/shard_map/all_to_all | solution.py:1279
  84.8 116.3 %all_to_all.30.x_ref = f32[8,77,16,128]{3,2,1,0:T(8,128)} all-to-all(f32[8,77,16,128]{3,2,1,0:T(8,128)} %get-tuple-element.70.s1), channel_id=1, replica_groups=mesh['mode'=8,'elem'=4] {'mode'}, dimensions={0} | all-to-all | bytes 10092544 | tf_op jit(solution)/shard_map/all_to_all | solution.py:1279
  201.1 4.3 all-to-all-start.2
  205.4 9.9 %shard_map.106 = (f32[49,128,128]{2,1,0:T(8,128)}, f32[49,128,128]{2,1,0:T(8,128)}) custom-call(bf16[512,768]{1,0:T(8,128)(2,1)} %constant.58.clone.t_ref, f32[8,49,16,128]{3,2,1,0:T(8,128)} %all-to-all-done.x_ref), custom_call_target="tpu_custom_call" | custom-call | flops 4932501504 | bytes 9633792 | tf_op jit(solution)/shard_map/pallas_call | solution.py:559
  215.3 9.9 %shard_map.107 = (f32[49,128,128]{2,1,0:T(8,128)}, f32[49,128,128]{2,1,0:T(8,128)}) custom-call(bf16[512,768]{1,0:T(8,128)(2,1)} %constant.58.clone.t_ref, f32[8,77,16,128]{3,2,1,0:T(8,128)} %all_to_all.30.x_ref), custom_call_target="tpu_custom_call" | custom-call | flops 4932501504 | bytes 9633792 | tf_op jit(solution)/shard_map/pallas_call | solution.py:559
  225.2 8.4 %shard_map.108 = (f32[49,128,128]{2,1,0:T(8,128)}, f32[49,128,128]{2,1,0:T(8,128)}) custom-call(f32[196,128]{1,0:T(8,128)} %reshape.75.m_ref, f32[49,128,128]{2,1,0:T(8,128)} %get-tuple-element.69.refs_0_, f32[49,128,128]{2,1,0:T(8,128)} %get-tuple-element.71.refs_1_), custom_call_target="tpu_custom_call" | custom-call | flops 48168960 | bytes 12845056 | tf_op jit(solution)/shard_map/pallas_call | solution.py:676
  233.6 8.4 %shard_map.109 = (f32[49,128,128]{2,1,0:T(8,128)}, f32[49,128,128]{2,1,0:T(8,128)}, f32[8,28,16,128]{3,2,1,0:T(8,128)}) custom-call(bf16[512,768]{1,0:T(8,128)(2,1)} %constant.58.clone.t_ref, bf16[256,768]{1,0:T(8,128)(2,1)} %constant.59.clone.i_ref.t_ref, f32[8,77,16,128]{3,2,1,0:T(8,128)} %all_to_all.30.x_ref, f32[49,128,128]{2,1,0:T(8,128)} %get-tuple-element.73.g_ref, ...), custom_call_target="tpu_custom_call" | custom-call | flops 4227858432 | bytes 11010048 | tf_op jit(solution)/shard_map/pallas_call | solution.py:606
  242.0 5.9 %all-to-all-start.4 = ((f32[8,28,16,128]{3,2,1,0:T(8,128)}), f32[8,28,16,128]{3,2,1,0:T(8,128)}, u32[]{:S(2)}, u32[]{:S(2)}) async-start(f32[8,28,16,128]{3,2,1,0:T(8,128)} %get-tuple-element.90), calls=%async_computation.4 | async-start | bytes 3670016 | tf_op jit(solution)/shard_map/all_to_all | solution.py:1279
  247.8 7.1 %shard_map.110 = (f32[49,128,128]{2,1,0:T(8,128)}, f32[49,128,128]{2,1,0:T(8,128)}, f32[8,140,8,128]{3,2,1,0:T(8,128)}) custom-call(bf16[512,768]{1,0:T(8,128)(2,1)} %constant.58.clone.t_ref, bf16[256,768]{1,0:T(8,128)(2,1)} %constant.59.clone.i_ref.t_ref, f32[8,21,16,128]{3,2,1,0:T(8,128)} %all-to-all-done.2.x_ref, ...), custom_call_target="tpu_custom_call", output_to_operand_aliasing={{0}: (5, {}), {1}: (6, {})} | custom-call | flops 3170893824 | bytes 8257536 | tf_op jit(solution)/shard_map/pallas_call | solution.py:606
  254.9 7.5 %shard_map.111.g_ref = f32[49,128,128]{2,1,0:T(8,128)} custom-call(f32[196,128]{1,0:T(8,128)} %reshape.75.m_ref, f32[49,128,128]{2,1,0:T(8,128)} %get-tuple-element.69.refs_0_, f32[49,128,128]{2,1,0:T(8,128)} %get-tuple-element.71.refs_1_, f32[49,128,128]{2,1,0:T(8,128)} %get-tuple-element.77.refs_2_.w_ref), custom_call_target="tpu_custom_call" | custom-call | flops 24084480 | bytes 12845056 | tf_op jit(solution)/shard_map/pallas_call | solution.py:676
  262.4 9.8 %shard_map.112 = (f32[8,140,8,128]{3,2,1,0:T(8,128)}, f32[8,98,8,128]{3,2,1,0:T(8,128)}) custom-call(bf16[256,768]{1,0:T(8,128)(2,1)} %constant.59.clone.i_ref.t_ref, f32[49,128,128]{2,1,0:T(8,128)} %get-tuple-element.79.g_ref, f32[49,128,128]{2,1,0:T(8,128)} %get-tuple-element.77.refs_2_.w_ref, ...), custom_call_target="tpu_custom_call", output_to_operand_aliasing={{0}: (4, {})} | custom-call | flops 2466250752 | bytes 12845056 | tf_op jit(solution)/shard_map/pallas_call | solution.py:705
  272.2 9.7 %shard_map.113 = (f32[8,140,8,128]{3,2,1,0:T(8,128)}, f32[8,98,8,128]{3,2,1,0:T(8,128)}) custom-call(bf16[256,768]{1,0:T(8,128)(2,1)} %constant.59.clone.i_ref.t_ref, f32[49,128,128]{2,1,0:T(8,128)} %shard_map.111.g_ref, f32[49,128,128]{2,1,0:T(8,128)} %get-tuple-element.77.refs_2_.w_ref, ...), custom_call_target="tpu_custom_call", output_to_operand_aliasing={{0}: (4, {}), {1}: (5, {})} | custom-call | flops 2466250752 | bytes 12845056 | tf_op jit(solution)/shard_map/pallas_call | solution.py:705
  281.9 7.3 %all-to-all-done.4.r0.refs_0_ = f32[8,28,16,128]{3,2,1,0:T(8,128)} async-done(((f32[8,28,16,128]{3,2,1,0:T(8,128)}), f32[8,28,16,128]{3,2,1,0:T(8,128)}, u32[]{:S(2)}, u32[]{:S(2)}) %all-to-all-start.4) | async-done | bytes 1835040 | tf_op jit(solution)/shard_map/all_to_all | solution.py:1279
  289.2 105.7 %all_to_all.31.refs_0_.refs_1_.refs_2_.r1.r2.refs_3_ = f32[8,140,8,128]{3,2,1,0:T(8,128)} all-to-all(f32[8,140,8,128]{3,2,1,0:T(8,128)} %get-tuple-element.91), channel_id=1, replica_groups=mesh['mode'=8,'elem'=4] {'mode'}, dimensions={0} | all-to-all | bytes 9175040 | tf_op jit(solution)/shard_map/all_to_all | solution.py:1279
  394.9 4.5 all-to-all-start.3
  399.3 10.0 %shard_map.114.s0 = f32[8,49,16,128]{3,2,1,0:T(8,128)} custom-call(f32[1568,128]{1,0:T(8,128)} %get-tuple-element.86.m_ref, f32[392,128]{1,0:T(8,128)} %reshape_reshape.4.q_ref, f32[16,128]{1,0:T(8,128)} %get-tuple-element.88.k_ref, f32[8,49,16,128]{3,2,1,0:T(8,128)} %shard_map.105.s0, f32[8,77,16,128]{3,2,1,0:T(8,128)} %get-tuple-element.70.s1, ...), custom_call_target="tpu_custom_call" | custom-call | flops 48168960 | bytes 12845056 | tf_op jit(solution)/shard_map/pallas_call | solution.py:757
  409.4 8.1 %shard_map.115.f_ref = f32[8,49,16,128]{3,2,1,0:T(8,128)} custom-call(f32[1568,128]{1,0:T(8,128)} %get-tuple-element.85.m_ref, f32[8,49,16,128]{3,2,1,0:T(8,128)} %shard_map.114.s0, f32[8,28,16,128]{3,2,1,0:T(8,128)} %all-to-all-done.4.r0.refs_0_, f32[8,140,8,128]{3,2,1,0:T(8,128)} %all_to_all.31.refs_0_.refs_1_.refs_2_.r1.r2.refs_3_, ...), custom_call_target="tpu_custom_call" | custom-call | flops 24084480 | bytes 9633792 | tf_op jit(solution)/shard_map/pallas_call | solution.py:808
  417.5 2.3 copy-done
  419.8 1.9 copy-done.1
  424.5 2.9 shard_map.116
  427.5 1.7 collective-permute-start.1
  429.2 1.3 collective-permute-done.b_ref
  430.6 3.7 shard_map.117
  434.3 2.2 collective-permute-start.2
  438.0 2.2 collective-permute-done.4.far
  440.1 4.0 shard_map.118
  448.2 3.6 shard_map.119
  452.8 1.4 collective-permute-start.9
  454.2 4.5 shard_map.121.refs_1_
  458.7 3.5 shard_map.122.refs_1_
  462.2 2.2 shard_map.120.refs_0_
  464.4 5.9 %all-to-all-done.3.refs_0_.r1.r2 = f32[8,98,8,128]{3,2,1,0:T(8,128)} async-done(((f32[8,98,8,128]{3,2,1,0:T(8,128)}), f32[8,98,8,128]{3,2,1,0:T(8,128)}, u32[]{:S(2)}, u32[]{:S(2)}) %all-to-all-start.3) | async-done | bytes 3211296 | tf_op jit(solution)/shard_map/all_to_all | solution.py:1279
  471.4 4.4 shard_map.125
  475.9 1.7 collective-permute-start.12
  477.6 1.3 collective-permute-done.11.b_ref
  479.0 3.7 shard_map.126
  482.7 1.6 collective-permute-start.13
  485.8 2.2 collective-permute-done.15.far
  488.0 4.0 shard_map.127
  495.8 3.6 shard_map.128
  500.6 1.4 collective-permute-start.20
  502.0 3.6 shard_map.123.refs_1_
  505.6 3.6 shard_map.124
  509.2 2.2 shard_map.129
  (106 shorter events, 26.4 us)
Async XLA Ops:
  5.3 79.5 %all-to-all-start = ((f32[8,49,16,128]{3,2,1,0:T(8,128)}), f32[8,49,16,128]{3,2,1,0:T(8,128)}, u32[]{:S(2)}, u32[]{:S(2)}) async-start(f32[8,49,16,128]{3,2,1,0:T(8,128)} %shard_map.105.s0), calls=%async_computation | async-start | bytes 6422528 | tf_op jit(solution)/shard_map/all_to_all | solution.py:1279
  24.7 1.2 copy-start.13
  24.7 1.2 copy-start.14
  24.7 1.2 copy-start.15
  24.7 1.2 copy-start.16
  24.7 1.2 copy-start.17
  24.7 1.2 copy-start.18
  201.1 40.8 %all-to-all-start.2 = ((f32[8,21,16,128]{3,2,1,0:T(8,128)}), f32[8,21,16,128]{3,2,1,0:T(8,128)}, u32[]{:S(2)}, u32[]{:S(2)}) async-start(f32[8,21,16,128]{3,2,1,0:T(8,128)} %get-tuple-element.72), calls=%async_computation.2 | async-start | bytes 2752512 | tf_op jit(solution)/shard_map/all_to_all | solution.py:1279
  242.0 47.2 %all-to-all-start.4 = ((f32[8,28,16,128]{3,2,1,0:T(8,128)}), f32[8,28,16,128]{3,2,1,0:T(8,128)}, u32[]{:S(2)}, u32[]{:S(2)}) async-start(f32[8,28,16,128]{3,2,1,0:T(8,128)} %get-tuple-element.90), calls=%async_computation.4 | async-start | bytes 3670016 | tf_op jit(solution)/shard_map/all_to_all | solution.py:1279
  394.9 75.4 %all-to-all-start.3 = ((f32[8,98,8,128]{3,2,1,0:T(8,128)}), f32[8,98,8,128]{3,2,1,0:T(8,128)}, u32[]{:S(2)}, u32[]{:S(2)}) async-start(f32[8,98,8,128]{3,2,1,0:T(8,128)} %get-tuple-element.84), calls=%async_computation.3 | async-start | bytes 6422528 | tf_op jit(solution)/shard_map/all_to_all | solution.py:1279
  417.5 2.3 copy-start
  419.8 1.9 copy-start.1
  421.7 1.1 copy-start.5
  422.8 0.9 copy-start.7
  423.8 0.7 copy-start.11
  424.5 6.1 %copy-start.3 = (f32[784,128]{1,0:T(8,128)S(1)}, f32[784,128]{1,0:T(8,128)}, u32[]{:S(2)}) copy-start(f32[784,128]{1,0:T(8,128)} %reshape.76.g_ref) | copy-start | bytes 1204228
  424.5 6.1 %copy-start.10 = (f32[2,8,128]{2,1,0:T(8,128)S(1)}, f32[2,8,128]{2,1,0:T(8,128)}, u32[]{:S(2)}) copy-start(f32[2,8,128]{2,1,0:T(8,128)} %broadcast_in_dim.46.k_ref) | copy-start | bytes 24580
  427.4 3.1 collective-permute-start
  427.5 3.1 collective-permute-start.1
  430.6 23.6 %slice-start = ((s8[4587520]{0:T(1024)(128)(4,1)}), s8[4194304]{0:T(1024)(128)(4,1)S(1)}, s32[]{:S(2)}) async-start(s8[4587520]{0:T(1024)(128)(4,1)} %bitcast.42), calls=%async_computation.6 | async-start | bytes 8388608
  434.3 3.7 collective-permute-start.2
  436.5 3.7 collective-permute-start.4
  437.0 3.1 collective-permute-start.3
  440.1 14.1 %slice-start.1 = ((s8[4587520]{0:T(1024)(128)(4,1)}), s8[393216]{0:T(1024)(128)(4,1)S(1)}, s32[]{:S(2)}) async-start(s8[4587520]{0:T(1024)(128)(4,1)} %bitcast.42), calls=%async_computation.7 | async-start | bytes 786432
  444.2 3.1 collective-permute-start.5
  444.5 3.7 collective-permute-start.7
  445.5 2.7 collective-permute-start.6
  451.8 10.4 %collective-permute-start.10 = (f32[2,8,128]{2,1,0:T(8,128)S(1)}, f32[2,8,128]{2,1,0:T(8,128)S(1)}, u32[]{:S(2)}, u32[]{:S(2)}) collective-permute-start(f32[2,8,128]{2,1,0:T(8,128)S(1)} %get-tuple-element.109.own), channel_id=1, source_target_pairs={{0,2},{1,3},{2,0},{3,1},{4,6},{5,7},{6,4},{7,5},{8,10},{9,11},{10,... | collective-permute-start | bytes 24584 | tf_op jit(solution)/shard_map/ppermute | solution.py:957
  452.8 9.4 %collective-permute-start.9 = (f32[2,8,128]{2,1,0:T(8,128)S(1)}, f32[2,8,128]{2,1,0:T(8,128)S(1)}, u32[]{:S(2)}, u32[]{:S(2)}) collective-permute-start(f32[2,8,128]{2,1,0:T(8,128)S(1)} %get-tuple-element.109.own), channel_id=1, source_target_pairs={{1,0},{2,1},{3,2},{0,3},{5,4},{6,5},{7,6},{4,7},{9,8},{10,9},{11,1... | collective-permute-start | bytes 24584 | tf_op jit(solution)/shard_map/ppermute | solution.py:952
  454.2 8.0 %collective-permute-start.8 = (f32[2,8,128]{2,1,0:T(8,128)S(1)}, f32[2,8,128]{2,1,0:T(8,128)S(1)}, u32[]{:S(2)}, u32[]{:S(2)}) collective-permute-start(f32[2,8,128]{2,1,0:T(8,128)S(1)} %get-tuple-element.109.own), channel_id=1, source_target_pairs={{0,1},{1,2},{2,3},{3,0},{4,5},{5,6},{6,7},{7,4},{8,9},{9,10},{10,1... | collective-permute-start | bytes 24584 | tf_op jit(solution)/shard_map/ppermute | solution.py:952
  462.2 8.1 %copy-start.2 = (f32[8,49,16,128]{3,2,1,0:T(8,128)S(1)}, f32[8,49,16,128]{3,2,1,0:T(8,128)}, u32[]{:S(2)}) copy-start(f32[8,49,16,128]{3,2,1,0:T(8,128)} %shard_map.115.f_ref) | copy-start | bytes 9633796
  462.2 8.1 %copy-start.8 = (f32[392,128]{1,0:T(8,128)S(1)}, f32[392,128]{1,0:T(8,128)}, u32[]{:S(2)}) copy-start(f32[392,128]{1,0:T(8,128)} %reshape_reshape.4.q_ref) | copy-start | bytes 602116
  462.2 8.1 %copy-start.12 = (f32[16,128]{1,0:T(8,128)S(1)}, f32[16,128]{1,0:T(8,128)}, u32[]{:S(2)}) copy-start(f32[16,128]{1,0:T(8,128)} %get-tuple-element.94.k_ref) | copy-start | bytes 24580
  470.3 1.1 copy-start.6
  471.4 7.6 %copy-start.4 = (f32[784,128]{1,0:T(8,128)S(1)}, f32[784,128]{1,0:T(8,128)}, u32[]{:S(2)}) copy-start(f32[784,128]{1,0:T(8,128)} %reshape.76.g_ref) | copy-start | bytes 1204228
  471.4 7.6 %copy-start.9 = (f32[2,8,128]{2,1,0:T(8,128)S(1)}, f32[2,8,128]{2,1,0:T(8,128)}, u32[]{:S(2)}) copy-start(f32[2,8,128]{2,1,0:T(8,128)} %broadcast_in_dim.48.k_ref) | copy-start | bytes 24580
  475.8 3.1 collective-permute-start.11
  475.9 3.1 collective-permute-start.12
  482.7 3.1 collective-permute-start.13
  484.3 3.7 collective-permute-start.15
  484.8 3.1 collective-permute-start.14
  492.0 3.1 collective-permute-start.16
  492.2 3.7 collective-permute-start.18
  493.3 2.5 collective-permute-start.17
  499.4 9.8 %collective-permute-start.21 = (f32[2,8,128]{2,1,0:T(8,128)S(1)}, f32[2,8,128]{2,1,0:T(8,128)S(1)}, u32[]{:S(2)}, u32[]{:S(2)}) collective-permute-start(f32[2,8,128]{2,1,0:T(8,128)S(1)} %get-tuple-element.129.own), channel_id=1, source_target_pairs={{0,2},{1,3},{2,0},{3,1},{4,6},{5,7},{6,4},{7,5},{8,10},{9,11},{10,... | collective-permute-start | bytes 24584 | tf_op jit(solution)/shard_map/ppermute | solution.py:957
  500.6 8.6 %collective-permute-start.20 = (f32[2,8,128]{2,1,0:T(8,128)S(1)}, f32[2,8,128]{2,1,0:T(8,128)S(1)}, u32[]{:S(2)}, u32[]{:S(2)}) collective-permute-start(f32[2,8,128]{2,1,0:T(8,128)S(1)} %get-tuple-element.129.own), channel_id=1, source_target_pairs={{1,0},{2,1},{3,2},{0,3},{5,4},{6,5},{7,6},{4,7},{9,8},{10,9},{11,1... | collective-permute-start | bytes 24584 | tf_op jit(solution)/shard_map/ppermute | solution.py:952
  502.0 7.2 %collective-permute-start.19 = (f32[2,8,128]{2,1,0:T(8,128)S(1)}, f32[2,8,128]{2,1,0:T(8,128)S(1)}, u32[]{:S(2)}, u32[]{:S(2)}) collective-permute-start(f32[2,8,128]{2,1,0:T(8,128)S(1)} %get-tuple-element.129.own), channel_id=1, source_target_pairs={{0,1},{1,2},{2,3},{3,0},{4,5},{5,6},{6,7},{7,4},{8,9},{9,10},{10,1... | collective-permute-start | bytes 24584 | tf_op jit(solution)/shard_map/ppermute | solution.py:952

commit v6 on v5

--- a/solution.py
+++ b/solution.py
@@ -580,7 +580,8 @@
     shape = jax.ShapeDtypeStruct((square, rows, lanes), jnp.float32)
 
     def body(t_ref, i_ref, x_ref, g_ref, s_ref, *refs):
-        w_ref, z_ref, o_ref, rhs_ref = refs[-4:]
+        w_ref, z_ref = refs[len(fields) : len(fields) + 2]
+        outs, rhs_ref = (refs[len(fields) + 2 : -1], refs[-1])
         points = three_pass(t_ref[...], rhs_ref, read_tiles(x_ref, rows, lanes))
         for b in range(NODES):
             w_ref[b] = points[0][b]
@@ -590,19 +591,20 @@
         for b in range(NODES):
             value = spectral[b].reshape(shares, pairs, lanes)
             if out is None:
-                o_ref[:, b] = value
+                for k in range(shares):
+                    outs[k][b] = value[k]
             else:
                 for g in range(2):
-                    o_ref[:, g * NODES + b] = value[:, g * group : (g + 1) * group]
+                    outs[0][:, g * NODES + b] = value[:, g * group : (g + 1) * group]
 
     spec = pl.BlockSpec((NODES, rows, lanes), lambda a: (start + a, 0, 0))
     if out is None:
-        out_spec = pl.BlockSpec((shares, NODES, pairs, lanes), lambda a: (0, a, 0, 0))
-        out_shape = jax.ShapeDtypeStruct((shares, count * NODES, pairs, lanes), jnp.float32)
+        out_spec = [pl.BlockSpec((NODES, pairs, lanes), lambda a: (a, 0, 0))] * shares
+        out_shape = [jax.ShapeDtypeStruct((count * NODES, pairs, lanes), jnp.float32)] * shares
     else:
         first = out[1]
-        out_spec = pl.BlockSpec((shares, 2 * NODES, group, lanes), lambda a: (0, first + a, 0, 0))
-        out_shape = jax.ShapeDtypeStruct(out[0], jnp.float32)
+        out_spec = [pl.BlockSpec((shares, 2 * NODES, group, lanes), lambda a: (0, first + a, 0, 0))]
+        out_shape = [jax.ShapeDtypeStruct(out[0], jnp.float32)]
     return call(
         body,
         (count,),
@@ -614,8 +616,8 @@
             spec,
         ]
         + [pl.BlockSpec(memory_space=pl.ANY)] * len(fields),
-        [spec, spec, out_spec],
-        [shape, shape, out_shape],
+        [spec, spec] + out_spec,
+        [shape, shape] + out_shape,
         scratch=[rhs_scratch(table, lanes)],
         flops=3 * table.shape[0] * table.shape[1] * count * NODES * lanes,
         aliases={5: 0, 6: 1} if fields else None,
@@ -683,6 +685,32 @@
         grant=WHOLE_GRANT,
         moved=(len(arrays) + count) * square * rows * lanes * 4,
     )(metrics, *arrays)
+
+
+def by_source(strips, place):
+    count = len(strips)
+    nodes = strips[0].shape[0]
+
+    def body(place_ref, *refs):
+        o_ref = refs[-1]
+        here = place_ref[0]
+
+        def node(n, carry):
+            for k in range(count):
+                o_ref[lax.rem(here - k + count, count), n] = refs[k][n]
+            return carry
+
+        lax.fori_loop(0, nodes, node, 0)
+
+    return call(
+        body,
+        (1,),
+        [pl.BlockSpec(memory_space=pltpu.SMEM)] + [whole(strips[0].shape)] * count,
+        whole((count,) + strips[0].shape),
+        jax.ShapeDtypeStruct((count,) + strips[0].shape, jnp.float32),
+        grant=WHOLE_GRANT,
+        moved=8 * count * strips[0].size,
+    )(jnp.full((1,), place, jnp.int32), *strips)
 
 
 def to_planes(partial, speed_z, slope_z, table, shares, place, shapes, buffers):
@@ -1266,6 +1294,9 @@
     flux = (both * scaled).reshape(4 * modes * square, lanes)
     small_flux = flux * time_step
     scaled = scaled.reshape(modes * square, lanes)
+    turned = lax.optimization_barrier(backward).reshape(2, modes, pairs, -1)
+    turned = jnp.roll(turned, -mode, axis=1)
+    turned = turned.reshape(backward.shape)
     pair = (first_plane // 2 + jnp.arange(pairs, dtype=jnp.int32)).astype(jnp.float32)
     wave = pair[:, None] * spanwise_wave
     low = (jnp.arange(lanes) < lanes // 2)[None, :]
@@ -1285,9 +1316,9 @@
     sent_0 = pack_first(rows, layers, pairs, lanes)
     sent_1, late_2, sent_2 = pack_rest(rows, layers, pairs, lanes, some)
     arrived_0 = exchange(sent_0)
-    sent_1, here, geo, flux, small_flux, scaled, waves, small_waves, shift = (
+    sent_1, here, geo, flux, small_flux, scaled, waves, small_waves, shift, turned = (
         lax.optimization_barrier(
-            (sent_1, here, geo, flux, small_flux, scaled, waves, small_waves, shift)
+            (sent_1, here, geo, flux, small_flux, scaled, waves, small_waves, shift, turned)
         )
     )
     arrived_1 = exchange(sent_1)
@@ -1295,12 +1326,13 @@
     speed_x, slope_0 = to_points(arrived_0, forward)
     speed_y, slope_1 = to_points(arrived_1, forward)
     speeds = [speed_x, speed_y]
-    partial = in_plane(speeds, speeds, here, table)
+    partial = in_plane(speeds, speeds[:1], here, table)
     rows_early = some // NODES
-    speed_z, slope_2, blocks = turn_around(
-        arrived_1, NODES, 0, rows_early, partial[0], slope_0, forward, backward, (), None
-    )
-    home_0 = exchange(blocks)
+    speed_z, slope_2, *strips = turn_around(
+        arrived_1, NODES, 0, rows_early, partial[0], slope_0, forward, turned, (), None
+    )
+    for k in range(1, modes):
+        strips[k] = lax.ppermute(strips[k], "mode", [(i, (i + k) % modes) for i in range(modes)])
     speed_z, slope_2, first_buffer = turn_around(
         arrived_2,
         0,
@@ -1313,10 +1345,13 @@
         (speed_z, slope_2),
         (first_shape, NODES),
     )
-    last = in_plane(speeds, [speed_z], here, table)[0]
+    middle, last = in_plane(speeds, [speed_y, speed_z], here, table)
     shapes = (first_shape, second_shape)
-    blocks = to_planes(partial[1], speed_z, slope_1, backward, modes, 0, shapes, (first_buffer,))
+    blocks = to_planes(
+        middle, speed_z, slope_1, backward, modes, 0, shapes, (first_buffer,)
+    )
     blocks = to_planes(last, speed_z, slope_2, backward, modes, 1, shapes, blocks)
+    home_0 = by_source(strips, mode)
     home_1 = exchange(blocks[0])
     home_2 = exchange(blocks[1])
     returned = (home_1, home_2)

time: 514 us -> 596 us (1.16)
  the two profiles are of different devices: /device:TPU:0 before, /device:TPU:25 now
where the time goes in v6:
time: 596 us; the launch traced here: 594 us
  blocking collectives  218 us (37%)
  Pallas kernels  154 us (26%)
  waiting for transfers between devices  110 us (18%)
  starting transfers between devices  91.4 us (15%)
  local copies, waits for them, and re-layouts  15.8 us (3%)
    all_to_all x2, blocking collectives, exchange(): lax.all_to_all(blocks, 'mode', split_axis=0, concat_axis=0, tiled=True)  218 us
    ppermute x7, starting transfers between devices, paired_step(): lax.ppermute(strips[k], 'mode', [(i, (i + k) % modes) for i in range(mode...  59.2 us
    all_to_all x3, waiting for transfers between devices, exchange(): lax.all_to_all(blocks, 'mode', split_axis=0, concat_axis=0, tiled=True)  51.6 us
    ppermute x7, waiting for transfers between devices, paired_step(): lax.ppermute(strips[k], 'mode', [(i, (i + k) % modes) for i in range(mode...  42.1 us
    pallas_call x2, Pallas kernels, to_points(): call(body, (NODES,), [whole(table.shape), pl.BlockSpec((shares, NODES, pa...  19.7 us
    pallas_call x2, Pallas kernels, to_planes(): call(body, (NODES,), [whole(table.shape), spec, spec, spec] + [pl.BlockSp...  19.5 us
    all_to_all x3, starting transfers between devices, exchange(): lax.all_to_all(blocks, 'mode', split_axis=0, concat_axis=0, tiled=True)  18.2 us
    pallas_call x2, Pallas kernels, turn_around(): call(body, (count,), [whole(table.shape), whole(back.shape), pl.BlockSpec...  15.9 us
  transfers between devices with their start and end apart: 32, of which 16 were waited for; matrix products, arithmetic and copies ran while one was open for 2% of the time, Pallas kernels for 16%

profile of v6, /device:TPU:25, one launch (start us, length us, event | category | flops | bytes accessed | tf_op | source)
XLA Modules:
  0.0 594.2 jit_solution(2259329745422873948)
XLA Ops:
  0.6 4.7 shard_map.105.s0
  5.3 5.5 all-to-all-start
  10.8 8.3 %shard_map.104 = (f32[8,77,16,128]{3,2,1,0:T(8,128)}, f32[8,21,16,128]{3,2,1,0:T(8,128)}, f32[8,49,16,128]{3,2,1,0:T(8,128)}) custom-call(f32[3,6272,128]{2,1,0:T(8,128)} %bitcast.49, f32[3,6272,128]{2,1,0:T(8,128)} %bitcast.50), custom_call_target="tpu_custom_call" | custom-call | bytes 16056320 | tf_op jit(solution)/shard_map/pallas_call | solution.py:447
  30.6 51.6 %all-to-all-done.x_ref = f32[8,49,16,128]{3,2,1,0:T(8,128)} async-done(((f32[8,49,16,128]{3,2,1,0:T(8,128)}), f32[8,49,16,128]{3,2,1,0:T(8,128)}, u32[]{:S(2)}, u32[]{:S(2)}) %all-to-all-start) | async-done | bytes 3211296 | tf_op jit(solution)/shard_map/all_to_all | solution.py:1310
  82.2 114.0 %all_to_all.25.x_ref = f32[8,77,16,128]{3,2,1,0:T(8,128)} all-to-all(f32[8,77,16,128]{3,2,1,0:T(8,128)} %get-tuple-element.78.s1), channel_id=1, replica_groups=mesh['mode'=8,'elem'=4] {'mode'}, dimensions={0} | all-to-all | bytes 10092544 | tf_op jit(solution)/shard_map/all_to_all | solution.py:1310
  196.2 6.3 %all-to-all-start.2 = ((f32[8,21,16,128]{3,2,1,0:T(8,128)}), f32[8,21,16,128]{3,2,1,0:T(8,128)}, u32[]{:S(2)}, u32[]{:S(2)}) async-start(f32[8,21,16,128]{3,2,1,0:T(8,128)} %get-tuple-element.80), calls=%async_computation.2 | async-start | bytes 2752512 | tf_op jit(solution)/shard_map/all_to_all | solution.py:1310
  202.5 9.9 %shard_map.106 = (f32[49,128,128]{2,1,0:T(8,128)}, f32[49,128,128]{2,1,0:T(8,128)}) custom-call(bf16[512,768]{1,0:T(8,128)(2,1)} %constant.78.clone.t_ref, f32[8,49,16,128]{3,2,1,0:T(8,128)} %all-to-all-done.x_ref), custom_call_target="tpu_custom_call" | custom-call | flops 4932501504 | bytes 9633792 | tf_op jit(solution)/shard_map/pallas_call | solution.py:559
  212.3 9.9 %shard_map.107 = (f32[49,128,128]{2,1,0:T(8,128)}, f32[49,128,128]{2,1,0:T(8,128)}) custom-call(bf16[512,768]{1,0:T(8,128)(2,1)} %constant.78.clone.t_ref, f32[8,77,16,128]{3,2,1,0:T(8,128)} %all_to_all.25.x_ref), custom_call_target="tpu_custom_call" | custom-call | flops 4932501504 | bytes 9633792 | tf_op jit(solution)/shard_map/pallas_call | solution.py:559
  222.2 6.4 %shard_map.108.g_ref = f32[49,128,128]{2,1,0:T(8,128)} custom-call(f32[196,128]{1,0:T(8,128)} %reshape.81.m_ref, f32[49,128,128]{2,1,0:T(8,128)} %get-tuple-element.77.refs_0_, f32[49,128,128]{2,1,0:T(8,128)} %get-tuple-element.79.refs_1_), custom_call_target="tpu_custom_call" | custom-call | flops 24084480 | bytes 9633792 | tf_op jit(solution)/shard_map/pallas_call | solution.py:678
  228.6 8.9 %shard_map.109 = (f32[49,128,128]{2,1,0:T(8,128)}, f32[49,128,128]{2,1,0:T(8,128)}, f32[28,16,128]{2,1,0:T(8,128)}, f32[28,16,128]{2,1,0:T(8,128)}, f32[28,16,12...) custom-call(bf16[512,768]{1,0:T(8,128)(2,1)} %constant.78.clone.t_re, ...), custom_call_target="tpu_custom_call" | custom-call | flops 4227858432 | bytes 11010048 | tf_op jit(solution)/shard_map/pallas_call | solution.py:608
  237.5 7.0 %shard_map.110 = (f32[49,128,128]{2,1,0:T(8,128)}, f32[49,128,128]{2,1,0:T(8,128)}, f32[8,140,8,128]{3,2,1,0:T(8,128)}) custom-call(bf16[512,768]{1,0:T(8,128)(2,1)} %constant.78.clone.t_ref, bf16[256,768]{1,0:T(8,128)(2,1)} %constant.79.clone.i_ref.t_ref, f32[8,21,16,128]{3,2,1,0:T(8,128)} %all-to-all-done.2.x_ref, ...), custom_call_target="tpu_custom_call", output_to_operand_aliasing={{0}: (5, {}), {1}: (6, {})} | custom-call | flops 3170893824 | bytes 8257536 | tf_op jit(solution)/shard_map/pallas_call | solution.py:608
  244.5 9.1 %shard_map.111 = (f32[49,128,128]{2,1,0:T(8,128)}, f32[49,128,128]{2,1,0:T(8,128)}) custom-call(f32[196,128]{1,0:T(8,128)} %reshape.81.m_ref, f32[49,128,128]{2,1,0:T(8,128)} %get-tuple-element.77.refs_0_, f32[49,128,128]{2,1,0:T(8,128)} %get-tuple-element.79.refs_1_, f32[49,128,128]{2,1,0:T(8,128)} %get-tuple-element.85.refs_2_.w_ref), custom_call_target="tpu_custom_call" | custom-call | flops 48168960 | bytes 16056320 | tf_op jit(solution)/shard_map/pallas_call | solution.py:678
  253.6 9.8 %shard_map.112 = (f32[8,140,8,128]{3,2,1,0:T(8,128)}, f32[8,98,8,128]{3,2,1,0:T(8,128)}) custom-call(bf16[256,768]{1,0:T(8,128)(2,1)} %constant.79.clone.i_ref.t_ref, f32[49,128,128]{2,1,0:T(8,128)} %get-tuple-element.88.g_ref, f32[49,128,128]{2,1,0:T(8,128)} %get-tuple-element.85.refs_2_.w_ref, ...), custom_call_target="tpu_custom_call", output_to_operand_aliasing={{0}: (4, {})} | custom-call | flops 2466250752 | bytes 12845056 | tf_op jit(solution)/shard_map/pallas_call | solution.py:733
  263.4 9.7 %shard_map.113 = (f32[8,140,8,128]{3,2,1,0:T(8,128)}, f32[8,98,8,128]{3,2,1,0:T(8,128)}) custom-call(bf16[256,768]{1,0:T(8,128)(2,1)} %constant.79.clone.i_ref.t_ref, f32[49,128,128]{2,1,0:T(8,128)} %get-tuple-element.86.g_ref, f32[49,128,128]{2,1,0:T(8,128)} %get-tuple-element.85.refs_2_.w_ref, ...), custom_call_target="tpu_custom_call", output_to_operand_aliasing={{0}: (4, {}), {1}: (5, {})} | custom-call | flops 2466250752 | bytes 12845056 | tf_op jit(solution)/shard_map/pallas_call | solution.py:733
  273.1 104.3 %all_to_all.26.refs_0_.refs_1_.refs_2_.r1.r2.refs_3_ = f32[8,140,8,128]{3,2,1,0:T(8,128)} all-to-all(f32[8,140,8,128]{3,2,1,0:T(8,128)} %get-tuple-element.107), channel_id=1, replica_groups=mesh['mode'=8,'elem'=4] {'mode'}, dimensions={0} | all-to-all | bytes 9175040 | tf_op jit(solution)/shard_map/all_to_all | solution.py:1310
  377.3 6.4 %all-to-all-start.3 = ((f32[8,98,8,128]{3,2,1,0:T(8,128)}), f32[8,98,8,128]{3,2,1,0:T(8,128)}, u32[]{:S(2)}, u32[]{:S(2)}) async-start(f32[8,98,8,128]{3,2,1,0:T(8,128)} %get-tuple-element.93), calls=%async_computation.3 | async-start | bytes 6422528 | tf_op jit(solution)/shard_map/all_to_all | solution.py:1310
  385.2 2.1 collective-permute-start.2
  387.4 2.2 collective-permute-start.4
  389.6 42.1 %collective-permute-done.refs_1_ = f32[28,16,128]{2,1,0:T(8,128)} collective-permute-done((f32[28,16,128]{2,1,0:T(8,128)S(1)}, f32[28,16,128]{2,1,0:T(8,128)}, u32[]{:S(2)}, u32[]{:S(2)}) %collective-permute-start) | collective-permute-done | bytes 229408 | tf_op jit(solution)/shard_map/ppermute | solution.py:1335
  431.7 48.4 %collective-permute-start.5 = (f32[28,16,128]{2,1,0:T(8,128)}, f32[28,16,128]{2,1,0:T(8,128)}, u32[]{:S(2)}, u32[]{:S(2)}) collective-permute-start(f32[28,16,128]{2,1,0:T(8,128)} %get-tuple-element.105), channel_id=1, source_target_pairs={{0,24},{4,28},{8,0},{12,4},{16,8},{20,12},{24,16},{28,20},{1,25},{... | collective-permute-start | bytes 688136 | tf_op jit(solution)/shard_map/ppermute | solution.py:1335
  480.1 4.9 collective-permute-start.6
  485.0 10.0 %shard_map.114.s0 = f32[8,49,16,128]{3,2,1,0:T(8,128)} custom-call(f32[1568,128]{1,0:T(8,128)} %get-tuple-element.95.m_ref, f32[392,128]{1,0:T(8,128)} %reshape_reshape.4.q_ref, f32[16,128]{1,0:T(8,128)} %get-tuple-element.97.k_ref, f32[8,49,16,128]{3,2,1,0:T(8,128)} %shard_map.105.s0, f32[8,77,16,128]{3,2,1,0:T(8,128)} %get-tuple-element.78.s1, ...), custom_call_target="tpu_custom_call" | custom-call | flops 48168960 | bytes 12845056 | tf_op jit(solution)/shard_map/pallas_call | solution.py:785
  495.0 3.6 shard_map.115.r0.refs_0_
  498.6 8.1 %shard_map.116.f_ref = f32[8,49,16,128]{3,2,1,0:T(8,128)} custom-call(f32[1568,128]{1,0:T(8,128)} %get-tuple-element.94.m_ref, f32[8,49,16,128]{3,2,1,0:T(8,128)} %shard_map.114.s0, f32[8,28,16,128]{3,2,1,0:T(8,128)} %shard_map.115.r0.refs_0_, f32[8,140,8,128]{3,2,1,0:T(8,128)} %all_to_all.26.refs_0_.refs_1_.refs_2_.r1.r2.refs_3_, ...), custom_call_target="tpu_custom_call" | custom-call | flops 24084480 | bytes 9633792 | tf_op jit(solution)/shard_map/pallas_call | solution.py:836
  506.7 2.3 copy-done
  509.0 1.9 copy-done.1
  513.6 2.9 shard_map.117
  516.6 2.0 collective-permute-start.7
  519.4 2.3 collective-permute-done.8.a_ref
  521.7 3.7 shard_map.118
  529.2 4.0 shard_map.119
  536.4 1.7 collective-permute-done.13.right
  538.1 3.6 shard_map.120
  542.3 1.5 collective-permute-start.15
  543.8 3.5 shard_map.122.refs_1_
  547.3 3.5 shard_map.123.refs_1_
  550.9 2.2 shard_map.121.refs_0_
  554.2 4.4 shard_map.126
  559.8 2.0 collective-permute-done.19.a_ref
  561.8 3.7 shard_map.127
  568.1 1.8 collective-permute-done.21.right
  569.9 4.0 shard_map.128
  575.7 2.0 collective-permute-done.25.far
  578.2 3.6 shard_map.129
  583.1 1.7 collective-permute-start.26
  584.9 3.6 shard_map.124.refs_1_
  588.5 3.6 shard_map.125
  592.1 2.2 shard_map.130
  (128 shorter events, 32.6 us)
Async XLA Ops:
  5.3 76.9 %all-to-all-start = ((f32[8,49,16,128]{3,2,1,0:T(8,128)}), f32[8,49,16,128]{3,2,1,0:T(8,128)}, u32[]{:S(2)}, u32[]{:S(2)}) async-start(f32[8,49,16,128]{3,2,1,0:T(8,128)} %shard_map.105.s0), calls=%async_computation | async-start | bytes 6422528 | tf_op jit(solution)/shard_map/all_to_all | solution.py:1310
  22.9 1.2 copy-start.15
  24.5 1.9 copy-start.14
  196.2 41.3 %all-to-all-start.2 = ((f32[8,21,16,128]{3,2,1,0:T(8,128)}), f32[8,21,16,128]{3,2,1,0:T(8,128)}, u32[]{:S(2)}, u32[]{:S(2)}) async-start(f32[8,21,16,128]{3,2,1,0:T(8,128)} %get-tuple-element.80), calls=%async_computation.2 | async-start | bytes 2752512 | tf_op jit(solution)/shard_map/all_to_all | solution.py:1310
  377.3 6.4 %copy-start.22 = (f32[28,16,128]{2,1,0:T(8,128)S(1)}, f32[28,16,128]{2,1,0:T(8,128)}, u32[]{:S(2)}) copy-start(f32[28,16,128]{2,1,0:T(8,128)} %get-tuple-element.100) | copy-start | bytes 688132
  377.3 7.6 %copy-start.21 = (f32[28,16,128]{2,1,0:T(8,128)S(1)}, f32[28,16,128]{2,1,0:T(8,128)}, u32[]{:S(2)}) copy-start(f32[28,16,128]{2,1,0:T(8,128)} %get-tuple-element.101) | copy-start | bytes 688132
  377.3 175.7 %all-to-all-start.3 = ((f32[8,98,8,128]{3,2,1,0:T(8,128)}), f32[8,98,8,128]{3,2,1,0:T(8,128)}, u32[]{:S(2)}, u32[]{:S(2)}) async-start(f32[8,98,8,128]{3,2,1,0:T(8,128)} %get-tuple-element.93), calls=%async_computation.3 | async-start | bytes 6422528 | tf_op jit(solution)/shard_map/all_to_all | solution.py:1310
  383.7 48.0 %collective-permute-start = (f32[28,16,128]{2,1,0:T(8,128)S(1)}, f32[28,16,128]{2,1,0:T(8,128)}, u32[]{:S(2)}, u32[]{:S(2)}) collective-permute-start(f32[28,16,128]{2,1,0:T(8,128)S(1)} %copy-done.22), channel_id=1, source_target_pairs={{0,4},{4,8},{8,12},{12,16},{16,20},{20,24},{24,28},{28,0},{1,5},{5... | collective-permute-start | bytes 688136 | tf_op jit(solution)/shard_map/ppermute | solution.py:1335
  384.9 95.1 %collective-permute-start.1 = (f32[28,16,128]{2,1,0:T(8,128)S(1)}, f32[28,16,128]{2,1,0:T(8,128)}, u32[]{:S(2)}, u32[]{:S(2)}) collective-permute-start(f32[28,16,128]{2,1,0:T(8,128)S(1)} %copy-done.21), channel_id=1, source_target_pairs={{0,8},{4,12},{8,16},{12,20},{16,24},{20,28},{24,0},{28,4},{1,9},{5... | collective-permute-start | bytes 688136 | tf_op jit(solution)/shard_map/ppermute | solution.py:1335
  385.2 109.8 %collective-permute-start.2 = (f32[28,16,128]{2,1,0:T(8,128)}, f32[28,16,128]{2,1,0:T(8,128)}, u32[]{:S(2)}, u32[]{:S(2)}) collective-permute-start(f32[28,16,128]{2,1,0:T(8,128)} %get-tuple-element.102), channel_id=1, source_target_pairs={{0,12},{4,16},{8,20},{12,24},{16,28},{20,0},{24,4},{28,8},{1,13},{... | collective-permute-start | bytes 688136 | tf_op jit(solution)/shard_map/ppermute | solution.py:1335
  387.3 107.7 %collective-permute-start.3 = (f32[28,16,128]{2,1,0:T(8,128)}, f32[28,16,128]{2,1,0:T(8,128)}, u32[]{:S(2)}, u32[]{:S(2)}) collective-permute-start(f32[28,16,128]{2,1,0:T(8,128)} %get-tuple-element.103), channel_id=1, source_target_pairs={{0,16},{4,20},{8,24},{12,28},{16,0},{20,4},{24,8},{28,12},{1,17},{... | collective-permute-start | bytes 688136 | tf_op jit(solution)/shard_map/ppermute | solution.py:1335
  387.4 107.6 %collective-permute-start.4 = (f32[28,16,128]{2,1,0:T(8,128)}, f32[28,16,128]{2,1,0:T(8,128)}, u32[]{:S(2)}, u32[]{:S(2)}) collective-permute-start(f32[28,16,128]{2,1,0:T(8,128)} %get-tuple-element.104), channel_id=1, source_target_pairs={{0,20},{4,24},{8,28},{12,0},{16,4},{20,8},{24,12},{28,16},{1,21},{... | collective-permute-start | bytes 688136 | tf_op jit(solution)/shard_map/ppermute | solution.py:1335
  431.7 63.3 %collective-permute-start.5 = (f32[28,16,128]{2,1,0:T(8,128)}, f32[28,16,128]{2,1,0:T(8,128)}, u32[]{:S(2)}, u32[]{:S(2)}) collective-permute-start(f32[28,16,128]{2,1,0:T(8,128)} %get-tuple-element.105), channel_id=1, source_target_pairs={{0,24},{4,28},{8,0},{12,4},{16,8},{20,12},{24,16},{28,20},{1,25},{... | collective-permute-start | bytes 688136 | tf_op jit(solution)/shard_map/ppermute | solution.py:1335
  480.1 15.0 %collective-permute-start.6 = (f32[28,16,128]{2,1,0:T(8,128)}, f32[28,16,128]{2,1,0:T(8,128)}, u32[]{:S(2)}, u32[]{:S(2)}) collective-permute-start(f32[28,16,128]{2,1,0:T(8,128)} %get-tuple-element.106), channel_id=1, source_target_pairs={{0,28},{4,0},{8,4},{12,8},{16,12},{20,16},{24,20},{28,24},{1,29},{... | collective-permute-start | bytes 688136 | tf_op jit(solution)/shard_map/ppermute | solution.py:1335
  506.7 2.3 copy-start
  509.0 1.9 copy-start.1
  513.6 8.0 %copy-start.3 = (f32[784,128]{1,0:T(8,128)S(1)}, f32[784,128]{1,0:T(8,128)}, u32[]{:S(2)}) copy-start(f32[784,128]{1,0:T(8,128)} %reshape.82.g_ref) | copy-start | bytes 1204228
  513.6 8.0 %copy-start.11 = (f32[2,8,128]{2,1,0:T(8,128)S(1)}, f32[2,8,128]{2,1,0:T(8,128)}, u32[]{:S(2)}) copy-start(f32[2,8,128]{2,1,0:T(8,128)} %broadcast_in_dim.49.k_ref) | copy-start | bytes 24580
  516.6 2.8 collective-permute-start.7
  518.6 3.1 collective-permute-start.8
  521.7 22.2 %slice-start = ((s8[4587520]{0:T(1024)(128)(4,1)}), s8[4194304]{0:T(1024)(128)(4,1)S(1)}, s32[]{:S(2)}) async-start(s8[4587520]{0:T(1024)(128)(4,1)} %bitcast.45), calls=%async_computation.5 | async-start | bytes 8388608
  525.4 1.2 collective-permute-start.9
  525.4 2.5 collective-permute-start.11
  525.8 3.4 collective-permute-start.10
  529.2 14.6 %slice-start.1 = ((s8[4587520]{0:T(1024)(128)(4,1)}), s8[393216]{0:T(1024)(128)(4,1)S(1)}, s32[]{:S(2)}) async-start(s8[4587520]{0:T(1024)(128)(4,1)} %bitcast.45), calls=%async_computation.6 | async-start | bytes 786432
  533.2 10.6 %copy-start.5 = (f32[8,28,16,128]{3,2,1,0:T(8,128)S(1)}, f32[8,28,16,128]{3,2,1,0:T(8,128)}, u32[]{:S(2)}) copy-start(f32[8,28,16,128]{3,2,1,0:T(8,128)} %shard_map.115.r0.refs_0_) | copy-start | bytes 5505028
  533.2 1.8 collective-permute-start.12
  533.8 2.5 collective-permute-start.14
  535.0 3.1 collective-permute-start.13
  541.7 9.1 %collective-permute-start.17 = (f32[2,8,128]{2,1,0:T(8,128)S(1)}, f32[2,8,128]{2,1,0:T(8,128)S(1)}, u32[]{:S(2)}, u32[]{:S(2)}) collective-permute-start(f32[2,8,128]{2,1,0:T(8,128)S(1)} %get-tuple-element.125.own), channel_id=1, source_target_pairs={{0,2},{1,3},{2,0},{3,1},{4,6},{5,7},{6,4},{7,5},{8,10},{9,11},{10,... | collective-permute-start | bytes 24584 | tf_op jit(solution)/shard_map/ppermute | solution.py:985
  542.1 8.8 %collective-permute-start.16 = (f32[2,8,128]{2,1,0:T(8,128)S(1)}, f32[2,8,128]{2,1,0:T(8,128)S(1)}, u32[]{:S(2)}, u32[]{:S(2)}) collective-permute-start(f32[2,8,128]{2,1,0:T(8,128)S(1)} %get-tuple-element.125.own), channel_id=1, source_target_pairs={{1,0},{2,1},{3,2},{0,3},{5,4},{6,5},{7,6},{4,7},{9,8},{10,9},{11,1... | collective-permute-start | bytes 24584 | tf_op jit(solution)/shard_map/ppermute | solution.py:980
  542.3 8.5 %collective-permute-start.15 = (f32[2,8,128]{2,1,0:T(8,128)S(1)}, f32[2,8,128]{2,1,0:T(8,128)S(1)}, u32[]{:S(2)}, u32[]{:S(2)}) collective-permute-start(f32[2,8,128]{2,1,0:T(8,128)S(1)} %get-tuple-element.125.own), channel_id=1, source_target_pairs={{0,1},{1,2},{2,3},{3,0},{4,5},{5,6},{6,7},{7,4},{8,9},{9,10},{10,1... | collective-permute-start | bytes 24584 | tf_op jit(solution)/shard_map/ppermute | solution.py:980
  550.8 2.2 copy-start.2
  550.9 2.2 copy-start.9
  550.9 2.2 copy-start.13
  554.2 7.6 %copy-start.4 = (f32[784,128]{1,0:T(8,128)S(1)}, f32[784,128]{1,0:T(8,128)}, u32[]{:S(2)}) copy-start(f32[784,128]{1,0:T(8,128)} %reshape.82.g_ref) | copy-start | bytes 1204228
  554.2 7.6 %copy-start.10 = (f32[2,8,128]{2,1,0:T(8,128)S(1)}, f32[2,8,128]{2,1,0:T(8,128)}, u32[]{:S(2)}) copy-start(f32[2,8,128]{2,1,0:T(8,128)} %broadcast_in_dim.51.k_ref) | copy-start | bytes 24580
  558.6 1.2 collective-permute-start.18
  558.7 3.1 collective-permute-start.19
  565.5 2.0 collective-permute-start.20
  565.6 2.5 collective-permute-start.22
  566.8 3.1 collective-permute-start.21
  573.9 1.7 collective-permute-start.23
  574.9 2.8 collective-permute-start.25
  575.1 3.1 collective-permute-start.24
  581.8 10.2 %collective-permute-start.28 = (f32[2,8,128]{2,1,0:T(8,128)S(1)}, f32[2,8,128]{2,1,0:T(8,128)S(1)}, u32[]{:S(2)}, u32[]{:S(2)}) collective-permute-start(f32[2,8,128]{2,1,0:T(8,128)S(1)} %get-tuple-element.145.own), channel_id=1, source_target_pairs={{0,2},{1,3},{2,0},{3,1},{4,6},{5,7},{6,4},{7,5},{8,10},{9,11},{10,... | collective-permute-start | bytes 24584 | tf_op jit(solution)/shard_map/ppermute | solution.py:985
  583.1 9.0 %collective-permute-start.27 = (f32[2,8,128]{2,1,0:T(8,128)S(1)}, f32[2,8,128]{2,1,0:T(8,128)S(1)}, u32[]{:S(2)}, u32[]{:S(2)}) collective-permute-start(f32[2,8,128]{2,1,0:T(8,128)S(1)} %get-tuple-element.145.own), channel_id=1, source_target_pairs={{1,0},{2,1},{3,2},{0,3},{5,4},{6,5},{7,6},{4,7},{9,8},{10,9},{11,1... | collective-permute-start | bytes 24584 | tf_op jit(solution)/shard_map/ppermute | solution.py:980
  583.1 9.0 %collective-permute-start.26 = (f32[2,8,128]{2,1,0:T(8,128)S(1)}, f32[2,8,128]{2,1,0:T(8,128)S(1)}, u32[]{:S(2)}, u32[]{:S(2)}) collective-permute-start(f32[2,8,128]{2,1,0:T(8,128)S(1)} %get-tuple-element.145.own), channel_id=1, source_target_pairs={{0,1},{1,2},{2,3},{3,0},{4,5},{5,6},{6,7},{7,4},{8,9},{9,10},{10,1... | collective-permute-start | bytes 24584 | tf_op jit(solution)/shard_map/ppermute | solution.py:980
  (9 other events, 9.7 us)

commit v7 on v5

--- a/solution.py
+++ b/solution.py
@@ -399,34 +399,55 @@
     )
 
 
-def pack_first(rows, layers, pairs, lanes):
+def pack_first(rows, place, layers, pairs, lanes):
     square = NODES * NODES
     unit = 2 * square * layers
-
-    def body(x_ref, o_ref, mid):
+    shares = 2 * layers
+
+    def body(place_ref, x_ref, *refs):
+        outs, (mid, held_ref) = (refs[:shares], refs[shares:])
+        here = place_ref[0]
+
         def write(d, n, value):
-            o_ref[d, n] = value
+            held_ref[d, n] = value
 
         pack_one(x_ref, write, mid, layers, lanes)
 
-    spec, shape = pack_specs(layers, pairs, lanes, square)
+        def row(a, carry):
+            for k in range(shares):
+                d = lax.rem(here + k, shares)
+                for b in range(NODES):
+                    outs[k][a * NODES + b] = held_ref[d, a * NODES + b]
+            return carry
+
+        lax.fori_loop(0, NODES, row, 0)
+
     return call(
         body,
         (pairs // 8,),
-        [pl.BlockSpec((1, 8 * unit, lanes), lambda g: (0, g, 0))],
-        spec,
-        shape,
-        scratch=[pltpu.VMEM((unit, 8, lanes), jnp.float32)],
+        [
+            pl.BlockSpec(memory_space=pltpu.SMEM),
+            pl.BlockSpec((1, 8 * unit, lanes), lambda g: (0, g, 0)),
+        ],
+        [pl.BlockSpec((square, 8, lanes), lambda g: (0, g, 0))] * shares,
+        [jax.ShapeDtypeStruct((square, pairs, lanes), jnp.float32)] * shares,
+        scratch=[
+            pltpu.VMEM((unit, 8, lanes), jnp.float32),
+            pltpu.VMEM((shares, square, 8, lanes), jnp.float32),
+        ],
         grant=WHOLE_GRANT,
         moved=2 * rows.shape[1] * lanes * 4,
-    )(rows)
+    )(jnp.full((1,), place, jnp.int32), rows)
 
 
 def pack_rest(rows, layers, pairs, lanes, early):
     square = NODES * NODES
     unit = 2 * square * layers
 
-    def body(x_ref, y_ref, o_ref, late_ref, whole_ref, mid):
+    def body(u_ref, x_ref, y_ref, o_ref, late_ref, whole_ref, zero_ref, mid):
+        def zeroth(d, n, value):
+            zero_ref[d, n] = value
+
         def first(d, n, value):
             o_ref[d, n] = value
 
@@ -439,15 +460,17 @@
 
         pack_one(x_ref, first, mid, layers, lanes)
         pack_one(y_ref, second, mid, layers, lanes)
+        pack_one(u_ref, zeroth, mid, layers, lanes)
 
     parts = [
         pack_specs(layers, pairs, lanes, nodes)
-        for nodes in (square + early, square - early, square)
+        for nodes in (square + early, square - early, square, square)
     ]
     return call(
         body,
         (pairs // 8,),
         [
+            pl.BlockSpec((1, 8 * unit, lanes), lambda g: (0, g, 0)),
             pl.BlockSpec((1, 8 * unit, lanes), lambda g: (1, g, 0)),
             pl.BlockSpec((1, 8 * unit, lanes), lambda g: (2, g, 0)),
         ],
@@ -456,7 +479,7 @@
         scratch=[pltpu.VMEM((unit, 8, lanes), jnp.float32)],
         grant=WHOLE_GRANT,
         moved=5 * rows.shape[1] * lanes * 4,
-    )(rows, rows)
+    )(rows, rows, rows)
 
 
 def unpack(arrays, specs, read_from, slots, layers, buffer, total, steps=2):
@@ -683,6 +706,32 @@
         grant=WHOLE_GRANT,
         moved=(len(arrays) + count) * square * rows * lanes * 4,
     )(metrics, *arrays)
+
+
+def by_source(strips, place):
+    count = len(strips)
+    nodes = strips[0].shape[0]
+
+    def body(place_ref, *refs):
+        o_ref = refs[-1]
+        here = place_ref[0]
+
+        def node(n, carry):
+            for k in range(count):
+                o_ref[lax.rem(here - k + count, count), n] = refs[k][n]
+            return carry
+
+        lax.fori_loop(0, nodes, node, 0)
+
+    return call(
+        body,
+        (1,),
+        [pl.BlockSpec(memory_space=pltpu.SMEM)] + [whole(strips[0].shape)] * count,
+        whole((count,) + strips[0].shape),
+        jax.ShapeDtypeStruct((count,) + strips[0].shape, jnp.float32),
+        grant=WHOLE_GRANT,
+        moved=8 * count * strips[0].size,
+    )(jnp.full((1,), place, jnp.int32), *strips)
 
 
 def to_planes(partial, speed_z, slope_z, table, shares, place, shapes, buffers):
@@ -1282,9 +1331,10 @@
     group = pairs // 2
     first_shape = (modes, 4 * square - 2 * some, group, lanes)
     second_shape = (modes, 2 * square, group, lanes)
-    sent_0 = pack_first(rows, layers, pairs, lanes)
-    sent_1, late_2, sent_2 = pack_rest(rows, layers, pairs, lanes, some)
-    arrived_0 = exchange(sent_0)
+    strips = list(pack_first(rows, mode, layers, pairs, lanes))
+    sent_1, late_2, sent_2, sent_0 = pack_rest(rows, layers, pairs, lanes, some)
+    for k in range(1, modes):
+        strips[k] = lax.ppermute(strips[k], "mode", [(i, (i + k) % modes) for i in range(modes)])
     sent_1, here, geo, flux, small_flux, scaled, waves, small_waves, shift = (
         lax.optimization_barrier(
             (sent_1, here, geo, flux, small_flux, scaled, waves, small_waves, shift)
@@ -1292,7 +1342,7 @@
     )
     arrived_1 = exchange(sent_1)
     arrived_2 = exchange(late_2)
-    speed_x, slope_0 = to_points(arrived_0, forward)
+    speed_x, slope_0 = to_points(by_source(strips, mode), forward)
     speed_y, slope_1 = to_points(arrived_1, forward)
     speeds = [speed_x, speed_y]
     partial = in_plane(speeds, speeds, here, table)

time: 514 us -> 565 us (1.099)
  starting transfers between devices: 41.3 us -> 73 us
  Pallas kernels: 151 us -> 160 us
    ppermute x0 -> x7, waiting for transfers between devices: none -> 54.3 us  [paired_step(): lax.ppermute(strips[k], 'mode', [(i, (i + k) % modes) for i in range(mode...]
    all_to_all x4 -> x3, waiting for transfers between devices: 66.4 us -> 14.8 us  [exchange(): lax.all_to_all(blocks, 'mode', split_axis=0, concat_axis=0, tiled=True)]
    ppermute x0 -> x7, starting transfers between devices: none -> 17.7 us  [paired_step(): lax.ppermute(strips[k], 'mode', [(i, (i + k) % modes) for i in range(mode...]
    all_to_all x4 -> x3, starting transfers between devices: 21.9 us -> 35.8 us  [exchange(): lax.all_to_all(blocks, 'mode', split_axis=0, concat_axis=0, tiled=True)]
  transfers between devices with their start and end apart: 26 -> 32, of which waited for: 12 -> 14; matrix products, arithmetic and copies ran while one was open for 2% -> 0% of each run, Pallas kernels for 25% -> 23%
where the time goes in v7:
time: 565 us; the launch traced here: 562 us
  blocking collectives  226 us (40%)
  Pallas kernels  160 us (28%)
  waiting for transfers between devices  79.8 us (14%)
  starting transfers between devices  73 us (13%)
  local copies, waits for them, and re-layouts  18.2 us (3%)
    all_to_all x2, blocking collectives, exchange(): lax.all_to_all(blocks, 'mode', split_axis=0, concat_axis=0, tiled=True)  226 us
    ppermute x7, waiting for transfers between devices, paired_step(): lax.ppermute(strips[k], 'mode', [(i, (i + k) % modes) for i in range(mode...  54.3 us
    all_to_all x3, starting transfers between devices, exchange(): lax.all_to_all(blocks, 'mode', split_axis=0, concat_axis=0, tiled=True)  35.8 us
    pallas_call x2, Pallas kernels, to_points(): call(body, (NODES,), [whole(table.shape), pl.BlockSpec((shares, NODES, pa...  19.7 us
    pallas_call x2, Pallas kernels, to_planes(): call(body, (NODES,), [whole(table.shape), spec, spec, spec] + [pl.BlockSp...  19.5 us
    ppermute x7, starting transfers between devices, paired_step(): lax.ppermute(strips[k], 'mode', [(i, (i + k) % modes) for i in range(mode...  17.7 us
    pallas_call x2, Pallas kernels, in_plane(): call(body, (rows // step,), [whole(metrics.shape)] + [spec] * len(arrays)...  16 us
    pallas_call x2, Pallas kernels, turn_around(): call(body, (count,), [whole(table.shape), whole(back.shape), pl.BlockSpec...  15.4 us
  transfers between devices with their start and end apart: 32, of which 14 were waited for; matrix products, arithmetic and copies ran while one was open for 0% of the time, Pallas kernels for 23%

profile of v7, /device:TPU:0, one launch (start us, length us, event | category | flops | bytes accessed | tf_op | source)
XLA Modules:
  0.0 562.5 jit_solution(3252792871515707076)
XLA Ops:
  11.4 11.4 %shard_map.104 = (f32[8,77,16,128]{3,2,1,0:T(8,128)}, f32[8,21,16,128]{3,2,1,0:T(8,128)}, f32[8,49,16,128]{3,2,1,0:T(8,128)}, f32[8,49,16,128]{3,2,1,0:T(8,128)}) custom-call(f32[3,6272,128]{2,1,0:T(8,128)} %bitcast.45, f32[3,6272,128]{2,1,0:T(8,128)} %bitcast.46, f32[3,6272,128]{2,1,0:T(8,128)} %bitcast.47), custom_call_target="tpu_custom_call" | custom-call | bytes 16056320 | tf_op jit(solution)/shard_map/pallas_call | solution.py:469
  22.9 2.7 broadcast_multiply_fusion
  27.6 119.4 %all_to_all.25.x_ref = f32[8,77,16,128]{3,2,1,0:T(8,128)} all-to-all(f32[8,77,16,128]{3,2,1,0:T(8,128)} %get-tuple-element.87.s1), channel_id=1, replica_groups=mesh['mode'=8,'elem'=4] {'mode'}, dimensions={0} | all-to-all | bytes 10092544 | tf_op jit(solution)/shard_map/all_to_all | solution.py:1328
  147.0 4.3 all-to-all-start.1
  151.3 5.2 shard_map.105
  156.5 1.9 collective-permute-start
  159.8 2.4 collective-permute-start.2
  163.6 2.4 collective-permute-start.4
  166.0 22.5 %collective-permute-done.refs_1_ = f32[49,16,128]{2,1,0:T(8,128)} collective-permute-done((f32[49,16,128]{2,1,0:T(8,128)}, f32[49,16,128]{2,1,0:T(8,128)}, u32[]{:S(2)}, u32[]{:S(2)}) %collective-permute-start) | collective-permute-done | bytes 401440 | tf_op jit(solution)/shard_map/ppermute | solution.py:1337
  188.6 8.0 %collective-permute-start.6 = (f32[49,16,128]{2,1,0:T(8,128)}, f32[49,16,128]{2,1,0:T(8,128)}, u32[]{:S(2)}, u32[]{:S(2)}) collective-permute-start(f32[49,16,128]{2,1,0:T(8,128)} %get-tuple-element.85), channel_id=1, source_target_pairs={{0,28},{4,0},{8,4},{12,8},{16,12},{20,16},{24,20},{28,24},{1,29},{... | collective-permute-start | bytes 1204232 | tf_op jit(solution)/shard_map/ppermute | solution.py:1337
  196.6 31.4 %collective-permute-done.2.refs_3_ = f32[49,16,128]{2,1,0:T(8,128)} collective-permute-done((f32[49,16,128]{2,1,0:T(8,128)}, f32[49,16,128]{2,1,0:T(8,128)}, u32[]{:S(2)}, u32[]{:S(2)}) %collective-permute-start.2) | collective-permute-done | bytes 401440 | tf_op jit(solution)/shard_map/ppermute | solution.py:1337
  228.5 4.9 shard_map.106.x_ref
  233.4 9.8 %shard_map.107 = (f32[49,128,128]{2,1,0:T(8,128)}, f32[49,128,128]{2,1,0:T(8,128)}) custom-call(bf16[512,768]{1,0:T(8,128)(2,1)} %constant.58.clone.t_ref, f32[8,49,16,128]{3,2,1,0:T(8,128)} %shard_map.106.x_ref), custom_call_target="tpu_custom_call" | custom-call | flops 4932501504 | bytes 9633792 | tf_op jit(solution)/shard_map/pallas_call | solution.py:582
  243.2 9.9 %shard_map.108 = (f32[49,128,128]{2,1,0:T(8,128)}, f32[49,128,128]{2,1,0:T(8,128)}) custom-call(bf16[512,768]{1,0:T(8,128)(2,1)} %constant.58.clone.t_ref, f32[8,77,16,128]{3,2,1,0:T(8,128)} %all_to_all.25.x_ref), custom_call_target="tpu_custom_call" | custom-call | flops 4932501504 | bytes 9633792 | tf_op jit(solution)/shard_map/pallas_call | solution.py:582
  253.1 8.4 %shard_map.109 = (f32[49,128,128]{2,1,0:T(8,128)}, f32[49,128,128]{2,1,0:T(8,128)}) custom-call(f32[196,128]{1,0:T(8,128)} %reshape.75.m_ref, f32[49,128,128]{2,1,0:T(8,128)} %get-tuple-element.86.refs_0_, f32[49,128,128]{2,1,0:T(8,128)} %get-tuple-element.88.refs_1_), custom_call_target="tpu_custom_call" | custom-call | flops 48168960 | bytes 12845056 | tf_op jit(solution)/shard_map/pallas_call | solution.py:699
  261.5 8.4 %shard_map.110 = (f32[49,128,128]{2,1,0:T(8,128)}, f32[49,128,128]{2,1,0:T(8,128)}, f32[8,28,16,128]{3,2,1,0:T(8,128)}) custom-call(bf16[512,768]{1,0:T(8,128)(2,1)} %constant.58.clone.t_ref, bf16[256,768]{1,0:T(8,128)(2,1)} %constant.59.clone.i_ref.t_ref, f32[8,77,16,128]{3,2,1,0:T(8,128)} %all_to_all.25.x_ref, f32[49,128,128]{2,1,0:T(8,128)} %get-tuple-element.90.g_ref, ...), custom_call_target="tpu_custom_call" | custom-call | flops 4227858432 | bytes 11010048 | tf_op jit(solution)/shard_map/pallas_call | solution.py:629
  269.9 27.1 %all-to-all-start.3 = ((f32[8,28,16,128]{3,2,1,0:T(8,128)}), f32[8,28,16,128]{3,2,1,0:T(8,128)}, u32[]{:S(2)}, u32[]{:S(2)}) async-start(f32[8,28,16,128]{3,2,1,0:T(8,128)} %get-tuple-element.108), calls=%async_computation.3 | async-start | bytes 3670016 | tf_op jit(solution)/shard_map/all_to_all | solution.py:1328
  297.0 7.0 %shard_map.111 = (f32[49,128,128]{2,1,0:T(8,128)}, f32[49,128,128]{2,1,0:T(8,128)}, f32[8,140,8,128]{3,2,1,0:T(8,128)}) custom-call(bf16[512,768]{1,0:T(8,128)(2,1)} %constant.58.clone.t_ref, bf16[256,768]{1,0:T(8,128)(2,1)} %constant.59.clone.i_ref.t_ref, f32[8,21,16,128]{3,2,1,0:T(8,128)} %all-to-all-done.1.x_ref, ...), custom_call_target="tpu_custom_call", output_to_operand_aliasing={{0}: (5, {}), {1}: (6, {})} | custom-call | flops 3170893824 | bytes 8257536 | tf_op jit(solution)/shard_map/pallas_call | solution.py:629
  304.1 7.5 %shard_map.112.g_ref = f32[49,128,128]{2,1,0:T(8,128)} custom-call(f32[196,128]{1,0:T(8,128)} %reshape.75.m_ref, f32[49,128,128]{2,1,0:T(8,128)} %get-tuple-element.86.refs_0_, f32[49,128,128]{2,1,0:T(8,128)} %get-tuple-element.88.refs_1_, f32[49,128,128]{2,1,0:T(8,128)} %get-tuple-element.94.refs_2_.w_ref), custom_call_target="tpu_custom_call" | custom-call | flops 24084480 | bytes 12845056 | tf_op jit(solution)/shard_map/pallas_call | solution.py:699
  311.6 9.8 %shard_map.113 = (f32[8,140,8,128]{3,2,1,0:T(8,128)}, f32[8,98,8,128]{3,2,1,0:T(8,128)}) custom-call(bf16[256,768]{1,0:T(8,128)(2,1)} %constant.59.clone.i_ref.t_ref, f32[49,128,128]{2,1,0:T(8,128)} %get-tuple-element.96.g_ref, f32[49,128,128]{2,1,0:T(8,128)} %get-tuple-element.94.refs_2_.w_ref, ...), custom_call_target="tpu_custom_call", output_to_operand_aliasing={{0}: (4, {})} | custom-call | flops 2466250752 | bytes 12845056 | tf_op jit(solution)/shard_map/pallas_call | solution.py:754
  321.4 9.7 %shard_map.114 = (f32[8,140,8,128]{3,2,1,0:T(8,128)}, f32[8,98,8,128]{3,2,1,0:T(8,128)}) custom-call(bf16[256,768]{1,0:T(8,128)(2,1)} %constant.59.clone.i_ref.t_ref, f32[49,128,128]{2,1,0:T(8,128)} %shard_map.112.g_ref, f32[49,128,128]{2,1,0:T(8,128)} %get-tuple-element.94.refs_2_.w_ref, ...), custom_call_target="tpu_custom_call", output_to_operand_aliasing={{0}: (4, {}), {1}: (5, {})} | custom-call | flops 2466250752 | bytes 12845056 | tf_op jit(solution)/shard_map/pallas_call | solution.py:754
  331.1 8.8 %all-to-all-done.3.r0.refs_0_ = f32[8,28,16,128]{3,2,1,0:T(8,128)} async-done(((f32[8,28,16,128]{3,2,1,0:T(8,128)}), f32[8,28,16,128]{3,2,1,0:T(8,128)}, u32[]{:S(2)}, u32[]{:S(2)}) %all-to-all-start.3) | async-done | bytes 1835040 | tf_op jit(solution)/shard_map/all_to_all | solution.py:1328
  339.9 106.1 %all_to_all.26.refs_0_.refs_1_.refs_2_.r1.r2.refs_3_ = f32[8,140,8,128]{3,2,1,0:T(8,128)} all-to-all(f32[8,140,8,128]{3,2,1,0:T(8,128)} %get-tuple-element.109), channel_id=1, replica_groups=mesh['mode'=8,'elem'=4] {'mode'}, dimensions={0} | all-to-all | bytes 9175040 | tf_op jit(solution)/shard_map/all_to_all | solution.py:1328
  446.0 4.5 all-to-all-start.2
  450.5 10.0 %shard_map.115.s0 = f32[8,49,16,128]{3,2,1,0:T(8,128)} custom-call(f32[1568,128]{1,0:T(8,128)} %get-tuple-element.103.m_ref, f32[392,128]{1,0:T(8,128)} %reshape_reshape.4.q_ref, f32[16,128]{1,0:T(8,128)} %get-tuple-element.105.k_ref, f32[8,49,16,128]{3,2,1,0:T(8,128)} %get-tuple-element.106.s0, f32[8,77,16,128]{3,2,1,0:T(8,128)} %get-tuple-element.87.s1, ...), custom_call_target="tpu_custom_call" | custom-call | flops 48168960 | bytes 12845056 | tf_op jit(solution)/shard_map/pallas_call | solution.py:806
  460.5 8.1 %shard_map.116.f_ref = f32[8,49,16,128]{3,2,1,0:T(8,128)} custom-call(f32[1568,128]{1,0:T(8,128)} %get-tuple-element.102.m_ref, f32[8,49,16,128]{3,2,1,0:T(8,128)} %shard_map.115.s0, f32[8,28,16,128]{3,2,1,0:T(8,128)} %all-to-all-done.3.r0.refs_0_, f32[8,140,8,128]{3,2,1,0:T(8,128)} %all_to_all.26.refs_0_.refs_1_.refs_2_.r1.r2.refs_3_, ...), custom_call_target="tpu_custom_call" | custom-call | flops 24084480 | bytes 9633792 | tf_op jit(solution)/shard_map/pallas_call | solution.py:857
  468.6 2.3 copy-done
  470.9 1.9 copy-done.1
  475.6 2.9 shard_map.117
  478.6 1.7 collective-permute-start.8
  481.7 3.7 shard_map.118
  485.4 2.0 collective-permute-start.9
  488.9 2.2 collective-permute-done.11.far
  491.1 4.0 shard_map.119
  498.9 3.6 shard_map.120
  505.3 4.5 shard_map.122.refs_1_
  509.7 3.5 shard_map.123.refs_1_
  513.2 2.2 shard_map.121.refs_0_
  515.4 5.9 %all-to-all-done.2.refs_0_.r1.r2 = f32[8,98,8,128]{3,2,1,0:T(8,128)} async-done(((f32[8,98,8,128]{3,2,1,0:T(8,128)}), f32[8,98,8,128]{3,2,1,0:T(8,128)}, u32[]{:S(2)}, u32[]{:S(2)}) %all-to-all-start.2) | async-done | bytes 3211296 | tf_op jit(solution)/shard_map/all_to_all | solution.py:1328
  522.5 4.4 shard_map.126
  527.0 1.7 collective-permute-start.19
  530.1 3.7 shard_map.127
  536.9 2.1 collective-permute-done.22.far
  539.0 4.0 shard_map.128
  546.9 3.6 shard_map.129
  553.1 3.6 shard_map.124.refs_1_
  556.7 3.6 shard_map.125
  560.3 2.2 shard_map.130
  (129 shorter events, 40.4 us)
Async XLA Ops:
  6.2 2.1 copy-start.13
  22.8 2.7 copy-start.21
  22.8 2.7 copy-start.22
  22.8 2.7 copy-start.23
  22.8 3.4 copy-start.20
  22.8 4.1 copy-start.19
  147.0 122.9 %all-to-all-start.1 = ((f32[8,21,16,128]{3,2,1,0:T(8,128)}), f32[8,21,16,128]{3,2,1,0:T(8,128)}, u32[]{:S(2)}, u32[]{:S(2)}) async-start(f32[8,21,16,128]{3,2,1,0:T(8,128)} %get-tuple-element.89), calls=%async_computation.1 | async-start | bytes 2752512 | tf_op jit(solution)/shard_map/all_to_all | solution.py:1328
  156.5 32.0 %collective-permute-start = (f32[49,16,128]{2,1,0:T(8,128)}, f32[49,16,128]{2,1,0:T(8,128)}, u32[]{:S(2)}, u32[]{:S(2)}) collective-permute-start(f32[49,16,128]{2,1,0:T(8,128)} %get-tuple-element.79), channel_id=1, source_target_pairs={{0,4},{4,8},{8,12},{12,16},{16,20},{20,24},{24,28},{28,0},{1,5},{5... | collective-permute-start | bytes 1204232 | tf_op jit(solution)/shard_map/ppermute | solution.py:1337
  158.4 30.3 %collective-permute-start.1 = (f32[49,16,128]{2,1,0:T(8,128)}, f32[49,16,128]{2,1,0:T(8,128)}, u32[]{:S(2)}, u32[]{:S(2)}) collective-permute-start(f32[49,16,128]{2,1,0:T(8,128)} %get-tuple-element.80), channel_id=1, source_target_pairs={{0,8},{4,12},{8,16},{12,20},{16,24},{20,28},{24,0},{28,4},{1,9},{5... | collective-permute-start | bytes 1204232 | tf_op jit(solution)/shard_map/ppermute | solution.py:1337
  159.8 68.2 %collective-permute-start.2 = (f32[49,16,128]{2,1,0:T(8,128)}, f32[49,16,128]{2,1,0:T(8,128)}, u32[]{:S(2)}, u32[]{:S(2)}) collective-permute-start(f32[49,16,128]{2,1,0:T(8,128)} %get-tuple-element.81), channel_id=1, source_target_pairs={{0,12},{4,16},{8,20},{12,24},{16,28},{20,0},{24,4},{28,8},{1,13},{... | collective-permute-start | bytes 1204232 | tf_op jit(solution)/shard_map/ppermute | solution.py:1337
  162.2 66.3 %collective-permute-start.3 = (f32[49,16,128]{2,1,0:T(8,128)}, f32[49,16,128]{2,1,0:T(8,128)}, u32[]{:S(2)}, u32[]{:S(2)}) collective-permute-start(f32[49,16,128]{2,1,0:T(8,128)} %get-tuple-element.82), channel_id=1, source_target_pairs={{0,16},{4,20},{8,24},{12,28},{16,0},{20,4},{24,8},{28,12},{1,17},{... | collective-permute-start | bytes 1204232 | tf_op jit(solution)/shard_map/ppermute | solution.py:1337
  163.6 64.8 %collective-permute-start.4 = (f32[49,16,128]{2,1,0:T(8,128)}, f32[49,16,128]{2,1,0:T(8,128)}, u32[]{:S(2)}, u32[]{:S(2)}) collective-permute-start(f32[49,16,128]{2,1,0:T(8,128)} %get-tuple-element.83), channel_id=1, source_target_pairs={{0,20},{4,24},{8,28},{12,0},{16,4},{20,8},{24,12},{28,16},{1,21},{... | collective-permute-start | bytes 1204232 | tf_op jit(solution)/shard_map/ppermute | solution.py:1337
  188.5 40.0 %collective-permute-start.5 = (f32[49,16,128]{2,1,0:T(8,128)}, f32[49,16,128]{2,1,0:T(8,128)}, u32[]{:S(2)}, u32[]{:S(2)}) collective-permute-start(f32[49,16,128]{2,1,0:T(8,128)} %get-tuple-element.84), channel_id=1, source_target_pairs={{0,24},{4,28},{8,0},{12,4},{16,8},{20,12},{24,16},{28,20},{1,25},{... | collective-permute-start | bytes 1204232 | tf_op jit(solution)/shard_map/ppermute | solution.py:1337
  188.6 39.9 %collective-permute-start.6 = (f32[49,16,128]{2,1,0:T(8,128)}, f32[49,16,128]{2,1,0:T(8,128)}, u32[]{:S(2)}, u32[]{:S(2)}) collective-permute-start(f32[49,16,128]{2,1,0:T(8,128)} %get-tuple-element.85), channel_id=1, source_target_pairs={{0,28},{4,0},{8,4},{12,8},{16,12},{20,16},{24,20},{28,24},{1,29},{... | collective-permute-start | bytes 1204232 | tf_op jit(solution)/shard_map/ppermute | solution.py:1337
  269.9 70.0 %all-to-all-start.3 = ((f32[8,28,16,128]{3,2,1,0:T(8,128)}), f32[8,28,16,128]{3,2,1,0:T(8,128)}, u32[]{:S(2)}, u32[]{:S(2)}) async-start(f32[8,28,16,128]{3,2,1,0:T(8,128)} %get-tuple-element.108), calls=%async_computation.3 | async-start | bytes 3670016 | tf_op jit(solution)/shard_map/all_to_all | solution.py:1328
  446.0 75.3 %all-to-all-start.2 = ((f32[8,98,8,128]{3,2,1,0:T(8,128)}), f32[8,98,8,128]{3,2,1,0:T(8,128)}, u32[]{:S(2)}, u32[]{:S(2)}) async-start(f32[8,98,8,128]{3,2,1,0:T(8,128)} %get-tuple-element.101), calls=%async_computation.2 | async-start | bytes 6422528 | tf_op jit(solution)/shard_map/all_to_all | solution.py:1328
  468.6 2.3 copy-start
  475.6 6.1 %copy-start.3 = (f32[784,128]{1,0:T(8,128)S(1)}, f32[784,128]{1,0:T(8,128)}, u32[]{:S(2)}) copy-start(f32[784,128]{1,0:T(8,128)} %reshape.76.g_ref) | copy-start | bytes 1204228
  475.6 6.1 %copy-start.10 = (f32[2,8,128]{2,1,0:T(8,128)S(1)}, f32[2,8,128]{2,1,0:T(8,128)}, u32[]{:S(2)}) copy-start(f32[2,8,128]{2,1,0:T(8,128)} %broadcast_in_dim.50.k_ref) | copy-start | bytes 24580
  478.5 3.1 collective-permute-start.7
  478.6 3.1 collective-permute-start.8
  481.7 23.5 %slice-start = ((s8[4587520]{0:T(1024)(128)(4,1)}), s8[4194304]{0:T(1024)(128)(4,1)S(1)}, s32[]{:S(2)}) async-start(s8[4587520]{0:T(1024)(128)(4,1)} %bitcast.43), calls=%async_computation.5 | async-start | bytes 8388608
  485.4 3.5 collective-permute-start.9
  487.4 3.7 collective-permute-start.11
  488.0 3.1 collective-permute-start.10
  491.1 14.2 %slice-start.1 = ((s8[4587520]{0:T(1024)(128)(4,1)}), s8[393216]{0:T(1024)(128)(4,1)S(1)}, s32[]{:S(2)}) async-start(s8[4587520]{0:T(1024)(128)(4,1)} %bitcast.43), calls=%async_computation.6 | async-start | bytes 786432
  495.1 3.1 collective-permute-start.12
  495.3 3.7 collective-permute-start.14
  496.4 2.5 collective-permute-start.13
  502.6 10.6 %collective-permute-start.17 = (f32[2,8,128]{2,1,0:T(8,128)S(1)}, f32[2,8,128]{2,1,0:T(8,128)S(1)}, u32[]{:S(2)}, u32[]{:S(2)}) collective-permute-start(f32[2,8,128]{2,1,0:T(8,128)S(1)} %get-tuple-element.127.own), channel_id=1, source_target_pairs={{0,2},{1,3},{2,0},{3,1},{4,6},{5,7},{6,4},{7,5},{8,10},{9,11},{10,... | collective-permute-start | bytes 24584 | tf_op jit(solution)/shard_map/ppermute | solution.py:1006
  503.8 9.4 %collective-permute-start.16 = (f32[2,8,128]{2,1,0:T(8,128)S(1)}, f32[2,8,128]{2,1,0:T(8,128)S(1)}, u32[]{:S(2)}, u32[]{:S(2)}) collective-permute-start(f32[2,8,128]{2,1,0:T(8,128)S(1)} %get-tuple-element.127.own), channel_id=1, source_target_pairs={{1,0},{2,1},{3,2},{0,3},{5,4},{6,5},{7,6},{4,7},{9,8},{10,9},{11,1... | collective-permute-start | bytes 24584 | tf_op jit(solution)/shard_map/ppermute | solution.py:1001
  505.2 8.0 %collective-permute-start.15 = (f32[2,8,128]{2,1,0:T(8,128)S(1)}, f32[2,8,128]{2,1,0:T(8,128)S(1)}, u32[]{:S(2)}, u32[]{:S(2)}) collective-permute-start(f32[2,8,128]{2,1,0:T(8,128)S(1)} %get-tuple-element.127.own), channel_id=1, source_target_pairs={{0,1},{1,2},{2,3},{3,0},{4,5},{5,6},{6,7},{7,4},{8,9},{9,10},{10,1... | collective-permute-start | bytes 24584 | tf_op jit(solution)/shard_map/ppermute | solution.py:1001
  513.2 8.1 %copy-start.2 = (f32[8,49,16,128]{3,2,1,0:T(8,128)S(1)}, f32[8,49,16,128]{3,2,1,0:T(8,128)}, u32[]{:S(2)}) copy-start(f32[8,49,16,128]{3,2,1,0:T(8,128)} %shard_map.116.f_ref) | copy-start | bytes 9633796
  513.2 8.1 %copy-start.8 = (f32[392,128]{1,0:T(8,128)S(1)}, f32[392,128]{1,0:T(8,128)}, u32[]{:S(2)}) copy-start(f32[392,128]{1,0:T(8,128)} %reshape_reshape.4.q_ref) | copy-start | bytes 602116
  513.2 8.1 %copy-start.12 = (f32[16,128]{1,0:T(8,128)S(1)}, f32[16,128]{1,0:T(8,128)}, u32[]{:S(2)}) copy-start(f32[16,128]{1,0:T(8,128)} %get-tuple-element.112.k_ref) | copy-start | bytes 24580
  522.5 7.6 %copy-start.4 = (f32[784,128]{1,0:T(8,128)S(1)}, f32[784,128]{1,0:T(8,128)}, u32[]{:S(2)}) copy-start(f32[784,128]{1,0:T(8,128)} %reshape.76.g_ref) | copy-start | bytes 1204228
  522.5 7.6 %copy-start.9 = (f32[2,8,128]{2,1,0:T(8,128)S(1)}, f32[2,8,128]{2,1,0:T(8,128)}, u32[]{:S(2)}) copy-start(f32[2,8,128]{2,1,0:T(8,128)} %broadcast_in_dim.52.k_ref) | copy-start | bytes 24580
  526.9 3.1 collective-permute-start.18
  527.0 3.1 collective-permute-start.19
  533.8 3.1 collective-permute-start.20
  535.4 3.7 collective-permute-start.22
  535.9 3.1 collective-permute-start.21
  543.1 3.1 collective-permute-start.23
  543.2 3.7 collective-permute-start.25
  544.4 2.5 collective-permute-start.24
  550.5 9.8 %collective-permute-start.28 = (f32[2,8,128]{2,1,0:T(8,128)S(1)}, f32[2,8,128]{2,1,0:T(8,128)S(1)}, u32[]{:S(2)}, u32[]{:S(2)}) collective-permute-start(f32[2,8,128]{2,1,0:T(8,128)S(1)} %get-tuple-element.147.own), channel_id=1, source_target_pairs={{0,2},{1,3},{2,0},{3,1},{4,6},{5,7},{6,4},{7,5},{8,10},{9,11},{10,... | collective-permute-start | bytes 24584 | tf_op jit(solution)/shard_map/ppermute | solution.py:1006
  551.7 8.6 %collective-permute-start.27 = (f32[2,8,128]{2,1,0:T(8,128)S(1)}, f32[2,8,128]{2,1,0:T(8,128)S(1)}, u32[]{:S(2)}, u32[]{:S(2)}) collective-permute-start(f32[2,8,128]{2,1,0:T(8,128)S(1)} %get-tuple-element.147.own), channel_id=1, source_target_pairs={{1,0},{2,1},{3,2},{0,3},{5,4},{6,5},{7,6},{4,7},{9,8},{10,9},{11,1... | collective-permute-start | bytes 24584 | tf_op jit(solution)/shard_map/ppermute | solution.py:1001
  553.1 7.2 %collective-permute-start.26 = (f32[2,8,128]{2,1,0:T(8,128)S(1)}, f32[2,8,128]{2,1,0:T(8,128)S(1)}, u32[]{:S(2)}, u32[]{:S(2)}) collective-permute-start(f32[2,8,128]{2,1,0:T(8,128)S(1)} %get-tuple-element.147.own), channel_id=1, source_target_pairs={{0,1},{1,2},{2,3},{3,0},{4,5},{5,6},{6,7},{7,4},{8,9},{9,10},{10,1... | collective-permute-start | bytes 24584 | tf_op jit(solution)/shard_map/ppermute | solution.py:1001
  (10 other events, 16.0 us)

commit v8 on v7

--- a/solution.py
+++ b/solution.py
@@ -603,7 +603,8 @@
     shape = jax.ShapeDtypeStruct((square, rows, lanes), jnp.float32)
 
     def body(t_ref, i_ref, x_ref, g_ref, s_ref, *refs):
-        w_ref, z_ref, o_ref, rhs_ref = refs[-4:]
+        w_ref, z_ref = refs[len(fields) : len(fields) + 2]
+        outs, rhs_ref = (refs[len(fields) + 2 : -1], refs[-1])
         points = three_pass(t_ref[...], rhs_ref, read_tiles(x_ref, rows, lanes))
         for b in range(NODES):
             w_ref[b] = points[0][b]
@@ -613,19 +614,20 @@
         for b in range(NODES):
             value = spectral[b].reshape(shares, pairs, lanes)
             if out is None:
-                o_ref[:, b] = value
+                outs[0][:, b] = value
             else:
-                for g in range(2):
-                    o_ref[:, g * NODES + b] = value[:, g * group : (g + 1) * group]
+                for k in range(shares):
+                    for g in range(2):
+                        outs[k][g * NODES + b] = value[k, g * group : (g + 1) * group]
 
     spec = pl.BlockSpec((NODES, rows, lanes), lambda a: (start + a, 0, 0))
     if out is None:
-        out_spec = pl.BlockSpec((shares, NODES, pairs, lanes), lambda a: (0, a, 0, 0))
-        out_shape = jax.ShapeDtypeStruct((shares, count * NODES, pairs, lanes), jnp.float32)
+        out_spec = [pl.BlockSpec((shares, NODES, pairs, lanes), lambda a: (0, a, 0, 0))]
+        out_shape = [jax.ShapeDtypeStruct((shares, count * NODES, pairs, lanes), jnp.float32)]
     else:
         first = out[1]
-        out_spec = pl.BlockSpec((shares, 2 * NODES, group, lanes), lambda a: (0, first + a, 0, 0))
-        out_shape = jax.ShapeDtypeStruct(out[0], jnp.float32)
+        out_spec = [pl.BlockSpec((2 * NODES, group, lanes), lambda a: (first + a, 0, 0))] * shares
+        out_shape = [jax.ShapeDtypeStruct(out[0], jnp.float32)] * shares
     return call(
         body,
         (count,),
@@ -637,8 +639,8 @@
             spec,
         ]
         + [pl.BlockSpec(memory_space=pl.ANY)] * len(fields),
-        [spec, spec, out_spec],
-        [shape, shape, out_shape],
+        [spec, spec] + out_spec,
+        [shape, shape] + out_shape,
         scratch=[rhs_scratch(table, lanes)],
         flops=3 * table.shape[0] * table.shape[1] * count * NODES * lanes,
         aliases={5: 0, 6: 1} if fields else None,
@@ -710,60 +712,62 @@
 
 def by_source(strips, place):
     count = len(strips)
-    nodes = strips[0].shape[0]
+    nodes, rows, lanes = strips[0].shape
+    step = 2 * NODES if nodes % (2 * NODES) == 0 else NODES
 
     def body(place_ref, *refs):
         o_ref = refs[-1]
         here = place_ref[0]
-
-        def node(n, carry):
-            for k in range(count):
-                o_ref[lax.rem(here - k + count, count), n] = refs[k][n]
-            return carry
-
-        lax.fori_loop(0, nodes, node, 0)
+        for k in range(count):
+            source = lax.rem(here - k + count, count)
+            for n in range(step):
+                o_ref[source, n] = refs[k][n]
 
     return call(
         body,
-        (1,),
-        [pl.BlockSpec(memory_space=pltpu.SMEM)] + [whole(strips[0].shape)] * count,
-        whole((count,) + strips[0].shape),
+        (nodes // step,),
+        [pl.BlockSpec(memory_space=pltpu.SMEM)]
+        + [pl.BlockSpec((step, rows, lanes), lambda i: (i, 0, 0))] * count,
+        pl.BlockSpec((count, step, rows, lanes), lambda i: (0, i, 0, 0)),
         jax.ShapeDtypeStruct((count,) + strips[0].shape, jnp.float32),
         grant=WHOLE_GRANT,
         moved=8 * count * strips[0].size,
     )(jnp.full((1,), place, jnp.int32), *strips)
 
 
-def to_planes(partial, speed_z, slope_z, table, shares, place, shapes, buffers):
+def to_planes(partial, speed_z, slope_z, table, place, comp, shapes, buffers):
     square, rows, lanes = partial.shape
+    shares = shapes[1][0]
     pairs = rows // shares
     group = pairs // 2
 
-    def body(t_ref, g_ref, w_ref, z_ref, *refs):
-        outs, rhs_ref = (refs[-3:-1], refs[-1])
+    def body(place_ref, t_ref, g_ref, w_ref, z_ref, *refs):
+        strips, o_ref, rhs_ref = (refs[-shares - 2 : -2], refs[-2], refs[-1])
+        here = place_ref[0]
         tiles = [g_ref[b] + w_ref[b] * z_ref[b] for b in range(NODES)]
         nodes = three_pass(t_ref[...], rhs_ref, tiles)[0]
         for b in range(NODES):
             out = nodes[b].reshape(shares, pairs, lanes)
-            for i in range(2):
-                outs[i][:, b] = out[:, i * group : (i + 1) * group]
+            for k in range(shares):
+                strips[k][b] = out[k, :group]
+                o_ref[lax.rem(here + k, shares), b] = out[k, group:]
 
     spec = pl.BlockSpec((NODES, rows, lanes), lambda a: (a, 0, 0))
-    out_spec = pl.BlockSpec((shares, NODES, group, lanes), lambda a: (0, place * NODES + a, 0, 0))
-    shapes = [jax.ShapeDtypeStruct(shape, jnp.float32) for shape in shapes]
     return call(
         body,
         (NODES,),
-        [whole(table.shape), spec, spec, spec]
+        [pl.BlockSpec(memory_space=pltpu.SMEM), whole(table.shape), spec, spec, spec]
         + [pl.BlockSpec(memory_space=pl.ANY)] * len(buffers),
-        [out_spec, out_spec],
-        shapes,
+        [pl.BlockSpec((NODES, group, lanes), lambda a: (comp * NODES + a, 0, 0))] * shares
+        + [pl.BlockSpec((shares, NODES, group, lanes), lambda a: (0, comp * NODES + a, 0, 0))],
+        [jax.ShapeDtypeStruct(shapes[0], jnp.float32)] * shares
+        + [jax.ShapeDtypeStruct(shapes[1], jnp.float32)],
         scratch=[rhs_scratch(table, lanes)],
         flops=2 * table.shape[0] * table.shape[1] * square * lanes,
+        aliases={5 + k: k for k in range(len(buffers))},
         grant=WHOLE_GRANT,
         moved=4 * square * rows * lanes * 4,
-        aliases={4 + k: k for k in range(len(buffers))},
-    )(table, partial, speed_z, slope_z, *buffers)
+    )(jnp.full((1,), place, jnp.int32), table, partial, speed_z, slope_z, *buffers)
 
 
 def velocity_part(sent, metrics, weights, waves, table):
@@ -1315,6 +1319,8 @@
     flux = (both * scaled).reshape(4 * modes * square, lanes)
     small_flux = flux * time_step
     scaled = scaled.reshape(modes * square, lanes)
+    turned = lax.optimization_barrier(backward).reshape(2, modes, pairs, -1)
+    turned = jnp.roll(turned, -mode, axis=1).reshape(backward.shape)
     pair = (first_plane // 2 + jnp.arange(pairs, dtype=jnp.int32)).astype(jnp.float32)
     wave = pair[:, None] * spanwise_wave
     low = (jnp.arange(lanes) < lanes // 2)[None, :]
@@ -1329,15 +1335,15 @@
 
     some = (NODES // 2 + 1) * NODES
     group = pairs // 2
-    first_shape = (modes, 4 * square - 2 * some, group, lanes)
+    first_shape = (4 * square - 2 * some, group, lanes)
     second_shape = (modes, 2 * square, group, lanes)
     strips = list(pack_first(rows, mode, layers, pairs, lanes))
     sent_1, late_2, sent_2, sent_0 = pack_rest(rows, layers, pairs, lanes, some)
     for k in range(1, modes):
         strips[k] = lax.ppermute(strips[k], "mode", [(i, (i + k) % modes) for i in range(modes)])
-    sent_1, here, geo, flux, small_flux, scaled, waves, small_waves, shift = (
+    sent_1, here, geo, flux, small_flux, scaled, waves, small_waves, shift, turned = (
         lax.optimization_barrier(
-            (sent_1, here, geo, flux, small_flux, scaled, waves, small_waves, shift)
+            (sent_1, here, geo, flux, small_flux, scaled, waves, small_waves, shift, turned)
         )
     )
     arrived_1 = exchange(sent_1)
@@ -1351,7 +1357,7 @@
         arrived_1, NODES, 0, rows_early, partial[0], slope_0, forward, backward, (), None
     )
     home_0 = exchange(blocks)
-    speed_z, slope_2, first_buffer = turn_around(
+    speed_z, slope_2, *buffers = turn_around(
         arrived_2,
         0,
         rows_early,
@@ -1359,16 +1365,20 @@
         partial[0],
         slope_0,
         forward,
-        backward,
+        turned,
         (speed_z, slope_2),
         (first_shape, NODES),
     )
     last = in_plane(speeds, [speed_z], here, table)[0]
     shapes = (first_shape, second_shape)
-    blocks = to_planes(partial[1], speed_z, slope_1, backward, modes, 0, shapes, (first_buffer,))
-    blocks = to_planes(last, speed_z, slope_2, backward, modes, 1, shapes, blocks)
-    home_1 = exchange(blocks[0])
-    home_2 = exchange(blocks[1])
+    buffers = to_planes(partial[1], speed_z, slope_1, turned, mode, 0, shapes, buffers)
+    *home_strips, second = to_planes(last, speed_z, slope_2, turned, mode, 1, shapes, buffers)
+    for k in range(1, modes):
+        home_strips[k] = lax.ppermute(
+            home_strips[k], "mode", [(i, (i + k) % modes) for i in range(modes)]
+        )
+    home_1 = by_source(home_strips, mode)
+    home_2 = exchange(second)
     returned = (home_1, home_2)
     base = velocity_part((sent_0, sent_1, sent_2), flux, scaled, waves, table)
 

time: 565 us -> 622 us (1.10)
  the two profiles are of different devices: /device:TPU:0 before, /device:TPU:9 now
where the time goes in v8:
time: 622 us; the launch traced here: 619 us
  waiting for transfers between devices  255 us (41%)
  Pallas kernels  168 us (27%)
  blocking collectives  116 us (19%)
  starting transfers between devices  53.1 us (9%)
  local copies, waits for them, and re-layouts  19.1 us (3%)
  other arithmetic  7.14 us (1%)
    ppermute x7, waiting for transfers between devices, paired_step(): lax.ppermute(home_strips[k], 'mode', [(i, (i + k) % modes) for i in range...  150 us
    all_to_all x1, blocking collectives, exchange(): lax.all_to_all(blocks, 'mode', split_axis=0, concat_axis=0, tiled=True)  116 us
    ppermute x7, waiting for transfers between devices, paired_step(): lax.ppermute(strips[k], 'mode', [(i, (i + k) % modes) for i in range(mode...  81.3 us
    pallas_call x2, Pallas kernels, to_points(): call(body, (NODES,), [whole(table.shape), pl.BlockSpec((shares, NODES, pa...  19.7 us
    pallas_call x2, Pallas kernels, to_planes(): call(body, (NODES,), [pl.BlockSpec(memory_space=pltpu.SMEM), whole(table....  19.4 us
    pallas_call x2, Pallas kernels, in_plane(): call(body, (rows // step,), [whole(metrics.shape)] + [spec] * len(arrays)...  15.9 us
    pallas_call x2, Pallas kernels, turn_around(): call(body, (count,), [whole(table.shape), whole(back.shape), pl.BlockSpec...  15.7 us
    all_to_all x3, starting transfers between devices, exchange(): lax.all_to_all(blocks, 'mode', split_axis=0, concat_axis=0, tiled=True)  15.4 us
  transfers between devices with their start and end apart: 39, of which 27 were waited for; matrix products, arithmetic and copies ran while one was open for 0% of the time, Pallas kernels for 22%

profile of v8, /device:TPU:9, one launch (start us, length us, event | category | flops | bytes accessed | tf_op | source)
XLA Modules:
  0.0 619.3 jit_solution(14081479481648387359)
XLA Ops:
  11.5 11.4 %shard_map.104 = (f32[8,77,16,128]{3,2,1,0:T(8,128)}, f32[8,21,16,128]{3,2,1,0:T(8,128)}, f32[8,49,16,128]{3,2,1,0:T(8,128)}, f32[8,49,16,128]{3,2,1,0:T(8,128)}) custom-call(f32[3,6272,128]{2,1,0:T(8,128)} %bitcast.47, f32[3,6272,128]{2,1,0:T(8,128)} %bitcast.48, f32[3,6272,128]{2,1,0:T(8,128)} %bitcast.49), custom_call_target="tpu_custom_call" | custom-call | bytes 16056320 | tf_op jit(solution)/shard_map/pallas_call | solution.py:469
  24.8 2.6 broadcast_multiply_fusion
  29.5 116.0 %all_to_all.20.x_ref = f32[8,77,16,128]{3,2,1,0:T(8,128)} all-to-all(f32[8,77,16,128]{3,2,1,0:T(8,128)} %get-tuple-element.110.s1), channel_id=1, replica_groups=mesh['mode'=8,'elem'=4] {'mode'}, dimensions={0} | all-to-all | bytes 10092544 | tf_op jit(solution)/shard_map/all_to_all | solution.py:1334
  145.5 5.1 all-to-all-start.1
  150.6 5.1 shard_map.105
  162.5 19.3 %collective-permute-done.refs_1_ = f32[49,16,128]{2,1,0:T(8,128)} collective-permute-done((f32[49,16,128]{2,1,0:T(8,128)}, f32[49,16,128]{2,1,0:T(8,128)}, u32[]{:S(2)}, u32[]{:S(2)}) %collective-permute-start) | collective-permute-done | bytes 401440 | tf_op jit(solution)/shard_map/ppermute | solution.py:1343
  181.8 3.0 collective-permute-start.5
  184.8 3.9 collective-permute-done.1.refs_2_
  188.7 4.7 collective-permute-start.6
  193.4 38.4 %collective-permute-done.2.refs_3_ = f32[49,16,128]{2,1,0:T(8,128)} collective-permute-done((f32[49,16,128]{2,1,0:T(8,128)}, f32[49,16,128]{2,1,0:T(8,128)}, u32[]{:S(2)}, u32[]{:S(2)}) %collective-permute-start.2) | collective-permute-done | bytes 401440 | tf_op jit(solution)/shard_map/ppermute | solution.py:1343
  231.8 8.6 %collective-permute-done.3.refs_4_ = f32[49,16,128]{2,1,0:T(8,128)} collective-permute-done((f32[49,16,128]{2,1,0:T(8,128)}, f32[49,16,128]{2,1,0:T(8,128)}, u32[]{:S(2)}, u32[]{:S(2)}) %collective-permute-start.3) | collective-permute-done | bytes 401440 | tf_op jit(solution)/shard_map/ppermute | solution.py:1343
  240.4 8.6 %collective-permute-done.4.refs_5_ = f32[49,16,128]{2,1,0:T(8,128)} collective-permute-done((f32[49,16,128]{2,1,0:T(8,128)}, f32[49,16,128]{2,1,0:T(8,128)}, u32[]{:S(2)}, u32[]{:S(2)}) %collective-permute-start.4) | collective-permute-done | bytes 401440 | tf_op jit(solution)/shard_map/ppermute | solution.py:1343
  249.0 2.5 collective-permute-done.6.refs_7_
  251.6 5.7 shard_map.106.x_ref
  257.3 9.9 %shard_map.107 = (f32[49,128,128]{2,1,0:T(8,128)}, f32[49,128,128]{2,1,0:T(8,128)}) custom-call(bf16[512,768]{1,0:T(8,128)(2,1)} %constant.78.clone.t_ref, f32[8,49,16,128]{3,2,1,0:T(8,128)} %shard_map.106.x_ref), custom_call_target="tpu_custom_call" | custom-call | flops 4932501504 | bytes 9633792 | tf_op jit(solution)/shard_map/pallas_call | solution.py:582
  267.2 9.8 %shard_map.108 = (f32[49,128,128]{2,1,0:T(8,128)}, f32[49,128,128]{2,1,0:T(8,128)}) custom-call(bf16[512,768]{1,0:T(8,128)(2,1)} %constant.78.clone.t_ref, f32[8,77,16,128]{3,2,1,0:T(8,128)} %all_to_all.20.x_ref), custom_call_target="tpu_custom_call" | custom-call | flops 4932501504 | bytes 9633792 | tf_op jit(solution)/shard_map/pallas_call | solution.py:582
  277.0 8.4 %shard_map.109 = (f32[49,128,128]{2,1,0:T(8,128)}, f32[49,128,128]{2,1,0:T(8,128)}) custom-call(f32[196,128]{1,0:T(8,128)} %reshape.81.m_ref, f32[49,128,128]{2,1,0:T(8,128)} %get-tuple-element.109.refs_0_, f32[49,128,128]{2,1,0:T(8,128)} %get-tuple-element.111.refs_1_), custom_call_target="tpu_custom_call" | custom-call | flops 48168960 | bytes 12845056 | tf_op jit(solution)/shard_map/pallas_call | solution.py:701
  285.4 8.4 %shard_map.110 = (f32[49,128,128]{2,1,0:T(8,128)}, f32[49,128,128]{2,1,0:T(8,128)}, f32[8,28,16,128]{3,2,1,0:T(8,128)}) custom-call(bf16[512,768]{1,0:T(8,128)(2,1)} %constant.78.clone.t_ref, bf16[256,768]{1,0:T(8,128)(2,1)} %constant.79.clone.i_ref, f32[8,77,16,128]{3,2,1,0:T(8,128)} %all_to_all.20.x_ref, f32[49,128,128]{2,1,0:T(8,128)} %get-tuple-element.113.g_ref, ...), custom_call_target="tpu_custom_call" | custom-call | flops 4227858432 | bytes 11010048 | tf_op jit(solution)/shard_map/pallas_call | solution.py:631
  293.8 4.6 all-to-all-start.3
  298.4 7.3 %shard_map.111 = (f32[49,128,128]{2,1,0:T(8,128)}, f32[49,128,128]{2,1,0:T(8,128)}, f32[140,8,128]{2,1,0:T(8,128)}, f32[140,8,128]{2,1,0:T(8,128)}, f32[140,8,12...) custom-call(bf16[512,768]{1,0:T(8,128)(2,1)} %constant.78.clone.t_re, ...), custom_call_target="tpu_custom_call", output_to_operand_aliasing={{0}: (5, {}), {1}: (6, {})} | custom-call | flops 3170893824 | bytes 8257536 | tf_op jit(solution)/shard_map/pallas_call | solution.py:631
  305.7 7.5 %shard_map.112.g_ref = f32[49,128,128]{2,1,0:T(8,128)} custom-call(f32[196,128]{1,0:T(8,128)} %reshape.81.m_ref, f32[49,128,128]{2,1,0:T(8,128)} %get-tuple-element.109.refs_0_, f32[49,128,128]{2,1,0:T(8,128)} %get-tuple-element.111.refs_1_, f32[49,128,128]{2,1,0:T(8,128)} %get-tuple-element.117.refs_2_.w_ref), custom_call_target="tpu_custom_call" | custom-call | flops 24084480 | bytes 12845056 | tf_op jit(solution)/shard_map/pallas_call | solution.py:701
  313.2 9.7 %shard_map.113 = (f32[140,8,128]{2,1,0:T(8,128)}, f32[140,8,128]{2,1,0:T(8,128)}, f32[140,8,128]{2,1,0:T(8,128)}, f32[140,8,128]{2,1,0:T(8,128)}, f32[140,8,128]...) custom-call(s32[1]{0:T(128)} %bitcast.place_ref, ...), custom_call_target="tpu_custom_call", output_to_operand_aliasing={{0}: (5, {}), {1}: (6, {}), {2}: (7, {}), {3}: (8, {}), {4}... | custom-call | flops 2466250752 | bytes 12845056 | tf_op jit(solution)/shard_map/pallas_call | solution.py:756
  322.9 9.7 %shard_map.114 = (f32[140,8,128]{2,1,0:T(8,128)}, f32[140,8,128]{2,1,0:T(8,128)}, f32[140,8,128]{2,1,0:T(8,128)}, f32[140,8,128]{2,1,0:T(8,128)}, f32[140,8,128]...) custom-call(s32[1]{0:T(128)} %bitcast.place_ref, ...), custom_call_target="tpu_custom_call", output_to_operand_aliasing={{0}: (5, {}), {1}: (6, {}), {2}: (7, {}), {3}: (8, {}), {4}... | custom-call | flops 2466250752 | bytes 12845056 | tf_op jit(solution)/shard_map/pallas_call | solution.py:756
  332.6 6.6 %all-to-all-done.3.r0.refs_0_ = f32[8,28,16,128]{3,2,1,0:T(8,128)} async-done(((f32[8,28,16,128]{3,2,1,0:T(8,128)}), f32[8,28,16,128]{3,2,1,0:T(8,128)}, u32[]{:S(2)}, u32[]{:S(2)}) %all-to-all-start.3) | async-done | bytes 1835040 | tf_op jit(solution)/shard_map/all_to_all | solution.py:1334
  339.3 5.8 all-to-all-start.2
  348.4 2.3 collective-permute-start.10
  351.9 58.6 %collective-permute-done.7.refs_1_ = f32[140,8,128]{2,1,0:T(8,128)S(1)} collective-permute-done((f32[140,8,128]{2,1,0:T(8,128)S(1)}, f32[140,8,128]{2,1,0:T(8,128)S(1)}, u32[]{:S(2)}, u32[]{:S(2)}) %collective-permute-start.7) | collective-permute-done | bytes 573472 | tf_op jit(solution)/shard_map/ppermute | solution.py:1377
  410.4 2.4 collective-permute-start.12
  412.8 64.0 %collective-permute-done.8.refs_2_ = f32[140,8,128]{2,1,0:T(8,128)S(1)} collective-permute-done((f32[140,8,128]{2,1,0:T(8,128)S(1)}, f32[140,8,128]{2,1,0:T(8,128)S(1)}, u32[]{:S(2)}, u32[]{:S(2)}) %collective-permute-start.8) | collective-permute-done | bytes 573472 | tf_op jit(solution)/shard_map/ppermute | solution.py:1377
  477.7 10.0 %shard_map.115.s0 = f32[8,49,16,128]{3,2,1,0:T(8,128)} custom-call(f32[1568,128]{1,0:T(8,128)} %get-tuple-element.140.m_ref, f32[392,128]{1,0:T(8,128)} %reshape_reshape.4.q_ref, f32[16,128]{1,0:T(8,128)} %get-tuple-element.142.k_ref, f32[8,49,16,128]{3,2,1,0:T(8,128)} %get-tuple-element.143.s0, f32[8,77,16,128]{3,2,1,0:T(8,128)} %get-tuple-element.110.s1, ...), custom_call_target="tpu_custom_call" | custom-call | flops 48168960 | bytes 12845056 | tf_op jit(solution)/shard_map/pallas_call | solution.py:810
  489.2 12.3 %collective-permute-done.10.refs_4_ = f32[140,8,128]{2,1,0:T(8,128)} collective-permute-done((f32[140,8,128]{2,1,0:T(8,128)}, f32[140,8,128]{2,1,0:T(8,128)}, u32[]{:S(2)}, u32[]{:S(2)}) %collective-permute-start.10) | collective-permute-done | bytes 573472 | tf_op jit(solution)/shard_map/ppermute | solution.py:1377
  501.5 12.3 %collective-permute-done.11.refs_5_ = f32[140,8,128]{2,1,0:T(8,128)} collective-permute-done((f32[140,8,128]{2,1,0:T(8,128)}, f32[140,8,128]{2,1,0:T(8,128)}, u32[]{:S(2)}, u32[]{:S(2)}) %collective-permute-start.11) | collective-permute-done | bytes 573472 | tf_op jit(solution)/shard_map/ppermute | solution.py:1377
  515.4 7.5 %shard_map.116.refs_0_.refs_1_.refs_2_.r1.r2.refs_3_ = f32[8,140,8,128]{3,2,1,0:T(8,128)} custom-call(s32[1]{0:T(128)} %bitcast.place_ref, f32[140,8,128]{2,1,0:T(8,128)} %get-tuple-element.146.refs_0_, f32[140,8,128]{2,1,0:T(8,128)} %copy-done.15, f32[140,8,128]{2,1,0:T(8,128)} %copy-done.16, f32[140,8,128]{2,1,0:T(8,128)} %collective-permute-done.9.refs_3_, ...), custom_call_target="tpu_custom_call" | custom-call | bytes 9175040 | tf_op jit(solution)/shard_map/pallas_call | solution.py:726
  522.9 8.1 %shard_map.117.f_ref = f32[8,49,16,128]{3,2,1,0:T(8,128)} custom-call(f32[1568,128]{1,0:T(8,128)} %get-tuple-element.139.m_ref, f32[8,49,16,128]{3,2,1,0:T(8,128)} %shard_map.115.s0, f32[8,28,16,128]{3,2,1,0:T(8,128)} %all-to-all-done.3.r0.refs_0_, f32[8,140,8,128]{3,2,1,0:T(8,128)} %shard_map.116.refs_0_.refs_1_.refs_2_.r1.r2.refs_3_, ...), custom_call_target="tpu_custom_call" | custom-call | flops 24084480 | bytes 9633792 | tf_op jit(solution)/shard_map/pallas_call | solution.py:861
  531.0 2.3 copy-done
  537.9 2.9 shard_map.118
  543.5 2.3 collective-permute-done.15.a_ref
  545.8 3.7 shard_map.119
  553.3 4.0 shard_map.120
  562.2 3.6 shard_map.121
  568.0 4.4 shard_map.123.refs_1_
  572.4 3.5 shard_map.124.refs_1_
  579.3 4.4 shard_map.127
  586.9 3.7 shard_map.128
  595.0 4.0 shard_map.129
  603.3 3.6 shard_map.130
  609.9 3.6 shard_map.125.refs_1_
  613.5 3.6 shard_map.126
  (152 shorter events, 68.3 us)
Async XLA Ops:
  22.9 5.9 copy-start.23
  145.5 148.3 %all-to-all-start.1 = ((f32[8,21,16,128]{3,2,1,0:T(8,128)}), f32[8,21,16,128]{3,2,1,0:T(8,128)}, u32[]{:S(2)}, u32[]{:S(2)}) async-start(f32[8,21,16,128]{3,2,1,0:T(8,128)} %get-tuple-element.112), calls=%async_computation.1 | async-start | bytes 2752512 | tf_op jit(solution)/shard_map/all_to_all | solution.py:1334
  155.7 26.1 %collective-permute-start = (f32[49,16,128]{2,1,0:T(8,128)}, f32[49,16,128]{2,1,0:T(8,128)}, u32[]{:S(2)}, u32[]{:S(2)}) collective-permute-start(f32[49,16,128]{2,1,0:T(8,128)} %get-tuple-element.102), channel_id=1, source_target_pairs={{0,4},{4,8},{8,12},{12,16},{16,20},{20,24},{24,28},{28,0},{1,5},{5... | collective-permute-start | bytes 1204232 | tf_op jit(solution)/shard_map/ppermute | solution.py:1343
  156.9 31.8 %collective-permute-start.1 = (f32[49,16,128]{2,1,0:T(8,128)}, f32[49,16,128]{2,1,0:T(8,128)}, u32[]{:S(2)}, u32[]{:S(2)}) collective-permute-start(f32[49,16,128]{2,1,0:T(8,128)} %get-tuple-element.103), channel_id=1, source_target_pairs={{0,8},{4,12},{8,16},{12,20},{16,24},{20,28},{24,0},{28,4},{1,9},{5... | collective-permute-start | bytes 1204232 | tf_op jit(solution)/shard_map/ppermute | solution.py:1343
  158.1 73.7 %collective-permute-start.2 = (f32[49,16,128]{2,1,0:T(8,128)}, f32[49,16,128]{2,1,0:T(8,128)}, u32[]{:S(2)}, u32[]{:S(2)}) collective-permute-start(f32[49,16,128]{2,1,0:T(8,128)} %get-tuple-element.104), channel_id=1, source_target_pairs={{0,12},{4,16},{8,20},{12,24},{16,28},{20,0},{24,4},{28,8},{1,13},{... | collective-permute-start | bytes 1204232 | tf_op jit(solution)/shard_map/ppermute | solution.py:1343
  159.1 81.3 %collective-permute-start.3 = (f32[49,16,128]{2,1,0:T(8,128)}, f32[49,16,128]{2,1,0:T(8,128)}, u32[]{:S(2)}, u32[]{:S(2)}) collective-permute-start(f32[49,16,128]{2,1,0:T(8,128)} %get-tuple-element.105), channel_id=1, source_target_pairs={{0,16},{4,20},{8,24},{12,28},{16,0},{20,4},{24,8},{28,12},{1,17},{... | collective-permute-start | bytes 1204232 | tf_op jit(solution)/shard_map/ppermute | solution.py:1343
  161.4 87.7 %collective-permute-start.4 = (f32[49,16,128]{2,1,0:T(8,128)}, f32[49,16,128]{2,1,0:T(8,128)}, u32[]{:S(2)}, u32[]{:S(2)}) collective-permute-start(f32[49,16,128]{2,1,0:T(8,128)} %get-tuple-element.106), channel_id=1, source_target_pairs={{0,20},{4,24},{8,28},{12,0},{16,4},{20,8},{24,12},{28,16},{1,21},{... | collective-permute-start | bytes 1204232 | tf_op jit(solution)/shard_map/ppermute | solution.py:1343
  181.8 67.3 %collective-permute-start.5 = (f32[49,16,128]{2,1,0:T(8,128)}, f32[49,16,128]{2,1,0:T(8,128)}, u32[]{:S(2)}, u32[]{:S(2)}) collective-permute-start(f32[49,16,128]{2,1,0:T(8,128)} %get-tuple-element.107), channel_id=1, source_target_pairs={{0,24},{4,28},{8,0},{12,4},{16,8},{20,12},{24,16},{28,20},{1,25},{... | collective-permute-start | bytes 1204232 | tf_op jit(solution)/shard_map/ppermute | solution.py:1343
  188.7 62.9 %collective-permute-start.6 = (f32[49,16,128]{2,1,0:T(8,128)}, f32[49,16,128]{2,1,0:T(8,128)}, u32[]{:S(2)}, u32[]{:S(2)}) collective-permute-start(f32[49,16,128]{2,1,0:T(8,128)} %get-tuple-element.108), channel_id=1, source_target_pairs={{0,28},{4,0},{8,4},{12,8},{16,12},{20,16},{24,20},{28,24},{1,29},{... | collective-permute-start | bytes 1204232 | tf_op jit(solution)/shard_map/ppermute | solution.py:1343
  293.8 45.5 %all-to-all-start.3 = ((f32[8,28,16,128]{3,2,1,0:T(8,128)}), f32[8,28,16,128]{3,2,1,0:T(8,128)}, u32[]{:S(2)}, u32[]{:S(2)}) async-start(f32[8,28,16,128]{3,2,1,0:T(8,128)} %get-tuple-element.145), calls=%async_computation.3 | async-start | bytes 3670016 | tf_op jit(solution)/shard_map/all_to_all | solution.py:1334
  339.3 7.0 %copy-start.14 = (f32[140,8,128]{2,1,0:T(8,128)S(1)}, f32[140,8,128]{2,1,0:T(8,128)}, u32[]{:S(2)}) copy-start(f32[140,8,128]{2,1,0:T(8,128)} %get-tuple-element.148) | copy-start | bytes 1720324
  339.3 238.8 %all-to-all-start.2 = ((f32[8,98,8,128]{3,2,1,0:T(8,128)}), f32[8,98,8,128]{3,2,1,0:T(8,128)}, u32[]{:S(2)}, u32[]{:S(2)}) async-start(f32[8,98,8,128]{3,2,1,0:T(8,128)} %get-tuple-element.138), calls=%async_computation.2 | async-start | bytes 6422528 | tf_op jit(solution)/shard_map/all_to_all | solution.py:1334
  345.0 65.4 %collective-permute-start.7 = (f32[140,8,128]{2,1,0:T(8,128)S(1)}, f32[140,8,128]{2,1,0:T(8,128)S(1)}, u32[]{:S(2)}, u32[]{:S(2)}) collective-permute-start(f32[140,8,128]{2,1,0:T(8,128)S(1)} %copy-done.13), channel_id=1, source_target_pairs={{0,4},{4,8},{8,12},{12,16},{16,20},{20,24},{24,28},{28,0},{1,5},{5... | collective-permute-start | bytes 1720328 | tf_op jit(solution)/shard_map/ppermute | solution.py:1377
  346.2 130.6 %collective-permute-start.8 = (f32[140,8,128]{2,1,0:T(8,128)S(1)}, f32[140,8,128]{2,1,0:T(8,128)S(1)}, u32[]{:S(2)}, u32[]{:S(2)}) collective-permute-start(f32[140,8,128]{2,1,0:T(8,128)S(1)} %copy-done.14), channel_id=1, source_target_pairs={{0,8},{4,12},{8,16},{12,20},{16,24},{20,28},{24,0},{28,4},{1,9},{5... | collective-permute-start | bytes 1720328 | tf_op jit(solution)/shard_map/ppermute | solution.py:1377
  347.4 141.8 %collective-permute-start.9 = (f32[140,8,128]{2,1,0:T(8,128)}, f32[140,8,128]{2,1,0:T(8,128)}, u32[]{:S(2)}, u32[]{:S(2)}) collective-permute-start(f32[140,8,128]{2,1,0:T(8,128)} %get-tuple-element.149), channel_id=1, source_target_pairs={{0,12},{4,16},{8,20},{12,24},{16,28},{20,0},{24,4},{28,8},{1,13},{... | collective-permute-start | bytes 1720328 | tf_op jit(solution)/shard_map/ppermute | solution.py:1377
  348.4 153.1 %collective-permute-start.10 = (f32[140,8,128]{2,1,0:T(8,128)}, f32[140,8,128]{2,1,0:T(8,128)}, u32[]{:S(2)}, u32[]{:S(2)}) collective-permute-start(f32[140,8,128]{2,1,0:T(8,128)} %get-tuple-element.150), channel_id=1, source_target_pairs={{0,16},{4,20},{8,24},{12,28},{16,0},{20,4},{24,8},{28,12},{1,17},{... | collective-permute-start | bytes 1720328 | tf_op jit(solution)/shard_map/ppermute | solution.py:1377
  350.7 163.1 %collective-permute-start.11 = (f32[140,8,128]{2,1,0:T(8,128)}, f32[140,8,128]{2,1,0:T(8,128)}, u32[]{:S(2)}, u32[]{:S(2)}) collective-permute-start(f32[140,8,128]{2,1,0:T(8,128)} %get-tuple-element.151), channel_id=1, source_target_pairs={{0,20},{4,24},{8,28},{12,0},{16,4},{20,8},{24,12},{28,16},{1,21},{... | collective-permute-start | bytes 1720328 | tf_op jit(solution)/shard_map/ppermute | solution.py:1377
  410.4 66.4 %copy-start.15 = (f32[140,8,128]{2,1,0:T(8,128)}, f32[140,8,128]{2,1,0:T(8,128)S(1)}, u32[]{:S(2)}) copy-start(f32[140,8,128]{2,1,0:T(8,128)S(1)} %collective-permute-done.7.refs_1_) | copy-start | bytes 1720324
  410.4 103.4 %collective-permute-start.12 = (f32[140,8,128]{2,1,0:T(8,128)}, f32[140,8,128]{2,1,0:T(8,128)}, u32[]{:S(2)}, u32[]{:S(2)}) collective-permute-start(f32[140,8,128]{2,1,0:T(8,128)} %get-tuple-element.152), channel_id=1, source_target_pairs={{0,24},{4,28},{8,0},{12,4},{16,8},{20,12},{24,16},{28,20},{1,25},{... | collective-permute-start | bytes 1720328 | tf_op jit(solution)/shard_map/ppermute | solution.py:1377
  477.7 37.7 %collective-permute-start.13 = (f32[140,8,128]{2,1,0:T(8,128)}, f32[140,8,128]{2,1,0:T(8,128)}, u32[]{:S(2)}, u32[]{:S(2)}) collective-permute-start(f32[140,8,128]{2,1,0:T(8,128)} %get-tuple-element.153), channel_id=1, source_target_pairs={{0,28},{4,0},{8,4},{12,8},{16,12},{20,16},{24,20},{28,24},{1,29},{... | collective-permute-start | bytes 1720328 | tf_op jit(solution)/shard_map/ppermute | solution.py:1377
  537.9 7.9 %copy-start.3 = (f32[784,128]{1,0:T(8,128)S(1)}, f32[784,128]{1,0:T(8,128)}, u32[]{:S(2)}) copy-start(f32[784,128]{1,0:T(8,128)} %reshape.82.g_ref) | copy-start | bytes 1204228
  537.9 7.9 %copy-start.10 = (f32[2,8,128]{2,1,0:T(8,128)S(1)}, f32[2,8,128]{2,1,0:T(8,128)}, u32[]{:S(2)}) copy-start(f32[2,8,128]{2,1,0:T(8,128)} %broadcast_in_dim.54.k_ref) | copy-start | bytes 24580
  540.9 2.6 collective-permute-start.14
  542.7 3.1 collective-permute-start.15
  545.8 22.1 %slice-start = ((s8[4587520]{0:T(1024)(128)(4,1)}), s8[4194304]{0:T(1024)(128)(4,1)S(1)}, s32[]{:S(2)}) async-start(s8[4587520]{0:T(1024)(128)(4,1)} %bitcast.45), calls=%async_computation.4 | async-start | bytes 8388608
  549.5 1.2 collective-permute-start.16
  549.6 2.5 collective-permute-start.18
  549.9 3.4 collective-permute-start.17
  553.3 14.6 %slice-start.1 = ((s8[4587520]{0:T(1024)(128)(4,1)}), s8[393216]{0:T(1024)(128)(4,1)S(1)}, s32[]{:S(2)}) async-start(s8[4587520]{0:T(1024)(128)(4,1)} %bitcast.45), calls=%async_computation.5 | async-start | bytes 786432
  557.4 1.8 collective-permute-start.19
  558.0 2.5 collective-permute-start.21
  559.2 3.1 collective-permute-start.20
  565.9 10.0 %collective-permute-start.24 = (f32[2,8,128]{2,1,0:T(8,128)S(1)}, f32[2,8,128]{2,1,0:T(8,128)S(1)}, u32[]{:S(2)}, u32[]{:S(2)}) collective-permute-start(f32[2,8,128]{2,1,0:T(8,128)S(1)} %get-tuple-element.171.own), channel_id=1, source_target_pairs={{0,2},{1,3},{2,0},{3,1},{4,6},{5,7},{6,4},{7,5},{8,10},{9,11},{10,... | collective-permute-start | bytes 24584 | tf_op jit(solution)/shard_map/ppermute | solution.py:1010
  566.2 9.7 %collective-permute-start.23 = (f32[2,8,128]{2,1,0:T(8,128)S(1)}, f32[2,8,128]{2,1,0:T(8,128)S(1)}, u32[]{:S(2)}, u32[]{:S(2)}) collective-permute-start(f32[2,8,128]{2,1,0:T(8,128)S(1)} %get-tuple-element.171.own), channel_id=1, source_target_pairs={{1,0},{2,1},{3,2},{0,3},{5,4},{6,5},{7,6},{4,7},{9,8},{10,9},{11,1... | collective-permute-start | bytes 24584 | tf_op jit(solution)/shard_map/ppermute | solution.py:1005
  566.4 9.5 %collective-permute-start.22 = (f32[2,8,128]{2,1,0:T(8,128)S(1)}, f32[2,8,128]{2,1,0:T(8,128)S(1)}, u32[]{:S(2)}, u32[]{:S(2)}) collective-permute-start(f32[2,8,128]{2,1,0:T(8,128)S(1)} %get-tuple-element.171.own), channel_id=1, source_target_pairs={{0,1},{1,2},{2,3},{3,0},{4,5},{5,6},{6,7},{7,4},{8,9},{9,10},{10,1... | collective-permute-start | bytes 24584 | tf_op jit(solution)/shard_map/ppermute | solution.py:1005
  579.3 7.6 %copy-start.4 = (f32[784,128]{1,0:T(8,128)S(1)}, f32[784,128]{1,0:T(8,128)}, u32[]{:S(2)}) copy-start(f32[784,128]{1,0:T(8,128)} %reshape.82.g_ref) | copy-start | bytes 1204228
  579.3 7.6 %copy-start.9 = (f32[2,8,128]{2,1,0:T(8,128)S(1)}, f32[2,8,128]{2,1,0:T(8,128)}, u32[]{:S(2)}) copy-start(f32[2,8,128]{2,1,0:T(8,128)} %broadcast_in_dim.56.k_ref) | copy-start | bytes 24580
  583.7 1.2 collective-permute-start.25
  583.7 3.1 collective-permute-start.26
  590.5 2.0 collective-permute-start.27
  590.6 2.5 collective-permute-start.29
  591.9 3.1 collective-permute-start.28
  599.0 1.7 collective-permute-start.30
  599.9 2.8 collective-permute-start.32
  600.2 3.1 collective-permute-start.31
  606.9 10.2 %collective-permute-start.35 = (f32[2,8,128]{2,1,0:T(8,128)S(1)}, f32[2,8,128]{2,1,0:T(8,128)S(1)}, u32[]{:S(2)}, u32[]{:S(2)}) collective-permute-start(f32[2,8,128]{2,1,0:T(8,128)S(1)} %get-tuple-element.191.own), channel_id=1, source_target_pairs={{0,2},{1,3},{2,0},{3,1},{4,6},{5,7},{6,4},{7,5},{8,10},{9,11},{10,... | collective-permute-start | bytes 24584 | tf_op jit(solution)/shard_map/ppermute | solution.py:1010
  608.2 9.0 %collective-permute-start.34 = (f32[2,8,128]{2,1,0:T(8,128)S(1)}, f32[2,8,128]{2,1,0:T(8,128)S(1)}, u32[]{:S(2)}, u32[]{:S(2)}) collective-permute-start(f32[2,8,128]{2,1,0:T(8,128)S(1)} %get-tuple-element.191.own), channel_id=1, source_target_pairs={{1,0},{2,1},{3,2},{0,3},{5,4},{6,5},{7,6},{4,7},{9,8},{10,9},{11,1... | collective-permute-start | bytes 24584 | tf_op jit(solution)/shard_map/ppermute | solution.py:1005
  608.2 9.0 %collective-permute-start.33 = (f32[2,8,128]{2,1,0:T(8,128)S(1)}, f32[2,8,128]{2,1,0:T(8,128)S(1)}, u32[]{:S(2)}, u32[]{:S(2)}) collective-permute-start(f32[2,8,128]{2,1,0:T(8,128)S(1)} %get-tuple-element.191.own), channel_id=1, source_target_pairs={{0,1},{1,2},{2,3},{3,0},{4,5},{5,6},{6,7},{7,4},{8,9},{9,10},{10,1... | collective-permute-start | bytes 24584 | tf_op jit(solution)/shard_map/ppermute | solution.py:1005
  (21 other events, 52.6 us)

commit v9 on v8

--- a/solution.py
+++ b/solution.py
@@ -944,12 +944,12 @@
                 ns = [a * NODES + b for b in range(NODES)]
                 line = apply_line(table, [r1[h, n] for n in ns])
                 for b, n in enumerate(ns):
-                    side[n] = side[n] + metric(3, n) * line[b]
+                    side[n] = side[n] + metric(1, n) * line[b]
             for b in range(NODES):
                 ns = [a * NODES + b for a in range(NODES)]
                 line = apply_line(table, [r1[h, n] for n in ns])
                 for a, n in enumerate(ns):
-                    side[n] = side[n] + metric(1, n) * line[a]
+                    side[n] = side[n] + metric(0, n) * line[a]
         rims = [[first_ref[0], last_ref[0]], [first_ref[1], last_ref[1]]]
         for n in range(square):
             left, right = (c0[n], c1[n])
@@ -1318,6 +1318,8 @@
     scaled = halves((metrics[3] * (-1.0 / time_step)).reshape(1, layers, square, lanes), modes)
     flux = (both * scaled).reshape(4 * modes * square, lanes)
     small_flux = flux * time_step
+    part = modes * square
+    side_flux = jnp.concatenate([small_flux[part : 2 * part], small_flux[3 * part :]])
     scaled = scaled.reshape(modes * square, lanes)
     turned = lax.optimization_barrier(backward).reshape(2, modes, pairs, -1)
     turned = jnp.roll(turned, -mode, axis=1).reshape(backward.shape)
@@ -1341,9 +1343,9 @@
     sent_1, late_2, sent_2, sent_0 = pack_rest(rows, layers, pairs, lanes, some)
     for k in range(1, modes):
         strips[k] = lax.ppermute(strips[k], "mode", [(i, (i + k) % modes) for i in range(modes)])
-    sent_1, here, geo, flux, small_flux, scaled, waves, small_waves, shift, turned = (
+    sent_1, here, geo, flux, small_flux, side_flux, scaled, waves, small_waves, shift, turned = (
         lax.optimization_barrier(
-            (sent_1, here, geo, flux, small_flux, scaled, waves, small_waves, shift, turned)
+            (sent_1, here, geo, flux, small_flux, side_flux, scaled, waves, small_waves, shift, turned)
         )
     )
     arrived_1 = exchange(sent_1)
@@ -1416,7 +1418,7 @@
 
     def solve(place, flat, own_shift, buffer):
         raw, first, last = right_side(
-            flat, returned[place], small_flux, scaled, small_waves, table, layers, place
+            flat, returned[place], side_flux, scaled, small_waves, table, layers, place
         )
         before, after = swap_rims(first, last)
         start, image, first, last = first_image(raw, before, after, own_shift, geo, layers, table)

time: 622 us -> 624 us (level)
  no operation moved by 1% of the time
where the time goes in v9:
time: 624 us; the launch traced here: 621 us
  waiting for transfers between devices  255 us (41%)
  Pallas kernels  168 us (27%)
  blocking collectives  116 us (19%)
  starting transfers between devices  53.1 us (9%)
  local copies, waits for them, and re-layouts  19.8 us (3%)
  other arithmetic  8.07 us (1%)
    ppermute x7, waiting for transfers between devices, paired_step(): lax.ppermute(home_strips[k], 'mode', [(i, (i + k) % modes) for i in range...  150 us
    all_to_all x1, blocking collectives, exchange(): lax.all_to_all(blocks, 'mode', split_axis=0, concat_axis=0, tiled=True)  116 us
    ppermute x7, waiting for transfers between devices, paired_step(): lax.ppermute(strips[k], 'mode', [(i, (i + k) % modes) for i in range(mode...  81.3 us
    pallas_call x2, Pallas kernels, to_points(): call(body, (NODES,), [whole(table.shape), pl.BlockSpec((shares, NODES, pa...  19.7 us
    pallas_call x2, Pallas kernels, to_planes(): call(body, (NODES,), [pl.BlockSpec(memory_space=pltpu.SMEM), whole(table....  19.3 us
    pallas_call x2, Pallas kernels, in_plane(): call(body, (rows // step,), [whole(metrics.shape)] + [spec] * len(arrays)...  16 us
    pallas_call x2, Pallas kernels, turn_around(): call(body, (count,), [whole(table.shape), whole(back.shape), pl.BlockSpec...  15.7 us
    all_to_all x3, starting transfers between devices, exchange(): lax.all_to_all(blocks, 'mode', split_axis=0, concat_axis=0, tiled=True)  15.4 us
  transfers between devices with their start and end apart: 39, of which 27 were waited for; matrix products, arithmetic and copies ran while one was open for 0% of the time, Pallas kernels for 22%

profile of v9, /device:TPU:9, one launch (start us, length us, event | category | flops | bytes accessed | tf_op | source)
XLA Modules:
  0.0 621.0 jit_solution(1519528665215033077)
XLA Ops:
  12.4 11.4 %shard_map.104 = (f32[8,77,16,128]{3,2,1,0:T(8,128)}, f32[8,21,16,128]{3,2,1,0:T(8,128)}, f32[8,49,16,128]{3,2,1,0:T(8,128)}, f32[8,49,16,128]{3,2,1,0:T(8,128)}) custom-call(f32[3,6272,128]{2,1,0:T(8,128)} %bitcast.47, f32[3,6272,128]{2,1,0:T(8,128)} %bitcast.48, f32[3,6272,128]{2,1,0:T(8,128)} %bitcast.49), custom_call_target="tpu_custom_call" | custom-call | bytes 16056320 | tf_op jit(solution)/shard_map/pallas_call | solution.py:469
  31.4 116.0 %all_to_all.20.x_ref = f32[8,77,16,128]{3,2,1,0:T(8,128)} all-to-all(f32[8,77,16,128]{3,2,1,0:T(8,128)} %get-tuple-element.111.s1), channel_id=1, replica_groups=mesh['mode'=8,'elem'=4] {'mode'}, dimensions={0} | all-to-all | bytes 10092544 | tf_op jit(solution)/shard_map/all_to_all | solution.py:1336
  147.4 5.1 all-to-all-start.1
  152.5 5.2 shard_map.105
  161.1 2.2 collective-permute-start.3
  164.5 19.2 %collective-permute-done.refs_1_ = f32[49,16,128]{2,1,0:T(8,128)} collective-permute-done((f32[49,16,128]{2,1,0:T(8,128)}, f32[49,16,128]{2,1,0:T(8,128)}, u32[]{:S(2)}, u32[]{:S(2)}) %collective-permute-start) | collective-permute-done | bytes 401440 | tf_op jit(solution)/shard_map/ppermute | solution.py:1345
  183.7 3.0 collective-permute-start.5
  186.7 3.9 collective-permute-done.1.refs_2_
  190.6 4.7 collective-permute-start.6
  195.3 38.4 %collective-permute-done.2.refs_3_ = f32[49,16,128]{2,1,0:T(8,128)} collective-permute-done((f32[49,16,128]{2,1,0:T(8,128)}, f32[49,16,128]{2,1,0:T(8,128)}, u32[]{:S(2)}, u32[]{:S(2)}) %collective-permute-start.2) | collective-permute-done | bytes 401440 | tf_op jit(solution)/shard_map/ppermute | solution.py:1345
  233.8 8.6 %collective-permute-done.3.refs_4_ = f32[49,16,128]{2,1,0:T(8,128)} collective-permute-done((f32[49,16,128]{2,1,0:T(8,128)}, f32[49,16,128]{2,1,0:T(8,128)}, u32[]{:S(2)}, u32[]{:S(2)}) %collective-permute-start.3) | collective-permute-done | bytes 401440 | tf_op jit(solution)/shard_map/ppermute | solution.py:1345
  242.4 8.6 %collective-permute-done.4.refs_5_ = f32[49,16,128]{2,1,0:T(8,128)} collective-permute-done((f32[49,16,128]{2,1,0:T(8,128)}, f32[49,16,128]{2,1,0:T(8,128)}, u32[]{:S(2)}, u32[]{:S(2)}) %collective-permute-start.4) | collective-permute-done | bytes 401440 | tf_op jit(solution)/shard_map/ppermute | solution.py:1345
  251.0 2.5 collective-permute-done.6.refs_7_
  253.5 5.7 shard_map.106.x_ref
  259.2 9.9 %shard_map.107 = (f32[49,128,128]{2,1,0:T(8,128)}, f32[49,128,128]{2,1,0:T(8,128)}) custom-call(bf16[512,768]{1,0:T(8,128)(2,1)} %constant.78.clone.t_ref, f32[8,49,16,128]{3,2,1,0:T(8,128)} %shard_map.106.x_ref), custom_call_target="tpu_custom_call" | custom-call | flops 4932501504 | bytes 9633792 | tf_op jit(solution)/shard_map/pallas_call | solution.py:582
  269.1 9.8 %shard_map.108 = (f32[49,128,128]{2,1,0:T(8,128)}, f32[49,128,128]{2,1,0:T(8,128)}) custom-call(bf16[512,768]{1,0:T(8,128)(2,1)} %constant.78.clone.t_ref, f32[8,77,16,128]{3,2,1,0:T(8,128)} %all_to_all.20.x_ref), custom_call_target="tpu_custom_call" | custom-call | flops 4932501504 | bytes 9633792 | tf_op jit(solution)/shard_map/pallas_call | solution.py:582
  278.9 8.5 %shard_map.109 = (f32[49,128,128]{2,1,0:T(8,128)}, f32[49,128,128]{2,1,0:T(8,128)}) custom-call(f32[196,128]{1,0:T(8,128)} %reshape.81.m_ref, f32[49,128,128]{2,1,0:T(8,128)} %get-tuple-element.110.refs_0_, f32[49,128,128]{2,1,0:T(8,128)} %get-tuple-element.112.refs_1_), custom_call_target="tpu_custom_call" | custom-call | flops 48168960 | bytes 12845056 | tf_op jit(solution)/shard_map/pallas_call | solution.py:701
  287.4 8.4 %shard_map.110 = (f32[49,128,128]{2,1,0:T(8,128)}, f32[49,128,128]{2,1,0:T(8,128)}, f32[8,28,16,128]{3,2,1,0:T(8,128)}) custom-call(bf16[512,768]{1,0:T(8,128)(2,1)} %constant.78.clone.t_ref, bf16[256,768]{1,0:T(8,128)(2,1)} %constant.79.clone.i_ref, f32[8,77,16,128]{3,2,1,0:T(8,128)} %all_to_all.20.x_ref, f32[49,128,128]{2,1,0:T(8,128)} %get-tuple-element.114.g_ref, ...), custom_call_target="tpu_custom_call" | custom-call | flops 4227858432 | bytes 11010048 | tf_op jit(solution)/shard_map/pallas_call | solution.py:631
  295.8 4.6 all-to-all-start.3
  300.3 7.3 %shard_map.111 = (f32[49,128,128]{2,1,0:T(8,128)}, f32[49,128,128]{2,1,0:T(8,128)}, f32[140,8,128]{2,1,0:T(8,128)}, f32[140,8,128]{2,1,0:T(8,128)}, f32[140,8,12...) custom-call(bf16[512,768]{1,0:T(8,128)(2,1)} %constant.78.clone.t_re, ...), custom_call_target="tpu_custom_call", output_to_operand_aliasing={{0}: (5, {}), {1}: (6, {})} | custom-call | flops 3170893824 | bytes 8257536 | tf_op jit(solution)/shard_map/pallas_call | solution.py:631
  307.6 7.5 %shard_map.112.g_ref = f32[49,128,128]{2,1,0:T(8,128)} custom-call(f32[196,128]{1,0:T(8,128)} %reshape.81.m_ref, f32[49,128,128]{2,1,0:T(8,128)} %get-tuple-element.110.refs_0_, f32[49,128,128]{2,1,0:T(8,128)} %get-tuple-element.112.refs_1_, f32[49,128,128]{2,1,0:T(8,128)} %get-tuple-element.118.refs_2_.w_ref), custom_call_target="tpu_custom_call" | custom-call | flops 24084480 | bytes 12845056 | tf_op jit(solution)/shard_map/pallas_call | solution.py:701
  315.2 9.7 %shard_map.113 = (f32[140,8,128]{2,1,0:T(8,128)}, f32[140,8,128]{2,1,0:T(8,128)}, f32[140,8,128]{2,1,0:T(8,128)}, f32[140,8,128]{2,1,0:T(8,128)}, f32[140,8,128]...) custom-call(s32[1]{0:T(128)} %bitcast.place_ref, ...), custom_call_target="tpu_custom_call", output_to_operand_aliasing={{0}: (5, {}), {1}: (6, {}), {2}: (7, {}), {3}: (8, {}), {4}... | custom-call | flops 2466250752 | bytes 12845056 | tf_op jit(solution)/shard_map/pallas_call | solution.py:756
  324.8 9.7 %shard_map.114 = (f32[140,8,128]{2,1,0:T(8,128)}, f32[140,8,128]{2,1,0:T(8,128)}, f32[140,8,128]{2,1,0:T(8,128)}, f32[140,8,128]{2,1,0:T(8,128)}, f32[140,8,128]...) custom-call(s32[1]{0:T(128)} %bitcast.place_ref, ...), custom_call_target="tpu_custom_call", output_to_operand_aliasing={{0}: (5, {}), {1}: (6, {}), {2}: (7, {}), {3}: (8, {}), {4}... | custom-call | flops 2466250752 | bytes 12845056 | tf_op jit(solution)/shard_map/pallas_call | solution.py:756
  334.5 6.7 %all-to-all-done.3.r0.refs_0_ = f32[8,28,16,128]{3,2,1,0:T(8,128)} async-done(((f32[8,28,16,128]{3,2,1,0:T(8,128)}), f32[8,28,16,128]{3,2,1,0:T(8,128)}, u32[]{:S(2)}, u32[]{:S(2)}) %all-to-all-start.3) | async-done | bytes 1835040 | tf_op jit(solution)/shard_map/all_to_all | solution.py:1336
  341.2 5.8 all-to-all-start.2
  350.3 2.3 collective-permute-start.10
  353.8 58.6 %collective-permute-done.7.refs_1_ = f32[140,8,128]{2,1,0:T(8,128)S(1)} collective-permute-done((f32[140,8,128]{2,1,0:T(8,128)S(1)}, f32[140,8,128]{2,1,0:T(8,128)S(1)}, u32[]{:S(2)}, u32[]{:S(2)}) %collective-permute-start.7) | collective-permute-done | bytes 573472 | tf_op jit(solution)/shard_map/ppermute | solution.py:1379
  412.4 2.4 collective-permute-start.12
  414.8 64.0 %collective-permute-done.8.refs_2_ = f32[140,8,128]{2,1,0:T(8,128)S(1)} collective-permute-done((f32[140,8,128]{2,1,0:T(8,128)S(1)}, f32[140,8,128]{2,1,0:T(8,128)S(1)}, u32[]{:S(2)}, u32[]{:S(2)}) %collective-permute-start.8) | collective-permute-done | bytes 573472 | tf_op jit(solution)/shard_map/ppermute | solution.py:1379
  479.6 10.0 %shard_map.115.s0 = f32[8,49,16,128]{3,2,1,0:T(8,128)} custom-call(f32[1568,128]{1,0:T(8,128)} %get-tuple-element.141.m_ref, f32[392,128]{1,0:T(8,128)} %reshape_reshape.4.q_ref, f32[16,128]{1,0:T(8,128)} %get-tuple-element.143.k_ref, f32[8,49,16,128]{3,2,1,0:T(8,128)} %get-tuple-element.144.s0, f32[8,77,16,128]{3,2,1,0:T(8,128)} %get-tuple-element.111.s1, ...), custom_call_target="tpu_custom_call" | custom-call | flops 48168960 | bytes 12845056 | tf_op jit(solution)/shard_map/pallas_call | solution.py:810
  491.2 12.3 %collective-permute-done.10.refs_4_ = f32[140,8,128]{2,1,0:T(8,128)} collective-permute-done((f32[140,8,128]{2,1,0:T(8,128)}, f32[140,8,128]{2,1,0:T(8,128)}, u32[]{:S(2)}, u32[]{:S(2)}) %collective-permute-start.10) | collective-permute-done | bytes 573472 | tf_op jit(solution)/shard_map/ppermute | solution.py:1379
  503.5 12.3 %collective-permute-done.11.refs_5_ = f32[140,8,128]{2,1,0:T(8,128)} collective-permute-done((f32[140,8,128]{2,1,0:T(8,128)}, f32[140,8,128]{2,1,0:T(8,128)}, u32[]{:S(2)}, u32[]{:S(2)}) %collective-permute-start.11) | collective-permute-done | bytes 573472 | tf_op jit(solution)/shard_map/ppermute | solution.py:1379
  517.3 7.5 %shard_map.116.refs_0_.refs_1_.refs_2_.r1.r2.refs_3_ = f32[8,140,8,128]{3,2,1,0:T(8,128)} custom-call(s32[1]{0:T(128)} %bitcast.place_ref, f32[140,8,128]{2,1,0:T(8,128)} %get-tuple-element.147.refs_0_, f32[140,8,128]{2,1,0:T(8,128)} %copy-done.16, f32[140,8,128]{2,1,0:T(8,128)} %copy-done.17, f32[140,8,128]{2,1,0:T(8,128)} %collective-permute-done.9.refs_3_, ...), custom_call_target="tpu_custom_call" | custom-call | bytes 9175040 | tf_op jit(solution)/shard_map/pallas_call | solution.py:726
  524.8 8.1 %shard_map.117.f_ref = f32[8,49,16,128]{3,2,1,0:T(8,128)} custom-call(f32[1568,128]{1,0:T(8,128)} %copy-done.13, f32[8,49,16,128]{3,2,1,0:T(8,128)} %shard_map.115.s0, f32[8,28,16,128]{3,2,1,0:T(8,128)} %all-to-all-done.3.r0.refs_0_, f32[8,140,8,128]{3,2,1,0:T(8,128)} %shard_map.116.refs_0_.refs_1_.refs_2_.r1.r2.refs_3_, ...), custom_call_target="tpu_custom_call" | custom-call | flops 24084480 | bytes 9633792 | tf_op jit(solution)/shard_map/pallas_call | solution.py:861
  532.9 2.3 copy-done
  539.7 2.9 shard_map.118
  545.4 2.3 collective-permute-done.15.a_ref
  547.6 3.7 shard_map.119
  555.2 4.0 shard_map.120
  564.1 3.6 shard_map.121
  569.8 4.4 shard_map.123.refs_1_
  574.2 3.5 shard_map.124.refs_1_
  580.9 4.4 shard_map.127
  588.5 3.7 shard_map.128
  596.7 4.0 shard_map.129
  605.0 3.6 shard_map.130
  611.6 3.6 shard_map.125.refs_1_
  615.2 3.6 shard_map.126
  (146 shorter events, 70.4 us)
Async XLA Ops:
  147.4 148.4 %all-to-all-start.1 = ((f32[8,21,16,128]{3,2,1,0:T(8,128)}), f32[8,21,16,128]{3,2,1,0:T(8,128)}, u32[]{:S(2)}, u32[]{:S(2)}) async-start(f32[8,21,16,128]{3,2,1,0:T(8,128)} %get-tuple-element.113), calls=%async_computation.1 | async-start | bytes 2752512 | tf_op jit(solution)/shard_map/all_to_all | solution.py:1336
  157.7 26.0 %collective-permute-start = (f32[49,16,128]{2,1,0:T(8,128)}, f32[49,16,128]{2,1,0:T(8,128)}, u32[]{:S(2)}, u32[]{:S(2)}) collective-permute-start(f32[49,16,128]{2,1,0:T(8,128)} %get-tuple-element.103), channel_id=1, source_target_pairs={{0,4},{4,8},{8,12},{12,16},{16,20},{20,24},{24,28},{28,0},{1,5},{5... | collective-permute-start | bytes 1204232 | tf_op jit(solution)/shard_map/ppermute | solution.py:1345
  158.9 31.8 %collective-permute-start.1 = (f32[49,16,128]{2,1,0:T(8,128)}, f32[49,16,128]{2,1,0:T(8,128)}, u32[]{:S(2)}, u32[]{:S(2)}) collective-permute-start(f32[49,16,128]{2,1,0:T(8,128)} %get-tuple-element.104), channel_id=1, source_target_pairs={{0,8},{4,12},{8,16},{12,20},{16,24},{20,28},{24,0},{28,4},{1,9},{5... | collective-permute-start | bytes 1204232 | tf_op jit(solution)/shard_map/ppermute | solution.py:1345
  160.1 73.7 %collective-permute-start.2 = (f32[49,16,128]{2,1,0:T(8,128)}, f32[49,16,128]{2,1,0:T(8,128)}, u32[]{:S(2)}, u32[]{:S(2)}) collective-permute-start(f32[49,16,128]{2,1,0:T(8,128)} %get-tuple-element.105), channel_id=1, source_target_pairs={{0,12},{4,16},{8,20},{12,24},{16,28},{20,0},{24,4},{28,8},{1,13},{... | collective-permute-start | bytes 1204232 | tf_op jit(solution)/shard_map/ppermute | solution.py:1345
  161.1 81.3 %collective-permute-start.3 = (f32[49,16,128]{2,1,0:T(8,128)}, f32[49,16,128]{2,1,0:T(8,128)}, u32[]{:S(2)}, u32[]{:S(2)}) collective-permute-start(f32[49,16,128]{2,1,0:T(8,128)} %get-tuple-element.106), channel_id=1, source_target_pairs={{0,16},{4,20},{8,24},{12,28},{16,0},{20,4},{24,8},{28,12},{1,17},{... | collective-permute-start | bytes 1204232 | tf_op jit(solution)/shard_map/ppermute | solution.py:1345
  163.3 87.7 %collective-permute-start.4 = (f32[49,16,128]{2,1,0:T(8,128)}, f32[49,16,128]{2,1,0:T(8,128)}, u32[]{:S(2)}, u32[]{:S(2)}) collective-permute-start(f32[49,16,128]{2,1,0:T(8,128)} %get-tuple-element.107), channel_id=1, source_target_pairs={{0,20},{4,24},{8,28},{12,0},{16,4},{20,8},{24,12},{28,16},{1,21},{... | collective-permute-start | bytes 1204232 | tf_op jit(solution)/shard_map/ppermute | solution.py:1345
  183.7 67.3 %collective-permute-start.5 = (f32[49,16,128]{2,1,0:T(8,128)}, f32[49,16,128]{2,1,0:T(8,128)}, u32[]{:S(2)}, u32[]{:S(2)}) collective-permute-start(f32[49,16,128]{2,1,0:T(8,128)} %get-tuple-element.108), channel_id=1, source_target_pairs={{0,24},{4,28},{8,0},{12,4},{16,8},{20,12},{24,16},{28,20},{1,25},{... | collective-permute-start | bytes 1204232 | tf_op jit(solution)/shard_map/ppermute | solution.py:1345
  190.6 62.9 %collective-permute-start.6 = (f32[49,16,128]{2,1,0:T(8,128)}, f32[49,16,128]{2,1,0:T(8,128)}, u32[]{:S(2)}, u32[]{:S(2)}) collective-permute-start(f32[49,16,128]{2,1,0:T(8,128)} %get-tuple-element.109), channel_id=1, source_target_pairs={{0,28},{4,0},{8,4},{12,8},{16,12},{20,16},{24,20},{28,24},{1,29},{... | collective-permute-start | bytes 1204232 | tf_op jit(solution)/shard_map/ppermute | solution.py:1345
  295.8 45.5 %all-to-all-start.3 = ((f32[8,28,16,128]{3,2,1,0:T(8,128)}), f32[8,28,16,128]{3,2,1,0:T(8,128)}, u32[]{:S(2)}, u32[]{:S(2)}) async-start(f32[8,28,16,128]{3,2,1,0:T(8,128)} %get-tuple-element.146), calls=%async_computation.3 | async-start | bytes 3670016 | tf_op jit(solution)/shard_map/all_to_all | solution.py:1336
  341.2 5.8 copy-start.14
  341.2 7.0 %copy-start.15 = (f32[140,8,128]{2,1,0:T(8,128)S(1)}, f32[140,8,128]{2,1,0:T(8,128)}, u32[]{:S(2)}) copy-start(f32[140,8,128]{2,1,0:T(8,128)} %get-tuple-element.149) | copy-start | bytes 1720324
  341.2 238.7 %all-to-all-start.2 = ((f32[8,98,8,128]{3,2,1,0:T(8,128)}), f32[8,98,8,128]{3,2,1,0:T(8,128)}, u32[]{:S(2)}, u32[]{:S(2)}) async-start(f32[8,98,8,128]{3,2,1,0:T(8,128)} %get-tuple-element.139), calls=%async_computation.2 | async-start | bytes 6422528 | tf_op jit(solution)/shard_map/all_to_all | solution.py:1336
  347.0 65.4 %collective-permute-start.7 = (f32[140,8,128]{2,1,0:T(8,128)S(1)}, f32[140,8,128]{2,1,0:T(8,128)S(1)}, u32[]{:S(2)}, u32[]{:S(2)}) collective-permute-start(f32[140,8,128]{2,1,0:T(8,128)S(1)} %copy-done.14), channel_id=1, source_target_pairs={{0,4},{4,8},{8,12},{12,16},{16,20},{20,24},{24,28},{28,0},{1,5},{5... | collective-permute-start | bytes 1720328 | tf_op jit(solution)/shard_map/ppermute | solution.py:1379
  348.2 130.6 %collective-permute-start.8 = (f32[140,8,128]{2,1,0:T(8,128)S(1)}, f32[140,8,128]{2,1,0:T(8,128)S(1)}, u32[]{:S(2)}, u32[]{:S(2)}) collective-permute-start(f32[140,8,128]{2,1,0:T(8,128)S(1)} %copy-done.15), channel_id=1, source_target_pairs={{0,8},{4,12},{8,16},{12,20},{16,24},{20,28},{24,0},{28,4},{1,9},{5... | collective-permute-start | bytes 1720328 | tf_op jit(solution)/shard_map/ppermute | solution.py:1379
  349.4 141.8 %collective-permute-start.9 = (f32[140,8,128]{2,1,0:T(8,128)}, f32[140,8,128]{2,1,0:T(8,128)}, u32[]{:S(2)}, u32[]{:S(2)}) collective-permute-start(f32[140,8,128]{2,1,0:T(8,128)} %get-tuple-element.150), channel_id=1, source_target_pairs={{0,12},{4,16},{8,20},{12,24},{16,28},{20,0},{24,4},{28,8},{1,13},{... | collective-permute-start | bytes 1720328 | tf_op jit(solution)/shard_map/ppermute | solution.py:1379
  350.3 153.1 %collective-permute-start.10 = (f32[140,8,128]{2,1,0:T(8,128)}, f32[140,8,128]{2,1,0:T(8,128)}, u32[]{:S(2)}, u32[]{:S(2)}) collective-permute-start(f32[140,8,128]{2,1,0:T(8,128)} %get-tuple-element.151), channel_id=1, source_target_pairs={{0,16},{4,20},{8,24},{12,28},{16,0},{20,4},{24,8},{28,12},{1,17},{... | collective-permute-start | bytes 1720328 | tf_op jit(solution)/shard_map/ppermute | solution.py:1379
  352.6 163.1 %collective-permute-start.11 = (f32[140,8,128]{2,1,0:T(8,128)}, f32[140,8,128]{2,1,0:T(8,128)}, u32[]{:S(2)}, u32[]{:S(2)}) collective-permute-start(f32[140,8,128]{2,1,0:T(8,128)} %get-tuple-element.152), channel_id=1, source_target_pairs={{0,20},{4,24},{8,28},{12,0},{16,4},{20,8},{24,12},{28,16},{1,21},{... | collective-permute-start | bytes 1720328 | tf_op jit(solution)/shard_map/ppermute | solution.py:1379
  412.4 66.4 %copy-start.16 = (f32[140,8,128]{2,1,0:T(8,128)}, f32[140,8,128]{2,1,0:T(8,128)S(1)}, u32[]{:S(2)}) copy-start(f32[140,8,128]{2,1,0:T(8,128)S(1)} %collective-permute-done.7.refs_1_) | copy-start | bytes 1720324
  412.4 103.4 %collective-permute-start.12 = (f32[140,8,128]{2,1,0:T(8,128)}, f32[140,8,128]{2,1,0:T(8,128)}, u32[]{:S(2)}, u32[]{:S(2)}) collective-permute-start(f32[140,8,128]{2,1,0:T(8,128)} %get-tuple-element.153), channel_id=1, source_target_pairs={{0,24},{4,28},{8,0},{12,4},{16,8},{20,12},{24,16},{28,20},{1,25},{... | collective-permute-start | bytes 1720328 | tf_op jit(solution)/shard_map/ppermute | solution.py:1379
  479.6 37.7 %collective-permute-start.13 = (f32[140,8,128]{2,1,0:T(8,128)}, f32[140,8,128]{2,1,0:T(8,128)}, u32[]{:S(2)}, u32[]{:S(2)}) collective-permute-start(f32[140,8,128]{2,1,0:T(8,128)} %get-tuple-element.154), channel_id=1, source_target_pairs={{0,28},{4,0},{8,4},{12,8},{16,12},{20,16},{24,20},{28,24},{1,29},{... | collective-permute-start | bytes 1720328 | tf_op jit(solution)/shard_map/ppermute | solution.py:1379
  539.7 7.9 %copy-start.3 = (f32[784,128]{1,0:T(8,128)S(1)}, f32[784,128]{1,0:T(8,128)}, u32[]{:S(2)}) copy-start(f32[784,128]{1,0:T(8,128)} %reshape.82.g_ref) | copy-start | bytes 1204228
  539.7 7.9 %copy-start.10 = (f32[2,8,128]{2,1,0:T(8,128)S(1)}, f32[2,8,128]{2,1,0:T(8,128)}, u32[]{:S(2)}) copy-start(f32[2,8,128]{2,1,0:T(8,128)} %broadcast_in_dim.54.k_ref) | copy-start | bytes 24580
  542.7 2.7 collective-permute-start.14
  544.6 3.1 collective-permute-start.15
  547.6 22.1 %slice-start = ((s8[4587520]{0:T(1024)(128)(4,1)}), s8[4194304]{0:T(1024)(128)(4,1)S(1)}, s32[]{:S(2)}) async-start(s8[4587520]{0:T(1024)(128)(4,1)} %bitcast.45), calls=%async_computation.4 | async-start | bytes 8388608
  551.3 1.2 collective-permute-start.16
  551.4 2.5 collective-permute-start.18
  551.7 3.4 collective-permute-start.17
  555.2 14.6 %slice-start.1 = ((s8[4587520]{0:T(1024)(128)(4,1)}), s8[393216]{0:T(1024)(128)(4,1)S(1)}, s32[]{:S(2)}) async-start(s8[4587520]{0:T(1024)(128)(4,1)} %bitcast.45), calls=%async_computation.5 | async-start | bytes 786432
  559.2 1.8 collective-permute-start.19
  559.8 2.5 collective-permute-start.21
  561.0 3.1 collective-permute-start.20
  567.7 10.0 %collective-permute-start.24 = (f32[2,8,128]{2,1,0:T(8,128)S(1)}, f32[2,8,128]{2,1,0:T(8,128)S(1)}, u32[]{:S(2)}, u32[]{:S(2)}) collective-permute-start(f32[2,8,128]{2,1,0:T(8,128)S(1)} %get-tuple-element.173.own), channel_id=1, source_target_pairs={{0,2},{1,3},{2,0},{3,1},{4,6},{5,7},{6,4},{7,5},{8,10},{9,11},{10,... | collective-permute-start | bytes 24584 | tf_op jit(solution)/shard_map/ppermute | solution.py:1010
  568.0 9.7 %collective-permute-start.23 = (f32[2,8,128]{2,1,0:T(8,128)S(1)}, f32[2,8,128]{2,1,0:T(8,128)S(1)}, u32[]{:S(2)}, u32[]{:S(2)}) collective-permute-start(f32[2,8,128]{2,1,0:T(8,128)S(1)} %get-tuple-element.173.own), channel_id=1, source_target_pairs={{1,0},{2,1},{3,2},{0,3},{5,4},{6,5},{7,6},{4,7},{9,8},{10,9},{11,1... | collective-permute-start | bytes 24584 | tf_op jit(solution)/shard_map/ppermute | solution.py:1005
  568.3 9.5 %collective-permute-start.22 = (f32[2,8,128]{2,1,0:T(8,128)S(1)}, f32[2,8,128]{2,1,0:T(8,128)S(1)}, u32[]{:S(2)}, u32[]{:S(2)}) collective-permute-start(f32[2,8,128]{2,1,0:T(8,128)S(1)} %get-tuple-element.173.own), channel_id=1, source_target_pairs={{0,1},{1,2},{2,3},{3,0},{4,5},{5,6},{6,7},{7,4},{8,9},{9,10},{10,1... | collective-permute-start | bytes 24584 | tf_op jit(solution)/shard_map/ppermute | solution.py:1005
  580.9 7.6 %copy-start.4 = (f32[784,128]{1,0:T(8,128)S(1)}, f32[784,128]{1,0:T(8,128)}, u32[]{:S(2)}) copy-start(f32[784,128]{1,0:T(8,128)} %reshape.82.g_ref) | copy-start | bytes 1204228
  580.9 7.6 %copy-start.9 = (f32[2,8,128]{2,1,0:T(8,128)S(1)}, f32[2,8,128]{2,1,0:T(8,128)}, u32[]{:S(2)}) copy-start(f32[2,8,128]{2,1,0:T(8,128)} %broadcast_in_dim.56.k_ref) | copy-start | bytes 24580
  585.3 1.2 collective-permute-start.25
  585.4 3.1 collective-permute-start.26
  592.2 2.1 collective-permute-start.27
  592.3 2.5 collective-permute-start.29
  593.6 3.1 collective-permute-start.28
  600.7 1.7 collective-permute-start.30
  601.6 2.8 collective-permute-start.32
  601.9 3.1 collective-permute-start.31
  608.6 10.2 %collective-permute-start.35 = (f32[2,8,128]{2,1,0:T(8,128)S(1)}, f32[2,8,128]{2,1,0:T(8,128)S(1)}, u32[]{:S(2)}, u32[]{:S(2)}) collective-permute-start(f32[2,8,128]{2,1,0:T(8,128)S(1)} %get-tuple-element.193.own), channel_id=1, source_target_pairs={{0,2},{1,3},{2,0},{3,1},{4,6},{5,7},{6,4},{7,5},{8,10},{9,11},{10,... | collective-permute-start | bytes 24584 | tf_op jit(solution)/shard_map/ppermute | solution.py:1010
  609.9 9.0 %collective-permute-start.34 = (f32[2,8,128]{2,1,0:T(8,128)S(1)}, f32[2,8,128]{2,1,0:T(8,128)S(1)}, u32[]{:S(2)}, u32[]{:S(2)}) collective-permute-start(f32[2,8,128]{2,1,0:T(8,128)S(1)} %get-tuple-element.193.own), channel_id=1, source_target_pairs={{1,0},{2,1},{3,2},{0,3},{5,4},{6,5},{7,6},{4,7},{9,8},{10,9},{11,1... | collective-permute-start | bytes 24584 | tf_op jit(solution)/shard_map/ppermute | solution.py:1005
  609.9 9.0 %collective-permute-start.33 = (f32[2,8,128]{2,1,0:T(8,128)S(1)}, f32[2,8,128]{2,1,0:T(8,128)S(1)}, u32[]{:S(2)}, u32[]{:S(2)}) collective-permute-start(f32[2,8,128]{2,1,0:T(8,128)S(1)} %get-tuple-element.193.own), channel_id=1, source_target_pairs={{0,1},{1,2},{2,3},{3,0},{4,5},{5,6},{6,7},{7,4},{8,9},{9,10},{10,1... | collective-permute-start | bytes 24584 | tf_op jit(solution)/shard_map/ppermute | solution.py:1005
  (17 other events, 23.1 us)
